TPU v7x, 32 devices: a whole 2x2x4 slice. The times are simulated.
32 devices in a mesh: seq: 8 (over z, y), fsdp: 4 (over x, core).
Axes of the slice: x: 2, y: 2, z: 4, core: 2. Of those that a mesh axis runs over, the one named last changes fastest.
Arguments:
- tokens: bfloat16 [4, 2560, 1024], P('fsdp', 'seq'), may hold values from -6 to 6
- cotangent: bfloat16 [4, 2560, 1024], P('fsdp', 'seq'), may hold values from -6 to 6
- query_weight: bfloat16 [1024, 1024], P('fsdp'), may hold values from -0.25 to 0.25
- key_weight: bfloat16 [1024, 1024], P('fsdp'), may hold values from -0.1875 to 0.1875
- value_weight: bfloat16 [1024, 1024], P('fsdp'), may hold values from -0.1875 to 0.1875
- output_weight: bfloat16 [1024, 1024], P('fsdp'), may hold values from -3 to 3
- gate_weight: bfloat16 [1024, 2816], P('fsdp'), may hold values from -0.1875 to 0.1875
- up_weight: bfloat16 [1024, 2816], P('fsdp'), may hold values from -0.1875 to 0.1875
- down_weight: bfloat16 [2816, 1024], P('fsdp'), may hold values from -0.109375 to 0.109375
- attention_gain: bfloat16 [1024], P('fsdp'), may hold values from 0.099609375 to 1.8984375
- feedforward_gain: bfloat16 [1024], P('fsdp'), may hold values from 0.099609375 to 1.8984375
- lengths: int32 [4, 2], P('fsdp'), may hold values from 0 to 2560, as said below
- token_order: int32 [4, 2560], P('fsdp'), may hold values from 0 to 2559, each once within a row
- real_token: int32 [4, 2560], P('fsdp'), may hold values 0 or 1
Outputs:
- layer_out: bfloat16 [4, 2560, 1024], P('fsdp', 'seq')
- input_grad: float32 [4, 2560, 1024], P('fsdp', 'seq')
- query_grad: float32 [1024, 1024], P('fsdp')
- key_grad: float32 [1024, 1024], P('fsdp')
- value_grad: float32 [1024, 1024], P('fsdp')
- output_grad: float32 [1024, 1024], P('fsdp')
- gate_grad: float32 [1024, 2816], P('fsdp')
- up_grad: float32 [1024, 2816], P('fsdp')
- down_grad: float32 [2816, 1024], P('fsdp')
- attention_gain_grad: float32 [1024], P('fsdp')
- feedforward_gain_grad: float32 [1024], P('fsdp')
Inputs may be any that keep to these rules, and one draw needn't show every extreme that they name: Each row lists its sequences' lengths first, each 1024 or more, then zeros; a row's entries sum to 2560; in every draw some row is one sequence of 2560 tokens. `token_order`: each row is a permutation of the 2560 given positions of its group. `real_token`: 1 marks a real token, 0 padding.
All inputs are finite; a program needn't handle non-finite values. No bound on the sum of `real_token` on one device may be relied on, other than what follows from the above.
Results may differ from a plain program's by a relative error of at most 0.02.
Values may be sent and summed in bfloat16 or wider, within the bound.
No kernel may reach another device: no remote copies, remote signals or barrier semaphores. Data moves between devices by JAX's collectives and lax.ppermute only.
A program may use at most 192 MiB of HBM per device.

v0:
```python
import jax
import jax.numpy as jnp
from jax import lax
from jax.sharding import PartitionSpec as P

HD = 64


EPSILON = 1e-06
NEGATIVE_FILL = -1e30


def matmul(left_side, right_side):
    return jnp.dot(left_side, right_side, preferred_element_type=jnp.float32)


def outer_sum(left_side, right_side):
    return jnp.einsum("nd,ne->de", left_side, right_side, preferred_element_type=jnp.float32)


def back_product(left_side, right_side):
    return jnp.einsum("ne,de->nd", left_side, right_side, preferred_element_type=jnp.float32)


def normed(values):
    scaling = lax.rsqrt(jnp.mean(values * values, axis=-1, keepdims=True) + EPSILON)
    return (values * scaling, scaling)


def norm_back(incoming, values, scaling):
    centre = jnp.mean(incoming * values, axis=-1, keepdims=True)
    return scaling * incoming - values * scaling**3 * centre


def gelu_tanh(values):
    return jax.nn.gelu(values, approximate=True)


def segment_table(lengths_row, group_size, block_size):
    ends_at = jnp.cumsum(lengths_row)
    starts_at = ends_at - lengths_row
    positions = jnp.arange(group_size, dtype=jnp.int32)
    segment_ids = jnp.sum((positions[:, None] >= ends_at[None, :]).astype(jnp.int32), axis=1)
    first_ids = segment_ids[::block_size]
    last_ids = segment_ids[block_size - 1 :: block_size]
    slot_ids = jnp.arange(lengths_row.shape[0], dtype=jnp.int32)
    lower_rows = jnp.sum(
        jnp.where(slot_ids[None, :] == first_ids[:, None], starts_at[None, :], 0), axis=1
    )
    upper_rows = jnp.sum(
        jnp.where(slot_ids[None, :] == last_ids[:, None], ends_at[None, :], 0), axis=1
    )
    return (segment_ids, lower_rows // block_size, (upper_rows + block_size - 1) // block_size)


def to_heads(given_rows, order_row, heads_here):
    packed = given_rows[order_row]
    return packed.reshape(packed.shape[0], heads_here, -1).transpose(1, 0, 2)


def from_heads(head_rows, order_row):
    rows_first = head_rows.transpose(1, 0, 2).reshape(head_rows.shape[1], -1)
    return jnp.zeros_like(rows_first).at[order_row].set(rows_first)


def on_device(
    tokens,
    cotangent,
    query_weight,
    key_weight,
    value_weight,
    output_weight,
    gate_weight,
    up_weight,
    down_weight,
    attention_gain,
    feedforward_gain,
    lengths,
    token_order,
    real_token,
):
    local_rows = tokens.shape[1]
    model_width = tokens.shape[2]
    seq_count = lax.axis_size("seq")
    group_size = local_rows * seq_count
    block_size = min(512, group_size)
    block_count = group_size // block_size
    heads_here = model_width // seq_count // HD
    score_scale = float(HD) ** (-0.5)
    order_row = token_order[0]
    real_row = real_token[0]
    segment_ids, lower_table, upper_table = segment_table(lengths[0], group_size, block_size)
    lower_blocks = jnp.zeros((block_count,), jnp.int32)
    upper_blocks = jnp.full((block_count,), block_count, jnp.int32)
    attention_set = (
        lax.all_gather(query_weight, "fsdp", axis=0, tiled=True),
        lax.all_gather(key_weight, "fsdp", axis=0, tiled=True),
        lax.all_gather(value_weight, "fsdp", axis=0, tiled=True),
        lax.all_gather(output_weight, "fsdp", axis=0, tiled=True),
        lax.all_gather(attention_gain, "fsdp", axis=0, tiled=True),
    )
    inputs = tokens[0].astype(jnp.float32)
    first_normed, first_scaling = normed(inputs)
    first_hidden = (first_normed * attention_set[4].astype(jnp.float32)).astype(jnp.bfloat16)
    queries = matmul(first_hidden, attention_set[0]).astype(jnp.bfloat16)
    key_rows = matmul(first_hidden, attention_set[1]).astype(jnp.bfloat16)
    value_rows = matmul(first_hidden, attention_set[2]).astype(jnp.bfloat16)
    head_queries, head_keys, head_values = (
        lax.all_to_all(queries, "seq", split_axis=1, concat_axis=0, tiled=True),
        lax.all_to_all(key_rows, "seq", split_axis=1, concat_axis=0, tiled=True),
        lax.all_to_all(value_rows, "seq", split_axis=1, concat_axis=0, tiled=True),
    )
    packed_q = to_heads(head_queries, order_row, heads_here)
    packed_k = to_heads(head_keys, order_row, heads_here)
    packed_v = to_heads(head_values, order_row, heads_here)

    def tile_scores(query_block, query_first, key_block):
        key_first = key_block * block_size
        key_tile = lax.dynamic_slice_in_dim(packed_k, key_first, block_size, axis=1)
        scores = (
            jnp.einsum("hqd,hkd->hqk", query_block, key_tile, preferred_element_type=jnp.float32)
            * score_scale
        )
        query_segment = lax.dynamic_slice_in_dim(segment_ids, query_first, block_size)
        key_segment = lax.dynamic_slice_in_dim(segment_ids, key_first, block_size)
        key_real = lax.dynamic_slice_in_dim(real_row, key_first, block_size)
        offsets = jnp.arange(block_size, dtype=jnp.int32)
        same_place = (query_first + offsets)[:, None] == (key_first + offsets)[None, :]
        allowed = (query_segment[:, None] == key_segment[None, :]) & (
            (key_real[None, :] > 0) | same_place
        )
        return (scores, allowed[None], key_first, key_tile)

    def forward_block(block_index):
        query_first = block_index * block_size
        query_block = lax.dynamic_slice_in_dim(packed_q, query_first, block_size, axis=1)

        def max_step(key_block, running):
            run_max, run_sum = running
            scores, allowed, key_first, key_tile = tile_scores(query_block, query_first, key_block)
            new_max = jnp.maximum(
                run_max, jnp.max(jnp.where(allowed, scores, NEGATIVE_FILL), axis=-1)
            )
            weights_tile = jnp.where(allowed, jnp.exp(scores - new_max[..., None]), 0.0)
            return (new_max, run_sum * jnp.exp(run_max - new_max) + jnp.sum(weights_tile, axis=-1))

        start_state = (
            jnp.full((heads_here, block_size), NEGATIVE_FILL, jnp.float32),
            jnp.zeros((heads_here, block_size), jnp.float32),
        )
        run_max, run_sum = lax.fori_loop(
            lower_blocks[block_index], upper_blocks[block_index], max_step, start_state
        )
        log_total = run_max + jnp.log(run_sum)

        def value_step(key_block, attended_sum):
            scores, allowed, key_first, key_tile = tile_scores(query_block, query_first, key_block)
            probabilities = jnp.where(allowed, jnp.exp(scores - log_total[..., None]), 0.0).astype(
                jnp.bfloat16
            )
            value_tile = lax.dynamic_slice_in_dim(packed_v, key_first, block_size, axis=1)
            return attended_sum + jnp.einsum(
                "hqk,hkd->hqd", probabilities, value_tile, preferred_element_type=jnp.float32
            )

        attended_sum = lax.fori_loop(
            lower_blocks[block_index],
            upper_blocks[block_index],
            value_step,
            jnp.zeros((heads_here, block_size, HD), jnp.float32),
        )
        return (attended_sum.astype(jnp.bfloat16), log_total, attended_sum)

    block_outputs, block_totals, block_sums = lax.map(
        forward_block, jnp.arange(block_count, dtype=jnp.int32)
    )
    packed_out = block_outputs.transpose(1, 0, 2, 3).reshape(heads_here, group_size, HD)
    packed_sums = block_sums.transpose(1, 0, 2, 3).reshape(heads_here, group_size, HD)
    log_totals = block_totals.transpose(1, 0, 2).reshape(heads_here, group_size)
    attended_rows = lax.all_to_all(
        from_heads(packed_out, order_row), "seq", split_axis=0, concat_axis=1, tiled=True
    )
    feedforward_set = (
        lax.all_gather(gate_weight, "fsdp", axis=0, tiled=True),
        lax.all_gather(up_weight, "fsdp", axis=0, tiled=True),
        lax.all_gather(down_weight, "fsdp", axis=0, tiled=True),
        lax.all_gather(feedforward_gain, "fsdp", axis=0, tiled=True),
    )
    middle = inputs + matmul(attended_rows, attention_set[3])
    second_normed, second_scaling = normed(middle)
    second_hidden = (second_normed * feedforward_set[3].astype(jnp.float32)).astype(jnp.bfloat16)
    gate_values = matmul(second_hidden, feedforward_set[0])
    up_values = matmul(second_hidden, feedforward_set[1])
    gelu_values, gelu_pullback = jax.vjp(gelu_tanh, gate_values)
    activated = (gelu_values * up_values).astype(jnp.bfloat16)
    layer_out = (middle + matmul(activated, feedforward_set[2])).astype(jnp.bfloat16)
    backward_feedforward = (
        lax.all_gather(gate_weight, "fsdp", axis=0, tiled=True),
        lax.all_gather(up_weight, "fsdp", axis=0, tiled=True),
        lax.all_gather(down_weight, "fsdp", axis=0, tiled=True),
        lax.all_gather(feedforward_gain, "fsdp", axis=0, tiled=True),
    )
    out_grad = cotangent[0]
    down_term = outer_sum(activated, out_grad)
    act_grad = back_product(out_grad, backward_feedforward[2])
    up_rows_grad = (act_grad * gelu_values).astype(jnp.bfloat16)
    gate_rows_grad = gelu_pullback(act_grad * up_values)[0].astype(jnp.bfloat16)
    gate_term = outer_sum(second_hidden, gate_rows_grad)
    up_term = outer_sum(second_hidden, up_rows_grad)
    second_grad = back_product(gate_rows_grad, backward_feedforward[0]) + back_product(
        up_rows_grad, backward_feedforward[1]
    )
    second_gain_term = jnp.sum(second_grad * second_normed, axis=0)
    middle_grad = out_grad.astype(jnp.float32) + norm_back(
        second_grad * backward_feedforward[3].astype(jnp.float32), middle, second_scaling
    )
    branch_grad = middle_grad.astype(jnp.bfloat16)
    backward_attention = (
        lax.all_gather(query_weight, "fsdp", axis=0, tiled=True),
        lax.all_gather(key_weight, "fsdp", axis=0, tiled=True),
        lax.all_gather(value_weight, "fsdp", axis=0, tiled=True),
        lax.all_gather(output_weight, "fsdp", axis=0, tiled=True),
        lax.all_gather(attention_gain, "fsdp", axis=0, tiled=True),
    )
    output_term = outer_sum(attended_rows, branch_grad)
    attended_grad = back_product(branch_grad, backward_attention[3]).astype(jnp.bfloat16)
    head_grads = lax.all_to_all(attended_grad, "seq", split_axis=1, concat_axis=0, tiled=True)
    packed_grad = to_heads(head_grads, order_row, heads_here)
    row_deltas = jnp.sum(packed_grad.astype(jnp.float32) * packed_sums, axis=-1)

    def backward_block(running, block_index):
        key_acc, value_acc = running
        query_first = block_index * block_size
        query_block = lax.dynamic_slice_in_dim(packed_q, query_first, block_size, axis=1)
        grad_block = lax.dynamic_slice_in_dim(packed_grad, query_first, block_size, axis=1)
        log_total = lax.dynamic_slice_in_dim(log_totals, query_first, block_size, axis=1)
        row_delta = lax.dynamic_slice_in_dim(row_deltas, query_first, block_size, axis=1)

        def grad_step(key_block, state):
            query_acc, key_sum, value_sum = state
            scores, allowed, key_first, key_tile = tile_scores(query_block, query_first, key_block)
            probabilities = jnp.where(allowed, jnp.exp(scores - log_total[..., None]), 0.0)
            value_tile = lax.dynamic_slice_in_dim(packed_v, key_first, block_size, axis=1)
            prob_grad = jnp.einsum(
                "hqd,hkd->hqk", grad_block, value_tile, preferred_element_type=jnp.float32
            )
            score_grad = (probabilities * (prob_grad - row_delta[..., None])).astype(jnp.bfloat16)
            query_acc = query_acc + jnp.einsum(
                "hqk,hkd->hqd", score_grad, key_tile, preferred_element_type=jnp.float32
            )
            key_part = jnp.einsum(
                "hqk,hqd->hkd", score_grad, query_block, preferred_element_type=jnp.float32
            )
            value_part = jnp.einsum(
                "hqk,hqd->hkd",
                probabilities.astype(jnp.bfloat16),
                grad_block,
                preferred_element_type=jnp.float32,
            )
            key_sum = lax.dynamic_update_slice_in_dim(
                key_sum,
                lax.dynamic_slice_in_dim(key_sum, key_first, block_size, axis=1) + key_part,
                key_first,
                axis=1,
            )
            value_sum = lax.dynamic_update_slice_in_dim(
                value_sum,
                lax.dynamic_slice_in_dim(value_sum, key_first, block_size, axis=1) + value_part,
                key_first,
                axis=1,
            )
            return (query_acc, key_sum, value_sum)

        start_state = (jnp.zeros((heads_here, block_size, HD), jnp.float32), key_acc, value_acc)
        query_acc, key_acc, value_acc = lax.fori_loop(
            lower_blocks[block_index], upper_blocks[block_index], grad_step, start_state
        )
        return ((key_acc, value_acc), (query_acc * score_scale).astype(jnp.bfloat16))

    empty_heads = jnp.zeros((heads_here, group_size, HD), jnp.float32)
    (key_acc, value_acc), query_blocks = lax.scan(
        backward_block, (empty_heads, empty_heads), jnp.arange(block_count, dtype=jnp.int32)
    )
    packed_query_grad = query_blocks.transpose(1, 0, 2, 3).reshape(heads_here, group_size, HD)
    packed_key_grad = (key_acc * score_scale).astype(jnp.bfloat16)
    packed_value_grad = value_acc.astype(jnp.bfloat16)
    query_grad_rows, key_grad_rows, value_grad_rows = (
        lax.all_to_all(
            from_heads(packed_query_grad, order_row), "seq", split_axis=0, concat_axis=1, tiled=True
        ),
        lax.all_to_all(
            from_heads(packed_key_grad, order_row), "seq", split_axis=0, concat_axis=1, tiled=True
        ),
        lax.all_to_all(
            from_heads(packed_value_grad, order_row), "seq", split_axis=0, concat_axis=1, tiled=True
        ),
    )
    query_term = outer_sum(first_hidden, query_grad_rows)
    key_term = outer_sum(first_hidden, key_grad_rows)
    value_term = outer_sum(first_hidden, value_grad_rows)
    first_grad = (
        back_product(query_grad_rows, backward_attention[0])
        + back_product(key_grad_rows, backward_attention[1])
        + back_product(value_grad_rows, backward_attention[2])
    )
    first_gain_term = jnp.sum(first_grad * first_normed, axis=0)
    input_grad = middle_grad + norm_back(
        first_grad * backward_attention[4].astype(jnp.float32), inputs, first_scaling
    )
    terms = (
        query_term,
        key_term,
        value_term,
        output_term,
        gate_term,
        up_term,
        down_term,
        first_gain_term,
        second_gain_term,
    )
    shares = (
        lax.psum_scatter(
            terms[0].astype(jnp.bfloat16), "fsdp", scatter_dimension=0, tiled=True
        ).astype(jnp.float32),
        lax.psum_scatter(
            terms[1].astype(jnp.bfloat16), "fsdp", scatter_dimension=0, tiled=True
        ).astype(jnp.float32),
        lax.psum_scatter(
            terms[2].astype(jnp.bfloat16), "fsdp", scatter_dimension=0, tiled=True
        ).astype(jnp.float32),
        lax.psum_scatter(
            terms[3].astype(jnp.bfloat16), "fsdp", scatter_dimension=0, tiled=True
        ).astype(jnp.float32),
        lax.psum_scatter(
            terms[4].astype(jnp.bfloat16), "fsdp", scatter_dimension=0, tiled=True
        ).astype(jnp.float32),
        lax.psum_scatter(
            terms[5].astype(jnp.bfloat16), "fsdp", scatter_dimension=0, tiled=True
        ).astype(jnp.float32),
        lax.psum_scatter(
            terms[6].astype(jnp.bfloat16), "fsdp", scatter_dimension=0, tiled=True
        ).astype(jnp.float32),
        lax.psum_scatter(
            terms[7].astype(jnp.bfloat16), "fsdp", scatter_dimension=0, tiled=True
        ).astype(jnp.float32),
        lax.psum_scatter(
            terms[8].astype(jnp.bfloat16), "fsdp", scatter_dimension=0, tiled=True
        ).astype(jnp.float32),
    )
    summed = (
        lax.psum(shares[0].astype(jnp.bfloat16), "seq").astype(jnp.float32),
        lax.psum(shares[1].astype(jnp.bfloat16), "seq").astype(jnp.float32),
        lax.psum(shares[2].astype(jnp.bfloat16), "seq").astype(jnp.float32),
        lax.psum(shares[3].astype(jnp.bfloat16), "seq").astype(jnp.float32),
        lax.psum(shares[4].astype(jnp.bfloat16), "seq").astype(jnp.float32),
        lax.psum(shares[5].astype(jnp.bfloat16), "seq").astype(jnp.float32),
        lax.psum(shares[6].astype(jnp.bfloat16), "seq").astype(jnp.float32),
        lax.psum(shares[7].astype(jnp.bfloat16), "seq").astype(jnp.float32),
        lax.psum(shares[8].astype(jnp.bfloat16), "seq").astype(jnp.float32),
    )
    return (
        layer_out[None],
        input_grad[None],
        summed[0],
        summed[1],
        summed[2],
        summed[3],
        summed[4],
        summed[5],
        summed[6],
        summed[7],
        summed[8],
    )


def solution(mesh):
    in_specs = (
        P("fsdp", "seq", None),
        P("fsdp", "seq", None),
        P("fsdp", None),
        P("fsdp", None),
        P("fsdp", None),
        P("fsdp", None),
        P("fsdp", None),
        P("fsdp", None),
        P("fsdp", None),
        P("fsdp"),
        P("fsdp"),
        P("fsdp", None),
        P("fsdp", None),
        P("fsdp", None),
    )
    out_specs = (
        P("fsdp", "seq", None),
        P("fsdp", "seq", None),
        P("fsdp", None),
        P("fsdp", None),
        P("fsdp", None),
        P("fsdp", None),
        P("fsdp", None),
        P("fsdp", None),
        P("fsdp", None),
        P("fsdp"),
        P("fsdp"),
    )
    return jax.shard_map(
        on_device, mesh=mesh, in_specs=in_specs, out_specs=out_specs, check_vma=False
    )
```

profile of v0, /device:TPU:0, one launch (start us, length us, event | category | flops | bytes accessed | tf_op | source)
XLA Modules:
  0.0 1143.2 jit_solution(5241365287118811720)
XLA Ops:
  11.2 6.0 all-gather
  18.0 16.9 %all-gather.10.cloned.1.call-done = bf16[1024,1024]{1,0:T(8,128)(2,1)} async-done(((bf16[256,1024]{1,0:T(8,128)(2,1)}), bf16[1024,1024]{1,0:T(8,128)(2,1)}) %all-gather.10.cloned.1.call-update) | async-done | bytes 2097168 | tf_op jit(solution)/shard_map/all_gather | solution.py:96
  38.3 5.5 all-to-all-start
  43.9 15.2 %all-gather.12.cloned.1.call-done = bf16[1024,1024]{1,0:T(8,128)(2,1)} async-done(((bf16[256,1024]{1,0:T(8,128)(2,1)}), bf16[1024,1024]{1,0:T(8,128)(2,1)}) %all-gather.12.cloned.1.call-update) | async-done | bytes 2097168 | tf_op jit(solution)/shard_map/all_gather | solution.py:97
  62.5 5.5 all-to-all-start.1
  68.0 15.2 %all-gather.14.cloned.1.call-done = bf16[1024,1024]{1,0:T(8,128)(2,1)} async-done(((bf16[256,1024]{1,0:T(8,128)(2,1)}), bf16[1024,1024]{1,0:T(8,128)(2,1)}) %all-gather.14.cloned.1.call-update) | async-done | bytes 2097168 | tf_op jit(solution)/shard_map/all_gather | solution.py:98
  86.8 5.5 all-to-all-start.2
  117.0 157.8 %while.75 = (s32[]{:T(128)}, bf16[5,2,512,64]{2,3,1,0:T(8,128)(2,1)}, f32[5,2,512]{2,1,0:T(2,128)}, f32[5,2,512,64]{2,3,1,0:T(8,128)}, s32[5]{0:T(128)S(1)}, /*i...) while((s32[]{:T(128)}, ...), condition=%wide.region_10.11_spmd, body=%wide.region_3.10_spmd.sunk | while | flops 209396752 | bytes 7985029 | solution.py:174
  119.3 12.0 %while.78 = (s32[]{:T(128)}, f32[2,512]{1,0:T(2,128)S(1)}, f32[2,512]{1,0:T(2,128)S(1)}, s32[512]{0:T(512)S(1)}, s32[2560]{0:T(1024)S(1)}, /*index=5*/s32[2560]{...) while((s32[]{:T(128)}, f32[2,512]{1,0:T(2,128)S(1)}, ...), condition=%wide.region_7.7_spmd.clone, body=%wide.region_4.6_spmd.clone.sunk | while | flops 71834120 | bytes 5315786 | solution.py:151
  132.0 15.2 %while.79 = (s32[]{:T(128)}, f32[2,512,64]{1,2,0:T(8,128)S(1)}, s32[512]{0:T(512)S(1)}, s32[2560]{0:T(1024)S(1)}, s32[2560]{0:T(1024)}, /*index=5*/s32[]{:T(128)...) while((s32[]{:T(128)}, f32[2,512,64]{1,2,0:T(8,128)S(1)}, ...), condition=%wide.region_9.9_spmd.clone, body=%wide.region_8.8_spmd.clone.sunk | while | flops 137496064 | bytes 1467084 | solution.py:166
  150.9 12.0 %while.78 = (s32[]{:T(128)}, f32[2,512]{1,0:T(2,128)S(1)}, f32[2,512]{1,0:T(2,128)S(1)}, s32[512]{0:T(512)S(1)}, s32[2560]{0:T(1024)S(1)}, /*index=5*/s32[2560]{...) while((s32[]{:T(128)}, f32[2,512]{1,0:T(2,128)S(1)}, ...), condition=%wide.region_7.7_spmd.clone, body=%wide.region_4.6_spmd.clone.sunk | while | flops 71834120 | bytes 5315786 | solution.py:151
  163.5 15.2 %while.79 = (s32[]{:T(128)}, f32[2,512,64]{1,2,0:T(8,128)S(1)}, s32[512]{0:T(512)S(1)}, s32[2560]{0:T(1024)S(1)}, s32[2560]{0:T(1024)}, /*index=5*/s32[]{:T(128)...) while((s32[]{:T(128)}, f32[2,512,64]{1,2,0:T(8,128)S(1)}, ...), condition=%wide.region_9.9_spmd.clone, body=%wide.region_8.8_spmd.clone.sunk | while | flops 137496064 | bytes 1467084 | solution.py:166
  182.4 12.0 %while.78 = (s32[]{:T(128)}, f32[2,512]{1,0:T(2,128)S(1)}, f32[2,512]{1,0:T(2,128)S(1)}, s32[512]{0:T(512)S(1)}, s32[2560]{0:T(1024)S(1)}, /*index=5*/s32[2560]{...) while((s32[]{:T(128)}, f32[2,512]{1,0:T(2,128)S(1)}, ...), condition=%wide.region_7.7_spmd.clone, body=%wide.region_4.6_spmd.clone.sunk | while | flops 71834120 | bytes 5315786 | solution.py:151
  195.1 15.3 %while.79 = (s32[]{:T(128)}, f32[2,512,64]{1,2,0:T(8,128)S(1)}, s32[512]{0:T(512)S(1)}, s32[2560]{0:T(1024)S(1)}, s32[2560]{0:T(1024)}, /*index=5*/s32[]{:T(128)...) while((s32[]{:T(128)}, f32[2,512,64]{1,2,0:T(8,128)S(1)}, ...), condition=%wide.region_9.9_spmd.clone, body=%wide.region_8.8_spmd.clone.sunk | while | flops 137496064 | bytes 1467084 | solution.py:166
  214.0 12.0 %while.78 = (s32[]{:T(128)}, f32[2,512]{1,0:T(2,128)S(1)}, f32[2,512]{1,0:T(2,128)S(1)}, s32[512]{0:T(512)S(1)}, s32[2560]{0:T(1024)S(1)}, /*index=5*/s32[2560]{...) while((s32[]{:T(128)}, f32[2,512]{1,0:T(2,128)S(1)}, ...), condition=%wide.region_7.7_spmd.clone, body=%wide.region_4.6_spmd.clone.sunk | while | flops 71834120 | bytes 5315786 | solution.py:151
  226.7 15.2 %while.79 = (s32[]{:T(128)}, f32[2,512,64]{1,2,0:T(8,128)S(1)}, s32[512]{0:T(512)S(1)}, s32[2560]{0:T(1024)S(1)}, s32[2560]{0:T(1024)}, /*index=5*/s32[]{:T(128)...) while((s32[]{:T(128)}, f32[2,512,64]{1,2,0:T(8,128)S(1)}, ...), condition=%wide.region_9.9_spmd.clone, body=%wide.region_8.8_spmd.clone.sunk | while | flops 137496064 | bytes 1467084 | solution.py:166
  245.5 12.0 %while.78 = (s32[]{:T(128)}, f32[2,512]{1,0:T(2,128)S(1)}, f32[2,512]{1,0:T(2,128)S(1)}, s32[512]{0:T(512)S(1)}, s32[2560]{0:T(1024)S(1)}, /*index=5*/s32[2560]{...) while((s32[]{:T(128)}, f32[2,512]{1,0:T(2,128)S(1)}, ...), condition=%wide.region_7.7_spmd.clone, body=%wide.region_4.6_spmd.clone.sunk | while | flops 71834120 | bytes 5315786 | solution.py:151
  258.2 15.2 %while.79 = (s32[]{:T(128)}, f32[2,512,64]{1,2,0:T(8,128)S(1)}, s32[512]{0:T(512)S(1)}, s32[2560]{0:T(1024)S(1)}, s32[2560]{0:T(1024)}, /*index=5*/s32[]{:T(128)...) while((s32[]{:T(128)}, f32[2,512,64]{1,2,0:T(8,128)S(1)}, ...), condition=%wide.region_9.9_spmd.clone, body=%wide.region_8.8_spmd.clone.sunk | while | flops 137496064 | bytes 1467084 | solution.py:166
  276.3 7.9 scatter_custom_fusion
  293.2 12.1 %all-to-all-done.3 = bf16[8,320,128]{2,1,0:T(8,128)(2,1)S(1)} async-done(((bf16[8,320,128]{2,1,0:T(8,128)(2,1)}), bf16[8,320,128]{2,1,0:T(8,128)(2,1)S(1)}, u32[]{:S(2)}, u32[]{:S(2)}) %all-to-all-start.3) | async-done | bytes 655392 | tf_op jit(solution)/shard_map/all_to_all | solution.py:180
  308.1 6.9 fusion.104
  315.1 6.5 fusion.105
  321.5 9.3 multiply_convert_fusion.1
  330.8 6.0 fusion.106
  352.9 11.9 %all-to-all-done.4 = bf16[320,8,128]{2,0,1:T(8,128)(2,1)S(1)} async-done(((bf16[320,8,128]{2,0,1:T(8,128)(2,1)}), bf16[320,8,128]{2,0,1:T(8,128)(2,1)S(1)}, u32[]{:S(2)}, u32[]{:S(2)}) %all-to-all-start.4) | async-done | bytes 655392 | tf_op jit(solution)/shard_map/all_to_all | solution.py:227
  376.1 218.8 %while.77 = (s32[]{:T(128)}, f32[2,2560,64]{1,2,0:T(8,128)S(1)}, f32[2,2560,64]{1,2,0:T(8,128)}, bf16[5,2,512,64]{2,3,1,0:T(8,128)(2,1)}, s32[5]{0:T(128)}, /*in...) while((s32[]{:T(128)}, f32[2,2560,64]{1,2,0:T(8,128)S(1)}, ...), condition=%wide.region_18.19_spmd, body=%wide.region_15.18_spmd.sunk | while | flops 340657664 | bytes 13418652 | solution.py:281
  381.1 38.1 %while.80 = (s32[]{:T(128)}, f32[2,512,64]{1,2,0:T(8,128)S(1)}, f32[2,2560,64]{1,2,0:T(8,128)S(1)}, f32[2,2560,64]{1,2,0:T(8,128)}, s32[512]{0:T(512)}, /*index=...) while((s32[]{:T(128)}, f32[2,512,64]{1,2,0:T(8,128)S(1)}, ...), condition=%wide.region_17.17_spmd.clone, body=%wide.region_16.16_spmd.clone.sunk | while | flops 340526592 | bytes 12479745 | solution.py:275
  424.9 38.1 %while.80 = (s32[]{:T(128)}, f32[2,512,64]{1,2,0:T(8,128)S(1)}, f32[2,2560,64]{1,2,0:T(8,128)S(1)}, f32[2,2560,64]{1,2,0:T(8,128)}, s32[512]{0:T(512)}, /*index=...) while((s32[]{:T(128)}, f32[2,512,64]{1,2,0:T(8,128)S(1)}, ...), condition=%wide.region_17.17_spmd.clone, body=%wide.region_16.16_spmd.clone.sunk | while | flops 340526592 | bytes 12479745 | solution.py:275
  468.7 38.1 %while.80 = (s32[]{:T(128)}, f32[2,512,64]{1,2,0:T(8,128)S(1)}, f32[2,2560,64]{1,2,0:T(8,128)S(1)}, f32[2,2560,64]{1,2,0:T(8,128)}, s32[512]{0:T(512)}, /*index=...) while((s32[]{:T(128)}, f32[2,512,64]{1,2,0:T(8,128)S(1)}, ...), condition=%wide.region_17.17_spmd.clone, body=%wide.region_16.16_spmd.clone.sunk | while | flops 340526592 | bytes 12479745 | solution.py:275
  512.4 38.1 %while.80 = (s32[]{:T(128)}, f32[2,512,64]{1,2,0:T(8,128)S(1)}, f32[2,2560,64]{1,2,0:T(8,128)S(1)}, f32[2,2560,64]{1,2,0:T(8,128)}, s32[512]{0:T(512)}, /*index=...) while((s32[]{:T(128)}, f32[2,512,64]{1,2,0:T(8,128)S(1)}, ...), condition=%wide.region_17.17_spmd.clone, body=%wide.region_16.16_spmd.clone.sunk | while | flops 340526592 | bytes 12479745 | solution.py:275
  556.2 38.1 %while.80 = (s32[]{:T(128)}, f32[2,512,64]{1,2,0:T(8,128)S(1)}, f32[2,2560,64]{1,2,0:T(8,128)S(1)}, f32[2,2560,64]{1,2,0:T(8,128)}, s32[512]{0:T(512)}, /*index=...) while((s32[]{:T(128)}, f32[2,512,64]{1,2,0:T(8,128)S(1)}, ...), condition=%wide.region_17.17_spmd.clone, body=%wide.region_16.16_spmd.clone.sunk | while | flops 340526592 | bytes 12479745 | solution.py:275
  595.4 7.3 scatter_custom_fusion.2
  602.7 21.1 %all_to_all.152 = bf16[8,320,128]{2,1,0:T(8,128)(2,1)S(1)} all-to-all(bf16[8,320,128]{2,1,0:T(8,128)(2,1)S(1)} %bitcast.309), channel_id=1, replica_groups=mesh['seq'=8,'fsdp'=4] {'seq'}, dimensions={0} | all-to-all | bytes 1310720 | tf_op jit(solution)/shard_map/all_to_all | solution.py:291
  628.4 7.3 scatter_custom_fusion.3
  635.7 20.6 %all_to_all.153 = bf16[8,320,128]{2,1,0:T(8,128)(2,1)S(1)} all-to-all(bf16[8,320,128]{2,1,0:T(8,128)(2,1)S(1)} %bitcast.310), channel_id=1, replica_groups=mesh['seq'=8,'fsdp'=4] {'seq'}, dimensions={0} | all-to-all | bytes 1310720 | tf_op jit(solution)/shard_map/all_to_all | solution.py:294
  661.3 7.3 scatter_custom_fusion.1
  668.6 20.4 %all_to_all.154 = bf16[8,320,128]{2,1,0:T(8,128)(2,1)S(1)} all-to-all(bf16[8,320,128]{2,1,0:T(8,128)(2,1)S(1)} %bitcast.307), channel_id=1, replica_groups=mesh['seq'=8,'fsdp'=4] {'seq'}, dimensions={0} | all-to-all | bytes 1310720 | tf_op jit(solution)/shard_map/all_to_all | solution.py:288
  693.6 6.5 convolution_convert_fusion.2
  700.2 6.7 convolution_convert_fusion.1
  708.0 6.6 convolution_convert_fusion
  714.9 10.1 reduce-scatter.8.cloned.1.call-done
  725.0 57.3 %reduce-scatter.16.cloned.1.call-done = bf16[256,2816]{1,0:T(8,128)(2,1)} async-done(((bf16[1024,2816]{1,0:T(8,128)(2,1)}), bf16[256,2816]{1,0:T(8,128)(2,1)}) %reduce-scatter.16.cloned.1.call-update) | async-done | bytes 1441808 | tf_op jit(solution)/shard_map/reduce_scatter | solution.py:334
  782.3 57.6 %reduce-scatter.18.cloned.1.call-done = bf16[256,2816]{1,0:T(8,128)(2,1)} async-done(((bf16[1024,2816]{1,0:T(8,128)(2,1)}), bf16[256,2816]{1,0:T(8,128)(2,1)}) %reduce-scatter.18.cloned.1.call-update) | async-done | bytes 1441808 | tf_op jit(solution)/shard_map/reduce_scatter | solution.py:337
  839.9 57.3 %reduce-scatter.20.cloned.1.call-done = bf16[704,1024]{1,0:T(8,128)(2,1)} async-done(((bf16[2816,1024]{1,0:T(8,128)(2,1)}), bf16[704,1024]{1,0:T(8,128)(2,1)}) %reduce-scatter.20.cloned.1.call-update) | async-done | bytes 1441808 | tf_op jit(solution)/shard_map/reduce_scatter | solution.py:340
  899.1 6.2 fusion.64
  911.0 6.0 all-reduce.4
  917.1 22.7 %all-reduce.2 = (bf16[256]{0:T(256)(128)(2,1)S(1)}, bf16[256]{0:T(256)(128)(2,1)S(1)}) all-reduce(bf16[256]{0:T(256)(128)(2,1)S(1)} %dynamic-slice.1, bf16[256]{0:T(256)(128)(2,1)S(1)} %dynamic-slice.3), channel_id=1, replica_groups=mesh['seq'=8,'fsdp'=4] {'seq'}, use_global_device_ids=true, to_apply=%region_39.40 | all-reduce | flops 512 | bytes 2048 | tf_op jit(solution)/shard_map/psum | solution.py:358
  943.8 181.2 %all-reduce.7.cloned.1.call-done = (bf16[256,1024]{1,0:T(8,128)(2,1)}, bf16[256,1024]{1,0:T(8,128)(2,1)}, bf16[256,1024]{1,0:T(8,128)(2,1)}, bf16[256,1024]{1,0:...) async-done(((bf16[256,1024]{1,0:T(8,128)(2,1)}, bf16[256,1024]{1,0:T(8,128)(2,1)}, bf16[256,1024]{1,0:T(8,128)(2,1)}, ...) | async-done | bytes 6422544 | tf_op jit(solution)/shard_map/psum | solution.py:351
  (851 shorter events, 484.3 us)
Async XLA Ops:
  7.2 27.7 %all-gather.10.cloned.1.call-start = ((), (), s32[]{:S(2)}) async-start(), calls=%async_computation.15 | async-start | bytes 2621440 | tf_op jit(solution)/shard_map/all_gather | solution.py:96
  7.9 51.2 %all-gather.12.cloned.1.call-start = ((), (), s32[]{:S(2)}) async-start(), calls=%async_computation.16 | async-start | bytes 2621440 | tf_op jit(solution)/shard_map/all_gather | solution.py:97
  8.7 74.6 %all-gather.14.cloned.1.call-start = ((), (), s32[]{:S(2)}) async-start(), calls=%async_computation.17 | async-start | bytes 2621440 | tf_op jit(solution)/shard_map/all_gather | solution.py:98
  9.4 7.8 copy-start.6
  9.4 283.8 %all-gather.16.cloned.1.call-start = ((), (), s32[]{:S(2)}) async-start(), calls=%async_computation.18 | async-start | bytes 2621440 | tf_op jit(solution)/shard_map/all_gather | solution.py:99
  10.0 298.1 %all-gather.18.cloned.1.call-start = ((), (), s32[]{:S(2)}) async-start(), calls=%async_computation.19 | async-start | bytes 7208960 | tf_op jit(solution)/shard_map/all_gather | solution.py:184
  10.6 304.5 %all-gather.20.cloned.1.call-start = ((), (), s32[]{:S(2)}) async-start(), calls=%async_computation.20 | async-start | bytes 7208960 | tf_op jit(solution)/shard_map/all_gather | solution.py:185
  17.2 66.1 %copy-start.25 = (f32[4,1,256]{2,1,0:T(1,128)}, f32[4,1,256]{2,1,0:T(1,128)S(1)}, u32[]{:S(2)}) copy-start(f32[4,1,256]{2,1,0:T(1,128)S(1)} %convert_element_type.209) | copy-start | bytes 12292
  18.0 65.3 %copy-start.30 = (f32[320]{0:T(512)}, f32[320]{0:T(512)S(1)}, u32[]{:S(2)}) copy-start(f32[320]{0:T(512)S(1)} %get-tuple-element.806) | copy-start | bytes 3844
  38.3 24.2 %all-to-all-start = ((bf16[320,8,128]{2,0,1:T(8,128)(2,1)}), bf16[320,8,128]{2,0,1:T(8,128)(2,1)S(1)}, u32[]{:S(2)}, u32[]{:S(2)}) async-start(bf16[320,8,128]{2,0,1:T(8,128)(2,1)} %bitcast.258), calls=%async_computation | async-start | bytes 1310720 | tf_op jit(solution)/shard_map/all_to_all | solution.py:109
  62.5 24.2 %all-to-all-start.1 = ((bf16[320,8,128]{2,0,1:T(8,128)(2,1)}), bf16[320,8,128]{2,0,1:T(8,128)(2,1)S(1)}, u32[]{:S(2)}, u32[]{:S(2)}) async-start(bf16[320,8,128]{2,0,1:T(8,128)(2,1)} %bitcast.257), calls=%async_computation.1 | async-start | bytes 1310720 | tf_op jit(solution)/shard_map/all_to_all | solution.py:110
  85.8 7.3 copy-start.38
  85.8 7.5 copy-start.27
  85.8 8.1 copy-start.28
  86.8 23.2 %all-to-all-start.2 = ((bf16[320,8,128]{2,0,1:T(8,128)(2,1)}), bf16[320,8,128]{2,0,1:T(8,128)(2,1)S(1)}, u32[]{:S(2)}, u32[]{:S(2)}) async-start(bf16[320,8,128]{2,0,1:T(8,128)(2,1)} %bitcast.256), calls=%async_computation.2 | async-start | bytes 1310720 | tf_op jit(solution)/shard_map/all_to_all | solution.py:111
  92.3 229.3 %all-gather.22.cloned.1.call-start = ((), (), s32[]{:S(2)}) async-start(), calls=%async_computation.21 | async-start | bytes 7208960 | tf_op jit(solution)/shard_map/all_gather | solution.py:186
  93.9 182.4 %copy-start.24 = (s32[2560]{0:T(1024)}, s32[2560]{0:T(1024)S(1)}, u32[]{:S(2)}) copy-start(s32[2560]{0:T(1024)S(1)} %fusion.97) | copy-start | bytes 30724
  276.0 11.9 %copy-start.39 = (bf16[256]{0:T(256)(128)(2,1)S(1)}, bf16[256]{0:T(256)(128)(2,1)}, u32[]{:S(2)}) copy-start(bf16[256]{0:T(256)(128)(2,1)} %param.34) | copy-start | bytes 1540
  276.0 29.3 %copy-start.7 = (bf16[1,320,1024]{2,1,0:T(8,128)(2,1)S(1)}, bf16[1,320,1024]{2,1,0:T(8,128)(2,1)}, u32[]{:S(2)}) copy-start(bf16[1,320,1024]{2,1,0:T(8,128)(2,1)} %param.24) | copy-start | bytes 1966084
  284.2 21.1 %all-to-all-start.3 = ((bf16[8,320,128]{2,1,0:T(8,128)(2,1)}), bf16[8,320,128]{2,1,0:T(8,128)(2,1)S(1)}, u32[]{:S(2)}, u32[]{:S(2)}) async-start(bf16[8,320,128]{2,1,0:T(8,128)(2,1)} %bitcast.26), calls=%async_computation.3 | async-start | bytes 1310720 | tf_op jit(solution)/shard_map/all_to_all | solution.py:180
  307.9 29.0 %copy-start.3 = (f32[320,1024]{1,0:T(8,128)}, f32[320,1024]{1,0:T(8,128)S(1)}, u32[]{:S(2)}) copy-start(f32[320,1024]{1,0:T(8,128)S(1)} %get-tuple-element.810) | copy-start | bytes 3932164
  308.1 7.0 copy-start.12
  330.8 6.1 copy-start.42
  330.8 6.1 copy-start.41
  330.8 6.1 copy-start.33
  336.9 2.8 copy-start.18
  339.8 2.0 copy-start.36
  341.8 8.4 copy-start
  343.6 21.1 %all-to-all-start.4 = ((bf16[320,8,128]{2,0,1:T(8,128)(2,1)}), bf16[320,8,128]{2,0,1:T(8,128)(2,1)S(1)}, u32[]{:S(2)}, u32[]{:S(2)}) async-start(bf16[320,8,128]{2,0,1:T(8,128)(2,1)} %bitcast.304), calls=%async_computation.4 | async-start | bytes 1310720 | tf_op jit(solution)/shard_map/all_to_all | solution.py:227
  347.3 367.6 %reduce-scatter.14.cloned.1.call-start = ((), (), s32[]{:S(2)}) async-start(), calls=%async_computation.25 | async-start | bytes 2621440 | tf_op jit(solution)/shard_map/reduce_scatter | solution.py:331
  352.8 362.1 %reduce-scatter.10.cloned.1.call-start = ((), (), s32[]{:S(2)}) async-start(), calls=%async_computation.23 | async-start | bytes 2621440 | tf_op jit(solution)/shard_map/reduce_scatter | solution.py:325
  595.0 28.8 %copy-start.8 = (bf16[1,320,1024]{2,1,0:T(8,128)(2,1)S(1)}, bf16[1,320,1024]{2,1,0:T(8,128)(2,1)}, u32[]{:S(2)}) copy-start(bf16[1,320,1024]{2,1,0:T(8,128)(2,1)} %param.24) | copy-start | bytes 1966084
  595.0 28.8 %copy-start.26 = (f32[4,1,256]{2,1,0:T(1,128)S(1)}, f32[4,1,256]{2,1,0:T(1,128)}, u32[]{:S(2)}) copy-start(f32[4,1,256]{2,1,0:T(1,128)} %copy-done.25) | copy-start | bytes 12292
  595.0 28.8 %copy-start.31 = (f32[320]{0:T(512)S(1)}, f32[320]{0:T(512)}, u32[]{:S(2)}) copy-start(f32[320]{0:T(512)} %copy-done.30) | copy-start | bytes 3844
  626.6 88.3 %reduce-scatter.12.cloned.1.call-start = ((), (), s32[]{:S(2)}) async-start(), calls=%async_computation.24 | async-start | bytes 2621440 | tf_op jit(solution)/shard_map/reduce_scatter | solution.py:328
  659.8 65.2 %reduce-scatter.8.cloned.1.call-start = ((), (), s32[]{:S(2)}) async-start(), calls=%async_computation.22 | async-start | bytes 2621440 | tf_op jit(solution)/shard_map/reduce_scatter | solution.py:322
  692.6 89.7 %reduce-scatter.16.cloned.1.call-start = ((), (), s32[]{:S(2)}) async-start(), calls=%async_computation.26 | async-start | bytes 7208960 | tf_op jit(solution)/shard_map/reduce_scatter | solution.py:334
  700.1 139.8 %reduce-scatter.18.cloned.1.call-start = ((), (), s32[]{:S(2)}) async-start(), calls=%async_computation.27 | async-start | bytes 7208960 | tf_op jit(solution)/shard_map/reduce_scatter | solution.py:337
  706.9 190.3 %reduce-scatter.20.cloned.1.call-start = ((), (), s32[]{:S(2)}) async-start(), calls=%async_computation.28 | async-start | bytes 7208960 | tf_op jit(solution)/shard_map/reduce_scatter | solution.py:340
  714.6 410.4 %all-reduce.7.cloned.1.call-start = ((), (), s32[]{:S(2)}) async-start(), calls=%async_computation.29 | async-start | bytes 12845056 | tf_op jit(solution)/shard_map/psum | solution.py:351
  899.1 6.2 copy-start.17
  899.1 6.2 copy-start.34
  908.8 2.2 copy-start.32
  908.8 32.3 %copy-start.1 = (f32[320,1024]{1,0:T(8,128)S(1)}, f32[320,1024]{1,0:T(8,128)}, u32[]{:S(2)}) copy-start(f32[320,1024]{1,0:T(8,128)} %copy-done) | copy-start | bytes 3932164
  908.8 32.3 %copy-start.29 = (f32[320]{0:T(512)S(1)}, f32[320]{0:T(512)}, u32[]{:S(2)}) copy-start(f32[320]{0:T(512)} %get-tuple-element.805) | copy-start | bytes 3844
  1125.0 3.2 copy-start.11
  1132.1 2.2 copy-start.21
  1133.2 2.2 copy-start.20
  (15 other events, 20.4 us)
Sparse Core Ops, SparseCore 0:
  9.6 25.2 all-gather.9
  36.4 22.5 all-gather.11
  60.6 22.5 all-gather.13
  84.7 22.6 all-gather.15
  108.8 43.4 all-gather.17
  153.7 43.2 all-gather.19
  198.6 43.4 all-gather.21
  352.9 31.8 reduce-scatter.13
  626.7 29.1 reduce-scatter.9
  660.0 30.2 reduce-scatter.11
  693.6 31.3 reduce-scatter.7
  727.4 54.8 reduce-scatter.15
  785.0 54.8 reduce-scatter.17
  842.3 54.8 reduce-scatter.19
  903.4 221.5 all-reduce.6
where the time goes:
time: 1160 us; the launch traced here: 1140 us
  waiting for transfers between devices  444 us (38%)
  matrix products  287 us (25%)
  other arithmetic  146 us (13%)
  local copies, waits for them, and re-layouts  113 us (10%)
  blocking collectives  102 us (9%)
  starting transfers between devices  25.3 us (2%)
  between operations  15.4 us (1%)
    psum x1, waiting for transfers between devices, on_device(): lax.psum(shares[0].astype(jnp.bfloat16), 'seq').astype(jnp.float32)  181 us
    reduce_scatter x1, waiting for transfers between devices, on_device(): lax.psum_scatter(terms[5].astype(jnp.bfloat16), 'fsdp', scatter_dimension...  57.6 us
    reduce_scatter x1, waiting for transfers between devices, on_device(): lax.psum_scatter(terms[4].astype(jnp.bfloat16), 'fsdp', scatter_dimension...  57.3 us
    reduce_scatter x1, waiting for transfers between devices, on_device(): lax.psum_scatter(terms[6].astype(jnp.bfloat16), 'fsdp', scatter_dimension...  57.3 us
    gt x75, other arithmetic, tile_scores(): key_real[None, :] > 0  57.2 us
    dot_general x25, matrix products, grad_step(): jnp.einsum('hqk,hqd->hkd', probabilities.astype(jnp.bfloat16), grad_block...  52.7 us
    dot_general x50, matrix products, tile_scores(): jnp.einsum('hqd,hkd->hqk', query_block, key_tile, preferred_element_type=...  51.7 us
    dot_general x25, matrix products, value_step(): jnp.einsum('hqk,hkd->hqd', probabilities, value_tile, preferred_element_t...  45.5 us
  transfers between devices with their start and end apart: 20, of which 11 were waited for; matrix products, arithmetic and copies ran while one was open for 44% of the time, Pallas kernels for 0%

commit v1 on v0

v1 whole, which is shorter than its diff:
```python
import functools

import jax
import jax.numpy as jnp
from jax import lax
from jax.experimental import pallas as pl
from jax.experimental.pallas import tpu as pltpu
from jax.sharding import PartitionSpec as P

HD = 64
LANES = 128
EPSILON = 1e-06
BLOCKED = -(2.0**100)
ROOT_2_PI = 0.7978845608028654
CUBIC = 0.044715
VMEM_LIMIT = 60 * 1024 * 1024

bf16 = jnp.bfloat16
f32 = jnp.float32


def mm(a, b):
    return jnp.dot(a, b, preferred_element_type=f32)


def mm_nt(a, b):
    return lax.dot_general(a, b, (((1,), (1,)), ((), ())), preferred_element_type=f32)


def mm_tn(a, b):
    return lax.dot_general(a, b, (((0,), (0,)), ((), ())), preferred_element_type=f32)


def params(**extra):
    return pltpu.CompilerParams(vmem_limit_bytes=VMEM_LIMIT, **extra)


def cost(flops, moved, transcendentals=0):
    return pl.CostEstimate(
        flops=int(flops), bytes_accessed=int(moved), transcendentals=int(transcendentals)
    )


def vmem():
    return pl.BlockSpec(memory_space=pltpu.VMEM)


def anywhere():
    return pl.BlockSpec(memory_space=pl.ANY)


def smem():
    return pl.BlockSpec(memory_space=pltpu.SMEM)


def lane_ids(rows):
    return lax.broadcasted_iota(jnp.int32, (rows, LANES), 1)


def split3(column):
    high = column.astype(bf16)
    rest = column - high.astype(f32)
    middle = rest.astype(bf16)
    low = (rest - middle.astype(f32)).astype(bf16)
    return (high.astype(f32), middle.astype(f32), low.astype(f32))


def project_kernel(heads, fresh, *refs):
    x_ref, gain_ref, w_ref, qt_ref, kt_ref = refs[:5]
    qa_ref, ka_ref, va_ref, h1_ref = refs[5:] if fresh else refs[9:]
    x = x_ref[...].astype(f32)
    scaling = lax.rsqrt(jnp.mean(x * x, axis=-1, keepdims=True) + EPSILON)
    h1 = (x * scaling * gain_ref[...].astype(f32)).astype(bf16)
    h1_ref[...] = h1
    qkv = mm(h1, w_ref[...])
    rows = x.shape[0]
    lane = lane_ids(rows)
    q = qkv[:, :LANES].astype(bf16) * jnp.asarray(HD**-0.5, bf16)
    k = qkv[:, LANES : 2 * LANES].astype(bf16)
    v = qkv[:, 2 * LANES :].astype(bf16)
    ones = jnp.where(lane % HD < 3, 1.0, 0.0).astype(bf16)
    for head in range(heads):
        own = lane // HD == head
        qa_ref[head] = jnp.where(own, q, qt_ref[...])
        ka_ref[head] = jnp.where(own, k, kt_ref[...])
        va_ref[head] = jnp.where(own, v, ones)


def project(slot, slots, heads, x, gain, w, q_table, k_table, previous):
    rows, width = x.shape
    total = rows * slots
    row_spec = pl.BlockSpec((rows, LANES), lambda i: (slot, 0))
    head_spec = pl.BlockSpec((heads, rows, LANES), lambda i: (0, slot, 0))
    shapes = [jax.ShapeDtypeStruct((heads, total, LANES), bf16)] * 3 + [
        jax.ShapeDtypeStruct((total, width), bf16)
    ]
    fresh = previous is None
    extra = () if fresh else tuple(previous)
    return pl.pallas_call(
        functools.partial(project_kernel, heads, fresh),
        grid=(1,),
        in_specs=[
            pl.BlockSpec((rows, width), lambda i: (0, 0)),
            pl.BlockSpec((1, width), lambda i: (0, 0)),
            pl.BlockSpec(w.shape, lambda i: (0, 0)),
            row_spec,
            row_spec,
        ]
        + [anywhere()] * len(extra),
        out_specs=[head_spec] * 3 + [pl.BlockSpec((rows, width), lambda i: (slot, 0))],
        out_shape=shapes,
        input_output_aliases={} if fresh else {5 + i: i for i in range(4)},
        compiler_params=params(),
        cost_estimate=cost(2 * rows * width * 3 * LANES, 4 * rows * width + 2 * w.size),
        name="project",
    )(x, gain, w, q_table, k_table, *extra)


def forward_kernel(heads, slots, rows, q_ref, k_ref, v_ref, *outs):
    lane = lane_ids(rows)
    att_refs, sum_ref, qb_ref = outs[:slots], outs[slots], outs[slots + 1]
    for index in range(slots):
        span = slice(index * rows, (index + 1) * rows)
        merged = None
        for head in range(heads):
            q = q_ref[head, span, :]
            own = lane // HD == head
            other = HD if head == 0 else 0
            scores = mm_nt(q, k_ref[head])
            key = k_ref[head, pl.ds(pl.multiple_of(outs[-1][index] * rows, rows), rows), :]
            value = v_ref[head, pl.ds(pl.multiple_of(outs[-1][index] * rows, rows), rows), :]
            q_wide = q.astype(f32)
            padded = q_wide[:, other + HD - 1 : other + HD] > 0.5
            own_score = jnp.sum(
                jnp.where(own, q_wide * key.astype(f32), 0.0), axis=-1, keepdims=True
            )
            top = jnp.max(scores, axis=-1, keepdims=True)
            top = jnp.where(padded, jnp.maximum(top, own_score), top)
            weights = jnp.exp(scores - top).astype(bf16)
            mixed = mm(weights, v_ref[head])
            own_weight = jnp.where(padded, jnp.exp(own_score - top), 0.0).astype(bf16).astype(f32)
            mixed = mixed + own_weight * value.astype(f32)
            total = mixed[:, other : other + 1]
            log_total = top + jnp.log(total)
            mixed = mixed * (1.0 / total)
            merged = mixed if merged is None else jnp.where(own, mixed, merged)
            parts = split3(-log_total)
            base = other + HD - 4
            filled = q_wide
            for place, part in enumerate(parts):
                filled = jnp.where(lane == base + place, part, filled)
            qb_ref[head, span, :] = filled.astype(bf16)
        att_refs[index][...] = merged.astype(bf16)
        sum_ref[span, :] = merged


def forward_body(heads, slots, rows, where_ref, *refs):
    forward_kernel(heads, slots, rows, *refs, where_ref)


def attend(qa, ka, va, group, slots):
    heads, total, _ = qa.shape
    rows = total // slots
    count = len(group)
    first = group[0]
    assert list(group) == list(range(first, first + count)) and first % count == 0
    span = rows * count
    where = jnp.arange(first, first + count, dtype=jnp.int32)
    return pl.pallas_call(
        functools.partial(forward_body, heads, count, rows),
        grid=(1,),
        in_specs=[
            smem(),
            pl.BlockSpec((heads, span, LANES), lambda i: (0, first // count, 0)),
            pl.BlockSpec(ka.shape, lambda i: (0, 0, 0)),
            pl.BlockSpec(va.shape, lambda i: (0, 0, 0)),
        ],
        out_specs=[pl.BlockSpec((rows, LANES), lambda i: (0, 0))] * count
        + [
            pl.BlockSpec((span, LANES), lambda i: (0, 0)),
            pl.BlockSpec((heads, span, LANES), lambda i: (0, 0, 0)),
        ],
        out_shape=[jax.ShapeDtypeStruct((rows, LANES), bf16)] * count
        + [
            jax.ShapeDtypeStruct((span, LANES), f32),
            jax.ShapeDtypeStruct((heads, span, LANES), bf16),
        ],
        compiler_params=params(),
        cost_estimate=cost(
            16 * heads * span * total * LANES, 4 * heads * total * LANES, heads * span * total
        ),
        name="attend",
    )(where, qa, ka, va)


def backward_kernel(heads, parts, rows, count, tile, first, has_dq, *refs):
    total = parts * rows
    dq_in, refs = (refs[0], refs[1:]) if has_dq else (None, refs)
    qb_refs = refs[:1]
    k_ref, v_ref, sum_ref = refs[1:4]
    grad_refs = refs[4 : 4 + parts]
    outs = refs[4 + parts :]
    dk_refs, dv_refs = outs[:count], outs[count : 2 * count]
    dq_ref = outs[2 * count]
    gb, dq_acc, dk_acc, dv_acc = outs[2 * count + 1 :]
    qb = qb_refs[0]
    lane = lane_ids(rows)
    for part in range(parts):
        span = slice(part * rows, (part + 1) * rows)
        grad = grad_refs[part][...].astype(f32)
        product = grad * sum_ref[span, :]
        for head in range(heads):
            other = HD if head == 0 else 0
            own = lane // HD == head
            delta = jnp.sum(jnp.where(own, product, 0.0), axis=-1, keepdims=True)
            filled = jnp.where(own, grad, 0.0)
            for place, piece in enumerate(split3(-delta)):
                filled = jnp.where(lane == other + place, piece, filled)
            gb[head, span, :] = filled.astype(bf16)
    if has_dq:
        dq_acc[...] = dq_in[...]
    else:
        dq_acc[...] = jnp.zeros_like(dq_acc)
    for index in range(count):
        begin = (first + index) * rows
        dk_acc[...] = jnp.zeros_like(dk_acc)
        dv_acc[...] = jnp.zeros_like(dv_acc)

        def step(number, carry):
            at = pl.ds(pl.multiple_of(number * tile, tile), tile)
            for head in range(heads):
                key = k_ref[head, begin : begin + rows, :]
                value = v_ref[head, begin : begin + rows, :]
                q = qb[head, at, :]
                g = gb[head, at, :]
                weights = jnp.exp(mm_nt(key, q))
                inner = mm_nt(value, g)
                score_grad = (weights * inner).astype(bf16)
                dv_acc[head] += mm(weights.astype(bf16), g)
                dk_acc[head] += mm(score_grad, q)
                dq_acc[head, at, :] += mm_tn(score_grad, key)
            return carry

        lax.fori_loop(0, total // tile, step, 0)
        span = slice(begin, begin + rows)
        dk_all, dv_all = None, None
        for head in range(heads):
            other = HD if head == 0 else 0
            own = lane // HD == head
            counted = own | ((lane >= other + HD - 4) & (lane < other + HD - 1))
            q = qb[head, span, :].astype(f32)
            k = k_ref[head, span, :].astype(f32)
            v = v_ref[head, span, :].astype(f32)
            g = gb[head, span, :].astype(f32)
            padded = q[:, other + HD - 1 : other + HD] > 0.5
            score = jnp.sum(jnp.where(counted, q * k, 0.0), axis=-1, keepdims=True)
            weight = jnp.where(padded, jnp.exp(score), 0.0)
            inner = jnp.sum(v * g, axis=-1, keepdims=True)
            score_grad = (weight * inner).astype(bf16).astype(f32)
            weight = weight.astype(bf16).astype(f32)
            dk = dk_acc[head] + score_grad * q
            dv = dv_acc[head] + weight * g
            dq_acc[head, span, :] += score_grad * k
            dk_all = dk if head == 0 else jnp.where(own, dk, dk_all)
            dv_all = dv if head == 0 else jnp.where(own, dv, dv_all)
        dk_refs[index][...] = dk_all.astype(bf16)
        dv_refs[index][...] = dv_all.astype(bf16)
    dq_ref[...] = dq_acc[...]


def attend_back(qb, ka, va, sums, grads, group, slots, dq_before):
    heads, total, _ = ka.shape
    rows = total // slots
    parts = len(grads)
    count = len(group)
    tile = 512
    part_rows = total // parts
    dq_shape = jax.ShapeDtypeStruct((heads, total, LANES), f32)
    inputs = ([] if dq_before is None else [dq_before]) + [qb, ka, va, sums] + list(grads)
    assert part_rows == rows
    out = pl.pallas_call(
        functools.partial(
            backward_kernel, heads, parts, rows, count, tile, group[0], dq_before is not None
        ),
        in_specs=[vmem()] * len(inputs),
        out_specs=[vmem()] * (2 * count + 1),
        out_shape=[jax.ShapeDtypeStruct((rows, LANES), bf16)] * (2 * count) + [dq_shape],
        scratch_shapes=[
            pltpu.VMEM((heads, total, LANES), bf16),
            pltpu.VMEM((heads, total, LANES), f32),
            pltpu.VMEM((heads, rows, LANES), f32),
            pltpu.VMEM((heads, rows, LANES), f32),
        ],
        compiler_params=params(),
        cost_estimate=cost(
            40 * heads * count * rows * total * LANES,
            12 * heads * total * LANES,
            heads * count * rows * total,
        ),
        name="attend_back",
    )(*inputs)
    return (out[:count], out[count : 2 * count], out[2 * count])


def middle_kernel(blocks, pieces, step_width, *refs):
    att_rows, w_rows = refs[0], refs[1]
    refs = refs[2:]
    att_refs = refs[:blocks]
    x_ref, c_ref, gain_ref = refs[blocks : blocks + 3]
    refs = refs[blocks + 3 :]
    wo_refs, wg_refs, wu_refs, wd_refs = [refs[i * pieces : (i + 1) * pieces] for i in range(4)]
    refs = refs[4 * pieces :]
    out_ref, dmid_ref = refs[:2]
    da_refs = refs[2 : 2 + blocks]
    refs = refs[2 + blocks :]
    og_refs, gg_refs, ug_refs, dg_refs = [refs[i * pieces : (i + 1) * pieces] for i in range(4)]
    refs = refs[4 * pieces :]
    wo, wg, wu, wd, og, gg, ug, dg, att, h2_ref, mid_ref, acc_out, acc_back = refs[:13]
    in_sems, out_sems = refs[13:]

    loads = []
    for number, (sources, target) in enumerate(((wo_refs, wo), (wg_refs, wg), (wu_refs, wu), (wd_refs, wd))):
        step_rows = target.shape[0] // pieces
        for piece in range(pieces):
            at = pl.ds(pl.multiple_of(w_rows[piece] * step_rows, step_rows), step_rows)
            copy = pltpu.make_async_copy(sources[piece], target.at[at, :], in_sems.at[number, piece])
            copy.start()
            loads.append(copy)

    width = x_ref.shape[1]
    block_width = width // blocks
    for block in range(blocks):
        at = pl.ds(pl.multiple_of(att_rows[block] * block_width, block_width), block_width)
        att[:, at] = att_refs[block][...]
    for copy in loads[:pieces]:
        copy.wait()
    gain = gain_ref[...].astype(f32)
    middle = x_ref[...].astype(f32) + mm(att[...], wo[...])
    scaling = lax.rsqrt(jnp.mean(middle * middle, axis=-1, keepdims=True) + EPSILON)
    h2_ref[...] = (middle * scaling * gain).astype(bf16)
    mid_ref[...] = middle
    acc_out[...] = jnp.zeros_like(acc_out)
    acc_back[...] = jnp.zeros_like(acc_back)
    for copy in loads[pieces:]:
        copy.wait()

    def column_step(number, carry):
        at = pl.ds(pl.multiple_of(number * step_width, step_width), step_width)
        h2 = h2_ref[...]
        c = c_ref[...]
        gate = mm(h2, wg[:, at])
        up = mm(h2, wu[:, at])
        act_grad = mm_nt(c, wd[at, :])
        square = gate * gate
        bend = jnp.tanh(gate * (ROOT_2_PI + (ROOT_2_PI * CUBIC) * square))
        half = 0.5 * (1.0 + bend)
        curve = gate * half
        slope = half + (0.5 * gate) * (1.0 - bend * bend) * (
            ROOT_2_PI + (3.0 * ROOT_2_PI * CUBIC) * square
        )
        act = (curve * up).astype(bf16)
        d_up = (act_grad * curve).astype(bf16)
        d_gate = (act_grad * up * slope).astype(bf16)
        acc_out[...] += mm(act, wd[at, :])
        dg[at, :] = mm_tn(act, c).astype(bf16)
        gg[:, at] = mm_tn(h2, d_gate).astype(bf16)
        ug[:, at] = mm_tn(h2, d_up).astype(bf16)
        acc_back[...] += mm_nt(d_gate, wg[:, at]) + mm_nt(d_up, wu[:, at])
        return carry

    lax.fori_loop(0, wg.shape[1] // step_width, column_step, 0)

    stores = []

    def send_out(number, source, targets):
        step_rows = source.shape[0] // pieces
        for piece in range(pieces):
            at = pl.ds(pl.multiple_of(w_rows[piece] * step_rows, step_rows), step_rows)
            copy = pltpu.make_async_copy(source.at[at, :], targets[piece], out_sems.at[number, piece])
            copy.start()
            stores.append(copy)

    send_out(1, gg, gg_refs)
    send_out(2, ug, ug_refs)
    send_out(3, dg, dg_refs)
    middle = mid_ref[...]
    scaling = lax.rsqrt(jnp.mean(middle * middle, axis=-1, keepdims=True) + EPSILON)
    out_ref[...] = (middle + acc_out[...]).astype(bf16)
    incoming = acc_back[...] * gain
    centre = jnp.mean(incoming * middle, axis=-1, keepdims=True)
    d_middle = (
        c_ref[...].astype(f32) + scaling * incoming - middle * (scaling * scaling * scaling * centre)
    )
    dmid_ref[...] = d_middle
    branch = d_middle.astype(bf16)
    og[...] = mm_tn(att[...], branch).astype(bf16)
    send_out(0, og, og_refs)
    att[...] = mm_nt(branch, wo[...]).astype(bf16)
    for block in range(blocks):
        at = pl.ds(pl.multiple_of(att_rows[block] * block_width, block_width), block_width)
        da_refs[block][...] = att[:, at]
    for copy in stores:
        copy.wait()


def middle_stage(att_rows, w_rows, att_blocks, x, c, gain, wo, wg, wu, wd):
    blocks, pieces = len(att_blocks), len(wo)
    rows, width = x.shape
    hidden = wg[0].shape[1]
    step_width = 256
    piece_shapes = [w[0].shape for w in (wo, wg, wu, wd)]
    out_shape = (
        [jax.ShapeDtypeStruct((rows, width), bf16), jax.ShapeDtypeStruct((rows, width), f32)]
        + [jax.ShapeDtypeStruct(att_blocks[0].shape, bf16)] * blocks
        + [jax.ShapeDtypeStruct(s, bf16) for s in piece_shapes for _ in range(pieces)]
    )
    full = [(width, width), (width, hidden), (width, hidden), (hidden, width)]
    weights = list(wo) + list(wg) + list(wu) + list(wd)
    out = pl.pallas_call(
        functools.partial(middle_kernel, blocks, pieces, step_width),
        in_specs=[smem(), smem()]
        + [vmem()] * (blocks + 3)
        + [pl.BlockSpec(memory_space=pltpu.HBM)] * len(weights),
        out_specs=[vmem()] * (2 + blocks) + [pl.BlockSpec(memory_space=pltpu.HBM)] * len(weights),
        out_shape=out_shape,
        scratch_shapes=[pltpu.VMEM(s, bf16) for s in full]
        + [pltpu.VMEM(s, bf16) for s in full]
        + [
            pltpu.VMEM((rows, width), bf16),
            pltpu.VMEM((rows, width), bf16),
            pltpu.VMEM((rows, width), f32),
            pltpu.VMEM((rows, width), f32),
            pltpu.VMEM((rows, width), f32),
            pltpu.SemaphoreType.DMA((4, pieces)),
            pltpu.SemaphoreType.DMA((4, pieces)),
        ],
        compiler_params=params(),
        cost_estimate=cost(
            2 * rows * width * (9 * hidden + 3 * width), 4 * (width * width + 3 * width * hidden)
        ),
        name="middle_stage",
    )(att_rows, w_rows, *att_blocks, x, c, gain, *weights)
    layer_out, d_middle = out[:2]
    d_att = out[2 : 2 + blocks]
    rest = out[2 + blocks :]
    grads = [rest[i * pieces : (i + 1) * pieces] for i in range(4)]
    return (layer_out, d_middle, d_att, grads)


def last_kernel(blocks, pieces, *refs):
    att_rows, w_rows = refs[0], refs[1]
    refs = refs[2:]
    grad_refs = [refs[i * blocks : (i + 1) * blocks] for i in range(3)]
    refs = refs[3 * blocks :]
    x_ref, dmid_ref, gain_ref = refs[:3]
    weight_refs = [refs[3 + i * pieces : 3 + (i + 1) * pieces] for i in range(3)]
    out_ref, grad, total = refs[3 + 3 * pieces :]
    width = x_ref.shape[1]
    block_width = width // blocks
    piece_width = width // pieces
    for kind in range(3):
        for block in range(blocks):
            at = pl.ds(pl.multiple_of(att_rows[block] * block_width, block_width), block_width)
            grad[kind, :, at] = grad_refs[kind][block][...]
    for piece in range(pieces):
        at = pl.ds(pl.multiple_of(w_rows[piece] * piece_width, piece_width), piece_width)
        total[:, at] = (
            mm_nt(grad[0], weight_refs[0][piece][...])
            + mm_nt(grad[1], weight_refs[1][piece][...])
            + mm_nt(grad[2], weight_refs[2][piece][...])
        )
    x = x_ref[...].astype(f32)
    scaling = lax.rsqrt(jnp.mean(x * x, axis=-1, keepdims=True) + EPSILON)
    incoming = total[...] * gain_ref[...].astype(f32)
    centre = jnp.mean(incoming * x, axis=-1, keepdims=True)
    out_ref[...] = dmid_ref[...] + scaling * incoming - x * (scaling * scaling * scaling * centre)


def last_stage(att_rows, w_rows, grads, x, d_middle, gain, weights):
    blocks, pieces = len(grads[0]), len(weights[0])
    rows, width = x.shape
    flat = [g for kind in grads for g in kind]
    flat_weights = [w for kind in weights for w in kind]
    return pl.pallas_call(
        functools.partial(last_kernel, blocks, pieces),
        in_specs=[smem(), smem()] + [vmem()] * (len(flat) + 3 + len(flat_weights)),
        out_specs=vmem(),
        out_shape=jax.ShapeDtypeStruct((rows, width), f32),
        scratch_shapes=[pltpu.VMEM((3, rows, width), bf16), pltpu.VMEM((rows, width), f32)],
        compiler_params=params(),
        cost_estimate=cost(6 * rows * width * width, 6 * width * width),
        name="last_stage",
    )(att_rows, w_rows, *flat, x, d_middle, gain, *flat_weights)


def flip(values, axis, delta):
    count = lax.axis_size(axis)
    return lax.ppermute(values, axis, [(i, i ^ delta) for i in range(count)])


def bits_of(count):
    return [1 << i for i in range(count.bit_length() - 1)]


def gather_pieces(values, axis):
    pieces = {0: values}
    for bit in reversed(bits_of(lax.axis_size(axis))):
        for delta in list(pieces):
            pieces[delta | bit] = flip(pieces[delta], axis, bit)
    return [pieces[delta] for delta in range(len(pieces))]


def add_low(a, b):
    return (a.astype(f32) + b.astype(f32)).astype(bf16)


def scatter_pieces(pieces, axis):
    current = dict(enumerate(pieces))
    for bit in bits_of(lax.axis_size(axis)):
        current = {
            delta: add_low(value, flip(current[delta | bit], axis, bit))
            for delta, value in current.items()
            if not delta & bit
        }
    return current[0]


def sum_over(values, axis):
    place = lax.axis_index(axis)
    bits = bits_of(lax.axis_size(axis))
    for bit in bits:
        half = values.shape[0] // 2
        mine = (place // bit) % 2
        kept = lax.dynamic_slice_in_dim(values, mine * half, half, axis=0)
        given = lax.dynamic_slice_in_dim(values, (1 - mine) * half, half, axis=0)
        values = add_low(kept, flip(given, axis, bit))
    return gather_rows(values, axis, reversed(bits))


def gather_rows(values, axis, bits):
    place = lax.axis_index(axis)
    for bit in bits:
        other = flip(values, axis, bit)
        upper = ((place // bit) % 2) == 1
        values = jnp.concatenate(
            [jnp.where(upper, other, values), jnp.where(upper, values, other)], axis=0
        )
    return values


def gather_blocks_chain(values):
    seq = lax.axis_index("seq")
    place = seq // 2

    def move(array, pairs):
        return lax.ppermute(
            array, "seq", [(a * 2 + low, b * 2 + low) for a, b in pairs for low in range(2)]
        )

    right_1 = move(values, [(1, 0), (2, 1), (3, 2)])
    left_1 = move(values, [(0, 1), (1, 2), (2, 3)])
    right_2 = move(right_1, [(1, 0), (2, 1)])
    left_2 = move(left_1, [(1, 2), (2, 3)])
    near = jnp.where(place % 2 == 0, right_1, left_1)
    far = jnp.where(place < 2, right_2, left_2)
    third = move(far, [(1, 0), (2, 3)])
    cross = jnp.where((place == 0) | (place == 3), third, jnp.where(place == 1, right_1, left_1))
    columns = [values, near, far, cross]
    blocks = []
    for column in columns:
        blocks += [column, flip(column, "seq", 1)]
    return blocks


def exchange_blocks(blocks):
    return [blocks[0]] + [flip(blocks[d], "seq", d) for d in range(1, len(blocks))]


def mask_tables(lengths_row, order_row, real_row, block_order, slots):
    total = order_row.shape[0]
    segments = lengths_row.shape[0]
    ends_at = jnp.cumsum(lengths_row)
    positions = jnp.arange(total, dtype=jnp.int32)
    packed_segment = jnp.sum((positions[:, None] >= ends_at[None, :]).astype(jnp.int32), axis=1)
    packed_code = packed_segment * 2 + (real_row > 0).astype(jnp.int32)
    code = jnp.sum(
        jnp.where(positions[:, None] == order_row[None, :], packed_code[None, :], 0), axis=1
    )
    code = jnp.take(code.reshape(slots, total // slots), block_order, axis=0).reshape(total, 1)
    segment, real = code // 2, code % 2
    lane = jnp.arange(LANES, dtype=jnp.int32)[None, :] % HD
    same = lane == segment
    q_table = jnp.where(same | ((lane == HD - 1) & (real == 0)), 1.0, 0.0).astype(bf16)
    open_to = same & (real == 1)
    k_table = jnp.where(
        lane < segments,
        jnp.where(open_to, 0.0, BLOCKED),
        jnp.where((lane >= HD - 4) & (lane < HD - 1), 1.0, 0.0),
    ).astype(bf16)
    return (q_table, k_table)


def on_device(
    tokens,
    cotangent,
    query_weight,
    key_weight,
    value_weight,
    output_weight,
    gate_weight,
    up_weight,
    down_weight,
    attention_gain,
    feedforward_gain,
    lengths,
    token_order,
    real_token,
):
    x, c = tokens[0], cotangent[0]
    rows, width = x.shape
    slots = lax.axis_size("seq")
    shards = lax.axis_size("fsdp")
    seq, shard = lax.axis_index("seq"), lax.axis_index("fsdp")
    direct = slots == 8 and shards == 4
    heads = width // slots // HD
    own_width = heads * HD
    zero = jnp.zeros((1,), jnp.int32)
    if direct:
        block_order = seq ^ jnp.arange(slots, dtype=jnp.int32)
        att_rows = block_order
        w_rows = shard ^ jnp.arange(shards, dtype=jnp.int32)
    else:
        block_order = jnp.arange(slots, dtype=jnp.int32)
        att_rows, w_rows = zero, zero

    def gather_weight(w):
        if direct:
            return gather_pieces(w, "fsdp")
        return [lax.all_gather(w, "fsdp", axis=0, tiled=True)]

    def reduce_weight(pieces):
        if direct:
            return sum_over(scatter_pieces(pieces, "fsdp"), "seq")
        part = lax.psum_scatter(pieces[0], "fsdp", scatter_dimension=0, tiled=True)
        return lax.psum(part, "seq")

    own_columns = [
        lax.dynamic_slice_in_dim(w, seq * own_width, own_width, axis=1)
        for w in (query_weight, key_weight, value_weight)
    ]
    own_columns = jnp.concatenate(
        [jnp.pad(w, ((0, 0), (0, LANES - own_width))) for w in own_columns], axis=1
    )
    gains = jnp.stack([attention_gain, feedforward_gain])
    if direct:
        column_pieces = jnp.stack(gather_pieces(own_columns, "fsdp"))
        own_columns_full = jnp.take(column_pieces, w_rows, axis=0).reshape(width, 3 * LANES)
        gain_pieces = jnp.stack(gather_pieces(gains, "fsdp"))
        gains_full = jnp.take(gain_pieces, w_rows, axis=0).transpose(1, 0, 2).reshape(2, width)
        x_blocks = gather_blocks_chain(x)
    else:
        own_columns_full = lax.all_gather(own_columns, "fsdp", axis=0, tiled=True)
        gains_full = lax.all_gather(gains, "fsdp", axis=1, tiled=True)
        gathered = lax.all_gather(x, "seq", axis=0)
        x_blocks = [gathered[i] for i in range(slots)]
    gain_1, gain_2 = gains_full[0:1], gains_full[1:2]

    q_table, k_table = mask_tables(lengths[0], token_order[0], real_token[0], block_order, slots)
    state = None
    for slot in range(slots):
        state = project(
            slot, slots, heads, x_blocks[slot], gain_1, own_columns_full, q_table, k_table, state
        )
    qa, ka, va, h1 = state

    att_slots, sums, qbs = [None] * slots, [None] * 4, [None] * 4
    per_call = slots // 4
    for quarter in (3, 2, 1, 0):
        group = list(range(quarter * per_call, (quarter + 1) * per_call))
        out = attend(qa, ka, va, group, slots)
        att_slots[quarter * per_call : (quarter + 1) * per_call] = out[:per_call]
        sums[quarter], qbs[quarter] = out[per_call], out[per_call + 1]
    sums = jnp.concatenate(sums, axis=0)
    qb = jnp.concatenate(qbs, axis=1)

    wo, wg, wu, wd = [
        gather_weight(w) for w in (output_weight, gate_weight, up_weight, down_weight)
    ]
    if direct:
        att_blocks = exchange_blocks(att_slots)
    else:
        stacked = jnp.concatenate(att_slots, axis=0)[:, :own_width]
        att_blocks = [lax.all_to_all(stacked, "seq", split_axis=0, concat_axis=1, tiled=True)]
    layer_out, d_middle, d_att, (og, gg, ug, dg) = middle_stage(
        att_rows, w_rows, att_blocks, x, c, gain_2, wo, wg, wu, wd
    )
    if direct:
        grad_blocks = exchange_blocks(d_att)
    else:
        moved = lax.all_to_all(d_att[0], "seq", split_axis=1, concat_axis=0, tiled=True)
        moved = jnp.pad(moved, ((0, 0), (0, LANES - own_width)))
        grad_blocks = [moved[i * rows : (i + 1) * rows] for i in range(slots)]

    down_grad = reduce_weight(dg)
    gate_grad = reduce_weight(gg)
    up_grad = reduce_weight(ug)
    output_grad = reduce_weight(og)

    qkv_weights = [gather_weight(w) for w in (query_weight, key_weight, value_weight)]
    dk_slots, dv_slots = [None] * slots, [None] * slots
    dq = None
    for quarter in (3, 2, 1, 0):
        group = list(range(quarter * per_call, (quarter + 1) * per_call))
        dk_part, dv_part, dq = attend_back(qb, ka, va, sums, grad_blocks, group, slots, dq)
        dk_slots[quarter * per_call : (quarter + 1) * per_call] = dk_part
        dv_slots[quarter * per_call : (quarter + 1) * per_call] = dv_part
    scale = HD**-0.5
    if heads == 2:
        lane = jnp.arange(LANES, dtype=jnp.int32)[None, :]
        dq = jnp.where(lane < HD, dq[0], dq[1])
    else:
        dq = dq[0]
    dq = (dq * scale).astype(bf16)
    dq_slots = [dq[i * rows : (i + 1) * rows] for i in range(slots)]
    all_grads = jnp.concatenate(
        [dq, jnp.concatenate(dk_slots, axis=0), jnp.concatenate(dv_slots, axis=0)], axis=1
    )
    if direct:
        moved_grads = [exchange_blocks(s) for s in (dq_slots, dk_slots, dv_slots)]
    else:
        moved_grads = [
            [
                lax.all_to_all(
                    all_grads[:, i * LANES : i * LANES + own_width],
                    "seq",
                    split_axis=0,
                    concat_axis=1,
                    tiled=True,
                )
            ]
            for i in range(3)
        ]
    own_term = mm_tn(h1, all_grads).astype(bf16)
    if direct:
        own_pieces = jnp.take(own_term.reshape(shards, width // shards, 3 * LANES), w_rows, axis=0)
        own_share = scatter_pieces([own_pieces[i] for i in range(shards)], "fsdp")
        all_shares = gather_rows(own_share[None], "seq", [4, 2, 1])
        all_shares = all_shares.reshape((2, 2, 2) + own_share.shape).transpose(2, 1, 0, 3, 4)
    else:
        own_share = lax.psum_scatter(own_term, "fsdp", scatter_dimension=0, tiled=True)
        all_shares = lax.all_gather(own_share, "seq", axis=0)
    shard_rows = width // shards
    all_shares = all_shares.reshape(slots, shard_rows, 3, LANES)[..., :own_width].astype(f32)
    query_grad, key_grad, value_grad = [
        all_shares[:, :, i, :].transpose(1, 0, 2).reshape(shard_rows, width) for i in range(3)
    ]
    input_grad = last_stage(att_rows, w_rows, moved_grads, x, d_middle, gain_1, qkv_weights)

    def gain_grad(terms, gain):
        summed = sum(jnp.sum(g * w.astype(f32), axis=1) for g, w in terms)
        return summed / gain.astype(f32)

    output_grad, gate_grad, up_grad, down_grad = [
        g.astype(f32) for g in (output_grad, gate_grad, up_grad, down_grad)
    ]
    attention_gain_grad = gain_grad(
        ((query_grad, query_weight), (key_grad, key_weight), (value_grad, value_weight)),
        attention_gain,
    )
    feedforward_gain_grad = gain_grad(
        ((gate_grad, gate_weight), (up_grad, up_weight)), feedforward_gain
    )
    return (
        layer_out[None],
        input_grad[None],
        query_grad,
        key_grad,
        value_grad,
        output_grad,
        gate_grad,
        up_grad,
        down_grad,
        attention_gain_grad,
        feedforward_gain_grad,
    )


def solution(mesh):
    in_specs = (
        P("fsdp", "seq", None),
        P("fsdp", "seq", None),
        P("fsdp", None),
        P("fsdp", None),
        P("fsdp", None),
        P("fsdp", None),
        P("fsdp", None),
        P("fsdp", None),
        P("fsdp", None),
        P("fsdp"),
        P("fsdp"),
        P("fsdp", None),
        P("fsdp", None),
        P("fsdp", None),
    )
    out_specs = (
        P("fsdp", "seq", None),
        P("fsdp", "seq", None),
        P("fsdp", None),
        P("fsdp", None),
        P("fsdp", None),
        P("fsdp", None),
        P("fsdp", None),
        P("fsdp", None),
        P("fsdp", None),
        P("fsdp"),
        P("fsdp"),
    )
    return jax.shard_map(
        on_device, mesh=mesh, in_specs=in_specs, out_specs=out_specs, check_vma=False
    )
```

time: 1160 us -> 707 us (0.61)
  matrix products: 287 us -> 6.29 us
  Pallas kernels: 0 us -> 177 us
  waiting for transfers between devices: 444 us -> 324 us
  blocking collectives: 102 us -> 0 us
  other arithmetic: 146 us -> 53.7 us
  local copies, waits for them, and re-layouts: 113 us -> 30.5 us
  starting transfers between devices: 25.3 us -> 107 us
  between operations: 15.4 us -> 2.88 us
    ppermute x0 -> x113, waiting for transfers between devices: none -> 324 us  [the longest x108 296 us: flip(): return lax.ppermute(values, axis, [(i, i ^ delta) for i in range(count)])]
    dot_general x196 -> x1, matrix products: 287 us -> 6.29 us  [mm_tn(): lax.dot_general(a, b, (((0,), (0,)), ((), ())), preferred_element_type=f32)]
    reduce_scatter x7 -> x0, waiting for transfers between devices: 182 us -> none  [the longest x1 57.6 us: on_device(): lax.psum_scatter(terms[5].astype(jnp.bfloat16), 'fsdp', scatter_dimension...]
    psum x1 -> x0, waiting for transfers between devices: 181 us -> none  [on_device(): lax.psum(shares[0].astype(jnp.bfloat16), 'seq').astype(jnp.float32)]
    pallas_call x0 -> x18, Pallas kernels: none -> 177 us  [the longest x4 71.8 us: attend_back(): pl.pallas_call(functools.partial(backward_kernel, heads, parts, rows, cou...]
    ppermute x0 -> x113, starting transfers between devices: none -> 107 us  [the longest x108 97.9 us: flip(): return lax.ppermute(values, axis, [(i, i ^ delta) for i in range(count)])]
    all_to_all x3 -> x0, blocking collectives: 62.1 us -> none  [the longest x1 21.1 us: on_device(): lax.all_to_all(from_heads(packed_key_grad, order_row), 'seq', split_axis=...]
    gt x75 -> x0, other arithmetic: 57.2 us -> none  [tile_scores(): key_real[None, :] > 0]
  transfers between devices with their start and end apart: 20 -> 113, of which waited for: 11 -> 52; matrix products, arithmetic and copies ran while one was open for 44% -> 12% of each run, Pallas kernels for 0% -> 19%
where the time goes in v1:
time: 707 us; the launch traced here: 701 us
  waiting for transfers between devices  324 us (46%)
  Pallas kernels  177 us (25%)
  starting transfers between devices  107 us (15%)
  other arithmetic  53.7 us (8%)
  local copies, waits for them, and re-layouts  30.5 us (4%)
    ppermute x108, waiting for transfers between devices, flip(): return lax.ppermute(values, axis, [(i, i ^ delta) for i in range(count)])  296 us
    ppermute x108, starting transfers between devices, flip(): return lax.ppermute(values, axis, [(i, i ^ delta) for i in range(count)])  97.9 us
    pallas_call x4, Pallas kernels, attend_back(): pl.pallas_call(functools.partial(backward_kernel, heads, parts, rows, cou...  71.8 us
    pallas_call x1, Pallas kernels, middle_stage(): pl.pallas_call(functools.partial(middle_kernel, blocks, pieces, step_widt...  40.6 us
    pallas_call x4, Pallas kernels, attend(): pl.pallas_call(functools.partial(forward_body, heads, count, rows), grid=...  31.8 us
    ppermute x5, waiting for transfers between devices, move(): lax.ppermute(array, 'seq', [(a * 2 + low, b * 2 + low) for a, b in pairs...  28.2 us
    pallas_call x8, Pallas kernels, project(): pl.pallas_call(functools.partial(project_kernel, heads, fresh), grid=(1,)...  24.3 us
    unnamed x227, local copies, waits for them, and re-layouts  16.3 us
  transfers between devices with their start and end apart: 113, of which 52 were waited for; matrix products, arithmetic and copies ran while one was open for 12% of the time, Pallas kernels for 19%

profile of v1, /device:TPU:0, one launch (start us, length us, event | category | flops | bytes accessed | tf_op | source)
XLA Modules:
  0.0 701.4 jit_solution(5958935200292551239)
XLA Ops:
  7.5 4.6 collective-permute-start.2
  30.1 13.6 %collective-permute-done.1 = bf16[320,1024]{1,0:T(8,128)(2,1)S(1)} collective-permute-done((bf16[320,1024]{1,0:T(8,128)(2,1)S(1)}, bf16[320,1024]{1,0:T(8,128)(2,1)S(1)}, u32[]{:S(2)}, u32[]{:S(2)}) %collective-permute-start.1) | collective-permute-done | bytes 655392 | tf_op jit(solution)/shard_map/ppermute | solution.py:556
  50.6 13.3 %collective-permute-done.4 = bf16[320,1024]{1,0:T(8,128)(2,1)} collective-permute-done((bf16[320,1024]{1,0:T(8,128)(2,1)}, bf16[320,1024]{1,0:T(8,128)(2,1)}, u32[]{:S(2)}, u32[]{:S(2)}) %collective-permute-start.4) | collective-permute-done | bytes 655392 | tf_op jit(solution)/shard_map/ppermute | solution.py:556
  73.1 6.4 collective-permute-done.12.refs_0_
  79.5 14.0 %collective-permute-done.13.refs_0_ = bf16[320,1024]{1,0:T(8,128)(2,1)} collective-permute-done((bf16[320,1024]{1,0:T(8,128)(2,1)S(1)}, bf16[320,1024]{1,0:T(8,128)(2,1)}, u32[]{:S(2)}, u32[]{:S(2)}) %collective-permute-start.13) | collective-permute-done | bytes 655392 | tf_op jit(solution)/shard_map/ppermute | solution.py:498
  94.2 12.4 %collective-permute-done.5.refs_0_ = bf16[320,1024]{1,0:T(8,128)(2,1)} collective-permute-done((bf16[320,1024]{1,0:T(8,128)(2,1)S(1)}, bf16[320,1024]{1,0:T(8,128)(2,1)}, u32[]{:S(2)}, u32[]{:S(2)}) %collective-permute-start.5) | collective-permute-done | bytes 655392 | tf_op jit(solution)/shard_map/ppermute | solution.py:498
  113.4 3.0 project.10
  119.5 3.0 project.12
  128.6 3.1 project.15
  131.7 7.8 %attend.7 = (bf16[320,128]{1,0:T(8,128)(2,1)}, bf16[320,128]{1,0:T(8,128)(2,1)}, f32[640,128]{1,0:T(8,128)}, bf16[2,640,128]{2,1,0:T(8,128)(2,1)}) custom-call(s32[2]{0:T(128)} %iota_add_fusion.where_ref, bf16[2,2560,128]{2,1,0:T(8,128)(2,1)} %get-tuple-element.134.refs_0_, bf16[2,2560,128]{2,1,0:T(8,128)(2,1)} %get-tuple-element.135.refs_1_.refs_2_, ...), custom_call_target="tpu_custom_call" | custom-call | flops 6710886400 | bytes 2621440 | tf_op jit(solution)/shard_map/attend/pallas_call | solution.py:169
  140.1 8.2 %attend.6 = (bf16[320,128]{1,0:T(8,128)(2,1)}, bf16[320,128]{1,0:T(8,128)(2,1)}, f32[640,128]{1,0:T(8,128)}, bf16[2,640,128]{2,1,0:T(8,128)(2,1)}) custom-call(s32[2]{0:T(128)} %iota_add_fusion.1.where_ref, bf16[2,2560,128]{2,1,0:T(8,128)(2,1)} %get-tuple-element.134.refs_0_, bf16[2,2560,128]{2,1,0:T(8,128)(2,1)} %get-tuple-element.135.refs_1_.refs_2_, ...), custom_call_target="tpu_custom_call" | custom-call | flops 6710886400 | bytes 2621440 | tf_op jit(solution)/shard_map/attend/pallas_call | solution.py:169
  149.0 27.2 %collective-permute-done.32.refs_27_ = bf16[704,1024]{1,0:T(8,128)(2,1)} collective-permute-done((bf16[704,1024]{1,0:T(8,128)(2,1)}, bf16[704,1024]{1,0:T(8,128)(2,1)}, u32[]{:S(2)}, u32[]{:S(2)}) %collective-permute-start.32) | collective-permute-done | bytes 1441824 | tf_op jit(solution)/shard_map/ppermute | solution.py:498
  177.2 7.8 %attend.4 = (bf16[320,128]{1,0:T(8,128)(2,1)}, bf16[320,128]{1,0:T(8,128)(2,1)}, f32[640,128]{1,0:T(8,128)}, bf16[2,640,128]{2,1,0:T(8,128)(2,1)}) custom-call(s32[2]{0:T(128)} %iota.49.where_ref, bf16[2,2560,128]{2,1,0:T(8,128)(2,1)} %get-tuple-element.134.refs_0_, bf16[2,2560,128]{2,1,0:T(8,128)(2,1)} %get-tuple-element.135.refs_1_.refs_2_, ...), custom_call_target="tpu_custom_call" | custom-call | flops 6710886400 | bytes 2621440 | tf_op jit(solution)/shard_map/attend/pallas_call | solution.py:169
  187.1 8.1 %attend.5 = (bf16[320,128]{1,0:T(8,128)(2,1)}, bf16[320,128]{1,0:T(8,128)(2,1)}, f32[640,128]{1,0:T(8,128)}, bf16[2,640,128]{2,1,0:T(8,128)(2,1)}) custom-call(s32[2]{0:T(128)} %iota_add_fusion.2.where_ref, bf16[2,2560,128]{2,1,0:T(8,128)(2,1)} %get-tuple-element.134.refs_0_, bf16[2,2560,128]{2,1,0:T(8,128)(2,1)} %get-tuple-element.135.refs_1_.refs_2_, ...), custom_call_target="tpu_custom_call" | custom-call | flops 6710886400 | bytes 2621440 | tf_op jit(solution)/shard_map/attend/pallas_call | solution.py:169
  195.2 3.5 collective-permute-start.20
  201.6 6.0 collective-permute-done.21.refs_9_
  210.9 3.1 collective-permute-done.19.refs_7_
  220.9 40.6 %middle_stage.1 = (bf16[320,1024]{1,0:T(8,128)(2,1)}, f32[320,1024]{1,0:T(8,128)}, bf16[320,128]{1,0:T(8,128)(2,1)}, bf16[320,128]{1,0:T(8,128)(2,1)}, bf16[320,...) custom-call(s32[8]{0:T(128)} %iota_xor_fusion.1.refs_0_, ...), custom_call_target="tpu_custom_call" | custom-call | flops 18622709760 | bytes 38797312 | tf_op jit(solution)/shard_map/middle_stage/pallas_call | solution.py:419
  279.8 17.2 %attend_back.4 = (bf16[320,128]{1,0:T(8,128)(2,1)}, bf16[320,128]{1,0:T(8,128)(2,1)}, bf16[320,128]{1,0:T(8,128)(2,1)}, bf16[320,128]{1,0:T(8,128)(2,1)}, f32[2,2560,128]{2,1,0:T(8,128)}) custom-call(bf16[2,2560,128]{2,1,0:T(8,128)(2,1)} %copy-done.54, bf16[2,2560,128]{2,1,0:T(8,128)(2,1)} %get-tuple-element.135.refs_1_.refs_2_, ...), custom_call_target="tpu_custom_call" | custom-call | flops 16777216000 | bytes 7864320 | tf_op jit(solution)/shard_map/attend_back/pallas_call | solution.py:281
  297.0 18.4 %attend_back.5 = (bf16[320,128]{1,0:T(8,128)(2,1)}, bf16[320,128]{1,0:T(8,128)(2,1)}, bf16[320,128]{1,0:T(8,128)(2,1)}, bf16[320,128]{1,0:T(8,128)(2,1)}, f32[2,2560,128]{2,1,0:T(8,128)}) custom-call(f32[2,2560,128]{2,1,0:T(8,128)} %get-tuple-element.162.refs_0_, bf16[2,2560,128]{2,1,0:T(8,128)(2,1)} %copy-done.54, ...), custom_call_target="tpu_custom_call" | custom-call | flops 16777216000 | bytes 7864320 | tf_op jit(solution)/shard_map/attend_back/pallas_call | solution.py:281
  315.3 18.0 %attend_back.6 = (bf16[320,128]{1,0:T(8,128)(2,1)}, bf16[320,128]{1,0:T(8,128)(2,1)}, bf16[320,128]{1,0:T(8,128)(2,1)}, bf16[320,128]{1,0:T(8,128)(2,1)}, f32[2,2560,128]{2,1,0:T(8,128)}) custom-call(f32[2,2560,128]{2,1,0:T(8,128)} %get-tuple-element.163.refs_0_, bf16[2,2560,128]{2,1,0:T(8,128)(2,1)} %copy-done.54, ...), custom_call_target="tpu_custom_call" | custom-call | flops 16777216000 | bytes 7864320 | tf_op jit(solution)/shard_map/attend_back/pallas_call | solution.py:281
  333.4 18.3 %attend_back.7 = (bf16[320,128]{1,0:T(8,128)(2,1)}, bf16[320,128]{1,0:T(8,128)(2,1)}, bf16[320,128]{1,0:T(8,128)(2,1)}, bf16[320,128]{1,0:T(8,128)(2,1)}, f32[2,2560,128]{2,1,0:T(8,128)}) custom-call(f32[2,2560,128]{2,1,0:T(8,128)} %get-tuple-element.164.refs_0_, bf16[2,2560,128]{2,1,0:T(8,128)(2,1)} %copy-done.54, ...), custom_call_target="tpu_custom_call" | custom-call | flops 16777216000 | bytes 7864320 | tf_op jit(solution)/shard_map/attend_back/pallas_call | solution.py:281
  357.7 6.3 fusion.6
  387.8 8.8 %collective-permute-done.44.refs_6_ = bf16[320,128]{1,0:T(8,128)(2,1)S(1)} collective-permute-done((bf16[320,128]{1,0:T(8,128)(2,1)S(1)}, bf16[320,128]{1,0:T(8,128)(2,1)S(1)}, u32[]{:S(2)}, u32[]{:S(2)}) %collective-permute-start.44) | collective-permute-done | bytes 81952 | tf_op jit(solution)/shard_map/ppermute | solution.py:498
  436.0 4.4 collective-permute-done.54.refs_17_
  443.2 8.2 %last_stage.1 = f32[320,1024]{1,0:T(8,128)} custom-call(s32[8]{0:T(128)} %iota_xor_fusion.1.refs_0_, s32[4]{0:T(128)} %iota_xor_fusion.refs_1_, bf16[320,128]{1,0:T(8,128)(2,1)} %get-tuple-element.267.refs_2_, bf16[320,128]{1,0:T(8,128)(2,1)} %copy-done.33, bf16[320,128]{1,0:T(8,128)(2,1)} %copy-done.34, bf16[320,128]{1,0:T(8,128)(2,1)} %copy-done.35, ...), custom_call_target="tpu_custom_call" | custom-call | flops 2013265920 | bytes 6291456 | tf_op jit(solution)/shard_map/last_stage/pallas_call | solution.py:484
  455.6 4.3 collective-permute-done.81
  463.2 3.7 collective-permute-done.82
  469.0 4.5 collective-permute-done.83
  475.9 3.4 collective-permute-done.84
  481.2 11.7 %collective-permute-done.76 = bf16[4,256,384]{2,1,0:T(8,128)(2,1)S(1)} collective-permute-done((bf16[4,256,384]{2,1,0:T(8,128)(2,1)S(1)}, bf16[4,256,384]{2,1,0:T(8,128)(2,1)S(1)}, u32[]{:S(2)}, u32[]{:S(2)}) %collective-permute-start.76) | collective-permute-done | bytes 786464 | tf_op jit(solution)/shard_map/ppermute | solution.py:498
  518.2 26.8 %collective-permute-done.88 = bf16[256,2816]{1,0:T(8,128)(2,1)S(1)} collective-permute-done((bf16[256,2816]{1,0:T(8,128)(2,1)S(1)}, bf16[256,2816]{1,0:T(8,128)(2,1)S(1)}, u32[]{:S(2)}, u32[]{:S(2)}) %collective-permute-start.88) | collective-permute-done | bytes 1441824 | tf_op jit(solution)/shard_map/ppermute | solution.py:498
  548.5 25.3 %collective-permute-done.106 = bf16[704,1024]{1,0:T(8,128)(2,1)S(1)} collective-permute-done((bf16[704,1024]{1,0:T(8,128)(2,1)S(1)}, bf16[704,1024]{1,0:T(8,128)(2,1)S(1)}, u32[]{:S(2)}, u32[]{:S(2)}) %collective-permute-start.106) | collective-permute-done | bytes 1441824 | tf_op jit(solution)/shard_map/ppermute | solution.py:498
  580.2 12.0 %collective-permute-done.107 = bf16[352,1024]{1,0:T(8,128)(2,1)S(1)} collective-permute-done((bf16[352,1024]{1,0:T(8,128)(2,1)S(1)}, bf16[352,1024]{1,0:T(8,128)(2,1)S(1)}, u32[]{:S(2)}, u32[]{:S(2)}) %collective-permute-start.107) | collective-permute-done | bytes 720928 | tf_op jit(solution)/shard_map/ppermute | solution.py:498
  595.8 3.9 collective-permute-done.90
  599.8 7.9 %collective-permute-done.108 = bf16[176,1024]{1,0:T(8,128)(2,1)S(1)} collective-permute-done((bf16[176,1024]{1,0:T(8,128)(2,1)S(1)}, bf16[176,1024]{1,0:T(8,128)(2,1)S(1)}, u32[]{:S(2)}, u32[]{:S(2)}) %collective-permute-start.108) | collective-permute-done | bytes 360480 | tf_op jit(solution)/shard_map/ppermute | solution.py:498
  611.0 10.7 %collective-permute-done.91 = bf16[32,2816]{1,0:T(8,128)(2,1)S(1)} collective-permute-done((bf16[32,2816]{1,0:T(8,128)(2,1)S(1)}, bf16[32,2816]{1,0:T(8,128)(2,1)S(1)}, u32[]{:S(2)}, u32[]{:S(2)}) %collective-permute-start.91) | collective-permute-done | bytes 180256 | tf_op jit(solution)/shard_map/ppermute | solution.py:498
  621.8 9.5 %collective-permute-done.109 = bf16[88,1024]{1,0:T(8,128)(2,1)S(1)} collective-permute-done((bf16[88,1024]{1,0:T(8,128)(2,1)S(1)}, bf16[88,1024]{1,0:T(8,128)(2,1)S(1)}, u32[]{:S(2)}, u32[]{:S(2)}) %collective-permute-start.109) | collective-permute-done | bytes 180256 | tf_op jit(solution)/shard_map/ppermute | solution.py:498
  631.5 3.7 collective-permute-done.101
  635.4 3.8 collective-permute-done.92
  642.2 7.6 %collective-permute-done.102 = bf16[64,2816]{1,0:T(8,128)(2,1)S(1)} collective-permute-done((bf16[64,2816]{1,0:T(8,128)(2,1)S(1)}, bf16[64,2816]{1,0:T(8,128)(2,1)S(1)}, u32[]{:S(2)}, u32[]{:S(2)}) %collective-permute-start.102) | collective-permute-done | bytes 360480 | tf_op jit(solution)/shard_map/ppermute | solution.py:498
  650.0 7.4 %collective-permute-done.93 = bf16[64,2816]{1,0:T(8,128)(2,1)S(1)} collective-permute-done((bf16[64,2816]{1,0:T(8,128)(2,1)S(1)}, bf16[64,2816]{1,0:T(8,128)(2,1)S(1)}, u32[]{:S(2)}, u32[]{:S(2)}) %collective-permute-start.93) | collective-permute-done | bytes 360480 | tf_op jit(solution)/shard_map/ppermute | solution.py:498
  657.8 7.4 %collective-permute-done.111 = bf16[176,1024]{1,0:T(8,128)(2,1)S(1)} collective-permute-done((bf16[176,1024]{1,0:T(8,128)(2,1)S(1)}, bf16[176,1024]{1,0:T(8,128)(2,1)S(1)}, u32[]{:S(2)}, u32[]{:S(2)}) %collective-permute-start.111) | collective-permute-done | bytes 360480 | tf_op jit(solution)/shard_map/ppermute | solution.py:498
  665.4 3.6 collective-permute-done.103
  669.3 15.2 %collective-permute-done.94 = bf16[128,2816]{1,0:T(8,128)(2,1)S(1)} collective-permute-done((bf16[128,2816]{1,0:T(8,128)(2,1)S(1)}, bf16[128,2816]{1,0:T(8,128)(2,1)S(1)}, u32[]{:S(2)}, u32[]{:S(2)}) %collective-permute-start.94) | collective-permute-done | bytes 720928 | tf_op jit(solution)/shard_map/ppermute | solution.py:498
  684.7 3.3 multiply_reduce_fusion
  688.0 3.3 multiply_reduce_fusion.1
  692.0 6.9 collective-permute-done.112
  (554 shorter events, 227.4 us)
Async XLA Ops:
  3.2 63.8 %collective-permute-start.10 = (bf16[256,384]{1,0:T(8,128)(2,1)S(1)}, bf16[256,384]{1,0:T(8,128)(2,1)S(1)}, u32[]{:S(2)}, u32[]{:S(2)}) collective-permute-start(bf16[256,384]{1,0:T(8,128)(2,1)S(1)} %get-tuple-element.281), channel_id=1, source_target_pairs={{0,2},{1,3},{2,0},{3,1},{4,6},{5,7},{6,4},{7,5},{8,10},{9,11},{10,... | collective-permute-start | bytes 589832 | tf_op jit(solution)/shard_map/ppermute | solution.py:498
  6.2 61.4 %collective-permute-start.9 = (bf16[256,384]{1,0:T(8,128)(2,1)S(1)}, bf16[256,384]{1,0:T(8,128)(2,1)S(1)}, u32[]{:S(2)}, u32[]{:S(2)}) collective-permute-start(bf16[256,384]{1,0:T(8,128)(2,1)S(1)} %get-tuple-element.281), channel_id=1, source_target_pairs={{0,1},{1,0},{2,3},{3,2},{4,5},{5,4},{6,7},{7,6},{8,9},{9,8},{10,11... | collective-permute-start | bytes 589832 | tf_op jit(solution)/shard_map/ppermute | solution.py:498
  6.2 19.2 %collective-permute-start = (bf16[320,1024]{1,0:T(8,128)(2,1)}, bf16[320,1024]{1,0:T(8,128)(2,1)S(1)}, u32[]{:S(2)}, u32[]{:S(2)}) collective-permute-start(bf16[320,1024]{1,0:T(8,128)(2,1)} %bitcast.84), channel_id=1, source_target_pairs={{8,0},{12,4},{16,8},{20,12},{24,16},{28,20},{9,1},{13,5},{17,9},{2... | collective-permute-start | bytes 1966088 | tf_op jit(solution)/shard_map/ppermute | solution.py:556
  7.5 19.2 %collective-permute-start.2 = (bf16[320,1024]{1,0:T(8,128)(2,1)}, bf16[320,1024]{1,0:T(8,128)(2,1)S(1)}, u32[]{:S(2)}, u32[]{:S(2)}) collective-permute-start(bf16[320,1024]{1,0:T(8,128)(2,1)} %bitcast.85), channel_id=1, source_target_pairs={{0,8},{4,12},{8,16},{12,20},{16,24},{20,28},{1,9},{5,13},{9,17},{1... | collective-permute-start | bytes 1966088 | tf_op jit(solution)/shard_map/ppermute | solution.py:556
  13.5 33.7 %collective-permute-start.7 = (bf16[2,256]{1,0:T(2,128)(2,1)S(1)}, bf16[2,256]{1,0:T(2,128)(2,1)S(1)}, u32[]{:S(2)}, u32[]{:S(2)}) collective-permute-start(bf16[2,256]{1,0:T(2,128)(2,1)S(1)} %pad_maximum_fusion.14), channel_id=1, source_target_pairs={{0,2},{1,3},{2,0},{3,1},{4,6},{5,7},{6,4},{7,5},{8,10},{9,11},{10,... | collective-permute-start | bytes 3080 | tf_op jit(solution)/shard_map/ppermute | solution.py:498
  44.6 19.3 %collective-permute-start.4 = (bf16[320,1024]{1,0:T(8,128)(2,1)}, bf16[320,1024]{1,0:T(8,128)(2,1)}, u32[]{:S(2)}, u32[]{:S(2)}) collective-permute-start(bf16[320,1024]{1,0:T(8,128)(2,1)} %broadcast_select_fusion.11.refs_0_), channel_id=1, source_target_pairs={{8,0},{12,4},{16,24},{20,28},{9,1},{13,5},{17,25},{21,29},{10,2},{... | collective-permute-start | bytes 1966088 | tf_op jit(solution)/shard_map/ppermute | solution.py:556
  47.7 24.1 %collective-permute-start.14 = (bf16[320,1024]{1,0:T(8,128)(2,1)S(1)}, bf16[320,1024]{1,0:T(8,128)(2,1)}, u32[]{:S(2)}, u32[]{:S(2)}) collective-permute-start(bf16[320,1024]{1,0:T(8,128)(2,1)S(1)} %bitcast.89), channel_id=1, source_target_pairs={{0,4},{4,0},{8,12},{12,8},{16,20},{20,16},{24,28},{28,24},{1,5},{5... | collective-permute-start | bytes 1966088 | tf_op jit(solution)/shard_map/ppermute | solution.py:498
  49.8 29.6 %collective-permute-start.12 = (bf16[320,1024]{1,0:T(8,128)(2,1)}, bf16[320,1024]{1,0:T(8,128)(2,1)}, u32[]{:S(2)}, u32[]{:S(2)}) collective-permute-start(bf16[320,1024]{1,0:T(8,128)(2,1)} %broadcast_select_fusion.11.refs_0_), channel_id=1, source_target_pairs={{0,4},{4,0},{8,12},{12,8},{16,20},{20,16},{24,28},{28,24},{1,5},{5... | collective-permute-start | bytes 1966088 | tf_op jit(solution)/shard_map/ppermute | solution.py:498
  65.5 28.1 %collective-permute-start.13 = (bf16[320,1024]{1,0:T(8,128)(2,1)S(1)}, bf16[320,1024]{1,0:T(8,128)(2,1)}, u32[]{:S(2)}, u32[]{:S(2)}) collective-permute-start(bf16[320,1024]{1,0:T(8,128)(2,1)S(1)} %get-tuple-element.248.refs_0_), channel_id=1, source_target_pairs={{0,4},{4,0},{8,12},{12,8},{16,20},{20,16},{24,28},{28,24},{1,5},{5... | collective-permute-start | bytes 1966088 | tf_op jit(solution)/shard_map/ppermute | solution.py:498
  67.0 39.6 %collective-permute-start.5 = (bf16[320,1024]{1,0:T(8,128)(2,1)S(1)}, bf16[320,1024]{1,0:T(8,128)(2,1)}, u32[]{:S(2)}, u32[]{:S(2)}) collective-permute-start(bf16[320,1024]{1,0:T(8,128)(2,1)S(1)} %get-tuple-element.249.refs_0_), channel_id=1, source_target_pairs={{0,4},{4,0},{8,12},{12,8},{16,20},{20,16},{24,28},{28,24},{1,5},{5... | collective-permute-start | bytes 1966088 | tf_op jit(solution)/shard_map/ppermute | solution.py:498
  69.1 62.5 %collective-permute-start.23 = (bf16[256,1024]{1,0:T(8,128)(2,1)}, bf16[256,1024]{1,0:T(8,128)(2,1)}, u32[]{:S(2)}, u32[]{:S(2)}) collective-permute-start(bf16[256,1024]{1,0:T(8,128)(2,1)} %refs_13_.1), channel_id=1, source_target_pairs={{0,2},{1,3},{2,0},{3,1},{4,6},{5,7},{6,4},{7,5},{8,10},{9,11},{10,... | collective-permute-start | bytes 1572872 | tf_op jit(solution)/shard_map/ppermute | solution.py:498
  71.8 76.7 %collective-permute-start.26 = (bf16[256,2816]{1,0:T(8,128)(2,1)}, bf16[256,2816]{1,0:T(8,128)(2,1)}, u32[]{:S(2)}, u32[]{:S(2)}) collective-permute-start(bf16[256,2816]{1,0:T(8,128)(2,1)} %refs_17_.1), channel_id=1, source_target_pairs={{0,2},{1,3},{2,0},{3,1},{4,6},{5,7},{6,4},{7,5},{8,10},{9,11},{10,... | collective-permute-start | bytes 4325384 | tf_op jit(solution)/shard_map/ppermute | solution.py:498
  79.5 96.7 %collective-permute-start.25 = (bf16[256,2816]{1,0:T(8,128)(2,1)}, bf16[256,2816]{1,0:T(8,128)(2,1)S(1)}, u32[]{:S(2)}, u32[]{:S(2)}) collective-permute-start(bf16[256,2816]{1,0:T(8,128)(2,1)} %refs_17_.1), channel_id=1, source_target_pairs={{0,1},{1,0},{2,3},{3,2},{4,5},{5,4},{6,7},{7,6},{8,9},{9,8},{10,11... | collective-permute-start | bytes 4325384 | tf_op jit(solution)/shard_map/ppermute | solution.py:498
  93.5 55.3 %collective-permute-start.29 = (bf16[256,2816]{1,0:T(8,128)(2,1)}, bf16[256,2816]{1,0:T(8,128)(2,1)}, u32[]{:S(2)}, u32[]{:S(2)}) collective-permute-start(bf16[256,2816]{1,0:T(8,128)(2,1)} %refs_21_.1), channel_id=1, source_target_pairs={{0,2},{1,3},{2,0},{3,1},{4,6},{5,7},{6,4},{7,5},{8,10},{9,11},{10,... | collective-permute-start | bytes 4325384 | tf_op jit(solution)/shard_map/ppermute | solution.py:498
  106.7 69.5 %collective-permute-start.32 = (bf16[704,1024]{1,0:T(8,128)(2,1)}, bf16[704,1024]{1,0:T(8,128)(2,1)}, u32[]{:S(2)}, u32[]{:S(2)}) collective-permute-start(bf16[704,1024]{1,0:T(8,128)(2,1)} %refs_25_.1), channel_id=1, source_target_pairs={{0,2},{1,3},{2,0},{3,1},{4,6},{5,7},{6,4},{7,5},{8,10},{9,11},{10,... | collective-permute-start | bytes 4325384 | tf_op jit(solution)/shard_map/ppermute | solution.py:498
  148.3 46.9 %collective-permute-start.28 = (bf16[256,2816]{1,0:T(8,128)(2,1)}, bf16[256,2816]{1,0:T(8,128)(2,1)}, u32[]{:S(2)}, u32[]{:S(2)}) collective-permute-start(bf16[256,2816]{1,0:T(8,128)(2,1)} %refs_21_.1), channel_id=1, source_target_pairs={{0,1},{1,0},{2,3},{3,2},{4,5},{5,4},{6,7},{7,6},{8,9},{9,8},{10,11... | collective-permute-start | bytes 4325384 | tf_op jit(solution)/shard_map/ppermute | solution.py:498
  148.5 51.2 %collective-permute-start.31 = (bf16[704,1024]{1,0:T(8,128)(2,1)}, bf16[704,1024]{1,0:T(8,128)(2,1)}, u32[]{:S(2)}, u32[]{:S(2)}) collective-permute-start(bf16[704,1024]{1,0:T(8,128)(2,1)} %refs_25_.1), channel_id=1, source_target_pairs={{0,1},{1,0},{2,3},{3,2},{4,5},{5,4},{6,7},{7,6},{8,9},{9,8},{10,11... | collective-permute-start | bytes 4325384 | tf_op jit(solution)/shard_map/ppermute | solution.py:498
  148.8 71.3 %collective-permute-start.27 = (bf16[256,2816]{1,0:T(8,128)(2,1)}, bf16[256,2816]{1,0:T(8,128)(2,1)}, u32[]{:S(2)}, u32[]{:S(2)}) collective-permute-start(bf16[256,2816]{1,0:T(8,128)(2,1)} %collective-permute-done.26.refs_19_), channel_id=1, source_target_pairs={{0,1},{1,0},{2,3},{3,2},{4,5},{5,4},{6,7},{7,6},{8,9},{9,8},{10,11... | collective-permute-start | bytes 4325384 | tf_op jit(solution)/shard_map/ppermute | solution.py:498
  176.1 44.0 %collective-permute-start.30 = (bf16[256,2816]{1,0:T(8,128)(2,1)}, bf16[256,2816]{1,0:T(8,128)(2,1)}, u32[]{:S(2)}, u32[]{:S(2)}) collective-permute-start(bf16[256,2816]{1,0:T(8,128)(2,1)} %collective-permute-done.29.refs_23_), channel_id=1, source_target_pairs={{0,1},{1,0},{2,3},{3,2},{4,5},{5,4},{6,7},{7,6},{8,9},{9,8},{10,11... | collective-permute-start | bytes 4325384 | tf_op jit(solution)/shard_map/ppermute | solution.py:498
  176.1 44.0 %collective-permute-start.33 = (bf16[704,1024]{1,0:T(8,128)(2,1)}, bf16[704,1024]{1,0:T(8,128)(2,1)}, u32[]{:S(2)}, u32[]{:S(2)}) collective-permute-start(bf16[704,1024]{1,0:T(8,128)(2,1)} %collective-permute-done.32.refs_27_), channel_id=1, source_target_pairs={{0,1},{1,0},{2,3},{3,2},{4,5},{5,4},{6,7},{7,6},{8,9},{9,8},{10,11... | collective-permute-start | bytes 4325384 | tf_op jit(solution)/shard_map/ppermute | solution.py:498
  272.9 93.1 %collective-permute-start.63 = (bf16[256,1024]{1,0:T(8,128)(2,1)S(1)}, bf16[256,1024]{1,0:T(8,128)(2,1)S(1)}, u32[]{:S(2)}, u32[]{:S(2)}) collective-permute-start(bf16[256,1024]{1,0:T(8,128)(2,1)S(1)} %copy-done.11), channel_id=1, source_target_pairs={{0,2},{1,3},{2,0},{3,1},{4,6},{5,7},{6,4},{7,5},{8,10},{9,11},{10,... | collective-permute-start | bytes 1572872 | tf_op jit(solution)/shard_map/ppermute | solution.py:498
  275.8 90.8 %collective-permute-start.66 = (bf16[256,1024]{1,0:T(8,128)(2,1)S(1)}, bf16[256,1024]{1,0:T(8,128)(2,1)}, u32[]{:S(2)}, u32[]{:S(2)}) collective-permute-start(bf16[256,1024]{1,0:T(8,128)(2,1)S(1)} %copy-done.9), channel_id=1, source_target_pairs={{0,2},{1,3},{2,0},{3,1},{4,6},{5,7},{6,4},{7,5},{8,10},{9,11},{10,... | collective-permute-start | bytes 1572872 | tf_op jit(solution)/shard_map/ppermute | solution.py:498
  277.5 89.2 %collective-permute-start.69 = (bf16[256,1024]{1,0:T(8,128)(2,1)S(1)}, bf16[256,1024]{1,0:T(8,128)(2,1)}, u32[]{:S(2)}, u32[]{:S(2)}) collective-permute-start(bf16[256,1024]{1,0:T(8,128)(2,1)S(1)} %copy-done.8), channel_id=1, source_target_pairs={{0,2},{1,3},{2,0},{3,1},{4,6},{5,7},{6,4},{7,5},{8,10},{9,11},{10,... | collective-permute-start | bytes 1572872 | tf_op jit(solution)/shard_map/ppermute | solution.py:498
  279.1 88.2 %collective-permute-start.62 = (bf16[256,1024]{1,0:T(8,128)(2,1)S(1)}, bf16[256,1024]{1,0:T(8,128)(2,1)}, u32[]{:S(2)}, u32[]{:S(2)}) collective-permute-start(bf16[256,1024]{1,0:T(8,128)(2,1)S(1)} %copy-done.11), channel_id=1, source_target_pairs={{0,1},{1,0},{2,3},{3,2},{4,5},{5,4},{6,7},{7,6},{8,9},{9,8},{10,11... | collective-permute-start | bytes 1572872 | tf_op jit(solution)/shard_map/ppermute | solution.py:498
  279.1 88.2 %collective-permute-start.65 = (bf16[256,1024]{1,0:T(8,128)(2,1)S(1)}, bf16[256,1024]{1,0:T(8,128)(2,1)}, u32[]{:S(2)}, u32[]{:S(2)}) collective-permute-start(bf16[256,1024]{1,0:T(8,128)(2,1)S(1)} %copy-done.9), channel_id=1, source_target_pairs={{0,1},{1,0},{2,3},{3,2},{4,5},{5,4},{6,7},{7,6},{8,9},{9,8},{10,11... | collective-permute-start | bytes 1572872 | tf_op jit(solution)/shard_map/ppermute | solution.py:498
  387.5 20.9 %collective-permute-start.74 = (bf16[1,256,384]{2,1,0:T(8,128)(2,1)S(1)}, bf16[1,256,384]{2,1,0:T(8,128)(2,1)S(1)}, u32[]{:S(2)}, u32[]{:S(2)}) collective-permute-start(bf16[1,256,384]{2,1,0:T(8,128)(2,1)S(1)} %fusion.13), channel_id=1, source_target_pairs={{0,16},{4,20},{8,24},{12,28},{16,0},{20,4},{24,8},{28,12},{1,17},{... | collective-permute-start | bytes 589832 | tf_op jit(solution)/shard_map/ppermute | solution.py:498
  396.6 25.5 %collective-permute-start.77 = (bf16[256,1024]{1,0:T(8,128)(2,1)}, bf16[256,1024]{1,0:T(8,128)(2,1)}, u32[]{:S(2)}, u32[]{:S(2)}) collective-permute-start(bf16[256,1024]{1,0:T(8,128)(2,1)} %get-tuple-element.185), channel_id=1, source_target_pairs={{0,1},{1,0},{2,3},{3,2},{4,5},{5,4},{6,7},{7,6},{8,9},{9,8},{10,11... | collective-permute-start | bytes 1572872 | tf_op jit(solution)/shard_map/ppermute | solution.py:498
  398.7 25.0 %collective-permute-start.79 = (bf16[256,1024]{1,0:T(8,128)(2,1)S(1)}, bf16[256,1024]{1,0:T(8,128)(2,1)}, u32[]{:S(2)}, u32[]{:S(2)}) collective-permute-start(bf16[256,1024]{1,0:T(8,128)(2,1)S(1)} %add_convert_fusion.13), channel_id=1, source_target_pairs={{0,2},{1,3},{2,0},{3,1},{4,6},{5,7},{6,4},{7,5},{8,10},{9,11},{10,... | collective-permute-start | bytes 1572872 | tf_op jit(solution)/shard_map/ppermute | solution.py:498
  417.0 42.9 %collective-permute-start.96 = (bf16[256,2816]{1,0:T(8,128)(2,1)}, bf16[256,2816]{1,0:T(8,128)(2,1)S(1)}, u32[]{:S(2)}, u32[]{:S(2)}) collective-permute-start(bf16[256,2816]{1,0:T(8,128)(2,1)} %get-tuple-element.195), channel_id=1, source_target_pairs={{0,1},{1,0},{2,3},{3,2},{4,5},{5,4},{6,7},{7,6},{8,9},{9,8},{10,11... | collective-permute-start | bytes 4325384 | tf_op jit(solution)/shard_map/ppermute | solution.py:498
  423.7 27.7 %collective-permute-start.75 = (bf16[2,256,384]{2,1,0:T(8,128)(2,1)}, bf16[2,256,384]{2,1,0:T(8,128)(2,1)}, u32[]{:S(2)}, u32[]{:S(2)}) collective-permute-start(bf16[2,256,384]{2,1,0:T(8,128)(2,1)} %pad_maximum_fusion.6), channel_id=1, source_target_pairs={{0,8},{4,12},{8,0},{12,4},{16,24},{20,28},{24,16},{28,20},{1,9},{5... | collective-permute-start | bytes 1179656 | tf_op jit(solution)/shard_map/ppermute | solution.py:498
  440.3 70.0 %collective-permute-start.95 = (bf16[256,2816]{1,0:T(8,128)(2,1)}, bf16[256,2816]{1,0:T(8,128)(2,1)}, u32[]{:S(2)}, u32[]{:S(2)}) collective-permute-start(bf16[256,2816]{1,0:T(8,128)(2,1)} %get-tuple-element.193), channel_id=1, source_target_pairs={{0,1},{1,0},{2,3},{3,2},{4,5},{5,4},{6,7},{7,6},{8,9},{9,8},{10,11... | collective-permute-start | bytes 4325384 | tf_op jit(solution)/shard_map/ppermute | solution.py:498
  441.6 25.3 %collective-permute-start.87 = (bf16[256,2816]{1,0:T(8,128)(2,1)}, bf16[256,2816]{1,0:T(8,128)(2,1)S(1)}, u32[]{:S(2)}, u32[]{:S(2)}) collective-permute-start(bf16[256,2816]{1,0:T(8,128)(2,1)} %get-tuple-element.191), channel_id=1, source_target_pairs={{0,1},{1,0},{2,3},{3,2},{4,5},{5,4},{6,7},{7,6},{8,9},{9,8},{10,11... | collective-permute-start | bytes 4325384 | tf_op jit(solution)/shard_map/ppermute | solution.py:498
  451.5 66.7 %collective-permute-start.86 = (bf16[256,2816]{1,0:T(8,128)(2,1)}, bf16[256,2816]{1,0:T(8,128)(2,1)}, u32[]{:S(2)}, u32[]{:S(2)}) collective-permute-start(bf16[256,2816]{1,0:T(8,128)(2,1)} %get-tuple-element.189), channel_id=1, source_target_pairs={{0,1},{1,0},{2,3},{3,2},{4,5},{5,4},{6,7},{7,6},{8,9},{9,8},{10,11... | collective-permute-start | bytes 4325384 | tf_op jit(solution)/shard_map/ppermute | solution.py:498
  466.8 81.6 %collective-permute-start.104 = (bf16[704,1024]{1,0:T(8,128)(2,1)}, bf16[704,1024]{1,0:T(8,128)(2,1)}, u32[]{:S(2)}, u32[]{:S(2)}) collective-permute-start(bf16[704,1024]{1,0:T(8,128)(2,1)} %get-tuple-element.197), channel_id=1, source_target_pairs={{0,1},{1,0},{2,3},{3,2},{4,5},{5,4},{6,7},{7,6},{8,9},{9,8},{10,11... | collective-permute-start | bytes 4325384 | tf_op jit(solution)/shard_map/ppermute | solution.py:498
  473.4 19.5 %collective-permute-start.76 = (bf16[4,256,384]{2,1,0:T(8,128)(2,1)S(1)}, bf16[4,256,384]{2,1,0:T(8,128)(2,1)S(1)}, u32[]{:S(2)}, u32[]{:S(2)}) collective-permute-start(bf16[4,256,384]{2,1,0:T(8,128)(2,1)S(1)} %pad_maximum_fusion.2), channel_id=1, source_target_pairs={{0,4},{4,0},{8,12},{12,8},{16,20},{20,16},{24,28},{28,24},{1,5},{5... | collective-permute-start | bytes 2359304 | tf_op jit(solution)/shard_map/ppermute | solution.py:498
  479.3 34.8 %collective-permute-start.97 = (bf16[256,2816]{1,0:T(8,128)(2,1)}, bf16[256,2816]{1,0:T(8,128)(2,1)}, u32[]{:S(2)}, u32[]{:S(2)}) collective-permute-start(bf16[256,2816]{1,0:T(8,128)(2,1)} %add_convert_fusion.4), channel_id=1, source_target_pairs={{0,2},{1,3},{2,0},{3,1},{4,6},{5,7},{6,4},{7,5},{8,10},{9,11},{10,... | collective-permute-start | bytes 4325384 | tf_op jit(solution)/shard_map/ppermute | solution.py:498
  507.1 37.9 %collective-permute-start.88 = (bf16[256,2816]{1,0:T(8,128)(2,1)S(1)}, bf16[256,2816]{1,0:T(8,128)(2,1)S(1)}, u32[]{:S(2)}, u32[]{:S(2)}) collective-permute-start(bf16[256,2816]{1,0:T(8,128)(2,1)S(1)} %copy-done.16), channel_id=1, source_target_pairs={{0,2},{1,3},{2,0},{3,1},{4,6},{5,7},{6,4},{7,5},{8,10},{9,11},{10,... | collective-permute-start | bytes 4325384 | tf_op jit(solution)/shard_map/ppermute | solution.py:498
  510.3 63.5 %collective-permute-start.106 = (bf16[704,1024]{1,0:T(8,128)(2,1)S(1)}, bf16[704,1024]{1,0:T(8,128)(2,1)S(1)}, u32[]{:S(2)}, u32[]{:S(2)}) collective-permute-start(bf16[704,1024]{1,0:T(8,128)(2,1)S(1)} %copy-done.17), channel_id=1, source_target_pairs={{0,2},{1,3},{2,0},{3,1},{4,6},{5,7},{6,4},{7,5},{8,10},{9,11},{10,... | collective-permute-start | bytes 4325384 | tf_op jit(solution)/shard_map/ppermute | solution.py:498
  516.7 61.0 %collective-permute-start.98 = (bf16[128,2816]{1,0:T(8,128)(2,1)S(1)}, bf16[128,2816]{1,0:T(8,128)(2,1)S(1)}, u32[]{:S(2)}, u32[]{:S(2)}) collective-permute-start(bf16[128,2816]{1,0:T(8,128)(2,1)S(1)} %constant_dynamic-slice_fusion.5), channel_id=1, source_target_pairs={{0,4},{4,0},{8,12},{12,8},{16,20},{20,16},{24,28},{28,24},{1,5},{5... | collective-permute-start | bytes 2162696 | tf_op jit(solution)/shard_map/ppermute | solution.py:498
  547.0 31.6 %collective-permute-start.89 = (bf16[128,2816]{1,0:T(8,128)(2,1)S(1)}, bf16[128,2816]{1,0:T(8,128)(2,1)S(1)}, u32[]{:S(2)}, u32[]{:S(2)}) collective-permute-start(bf16[128,2816]{1,0:T(8,128)(2,1)S(1)} %constant_dynamic-slice_fusion.8), channel_id=1, source_target_pairs={{0,4},{4,0},{8,12},{12,8},{16,20},{20,16},{24,28},{28,24},{1,5},{5... | collective-permute-start | bytes 2162696 | tf_op jit(solution)/shard_map/ppermute | solution.py:498
  578.7 20.9 %collective-permute-start.90 = (bf16[64,2816]{1,0:T(8,128)(2,1)S(1)}, bf16[64,2816]{1,0:T(8,128)(2,1)S(1)}, u32[]{:S(2)}, u32[]{:S(2)}) collective-permute-start(bf16[64,2816]{1,0:T(8,128)(2,1)S(1)} %constant_dynamic-slice_fusion.7), channel_id=1, source_target_pairs={{0,8},{4,12},{8,0},{12,4},{16,24},{20,28},{24,16},{28,20},{1,9},{5... | collective-permute-start | bytes 1081352 | tf_op jit(solution)/shard_map/ppermute | solution.py:498
  599.8 21.9 %collective-permute-start.91 = (bf16[32,2816]{1,0:T(8,128)(2,1)S(1)}, bf16[32,2816]{1,0:T(8,128)(2,1)S(1)}, u32[]{:S(2)}, u32[]{:S(2)}) collective-permute-start(bf16[32,2816]{1,0:T(8,128)(2,1)S(1)} %constant_dynamic-slice_fusion.6), channel_id=1, source_target_pairs={{0,16},{4,20},{8,24},{12,28},{16,0},{20,4},{24,8},{28,12},{1,17},{... | collective-permute-start | bytes 540680 | tf_op jit(solution)/shard_map/ppermute | solution.py:498
  607.9 23.4 %collective-permute-start.109 = (bf16[88,1024]{1,0:T(8,128)(2,1)S(1)}, bf16[88,1024]{1,0:T(8,128)(2,1)S(1)}, u32[]{:S(2)}, u32[]{:S(2)}) collective-permute-start(bf16[88,1024]{1,0:T(8,128)(2,1)S(1)} %constant_dynamic-slice_fusion), channel_id=1, source_target_pairs={{0,16},{4,20},{8,24},{12,28},{16,0},{20,4},{24,8},{28,12},{1,17},{... | collective-permute-start | bytes 540680 | tf_op jit(solution)/shard_map/ppermute | solution.py:498
  608.8 26.4 %collective-permute-start.101 = (bf16[32,2816]{1,0:T(8,128)(2,1)S(1)}, bf16[32,2816]{1,0:T(8,128)(2,1)S(1)}, u32[]{:S(2)}, u32[]{:S(2)}) collective-permute-start(bf16[32,2816]{1,0:T(8,128)(2,1)S(1)} %add_convert_fusion.21), channel_id=1, source_target_pairs={{0,16},{4,20},{8,24},{12,28},{16,0},{20,4},{24,8},{28,12},{1,17},{... | collective-permute-start | bytes 540680 | tf_op jit(solution)/shard_map/ppermute | solution.py:498
  642.1 23.0 %collective-permute-start.111 = (bf16[176,1024]{1,0:T(8,128)(2,1)S(1)}, bf16[176,1024]{1,0:T(8,128)(2,1)S(1)}, u32[]{:S(2)}, u32[]{:S(2)}) collective-permute-start(bf16[176,1024]{1,0:T(8,128)(2,1)S(1)} %pad_maximum_fusion.9), channel_id=1, source_target_pairs={{0,8},{4,12},{8,0},{12,4},{16,24},{20,28},{24,16},{28,20},{1,9},{5... | collective-permute-start | bytes 1081352 | tf_op jit(solution)/shard_map/ppermute | solution.py:498
  649.9 19.1 %collective-permute-start.103 = (bf16[128,2816]{1,0:T(8,128)(2,1)S(1)}, bf16[128,2816]{1,0:T(8,128)(2,1)S(1)}, u32[]{:S(2)}, u32[]{:S(2)}) collective-permute-start(bf16[128,2816]{1,0:T(8,128)(2,1)S(1)} %pad_maximum_fusion.4), channel_id=1, source_target_pairs={{0,4},{4,0},{8,12},{12,8},{16,20},{20,16},{24,28},{28,24},{1,5},{5... | collective-permute-start | bytes 2162696 | tf_op jit(solution)/shard_map/ppermute | solution.py:498
  657.7 26.8 %collective-permute-start.94 = (bf16[128,2816]{1,0:T(8,128)(2,1)S(1)}, bf16[128,2816]{1,0:T(8,128)(2,1)S(1)}, u32[]{:S(2)}, u32[]{:S(2)}) collective-permute-start(bf16[128,2816]{1,0:T(8,128)(2,1)S(1)} %pad_maximum_fusion.3), channel_id=1, source_target_pairs={{0,4},{4,0},{8,12},{12,8},{16,20},{20,16},{24,28},{28,24},{1,5},{5... | collective-permute-start | bytes 2162696 | tf_op jit(solution)/shard_map/ppermute | solution.py:498
  665.3 33.5 %collective-permute-start.112 = (bf16[352,1024]{1,0:T(8,128)(2,1)S(1)}, bf16[352,1024]{1,0:T(8,128)(2,1)S(1)}, u32[]{:S(2)}, u32[]{:S(2)}) collective-permute-start(bf16[352,1024]{1,0:T(8,128)(2,1)S(1)} %pad_maximum_fusion.5), channel_id=1, source_target_pairs={{0,4},{4,0},{8,12},{12,8},{16,20},{20,16},{24,28},{28,24},{1,5},{5... | collective-permute-start | bytes 2162696 | tf_op jit(solution)/shard_map/ppermute | solution.py:498
  (167 other events, 2070.1 us)

commit v2 on v1

v2 whole, which is shorter than its diff:
```python
import functools

import jax
import jax.numpy as jnp
from jax import lax
from jax.experimental import pallas as pl
from jax.experimental.pallas import tpu as pltpu
from jax.sharding import PartitionSpec as P

HD = 64
LANES = 128
EPSILON = 1e-06
BLOCKED = -(2.0**100)
ROOT_2_PI = 0.7978845608028654
CUBIC = 0.044715
VMEM_LIMIT = 60 * 1024 * 1024

bf16 = jnp.bfloat16
f32 = jnp.float32


def mm(a, b):
    return jnp.dot(a, b, preferred_element_type=f32)


def mm_nt(a, b):
    return lax.dot_general(a, b, (((1,), (1,)), ((), ())), preferred_element_type=f32)


def mm_tn(a, b):
    return lax.dot_general(a, b, (((0,), (0,)), ((), ())), preferred_element_type=f32)


def params(**extra):
    return pltpu.CompilerParams(vmem_limit_bytes=VMEM_LIMIT, **extra)


def cost(flops, moved, transcendentals=0):
    return pl.CostEstimate(
        flops=int(flops), bytes_accessed=int(moved), transcendentals=int(transcendentals)
    )


def vmem():
    return pl.BlockSpec(memory_space=pltpu.VMEM)


def anywhere():
    return pl.BlockSpec(memory_space=pl.ANY)


def smem():
    return pl.BlockSpec(memory_space=pltpu.SMEM)


def lane_ids(rows):
    return lax.broadcasted_iota(jnp.int32, (rows, LANES), 1)


def split3(column):
    high = column.astype(bf16)
    rest = column - high.astype(f32)
    middle = rest.astype(bf16)
    low = (rest - middle.astype(f32)).astype(bf16)
    return (high.astype(f32), middle.astype(f32), low.astype(f32))


def project_kernel(heads, fresh, *refs):
    x_ref, gain_ref, w_ref, qt_ref, kt_ref = refs[1:6]
    qa_ref, ka_ref, va_ref, h1_ref = refs[6:] if fresh else refs[10:]
    x = x_ref[...].astype(f32)
    scaling = lax.rsqrt(jnp.mean(x * x, axis=-1, keepdims=True) + EPSILON)
    h1 = (x * scaling * gain_ref[...].astype(f32)).astype(bf16)
    h1_ref[...] = h1
    qkv = mm(h1, w_ref[...])
    rows = x.shape[0]
    lane = lane_ids(rows)
    q = qkv[:, :LANES].astype(bf16) * jnp.asarray(HD**-0.5, bf16)
    k = qkv[:, LANES : 2 * LANES].astype(bf16)
    v = qkv[:, 2 * LANES :].astype(bf16)
    ones = jnp.where(lane % HD < 3, 1.0, 0.0).astype(bf16)
    for head in range(heads):
        own = lane // HD == head
        qa_ref[head] = jnp.where(own, q, qt_ref[...])
        ka_ref[head] = jnp.where(own, k, kt_ref[...])
        va_ref[head] = jnp.where(own, v, ones)


def project(slot, slots, heads, x, gain, w, q_table, k_table, previous):
    rows, width = x.shape
    total = rows * slots
    row_spec = pl.BlockSpec((rows, LANES), lambda i, s: (s[0], 0))
    head_spec = pl.BlockSpec((heads, rows, LANES), lambda i, s: (0, s[0], 0))
    shapes = [jax.ShapeDtypeStruct((heads, total, LANES), bf16)] * 3 + [
        jax.ShapeDtypeStruct((total, width), bf16)
    ]
    fresh = previous is None
    extra = () if fresh else tuple(previous)
    return pl.pallas_call(
        functools.partial(project_kernel, heads, fresh),
        grid_spec=pltpu.PrefetchScalarGridSpec(
            num_scalar_prefetch=1,
            grid=(1,),
            in_specs=[
                pl.BlockSpec((rows, width), lambda i, s: (0, 0)),
                pl.BlockSpec((1, width), lambda i, s: (0, 0)),
                pl.BlockSpec(w.shape, lambda i, s: (0, 0)),
                row_spec,
                row_spec,
            ]
            + [anywhere()] * len(extra),
            out_specs=[head_spec] * 3 + [pl.BlockSpec((rows, width), lambda i, s: (s[0], 0))],
        ),
        out_shape=shapes,
        input_output_aliases={} if fresh else {6 + i: i for i in range(4)},
        compiler_params=params(),
        cost_estimate=cost(2 * rows * width * 3 * LANES, 4 * rows * width + 2 * w.size),
        name="project",
    )(slot, x, gain, w, q_table, k_table, *extra)


def forward_kernel(heads, q_ref, k_near, v_near, k_ref, v_ref, att_ref, sum_ref, qb_ref):
    pack, rows = q_ref.shape[1], q_ref.shape[3]
    span = pack * rows
    lane = lane_ids(span)
    merged = None
    for head in range(heads):
        q = q_ref[head].reshape(span, LANES)
        key = k_near[head].reshape(span, LANES)
        value = v_near[head].reshape(span, LANES)
        own = lane // HD == head
        other = HD if head == 0 else 0
        scores = mm_nt(q, k_ref[head])
        q_wide = q.astype(f32)
        padded = q_wide[:, other + HD - 1 : other + HD] > 0.5
        own_score = jnp.sum(jnp.where(own, q_wide * key.astype(f32), 0.0), axis=-1, keepdims=True)
        top = jnp.max(scores, axis=-1, keepdims=True)
        top = jnp.where(padded, jnp.maximum(top, own_score), top)
        weights = jnp.exp(scores - top).astype(bf16)
        mixed = mm(weights, v_ref[head])
        own_weight = jnp.where(padded, jnp.exp(own_score - top), 0.0).astype(bf16).astype(f32)
        mixed = mixed + own_weight * value.astype(f32)
        total = mixed[:, other : other + 1]
        log_total = top + jnp.log(total)
        mixed = mixed * (1.0 / total)
        merged = mixed if merged is None else jnp.where(own, mixed, merged)
        filled = q_wide
        for place, part in enumerate(split3(-log_total)):
            filled = jnp.where(lane == other + HD - 4 + place, part, filled)
        qb_ref[head] = filled.astype(bf16).reshape(pack, 1, rows, LANES)
    att_ref[...] = merged.astype(bf16).reshape(pack, rows, LANES)
    sum_ref[...] = merged.reshape(pack, 1, rows, LANES)


def forward_body(heads, aliased, *refs):
    forward_kernel(heads, *(refs[:5] + refs[5 + aliased :]))


def attend(qa, ka, va, part, parts, slots, span, previous):
    heads, total, _ = qa.shape
    rows = total // slots // parts
    pack = max(1, min(slots, 320 // rows))
    shape = (heads, slots, parts, rows, LANES)
    view = [a.reshape(shape) for a in (qa, ka, va)]
    begin = span[0] // pack
    block = pl.BlockSpec((heads, pack, 1, rows, LANES), lambda i: (0, begin + i, part, 0, 0))
    whole = pl.BlockSpec(ka.shape, lambda i: (0, 0, 0))
    extra = tuple(previous)
    return pl.pallas_call(
        functools.partial(forward_body, heads, len(extra)),
        grid=((span[1] - span[0]) // pack,),
        in_specs=[block, block, block, whole, whole] + [anywhere()] * len(extra),
        out_specs=[
            pl.BlockSpec((pack, rows, LANES), lambda i: (begin + i, 0, 0)),
            pl.BlockSpec((pack, 1, rows, LANES), lambda i: (begin + i, part, 0, 0)),
            block,
        ],
        out_shape=[
            jax.ShapeDtypeStruct((slots, rows, LANES), bf16),
            jax.ShapeDtypeStruct(shape[1:], f32),
            jax.ShapeDtypeStruct(shape, bf16),
        ],
        input_output_aliases={5 + i: 3 - len(extra) + i for i in range(len(extra))},
        compiler_params=params(),
        cost_estimate=cost(
            8 * heads * total * total * LANES // parts,
            4 * heads * total * LANES,
            heads * total * total // parts,
        ),
        name="attend",
    )(*view, ka, va, *extra)


def backward_kernel(heads, part, parts, tile, *refs):
    first, last = part == 0, part == parts - 1
    qb_ref, k_ref, v_ref = refs[:3]
    if first:
        sum_ref, grad_ref, kv_ref, dq_ref, gb_ref, dk_acc, dv_acc = refs[3:]
        dq_acc = dq_ref
    elif last:
        gb_ref, dq_in, kv_ref, dq_ref, dq_acc, dk_acc, dv_acc = refs[3:]
    else:
        gb_ref, dq_in, kv_ref, dq_ref, dk_acc, dv_acc = refs[3:]
        dq_acc = dq_ref
    slots, rows = k_ref.shape[1], k_ref.shape[3]
    total = qb_ref.shape[1]
    span = slots * rows
    pack = max(1, min(slots, 320 // rows))
    if first:
        block_rows = grad_ref.shape[1]
        lane = lane_ids(block_rows)

        def prepare(slot, carry):
            at = pl.ds(pl.multiple_of(slot * block_rows, block_rows), block_rows)
            grad = grad_ref[slot].astype(f32)
            product = grad * sum_ref[at, :]
            for head in range(heads):
                other = HD if head == 0 else 0
                own = lane // HD == head
                delta = jnp.sum(jnp.where(own, product, 0.0), axis=-1, keepdims=True)
                filled = jnp.where(own, grad, 0.0)
                for place, piece in enumerate(split3(-delta)):
                    filled = jnp.where(lane == other + place, piece, filled)
                gb_ref[head, at, :] = filled.astype(bf16)
                dq_acc[head, at, :] = jnp.zeros((block_rows, LANES), f32)
            return carry

        lax.fori_loop(0, slots, prepare, 0)
    else:
        dq_acc[...] = dq_in[...]
    width = pack * rows
    lane = lane_ids(width)
    for index in range(slots // pack):
        keys = slice(index * pack, (index + 1) * pack)
        dk_acc[...] = jnp.zeros_like(dk_acc)
        dv_acc[...] = jnp.zeros_like(dv_acc)

        def step(number, carry):
            at = pl.ds(pl.multiple_of(number * tile, tile), tile)
            for head in range(heads):
                key = k_ref[head, keys].reshape(width, LANES)
                value = v_ref[head, keys].reshape(width, LANES)
                q = qb_ref[head, at, :]
                g = gb_ref[head, at, :]
                weights = jnp.exp(mm_nt(key, q))
                inner = mm_nt(value, g)
                score_grad = (weights * inner).astype(bf16)
                dv_acc[head] += mm(weights.astype(bf16), g)
                dk_acc[head] += mm(score_grad, q)
                dq_acc[head, at, :] += mm_tn(score_grad, key)
            return carry

        lax.fori_loop(0, total // tile, step, 0)
        dk_all, dv_all = None, None
        for head in range(heads):
            other = HD if head == 0 else 0
            own = lane // HD == head
            counted = own | ((lane >= other + HD - 4) & (lane < other + HD - 1))
            starts = [
                slot * (total // slots) + part * rows
                for slot in range(index * pack, (index + 1) * pack)
            ]
            q = jnp.concatenate([qb_ref[head, b : b + rows, :] for b in starts], axis=0).astype(f32)
            g = jnp.concatenate([gb_ref[head, b : b + rows, :] for b in starts], axis=0).astype(f32)
            k = k_ref[head, keys].reshape(width, LANES).astype(f32)
            v = v_ref[head, keys].reshape(width, LANES).astype(f32)
            padded = q[:, other + HD - 1 : other + HD] > 0.5
            score = jnp.sum(jnp.where(counted, q * k, 0.0), axis=-1, keepdims=True)
            weight = jnp.where(padded, jnp.exp(score), 0.0)
            inner = jnp.sum(v * g, axis=-1, keepdims=True)
            score_grad = (weight * inner).astype(bf16).astype(f32)
            weight = weight.astype(bf16).astype(f32)
            dk = dk_acc[head] + score_grad * q
            dv = dv_acc[head] + weight * g
            dq = score_grad * k
            for place, b in enumerate(starts):
                dq_acc[head, b : b + rows, :] += dq[place * rows : (place + 1) * rows, :]
            dk_all = dk if head == 0 else jnp.where(own, dk, dk_all)
            dv_all = dv if head == 0 else jnp.where(own, dv, dv_all)
        kv_ref[keys, 0] = dk_all.astype(bf16).reshape(pack, rows, LANES)
        kv_ref[keys, 1] = dv_all.astype(bf16).reshape(pack, rows, LANES)
    if last:
        block_rows = total // slots
        lane = lane_ids(block_rows)
        for slot in range(slots):
            at = slice(slot * block_rows, (slot + 1) * block_rows)
            dq = dq_acc[0, at, :]
            if heads == 2:
                dq = jnp.where(lane < HD, dq, dq_acc[1, at, :])
            dq_ref[slot] = (dq * HD**-0.5).astype(bf16)


def attend_back(qb, ka, va, part, parts, slots, sums, grads, state):
    heads, total, _ = ka.shape
    rows = total // slots // parts
    first, last = part == 0, part == parts - 1
    shape = (heads, slots, parts, rows, LANES)
    near = pl.BlockSpec((heads, slots, 1, rows, LANES), lambda i: (0, 0, part, 0, 0))
    wide = pl.BlockSpec((heads, total, LANES), lambda i: (0, 0, 0))
    pack = max(1, min(slots, 320 // rows))
    accumulator = pltpu.VMEM((heads, pack * rows, LANES), f32)
    if first:
        inputs = [sums, grads]
        in_specs = [
            pl.BlockSpec((total, LANES), lambda i: (0, 0)),
            pl.BlockSpec(grads.shape, lambda i: (0, 0, 0)),
        ]
    else:
        inputs, in_specs = list(state), [wide, wide]
    out_shape = [jax.ShapeDtypeStruct((slots, 2, rows, LANES), bf16)]
    out_specs = [pl.BlockSpec((slots, 2, rows, LANES), lambda i: (0, 0, 0, 0))]
    scratch = [accumulator, accumulator]
    if last:
        out_shape.append(jax.ShapeDtypeStruct((slots, total // slots, LANES), bf16))
        out_specs.append(pl.BlockSpec((slots, total // slots, LANES), lambda i: (0, 0, 0)))
        scratch = [pltpu.VMEM((heads, total, LANES), f32)] + scratch
    else:
        out_shape.append(jax.ShapeDtypeStruct((heads, total, LANES), f32))
        out_specs.append(wide)
    if first:
        out_shape.append(jax.ShapeDtypeStruct((heads, total, LANES), bf16))
        out_specs.append(wide)
    return pl.pallas_call(
        functools.partial(backward_kernel, heads, part, parts, 512),
        grid=(1,),
        in_specs=[wide, near, near] + in_specs,
        out_specs=out_specs,
        out_shape=out_shape,
        scratch_shapes=scratch,
        compiler_params=params(),
        cost_estimate=cost(
            20 * heads * total * total * LANES // parts,
            12 * heads * total * LANES,
            heads * total * total // parts,
        ),
        name="attend_back",
    )(qb, ka.reshape(shape), va.reshape(shape), *inputs)


def own_kernel(halves, *refs):
    w_rows, h_ref, dq_ref = refs[:3]
    parts = len(refs) - 4 - halves
    kv_refs, outs, term = refs[3 : 3 + parts], refs[3 + parts : -1], refs[-1]
    slots, _, rows, width = h_ref.shape
    total = slots * parts * rows
    term[:, :LANES] = mm_tn(
        h_ref[...].reshape(total, width), dq_ref[...].reshape(total, LANES)
    ).astype(bf16)
    for kind in range(2):
        summed = None
        for part in range(parts):
            piece = mm_tn(
                h_ref[:, part].reshape(slots * rows, width),
                kv_refs[part][:, kind].reshape(slots * rows, LANES),
            )
            summed = piece if summed is None else summed + piece
        term[:, (kind + 1) * LANES : (kind + 2) * LANES] = summed.astype(bf16)
    place_rows(halves, w_rows, term, outs)


def place_rows(halves, w_rows, source, outs):
    inner, step_rows = outs[0].shape[0], outs[0].shape[1]
    for half in range(halves):
        for index in range(inner):
            piece = index * halves + half
            at = pl.ds(pl.multiple_of(w_rows[piece] * step_rows, step_rows), step_rows)
            outs[half][index] = source[at, :]


def own_terms(w_rows, h1, dq, kvs, shards, halves):
    slots, rows = kvs[0].shape[0], kvs[0].shape[2]
    width = h1.shape[1]
    pieces = shards if halves == 2 else 1
    shape = jax.ShapeDtypeStruct((pieces // halves, width // pieces, 3 * LANES), bf16)
    return pl.pallas_call(
        functools.partial(own_kernel, halves),
        in_specs=[smem()] + [vmem()] * (2 + len(kvs)),
        out_specs=[vmem()] * halves,
        out_shape=[shape] * halves,
        scratch_shapes=[pltpu.VMEM((width, 3 * LANES), bf16)],
        compiler_params=params(),
        cost_estimate=cost(2 * h1.size * 3 * LANES, 2 * h1.size),
        name="own_terms",
    )(w_rows, h1.reshape(slots, len(kvs), rows, width), dq, *kvs)


def middle_kernel(parts, pieces, halves, step_width, layout, *refs):
    w_rows = refs[0]
    att_refs = refs[1 : 1 + parts]
    x_ref, c_ref, gain_ref = refs[1 + parts : 4 + parts]
    refs = refs[4 + parts :]
    sources, refs = refs[: len(layout)], refs[len(layout) :]
    out_ref, dmid_ref, da_ref = refs[:3]
    refs = refs[3:]
    og_refs, gg_refs, ug_refs, dg_refs = [refs[i * halves : (i + 1) * halves] for i in range(4)]
    refs = refs[4 * halves :]
    wo, wg, wu, wd, og, gg, ug, dg, att, h2_ref, h2t_ref, mid_ref, acc_out, acc_back = refs[:14]
    in_sems, out_sems = refs[14:]

    loads = [[], [], [], []]
    targets = (wo, wg, wu, wd)
    for place, (number, piece, offset) in enumerate(layout):
        target = targets[number]
        step_rows = target.shape[0] // pieces
        begin = pl.multiple_of(w_rows[piece] * step_rows + offset, 16)
        at = pl.ds(begin, sources[place].shape[0])
        copy = pltpu.make_async_copy(sources[place], target.at[at, :], in_sems.at[place])
        copy.start()
        loads[number].append(copy)

    rows, width = x_ref.shape
    blocks = da_ref.shape[0]
    block_width = width // blocks
    part_rows = rows // parts
    for part in range(parts):
        for block in range(blocks):
            att[
                part * part_rows : (part + 1) * part_rows,
                block * block_width : (block + 1) * block_width,
            ] = att_refs[part][block][:, :block_width]
    for copy in loads[0]:
        copy.wait()
    gain = gain_ref[...].astype(f32)
    middle = x_ref[...].astype(f32) + mm(att[...], wo[...])
    scaling = lax.rsqrt(jnp.mean(middle * middle, axis=-1, keepdims=True) + EPSILON)
    h2 = (middle * scaling * gain).astype(bf16)
    h2_ref[...] = h2
    h2t_ref[...] = h2.T
    mid_ref[...] = middle
    acc_out[...] = jnp.zeros_like(acc_out)
    acc_back[...] = jnp.zeros_like(acc_back)
    for copy in loads[1] + loads[2] + loads[3]:
        copy.wait()

    def row_copies(number, source, targets, columns):
        step_rows = source.shape[0] // pieces
        copies = []
        for piece in range(pieces):
            at = pl.ds(pl.multiple_of(w_rows[piece] * step_rows, step_rows), step_rows)
            target = targets[piece % halves].at[piece // halves, :, columns]
            copies.append(
                pltpu.make_async_copy(source.at[at, columns], target, out_sems.at[number, piece])
            )
        return copies

    def column_step(number, carry):
        at = pl.ds(pl.multiple_of(number * step_width, step_width), step_width)
        h2 = h2_ref[...]
        c = c_ref[...]
        gate = mm(h2, wg[:, at])
        up = mm(h2, wu[:, at])
        act_grad = mm_nt(c, wd[at, :])
        square = gate * gate
        bend = jnp.tanh(gate * (ROOT_2_PI + (ROOT_2_PI * CUBIC) * square))
        half = 0.5 * (1.0 + bend)
        curve = gate * half
        slope = half + (0.5 * gate) * (1.0 - bend * bend) * (
            ROOT_2_PI + (3.0 * ROOT_2_PI * CUBIC) * square
        )
        act = (curve * up).astype(bf16)
        d_up = (act_grad * curve).astype(bf16)
        d_gate = (act_grad * up * slope).astype(bf16)
        acc_out[...] += mm(act, wd[at, :])
        dg[at, :] = mm_tn(act, c).astype(bf16)
        gg[:, at] = mm(h2t_ref[...], d_gate).astype(bf16)
        ug[:, at] = mm(h2t_ref[...], d_up).astype(bf16)
        acc_back[...] += mm_nt(d_gate, wg[:, at]) + mm_nt(d_up, wu[:, at])
        for kind, source, targets in ((1, gg, gg_refs), (2, ug, ug_refs)):
            for copy in row_copies(kind, source, targets, at):
                copy.start()
        return carry

    lax.fori_loop(0, wg.shape[1] // step_width, column_step, 0)

    everything = slice(None)
    stores = row_copies(3, dg, dg_refs, everything)
    for copy in stores:
        copy.start()
    middle = mid_ref[...]
    scaling = lax.rsqrt(jnp.mean(middle * middle, axis=-1, keepdims=True) + EPSILON)
    out_ref[...] = (middle + acc_out[...]).astype(bf16)
    incoming = acc_back[...] * gain
    centre = jnp.mean(incoming * middle, axis=-1, keepdims=True)
    d_middle = (
        c_ref[...].astype(f32)
        + scaling * incoming
        - middle * (scaling * scaling * scaling * centre)
    )
    dmid_ref[...] = d_middle
    branch = d_middle.astype(bf16)
    og[...] = mm_tn(att[...], branch).astype(bf16)
    last_stores = row_copies(0, og, og_refs, everything)
    for copy in last_stores:
        copy.start()
    d_att = mm_nt(branch, wo[...]).astype(bf16)
    for block in range(blocks):
        piece = d_att[:, block * block_width : (block + 1) * block_width]
        if block_width < LANES:
            piece = jnp.concatenate([piece] * (LANES // block_width), axis=1)
        da_ref[block] = piece
    stores += row_copies(1, gg, gg_refs, everything) + row_copies(2, ug, ug_refs, everything)
    for copy in stores + last_stores:
        copy.wait()


def middle_stage(w_rows, att_parts, x, c, gain, wo, wg, wu, wd, pieces, halves):
    parts = len(att_parts)
    rows, width = x.shape
    hidden = wg[0][2].shape[1]
    layout = [
        (number, piece, offset)
        for number, entries in enumerate((wo, wg, wu, wd))
        for piece, offset, _ in entries
    ]
    weights = [w for entries in (wo, wg, wu, wd) for _, _, w in entries]
    slots = att_parts[0].shape[0]
    step_width = 256
    full = [(width, width), (width, hidden), (width, hidden), (hidden, width)]
    piece_shapes = [(a // pieces, b) for a, b in full]
    out_shape = [
        jax.ShapeDtypeStruct((rows, width), bf16),
        jax.ShapeDtypeStruct((rows, width), f32),
        jax.ShapeDtypeStruct((slots, rows, LANES), bf16),
    ] + [
        jax.ShapeDtypeStruct((pieces // halves,) + s, bf16)
        for s in piece_shapes
        for _ in range(halves)
    ]
    hbm = pl.BlockSpec(memory_space=pltpu.HBM)
    out = pl.pallas_call(
        functools.partial(middle_kernel, parts, pieces, halves, step_width, layout),
        in_specs=[smem()] + [vmem()] * (parts + 3) + [hbm] * len(weights),
        out_specs=[vmem()] * 3 + [hbm] * (4 * halves),
        out_shape=out_shape,
        scratch_shapes=[pltpu.VMEM(s, bf16) for s in full]
        + [pltpu.VMEM(s, bf16) for s in full]
        + [
            pltpu.VMEM((rows, width), bf16),
            pltpu.VMEM((rows, width), bf16),
            pltpu.VMEM((width, rows), bf16),
            pltpu.VMEM((rows, width), f32),
            pltpu.VMEM((rows, width), f32),
            pltpu.VMEM((rows, width), f32),
            pltpu.SemaphoreType.DMA((len(layout),)),
            pltpu.SemaphoreType.DMA((4, pieces)),
        ],
        compiler_params=params(),
        cost_estimate=cost(
            2 * rows * width * (9 * hidden + 3 * width), 4 * (width * width + 3 * width * hidden)
        ),
        name="middle_stage",
    )(w_rows, *att_parts, x, c, gain, *weights)
    return (out[:3], [out[3 + i * halves : 3 + (i + 1) * halves] for i in range(4)])


def last_kernel(parts, pieces, *refs):
    w_rows, dq_ref = refs[:2]
    kv_refs = refs[2 : 2 + parts]
    x_ref, dmid_ref, gain_ref = refs[2 + parts : 5 + parts]
    weight_refs = refs[5 + parts : 5 + parts + pieces]
    out_ref, grad, total = refs[5 + parts + pieces :]
    rows, width = x_ref.shape
    blocks = dq_ref.shape[0]
    block_width = width // blocks
    piece_width = width // pieces
    done = 0
    for part in range(parts):
        part_rows = kv_refs[part].shape[2]
        for block in range(blocks):
            lanes = slice(block * block_width, (block + 1) * block_width)
            for kind in range(2):
                grad[kind + 1, done : done + part_rows, lanes] = kv_refs[part][block, kind][
                    :, :block_width
                ]
        done += part_rows
    for block in range(blocks):
        lanes = slice(block * block_width, (block + 1) * block_width)
        grad[0, :, lanes] = dq_ref[block][:, :block_width]
    for piece in range(pieces):
        at = pl.ds(pl.multiple_of(w_rows[piece] * piece_width, piece_width), piece_width)
        w = weight_refs[piece]
        total[:, at] = (
            mm_nt(grad[0], w[:, :width])
            + mm_nt(grad[1], w[:, width : 2 * width])
            + mm_nt(grad[2], w[:, 2 * width :])
        )
    x = x_ref[...].astype(f32)
    scaling = lax.rsqrt(jnp.mean(x * x, axis=-1, keepdims=True) + EPSILON)
    incoming = total[...] * gain_ref[...].astype(f32)
    centre = jnp.mean(incoming * x, axis=-1, keepdims=True)
    out_ref[...] = dmid_ref[...] + scaling * incoming - x * (scaling * scaling * scaling * centre)


def last_stage(w_rows, dq, kvs, x, d_middle, gain, weights):
    rows, width = x.shape
    return pl.pallas_call(
        functools.partial(last_kernel, len(kvs), len(weights)),
        in_specs=[smem()] + [vmem()] * (4 + len(kvs) + len(weights)),
        out_specs=vmem(),
        out_shape=jax.ShapeDtypeStruct((rows, width), f32),
        scratch_shapes=[pltpu.VMEM((3, rows, width), bf16), pltpu.VMEM((rows, width), f32)],
        compiler_params=params(),
        cost_estimate=cost(6 * rows * width * width, 6 * width * width),
        name="last_stage",
    )(w_rows, dq, *kvs, x, d_middle, gain, *weights)


def flip(values, axis, delta):
    count = lax.axis_size(axis)
    return lax.ppermute(values, axis, [(i, i ^ delta) for i in range(count)])


def after(values, *others):
    return lax.optimization_barrier((values, *others))[0]


def bits_of(count):
    return [1 << i for i in range(count.bit_length() - 1)]


def add_low(a, b):
    return (a.astype(f32) + b.astype(f32)).astype(bf16)


def cut(values, start, size):
    return lax.dynamic_slice_in_dim(values, start, size, axis=0)


class Line:
    def __init__(self):
        self.last = None

    def hold(self, values):
        if self.last is not None:
            values = after(values, self.last)
        self.last = values
        return values


class Reduction:
    def __init__(self, kept, given, line):
        self.kept, self.given, self.line = kept, given, line

    def core(self):
        arrived = flip(self.given, "fsdp", 1)
        self.own = add_low(self.kept[0], arrived[0])
        self.send = add_low(self.kept[1], arrived[1])

    def across(self):
        self.arrived = flip(self.send, "fsdp", 2)

    def halve(self, bit):
        place = lax.axis_index("seq")
        half = self.own.shape[0] // 2
        mine = (place // bit) % 2
        keep, give = mine * half, (1 - mine) * half
        given = add_low(cut(self.own, give, half), cut(self.arrived, give, half))
        kept = add_low(cut(self.own, keep, half), cut(self.arrived, keep, half))
        self.own, self.arrived = kept, flip(self.line.hold(given), "seq", bit)

    def settle(self):
        self.own = add_low(self.own, self.arrived)
        self.joined = None

    def widen(self, bit):
        self.join()
        self.own = self.line.hold(self.own)
        self.arrived, self.joined = flip(self.own, "seq", bit), bit

    def join(self):
        if self.joined is None:
            return
        upper = ((lax.axis_index("seq") // self.joined) % 2) == 1
        first = jnp.where(upper, self.arrived, self.own)
        second = jnp.where(upper, self.own, self.arrived)
        self.own, self.joined = jnp.concatenate([first, second], axis=0), None


def mask_tables(lengths_row, order_row, real_row):
    total = order_row.shape[0]
    segments = lengths_row.shape[0]
    ends_at = jnp.cumsum(lengths_row)
    positions = jnp.arange(total, dtype=jnp.int32)
    packed_segment = jnp.sum((positions[:, None] >= ends_at[None, :]).astype(jnp.int32), axis=1)
    packed_code = packed_segment * 2 + (real_row > 0).astype(jnp.int32)
    code = jnp.sum(
        jnp.where(positions[:, None] == order_row[None, :], packed_code[None, :], 0), axis=1
    ).reshape(total, 1)
    segment, real = code // 2, code % 2
    lane = jnp.arange(LANES, dtype=jnp.int32)[None, :] % HD
    same = lane == segment
    q_table = jnp.where(same | ((lane == HD - 1) & (real == 0)), 1.0, 0.0).astype(bf16)
    open_to = same & (real == 1)
    k_table = jnp.where(
        lane < segments,
        jnp.where(open_to, 0.0, BLOCKED),
        jnp.where((lane >= HD - 4) & (lane < HD - 1), 1.0, 0.0),
    ).astype(bf16)
    return (q_table, k_table)


def move_chain(array, pairs):
    return lax.ppermute(
        array, "seq", [(a * 2 + low, b * 2 + low) for a, b in pairs for low in range(2)]
    )


def turn(blocks):
    return lax.all_to_all(blocks, "seq", split_axis=0, concat_axis=0, tiled=True)


def on_device(
    tokens,
    cotangent,
    query_weight,
    key_weight,
    value_weight,
    output_weight,
    gate_weight,
    up_weight,
    down_weight,
    attention_gain,
    feedforward_gain,
    lengths,
    token_order,
    real_token,
):
    x, c = tokens[0], cotangent[0]
    rows, width = x.shape
    slots = lax.axis_size("seq")
    shards = lax.axis_size("fsdp")
    seq, shard = lax.axis_index("seq"), lax.axis_index("fsdp")
    direct = slots == 8 and shards == 4
    heads = width // slots // HD
    own_width = heads * HD
    shard_rows = width // shards
    halves = 2 if direct else 1

    own_columns = [
        lax.dynamic_slice_in_dim(w, seq * own_width, own_width, axis=1)
        for w in (query_weight, key_weight, value_weight)
    ]
    gains = jnp.stack([attention_gain, feedforward_gain], axis=1)
    own_columns = jnp.concatenate(
        [jnp.pad(w, ((0, 0), (0, LANES - own_width))) for w in own_columns]
        + [jnp.pad(gains, ((0, 0), (0, LANES - 2)))],
        axis=1,
    )
    qkv_weight = jnp.concatenate([query_weight, key_weight, value_weight], axis=1)
    q_table, k_table = mask_tables(lengths[0], token_order[0], real_token[0])

    if direct:
        w_rows = shard ^ jnp.arange(shards, dtype=jnp.int32)
        place = seq // 2
        half = shard_rows // 2
        columns_x = flip(own_columns, "fsdp", 2)
        beside = flip(x, "seq", 1)
        right_1 = move_chain(x, [(1, 0), (2, 1), (3, 2)])
        left_1 = move_chain(x, [(0, 1), (1, 2), (2, 3)])
        output_x = flip(output_weight, "fsdp", 2)
        both = jnp.stack([own_columns, columns_x])
        both_c = flip(both, "fsdp", 1)
        column_pieces = jnp.stack([both[0], both_c[0], both[1], both_c[1]])
        columns_full = jnp.take(column_pieces, w_rows, axis=0).reshape(width, 4 * LANES)
        near = jnp.where(place % 2 == 0, right_1, left_1)
        right_1, left_1, near, _, _ = lax.optimization_barrier(
            (right_1, left_1, near, beside, output_x)
        )
        right_2 = move_chain(right_1, [(1, 0), (2, 1)])
        left_2 = move_chain(left_1, [(1, 2), (2, 3)])
        near_beside = flip(near, "seq", 1)
        gate_x1 = flip(after(gate_weight[:half], near), "fsdp", 2)
        far = jnp.where(place < 2, right_2, left_2)
        block_slots = [seq ^ d for d in range(slots)]
    else:
        w_rows = jnp.zeros((1,), jnp.int32)
        columns_full = lax.all_gather(own_columns, "fsdp", axis=0, tiled=True)
        gathered = lax.all_gather(x, "seq", axis=0)
        x_blocks = [gathered[i] for i in range(slots)]
        block_slots = [jnp.asarray(i, jnp.int32) for i in range(slots)]

    own_columns_full = columns_full[:, : 3 * LANES]
    gain_1 = columns_full[:, 3 * LANES].reshape(1, width)
    gain_2 = columns_full[:, 3 * LANES + 1].reshape(1, width)
    state = None

    def project_block(number, block, state):
        slot = block_slots[number].reshape(1).astype(jnp.int32)
        return project(
            slot, slots, heads, block, gain_1, own_columns_full, q_table, k_table, state
        )

    if direct:
        state = project_block(0, x, state)
        state = project_block(1, beside, state)
        far, _, _, _ = lax.optimization_barrier((far, near_beside, gate_x1, state[0]))
        third = move_chain(far, [(1, 0), (2, 3)])
        far_beside = flip(far, "seq", 1)
        gate_x2 = flip(after(gate_weight[half:], far), "fsdp", 2)
        gate_c = flip(after(gate_weight, far), "fsdp", 1)
        state = project_block(2, near, state)
        state = project_block(3, near_beside, state)
        state = project_block(4, far, state)
        cross = jnp.where(
            (place == 0) | (place == 3), third, jnp.where(place == 1, right_1, left_1)
        )
        cross, _, _, _, _ = lax.optimization_barrier(
            (cross, far_beside, gate_x2, gate_c, state[0])
        )
        cross_beside = flip(cross, "seq", 1)
        up_x1 = flip(after(up_weight[:half], cross), "fsdp", 2)
        gate_xc1 = flip(after(gate_x1, cross), "fsdp", 1)
        up_c = flip(after(up_weight, cross), "fsdp", 1)
        state = project_block(5, far_beside, state)
        state = project_block(6, cross, state)
        cross_beside, _, _, _ = lax.optimization_barrier((cross_beside, up_x1, gate_xc1, up_c))
        state = project_block(7, cross_beside, state)
    else:
        for number, block in enumerate(x_blocks):
            state = project_block(number, block, state)
    qa, ka, va, h1 = state

    att_first, sums, qb = attend(qa, ka, va, 0, 2, slots, (0, slots), ())
    middle_slot = slots // 2
    if direct:
        up_x2 = flip(after(up_weight[half:], qa), "fsdp", 2)
        down_x = flip(after(down_weight, qa), "fsdp", 2)
        gate_xc2 = flip(after(gate_x2, qa), "fsdp", 1)
        output_c = flip(after(output_weight, qa), "fsdp", 1)
        qb, _, _, _ = lax.optimization_barrier((qb, up_x2, gate_xc2, output_c))
    att_turned = turn(att_first)
    att_second, sums, qb = attend(
        qa, ka, va, 1, 2, slots, (0, middle_slot), (sums, qb)
    )
    if direct:
        output_xc = flip(after(output_x, att_first), "fsdp", 1)
        up_xc1 = flip(after(up_x1, att_first), "fsdp", 1)
        up_xc2 = flip(after(up_x2, att_first), "fsdp", 1)
        qb, _, _, _, _ = lax.optimization_barrier((qb, output_xc, up_xc1, up_xc2, att_turned))
    att_second, sums, qb = attend(
        qa, ka, va, 1, 2, slots, (middle_slot, slots), (att_second, sums, qb)
    )
    if direct:
        down_c = flip(after(down_weight, att_second), "fsdp", 1)
        down_xc = flip(after(down_x, att_second), "fsdp", 1)
        qkv_x = flip(after(qkv_weight, att_second), "fsdp", 2)
        wg = [
            (0, 0, gate_weight), (1, 0, gate_c), (2, 0, gate_x1), (2, half, gate_x2),
            (3, 0, gate_xc1), (3, half, gate_xc2),
        ]
        wu = [
            (0, 0, up_weight), (1, 0, up_c), (2, 0, up_x1), (2, half, up_x2),
            (3, 0, up_xc1), (3, half, up_xc2),
        ]
        wd = [(0, 0, down_weight), (1, 0, down_c), (2, 0, down_x), (3, 0, down_xc)]
        wo = [(0, 0, output_weight), (1, 0, output_c), (2, 0, output_x), (3, 0, output_xc)]
        pieces = shards
    else:
        wo, wg, wu, wd = [
            [(0, 0, lax.all_gather(w, "fsdp", axis=0, tiled=True))]
            for w in (output_weight, gate_weight, up_weight, down_weight)
        ]
        pieces = 1
    att_parts = [att_turned, turn(att_second)]
    total = rows * slots
    sums = sums.reshape(total, LANES)
    qb = qb.reshape(heads, total, LANES)

    (layer_out, d_middle, d_att), (og, gg, ug, dg) = middle_stage(
        w_rows, att_parts, x, c, gain_2, wo, wg, wu, wd, pieces, halves
    )
    grad_blocks = turn(d_att)
    parts = 4
    back = functools.partial(attend_back, qb, ka, va)
    if direct:
        line = Line()
        gate_r, up_r, down_r, output_r = [
            Reduction(kept, given, line) for kept, given in (gg, ug, dg, og)
        ]
        gate_r.given = after(gate_r.given, qkv_x)
        core_line = Line()
        for r in (gate_r, up_r, down_r, output_r):
            r.core()
            r.own, r.send = core_line.hold(r.own), core_line.hold(r.send)
            r.across()
        qkv_c = flip(after(qkv_weight, d_att), "fsdp", 1)
        grad_blocks = lax.optimization_barrier(
            (grad_blocks, gate_r.send, up_r.send, down_r.send, output_r.send)
        )[0]
    else:
        qkv_pieces = [lax.all_gather(qkv_weight, "fsdp", axis=0, tiled=True)]
    kv_0, dq, gb = back(0, parts, slots, sums, grad_blocks, None)
    kv_1, dq = back(1, parts, slots, None, None, (gb, dq))
    if direct:
        gate_r.arrived = after(gate_r.arrived, kv_1)
        gate_r.halve(1)
        gb = lax.optimization_barrier((gb, gate_r.own, qkv_c))[0]
    kv_early = turn(jnp.concatenate([kv_0, kv_1], axis=2))
    kv_2, dq = back(2, parts, slots, None, None, (gb, dq))
    if direct:
        up_r.arrived = after(up_r.arrived, kv_2)
        up_r.halve(2)
        gb = after(gb, up_r.own)
    kv_3, dq = back(3, parts, slots, None, None, (gb, dq))
    kv_late = jnp.concatenate([kv_2, kv_3], axis=2)
    late = turn(jnp.concatenate([kv_late.reshape(slots, rows, LANES), dq], axis=1))
    kv_late = late[:, :rows].reshape(kv_late.shape)
    dq_turned = late[:, rows:]
    if direct:
        gate_r.arrived = after(gate_r.arrived, kv_3)
        gate_r.halve(2)
        qkv_xc = flip(after(qkv_x, kv_2), "fsdp", 1)
        qkv_pieces = [qkv_weight, qkv_c, qkv_x, qkv_xc]
        dq = lax.optimization_barrier((dq, gate_r.own, kv_early))[0]
    own = own_terms(w_rows, h1, dq, [kv_0, kv_1, kv_2, kv_3], shards, halves)
    if direct:
        own_r = Reduction(*own, line)
        up_r.arrived = after(up_r.arrived, own[0])
        down_r.arrived = after(down_r.arrived, own[0])
        output_r.arrived = after(output_r.arrived, own[0])
        own_r.core()
        up_r.halve(1)
        down_r.halve(1)
        own_r.across()
        gate_r.halve(4)
        up_r.halve(4)
        output_r.halve(2)
        gate_r.settle()
        gate_r.widen(4)
        own_r.settle()
        own_r.own = own_r.own[None]
        own_r.widen(4)
        up_r.settle()
        up_r.widen(4)
        output_r.halve(1)
        down_r.halve(2)
        gate_r.own = after(gate_r.own, late)
        gate_r.widen(2)
        own_r.widen(2)
        up_r.widen(1)
        output_r.halve(4)
        down_r.halve(4)
        gate_r.widen(1)
        own_r.widen(1)
        input_grad = last_stage(
            w_rows, dq_turned, [kv_early, kv_late], x, d_middle, gain_1, qkv_pieces
        )
        up_r.widen(2)
        output_r.settle()
        output_r.widen(4)
        down_r.settle()
        down_r.own = after(down_r.own, input_grad)
        down_r.widen(4)
        output_r.widen(1)
        down_r.widen(2)
        output_r.widen(2)
        down_r.widen(1)
        for r in (gate_r, up_r, down_r, output_r, own_r):
            r.join()
        gate_grad, up_grad, down_grad, output_grad = [
            r.own for r in (gate_r, up_r, down_r, output_r)
        ]
        all_shares = own_r.own.reshape(2, 2, 2, shard_rows, 3 * LANES)
        all_shares = all_shares.transpose(2, 1, 0, 3, 4)
    else:
        own_share = lax.psum_scatter(own[0][0], "fsdp", scatter_dimension=0, tiled=True)
        all_shares = lax.all_gather(own_share, "seq", axis=0)
        gate_grad, up_grad, down_grad, output_grad = [
            lax.psum(lax.psum_scatter(g[0][0], "fsdp", scatter_dimension=0, tiled=True), "seq")
            for g in (gg, ug, dg, og)
        ]
    all_shares = all_shares.reshape(slots, shard_rows, 3, LANES)[..., :own_width].astype(f32)
    query_grad, key_grad, value_grad = [
        all_shares[:, :, i, :].transpose(1, 0, 2).reshape(shard_rows, width) for i in range(3)
    ]
    if not direct:
        input_grad = last_stage(
            w_rows, dq_turned, [kv_early, kv_late], x, d_middle, gain_1, qkv_pieces
        )

    def gain_grad(terms, gain):
        summed = sum(jnp.sum(g * w.astype(f32), axis=1) for g, w in terms)
        return summed / gain.astype(f32)

    output_grad, gate_grad, up_grad, down_grad = [
        g.astype(f32) for g in (output_grad, gate_grad, up_grad, down_grad)
    ]
    attention_gain_grad = gain_grad(
        ((query_grad, query_weight), (key_grad, key_weight), (value_grad, value_weight)),
        attention_gain,
    )
    feedforward_gain_grad = gain_grad(
        ((gate_grad, gate_weight), (up_grad, up_weight)), feedforward_gain
    )
    return (
        layer_out[None],
        input_grad[None],
        query_grad,
        key_grad,
        value_grad,
        output_grad,
        gate_grad,
        up_grad,
        down_grad,
        attention_gain_grad,
        feedforward_gain_grad,
    )


def solution(mesh):
    in_specs = (
        P("fsdp", "seq", None),
        P("fsdp", "seq", None),
        P("fsdp", None),
        P("fsdp", None),
        P("fsdp", None),
        P("fsdp", None),
        P("fsdp", None),
        P("fsdp", None),
        P("fsdp", None),
        P("fsdp"),
        P("fsdp"),
        P("fsdp", None),
        P("fsdp", None),
        P("fsdp", None),
    )
    out_specs = (
        P("fsdp", "seq", None),
        P("fsdp", "seq", None),
        P("fsdp", None),
        P("fsdp", None),
        P("fsdp", None),
        P("fsdp", None),
        P("fsdp", None),
        P("fsdp", None),
        P("fsdp", None),
        P("fsdp"),
        P("fsdp"),
    )
    return jax.shard_map(
        on_device, mesh=mesh, in_specs=in_specs, out_specs=out_specs, check_vma=False
    )
```

time: 707 us -> 505 us (0.71)
  waiting for transfers between devices: 324 us -> 126 us
  other arithmetic: 53.7 us -> 73.4 us
  starting transfers between devices: 107 us -> 91.9 us
    ppermute x108 -> x62, waiting for transfers between devices: 296 us -> 107 us  [flip(): return lax.ppermute(values, axis, [(i, i ^ delta) for i in range(count)])]
    ppermute x108 -> x62, starting transfers between devices: 97.9 us -> 55.1 us  [flip(): return lax.ppermute(values, axis, [(i, i ^ delta) for i in range(count)])]
    all_to_all x0 -> x5, starting transfers between devices: none -> 25.8 us  [turn(): lax.all_to_all(blocks, 'seq', split_axis=0, concat_axis=0, tiled=True)]
    convert_element_type x21, other arithmetic: 15.4 us -> 35.3 us  [add_low(): return (a.astype(f32) + b.astype(f32)).astype(bf16)]
    ppermute x5, waiting for transfers between devices: 28.2 us -> 11.3 us  [move_chain(): lax.ppermute(array, 'seq', [(a * 2 + low, b * 2 + low) for a, b in pairs...]
    unnamed x227 -> x96, local copies, waits for them, and re-layouts: 16.3 us -> 13.2 us
  transfers between devices with their start and end apart: 113 -> 72, of which waited for: 52 -> 24; matrix products, arithmetic and copies ran while one was open for 12% -> 18% of each run, Pallas kernels for 19% -> 35%
where the time goes in v2:
time: 505 us; the launch traced here: 497 us
  Pallas kernels  177 us (35%)
  waiting for transfers between devices  126 us (25%)
  starting transfers between devices  91.9 us (18%)
  other arithmetic  73.4 us (15%)
  local copies, waits for them, and re-layouts  26.8 us (5%)
    ppermute x62, waiting for transfers between devices, flip(): return lax.ppermute(values, axis, [(i, i ^ delta) for i in range(count)])  107 us
    pallas_call x4, Pallas kernels, attend_back(): pl.pallas_call(functools.partial(backward_kernel, heads, part, parts, 512...  65.4 us
    ppermute x62, starting transfers between devices, flip(): return lax.ppermute(values, axis, [(i, i ^ delta) for i in range(count)])  55.1 us
    pallas_call x1, Pallas kernels, middle_stage(): pl.pallas_call(functools.partial(middle_kernel, parts, pieces, halves, st...  36.8 us
    convert_element_type x21, other arithmetic, add_low(): return (a.astype(f32) + b.astype(f32)).astype(bf16)  35.3 us
    pallas_call x3, Pallas kernels, attend(): pl.pallas_call(functools.partial(forward_body, heads, len(extra)), grid=(...  34.5 us
    all_to_all x5, starting transfers between devices, turn(): lax.all_to_all(blocks, 'seq', split_axis=0, concat_axis=0, tiled=True)  25.8 us
    pallas_call x8, Pallas kernels, project(): pl.pallas_call(functools.partial(project_kernel, heads, fresh), grid_spec...  24.2 us
  transfers between devices with their start and end apart: 72, of which 24 were waited for; matrix products, arithmetic and copies ran while one was open for 18% of the time, Pallas kernels for 35%

profile of v2, /device:TPU:0, one launch (start us, length us, event | category | flops | bytes accessed | tf_op | source)
XLA Modules:
  0.0 496.7 jit_solution(11091657351907318577)
XLA Ops:
  0.7 3.0 collective-permute-start.2
  5.0 5.4 %collective-permute-start.1 = (bf16[320,1024]{1,0:T(8,128)(2,1)}, bf16[320,1024]{1,0:T(8,128)(2,1)}, u32[]{:S(2)}, u32[]{:S(2)}) collective-permute-start(bf16[320,1024]{1,0:T(8,128)(2,1)} %bitcast.109), channel_id=1, source_target_pairs={{0,8},{4,12},{8,16},{12,20},{16,24},{20,28},{1,9},{5,13},{9,17},{1... | collective-permute-start | bytes 1966088 | tf_op jit(solution)/shard_map/ppermute | solution.py:703
  16.4 2.9 select_reduce_fusion
  28.8 3.6 collective-permute-done.3.refs_8_
  40.9 3.0 project.8
  43.9 3.0 project.9
  46.9 4.2 collective-permute-done.4
  55.7 3.0 project.10
  58.8 3.0 project.11
  61.8 3.0 project.12
  64.8 7.1 %collective-permute-done.10 = bf16[320,1024]{1,0:T(8,128)(2,1)} collective-permute-done((bf16[320,1024]{1,0:T(8,128)(2,1)S(1)}, bf16[320,1024]{1,0:T(8,128)(2,1)}, u32[]{:S(2)}, u32[]{:S(2)}) %collective-permute-start.10) | collective-permute-done | bytes 655392 | tf_op jit(solution)/shard_map/ppermute | solution.py:703
  76.7 3.0 project.13
  79.7 3.0 project.14
  82.8 9.3 %collective-permute-done.14.refs_1_ = bf16[320,1024]{1,0:T(8,128)(2,1)S(1)} collective-permute-done((bf16[320,1024]{1,0:T(8,128)(2,1)}, bf16[320,1024]{1,0:T(8,128)(2,1)S(1)}, u32[]{:S(2)}, u32[]{:S(2)}) %collective-permute-start.14) | collective-permute-done | bytes 655392 | tf_op jit(solution)/shard_map/ppermute | solution.py:610
  93.1 3.0 project.15
  98.7 15.9 %attend.3 = (bf16[8,160,128]{2,1,0:T(8,128)(2,1)}, f32[8,2,160,128]{3,2,1,0:T(8,128)}, bf16[2,8,2,160,128]{4,3,2,1,0:T(8,128)(2,1)}) custom-call(bf16[2,8,2,160,128]{4,3,2,1,0:T(8,128)(2,1)} %bitcast.83, bf16[2,8,2,160,128]{4,3,2,1,0:T(8,128)(2,1)} %bitcast.86, bf16[2,8,2,160,128]{4,3,2,1,0:T(8,128)(2,1)} %bitcast.93, ...), custom_call_target="tpu_custom_call" | custom-call | flops 6710886400 | bytes 2621440 | tf_op jit(solution)/shard_map/attend/pallas_call | solution.py:169
  115.2 7.0 %all-to-all-start = ((bf16[8,160,128]{2,1,0:T(8,128)(2,1)}), bf16[8,160,128]{2,1,0:T(8,128)(2,1)S(1)}, u32[]{:S(2)}, u32[]{:S(2)}) async-start(bf16[8,160,128]{2,1,0:T(8,128)(2,1)} %get-tuple-element.188), calls=%async_computation | async-start | bytes 655360 | tf_op jit(solution)/shard_map/all_to_all | solution.py:709
  122.5 9.3 %attend.4 = (bf16[8,160,128]{2,1,0:T(8,128)(2,1)}, f32[8,2,160,128]{3,2,1,0:T(8,128)}, bf16[2,8,2,160,128]{4,3,2,1,0:T(8,128)(2,1)}) custom-call(bf16[2,8,2,160,128]{4,3,2,1,0:T(8,128)(2,1)} %bitcast.84, bf16[2,8,2,160,128]{4,3,2,1,0:T(8,128)(2,1)} %bitcast.87, bf16[2,8,2,160,128]{4,3,2,1,0:T(8,128)(2,1)} %bitcast.94, ...), custom_call_target="tpu_custom_call", output_to_operand_aliasing={{1}: (5, {}), {2}: (6, {})} | custom-call | flops 6710886400 | bytes 2621440 | tf_op jit(solution)/shard_map/attend/pallas_call | solution.py:169
  134.0 9.3 %attend.5 = (bf16[8,160,128]{2,1,0:T(8,128)(2,1)}, f32[8,2,160,128]{3,2,1,0:T(8,128)}, bf16[2,8,2,160,128]{4,3,2,1,0:T(8,128)(2,1)}) custom-call(bf16[2,8,2,160,128]{4,3,2,1,0:T(8,128)(2,1)} %bitcast.85, bf16[2,8,2,160,128]{4,3,2,1,0:T(8,128)(2,1)} %bitcast.88, ...), custom_call_target="tpu_custom_call", output_to_operand_aliasing={{0}: (5, {}), {1}: (6, {}), {2}: (7, {})} | custom-call | flops 6710886400 | bytes 2621440 | tf_op jit(solution)/shard_map/attend/pallas_call | solution.py:169
  144.8 7.2 %all-to-all-start.1 = ((bf16[8,160,128]{2,1,0:T(8,128)(2,1)}), bf16[8,160,128]{2,1,0:T(8,128)(2,1)S(1)}, u32[]{:S(2)}, u32[]{:S(2)}) async-start(bf16[8,160,128]{2,1,0:T(8,128)(2,1)} %get-tuple-element.202), calls=%async_computation.1 | async-start | bytes 655360 | tf_op jit(solution)/shard_map/all_to_all | solution.py:709
  156.9 5.6 %all-to-all-done.1.refs_2_ = bf16[8,160,128]{2,1,0:T(8,128)(2,1)S(1)} async-done(((bf16[8,160,128]{2,1,0:T(8,128)(2,1)}), bf16[8,160,128]{2,1,0:T(8,128)(2,1)S(1)}, u32[]{:S(2)}, u32[]{:S(2)}) %all-to-all-start.1) | async-done | bytes 327712 | tf_op jit(solution)/shard_map/all_to_all | solution.py:709
  163.2 36.8 %middle_stage.1 = (bf16[320,1024]{1,0:T(8,128)(2,1)}, f32[320,1024]{1,0:T(8,128)}, bf16[8,320,128]{2,1,0:T(8,128)(2,1)}, bf16[2,256,1024]{2,1,0:T(8,128)(2,1)}, ...) custom-call(s32[4]{0:T(128)} %iota_xor_fusion.refs_0_, ...), custom_call_target="tpu_custom_call" | custom-call | flops 18622709760 | bytes 38797312 | tf_op jit(solution)/shard_map/middle_stage/pallas_call | solution.py:530
  201.1 3.8 all-to-all-start.2
  205.0 10.4 %collective-permute-done.31 = bf16[2,256,1024]{2,1,0:T(8,128)(2,1)} collective-permute-done((bf16[2,256,1024]{2,1,0:T(8,128)(2,1)}, bf16[2,256,1024]{2,1,0:T(8,128)(2,1)}, u32[]{:S(2)}, u32[]{:S(2)}) %collective-permute-start.31) | collective-permute-done | bytes 1048608 | tf_op jit(solution)/shard_map/ppermute | solution.py:610
  215.4 3.1 fusion.8
  220.1 3.8 fusion.2
  223.9 4.6 fusion.4
  228.5 4.2 add_convert_fusion
  237.6 17.4 %attend_back.4 = (bf16[8,2,80,128]{3,2,1,0:T(8,128)(2,1)}, f32[2,2560,128]{2,1,0:T(8,128)}, bf16[2,2560,128]{2,1,0:T(8,128)(2,1)}) custom-call(bf16[2,2560,128]{2,1,0:T(8,128)(2,1)} %bitcast.120, bf16[2,8,4,80,128]{4,3,2,1,0:T(8,128)(2,1)} %bitcast.89, bf16[2,8,4,80,128]{4,3,2,1,0:T(8,128)(2,1)} %bitcast.96, f32[2560,128]{1,0:T(8,128)} %bitcast.119, ...), custom_call_target="tpu_custom_call" | custom-call | flops 8388608000 | bytes 7864320 | tf_op jit(solution)/shard_map/attend_back/pallas_call | solution.py:323
  255.0 16.2 %attend_back.5 = (bf16[8,2,80,128]{3,2,1,0:T(8,128)(2,1)}, f32[2,2560,128]{2,1,0:T(8,128)}) custom-call(bf16[2,2560,128]{2,1,0:T(8,128)(2,1)} %bitcast.121, bf16[2,8,4,80,128]{4,3,2,1,0:T(8,128)(2,1)} %bitcast.90, bf16[2,8,4,80,128]{4,3,2,1,0:T(8,128)(2,1)} %bitcast.97, bf16[2,2560,128]{2,1,0:T(8,128)(2,1)} %get-tuple-element.236.refs_3_, ...), custom_call_target="tpu_custom_call" | custom-call | flops 8388608000 | bytes 7864320 | tf_op jit(solution)/shard_map/attend_back/pallas_call | solution.py:323
  273.1 3.9 all-to-all-start.4
  277.0 3.2 fusion.5
  280.2 16.2 %attend_back.6 = (bf16[8,2,80,128]{3,2,1,0:T(8,128)(2,1)}, f32[2,2560,128]{2,1,0:T(8,128)}) custom-call(bf16[2,2560,128]{2,1,0:T(8,128)(2,1)} %bitcast.122, bf16[2,8,4,80,128]{4,3,2,1,0:T(8,128)(2,1)} %bitcast.91, bf16[2,8,4,80,128]{4,3,2,1,0:T(8,128)(2,1)} %bitcast.98, bf16[2,2560,128]{2,1,0:T(8,128)(2,1)} %get-tuple-element.236.refs_3_, ...), custom_call_target="tpu_custom_call" | custom-call | flops 8388608000 | bytes 7864320 | tf_op jit(solution)/shard_map/attend_back/pallas_call | solution.py:323
  302.6 15.6 %attend_back.7 = (bf16[8,2,80,128]{3,2,1,0:T(8,128)(2,1)}, bf16[8,320,128]{2,1,0:T(8,128)(2,1)}) custom-call(bf16[2,2560,128]{2,1,0:T(8,128)(2,1)} %bitcast.123, bf16[2,8,4,80,128]{4,3,2,1,0:T(8,128)(2,1)} %bitcast.92, bf16[2,8,4,80,128]{4,3,2,1,0:T(8,128)(2,1)} %bitcast.99, bf16[2,2560,128]{2,1,0:T(8,128)(2,1)} %get-tuple-element.236.refs_3_, ...), custom_call_target="tpu_custom_call" | custom-call | flops 8388608000 | bytes 7864320 | tf_op jit(solution)/shard_map/attend_back/pallas_call | solution.py:323
  322.7 3.9 all-to-all-start.3
  326.6 8.4 %own_terms.1 = (bf16[2,256,384]{2,1,0:T(8,128)(2,1)}, bf16[2,256,384]{2,1,0:T(8,128)(2,1)}) custom-call(s32[4]{0:T(128)} %iota_xor_fusion.refs_0_, bf16[8,4,80,1024]{3,2,1,0:T(8,128)(2,1)} %bitcast.82, bf16[8,320,128]{2,1,0:T(8,128)(2,1)} %get-tuple-element.245.refs_2_, bf16[8,2,80,128]{3,2,1,0:T(8,128)(2,1)} %get-tuple-element.240.refs_3_, ...), custom_call_target="tpu_custom_call" | custom-call | flops 2013265920 | bytes 5242880 | tf_op jit(solution)/shard_map/own_terms/pallas_call | solution.py:375
  345.4 8.4 %collective-permute-done.39 = bf16[64,2816]{1,0:T(8,128)(2,1)S(1)} collective-permute-done((bf16[64,2816]{1,0:T(8,128)(2,1)S(1)}, bf16[64,2816]{1,0:T(8,128)(2,1)S(1)}, u32[]{:S(2)}, u32[]{:S(2)}) %collective-permute-start.39) | collective-permute-done | bytes 360480 | tf_op jit(solution)/shard_map/ppermute | solution.py:610
  353.9 5.9 %collective-permute-start.42 = (bf16[32,2816]{1,0:T(8,128)(2,1)S(1)}, bf16[32,2816]{1,0:T(8,128)(2,1)S(1)}, u32[]{:S(2)}, u32[]{:S(2)}) collective-permute-start(bf16[32,2816]{1,0:T(8,128)(2,1)S(1)} %add_convert_fusion.29), channel_id=1, source_target_pairs={{0,16},{4,20},{8,24},{12,28},{16,0},{20,4},{24,8},{28,12},{1,17},{... | collective-permute-start | bytes 540680 | tf_op jit(solution)/shard_map/ppermute | solution.py:610
  361.2 11.2 %collective-permute-done.49 = bf16[32,2816]{1,0:T(8,128)(2,1)S(1)} collective-permute-done((bf16[32,2816]{1,0:T(8,128)(2,1)S(1)}, bf16[32,2816]{1,0:T(8,128)(2,1)S(1)}, u32[]{:S(2)}, u32[]{:S(2)}) %collective-permute-start.49) | collective-permute-done | bytes 180256 | tf_op jit(solution)/shard_map/ppermute | solution.py:610
  375.1 2.9 collective-permute-start.54
  383.2 14.9 %collective-permute-done.54 = bf16[32,2816]{1,0:T(8,128)(2,1)S(1)} collective-permute-done((bf16[32,2816]{1,0:T(8,128)(2,1)S(1)}, bf16[32,2816]{1,0:T(8,128)(2,1)S(1)}, u32[]{:S(2)}, u32[]{:S(2)}) %collective-permute-start.54) | collective-permute-done | bytes 180256 | tf_op jit(solution)/shard_map/ppermute | solution.py:610
  398.2 4.1 collective-permute-done.45
  411.4 7.7 %last_stage.1 = f32[320,1024]{1,0:T(8,128)} custom-call(s32[4]{0:T(128)} %iota_xor_fusion.refs_0_, bf16[8,320,128]{2,1,0:T(8,128)(2,1)} %get-tuple-element.343.refs_1_, bf16[8,2,160,128]{3,2,1,0:T(8,128)(2,1)} %copy-done.15, bf16[8,2,160,128]{3,2,1,0:T(8,128)(2,1)} %bitcast.106, bf16[320,1024]{1,0:T(8,128)(2,1)} %bitcast.112, ...), custom_call_target="tpu_custom_call" | custom-call | flops 2013265920 | bytes 6291456 | tf_op jit(solution)/shard_map/last_stage/pallas_call | solution.py:596
  419.1 3.9 collective-permute-done.56
  431.6 7.4 %collective-permute-done.58 = bf16[32,1024]{1,0:T(8,128)(2,1)S(1)} collective-permute-done((bf16[32,1024]{1,0:T(8,128)(2,1)S(1)}, bf16[32,1024]{1,0:T(8,128)(2,1)S(1)}, u32[]{:S(2)}, u32[]{:S(2)}) %collective-permute-start.58) | collective-permute-done | bytes 65568 | tf_op jit(solution)/shard_map/ppermute | solution.py:610
  441.8 3.1 collective-permute-done.60
  449.1 5.1 %collective-permute-done.62 = bf16[128,1024]{1,0:T(8,128)(2,1)S(1)} collective-permute-done((bf16[128,1024]{1,0:T(8,128)(2,1)S(1)}, bf16[128,1024]{1,0:T(8,128)(2,1)S(1)}, u32[]{:S(2)}, u32[]{:S(2)}) %collective-permute-start.62) | collective-permute-done | bytes 262176 | tf_op jit(solution)/shard_map/ppermute | solution.py:610
  455.6 16.6 %collective-permute-done.65 = bf16[176,1024]{1,0:T(8,128)(2,1)S(1)} collective-permute-done((bf16[176,1024]{1,0:T(8,128)(2,1)S(1)}, bf16[176,1024]{1,0:T(8,128)(2,1)S(1)}, u32[]{:S(2)}, u32[]{:S(2)}) %collective-permute-start.65) | collective-permute-done | bytes 360480 | tf_op jit(solution)/shard_map/ppermute | solution.py:610
  (314 shorter events, 137.8 us)
Async XLA Ops:
  0.7 31.8 %collective-permute-start.2 = (bf16[320,1024]{1,0:T(8,128)(2,1)}, bf16[320,1024]{1,0:T(8,128)(2,1)S(1)}, u32[]{:S(2)}, u32[]{:S(2)}) collective-permute-start(bf16[320,1024]{1,0:T(8,128)(2,1)} %bitcast.107), channel_id=1, source_target_pairs={{0,4},{4,0},{8,12},{12,8},{16,20},{20,16},{24,28},{28,24},{1,5},{5... | collective-permute-start | bytes 1966088 | tf_op jit(solution)/shard_map/ppermute | solution.py:610
  3.7 23.1 %collective-permute-start = (bf16[320,1024]{1,0:T(8,128)(2,1)}, bf16[320,1024]{1,0:T(8,128)(2,1)}, u32[]{:S(2)}, u32[]{:S(2)}) collective-permute-start(bf16[320,1024]{1,0:T(8,128)(2,1)} %bitcast.108), channel_id=1, source_target_pairs={{8,0},{12,4},{16,8},{20,12},{24,16},{28,20},{9,1},{13,5},{17,9},{2... | collective-permute-start | bytes 1966088 | tf_op jit(solution)/shard_map/ppermute | solution.py:703
  5.0 21.8 %collective-permute-start.1 = (bf16[320,1024]{1,0:T(8,128)(2,1)}, bf16[320,1024]{1,0:T(8,128)(2,1)}, u32[]{:S(2)}, u32[]{:S(2)}) collective-permute-start(bf16[320,1024]{1,0:T(8,128)(2,1)} %bitcast.109), channel_id=1, source_target_pairs={{0,8},{4,12},{8,16},{12,20},{16,24},{20,28},{1,9},{5,13},{9,17},{1... | collective-permute-start | bytes 1966088 | tf_op jit(solution)/shard_map/ppermute | solution.py:703
  32.5 19.8 %collective-permute-start.6 = (bf16[320,1024]{1,0:T(8,128)(2,1)}, bf16[320,1024]{1,0:T(8,128)(2,1)}, u32[]{:S(2)}, u32[]{:S(2)}) collective-permute-start(bf16[320,1024]{1,0:T(8,128)(2,1)} %broadcast_select_fusion.8.refs_1_), channel_id=1, source_target_pairs={{0,4},{4,0},{8,12},{12,8},{16,20},{20,16},{24,28},{28,24},{1,5},{5... | collective-permute-start | bytes 1966088 | tf_op jit(solution)/shard_map/ppermute | solution.py:610
  33.0 19.3 %collective-permute-start.7 = (bf16[128,2816]{1,0:T(8,128)(2,1)}, bf16[128,2816]{1,0:T(8,128)(2,1)}, u32[]{:S(2)}, u32[]{:S(2)}) collective-permute-start(bf16[128,2816]{1,0:T(8,128)(2,1)} %get-tuple-element.148), channel_id=1, source_target_pairs={{0,2},{1,3},{2,0},{3,1},{4,6},{5,7},{6,4},{7,5},{8,10},{9,11},{10,... | collective-permute-start | bytes 2162696 | tf_op jit(solution)/shard_map/ppermute | solution.py:610
  52.3 21.8 %collective-permute-start.13 = (bf16[256,2816]{1,0:T(8,128)(2,1)S(1)}, bf16[256,2816]{1,0:T(8,128)(2,1)}, u32[]{:S(2)}, u32[]{:S(2)}) collective-permute-start(bf16[256,2816]{1,0:T(8,128)(2,1)S(1)} %copy-done), channel_id=1, source_target_pairs={{0,1},{1,0},{2,3},{3,2},{4,5},{5,4},{6,7},{7,6},{8,9},{9,8},{10,11... | collective-permute-start | bytes 4325384 | tf_op jit(solution)/shard_map/ppermute | solution.py:610
  52.4 19.5 %collective-permute-start.10 = (bf16[320,1024]{1,0:T(8,128)(2,1)S(1)}, bf16[320,1024]{1,0:T(8,128)(2,1)}, u32[]{:S(2)}, u32[]{:S(2)}) collective-permute-start(bf16[320,1024]{1,0:T(8,128)(2,1)S(1)} %broadcast_select_fusion.9.refs_1_), channel_id=1, source_target_pairs={{8,0},{12,4},{16,24},{20,28},{9,1},{13,5},{17,25},{21,29},{10,2},{... | collective-permute-start | bytes 1966088 | tf_op jit(solution)/shard_map/ppermute | solution.py:703
  53.9 20.2 %collective-permute-start.12 = (bf16[128,2816]{1,0:T(8,128)(2,1)}, bf16[128,2816]{1,0:T(8,128)(2,1)}, u32[]{:S(2)}, u32[]{:S(2)}) collective-permute-start(bf16[128,2816]{1,0:T(8,128)(2,1)} %get-tuple-element.155), channel_id=1, source_target_pairs={{0,2},{1,3},{2,0},{3,1},{4,6},{5,7},{6,4},{7,5},{8,10},{9,11},{10,... | collective-permute-start | bytes 2162696 | tf_op jit(solution)/shard_map/ppermute | solution.py:610
  54.5 19.6 %collective-permute-start.11 = (bf16[320,1024]{1,0:T(8,128)(2,1)S(1)}, bf16[320,1024]{1,0:T(8,128)(2,1)}, u32[]{:S(2)}, u32[]{:S(2)}) collective-permute-start(bf16[320,1024]{1,0:T(8,128)(2,1)S(1)} %broadcast_select_fusion.9.refs_1_), channel_id=1, source_target_pairs={{0,4},{4,0},{8,12},{12,8},{16,20},{20,16},{24,28},{28,24},{1,5},{5... | collective-permute-start | bytes 1966088 | tf_op jit(solution)/shard_map/ppermute | solution.py:610
  74.1 19.0 %collective-permute-start.17 = (bf16[256,2816]{1,0:T(8,128)(2,1)S(1)}, bf16[256,2816]{1,0:T(8,128)(2,1)}, u32[]{:S(2)}, u32[]{:S(2)}) collective-permute-start(bf16[256,2816]{1,0:T(8,128)(2,1)S(1)} %copy-done.2), channel_id=1, source_target_pairs={{0,1},{1,0},{2,3},{3,2},{4,5},{5,4},{6,7},{7,6},{8,9},{9,8},{10,11... | collective-permute-start | bytes 4325384 | tf_op jit(solution)/shard_map/ppermute | solution.py:610
  74.9 18.2 %collective-permute-start.15 = (bf16[128,2816]{1,0:T(8,128)(2,1)S(1)}, bf16[128,2816]{1,0:T(8,128)(2,1)}, u32[]{:S(2)}, u32[]{:S(2)}) collective-permute-start(bf16[128,2816]{1,0:T(8,128)(2,1)S(1)} %get-tuple-element.170), channel_id=1, source_target_pairs={{0,2},{1,3},{2,0},{3,1},{4,6},{5,7},{6,4},{7,5},{8,10},{9,11},{10,... | collective-permute-start | bytes 2162696 | tf_op jit(solution)/shard_map/ppermute | solution.py:610
  96.1 19.1 %collective-permute-start.18 = (bf16[128,2816]{1,0:T(8,128)(2,1)S(1)}, bf16[128,2816]{1,0:T(8,128)(2,1)S(1)}, u32[]{:S(2)}, u32[]{:S(2)}) collective-permute-start(bf16[128,2816]{1,0:T(8,128)(2,1)S(1)} %get-tuple-element.191), channel_id=1, source_target_pairs={{0,2},{1,3},{2,0},{3,1},{4,6},{5,7},{6,4},{7,5},{8,10},{9,11},{10,... | collective-permute-start | bytes 2162696 | tf_op jit(solution)/shard_map/ppermute | solution.py:610
  97.4 25.1 %collective-permute-start.19 = (bf16[128,2816]{1,0:T(8,128)(2,1)}, bf16[128,2816]{1,0:T(8,128)(2,1)}, u32[]{:S(2)}, u32[]{:S(2)}) collective-permute-start(bf16[128,2816]{1,0:T(8,128)(2,1)} %collective-permute-done.12.refs_13_), channel_id=1, source_target_pairs={{0,1},{1,0},{2,3},{3,2},{4,5},{5,4},{6,7},{7,6},{8,9},{9,8},{10,11... | collective-permute-start | bytes 2162696 | tf_op jit(solution)/shard_map/ppermute | solution.py:610
  97.4 24.8 %collective-permute-start.20 = (bf16[256,1024]{1,0:T(8,128)(2,1)}, bf16[256,1024]{1,0:T(8,128)(2,1)}, u32[]{:S(2)}, u32[]{:S(2)}) collective-permute-start(bf16[256,1024]{1,0:T(8,128)(2,1)} %refs_6_.1), channel_id=1, source_target_pairs={{0,1},{1,0},{2,3},{3,2},{4,5},{5,4},{6,7},{7,6},{8,9},{9,8},{10,11... | collective-permute-start | bytes 1572872 | tf_op jit(solution)/shard_map/ppermute | solution.py:610
  97.9 46.4 %collective-permute-start.25 = (bf16[704,1024]{1,0:T(8,128)(2,1)}, bf16[704,1024]{1,0:T(8,128)(2,1)S(1)}, u32[]{:S(2)}, u32[]{:S(2)}) collective-permute-start(bf16[704,1024]{1,0:T(8,128)(2,1)} %refs_22_.1), channel_id=1, source_target_pairs={{0,2},{1,3},{2,0},{3,1},{4,6},{5,7},{6,4},{7,5},{8,10},{9,11},{10,... | collective-permute-start | bytes 4325384 | tf_op jit(solution)/shard_map/ppermute | solution.py:610
  114.6 18.6 %collective-permute-start.22 = (bf16[128,2816]{1,0:T(8,128)(2,1)}, bf16[128,2816]{1,0:T(8,128)(2,1)}, u32[]{:S(2)}, u32[]{:S(2)}) collective-permute-start(bf16[128,2816]{1,0:T(8,128)(2,1)} %collective-permute-done.15.refs_18_), channel_id=1, source_target_pairs={{0,1},{1,0},{2,3},{3,2},{4,5},{5,4},{6,7},{7,6},{8,9},{9,8},{10,11... | collective-permute-start | bytes 2162696 | tf_op jit(solution)/shard_map/ppermute | solution.py:610
  144.3 18.1 %collective-permute-start.24 = (bf16[704,1024]{1,0:T(8,128)(2,1)}, bf16[704,1024]{1,0:T(8,128)(2,1)}, u32[]{:S(2)}, u32[]{:S(2)}) collective-permute-start(bf16[704,1024]{1,0:T(8,128)(2,1)} %refs_22_.1), channel_id=1, source_target_pairs={{0,1},{1,0},{2,3},{3,2},{4,5},{5,4},{6,7},{7,6},{8,9},{9,8},{10,11... | collective-permute-start | bytes 4325384 | tf_op jit(solution)/shard_map/ppermute | solution.py:610
  155.8 44.7 %collective-permute-start.27 = (bf16[256,3072]{1,0:T(8,128)(2,1)}, bf16[256,3072]{1,0:T(8,128)(2,1)}, u32[]{:S(2)}, u32[]{:S(2)}) collective-permute-start(bf16[256,3072]{1,0:T(8,128)(2,1)} %constant_dynamic-update-slice_fusion.refs_7_), channel_id=1, source_target_pairs={{0,2},{1,3},{2,0},{3,1},{4,6},{5,7},{6,4},{7,5},{8,10},{9,11},{10,... | collective-permute-start | bytes 4718600 | tf_op jit(solution)/shard_map/ppermute | solution.py:610
  200.0 18.5 %collective-permute-start.29 = (bf16[2,256,2816]{2,1,0:T(8,128)(2,1)}, bf16[2,256,2816]{2,1,0:T(8,128)(2,1)S(1)}, u32[]{:S(2)}, u32[]{:S(2)}) collective-permute-start(bf16[2,256,2816]{2,1,0:T(8,128)(2,1)} %get-tuple-element.215), channel_id=1, source_target_pairs={{0,1},{1,0},{2,3},{3,2},{4,5},{5,4},{6,7},{7,6},{8,9},{9,8},{10,11... | collective-permute-start | bytes 8650760 | tf_op jit(solution)/shard_map/ppermute | solution.py:610
  200.1 23.8 %collective-permute-start.30 = (bf16[2,704,1024]{2,1,0:T(8,128)(2,1)}, bf16[2,704,1024]{2,1,0:T(8,128)(2,1)}, u32[]{:S(2)}, u32[]{:S(2)}) collective-permute-start(bf16[2,704,1024]{2,1,0:T(8,128)(2,1)} %get-tuple-element.219), channel_id=1, source_target_pairs={{0,1},{1,0},{2,3},{3,2},{4,5},{5,4},{6,7},{7,6},{8,9},{9,8},{10,11... | collective-permute-start | bytes 8650760 | tf_op jit(solution)/shard_map/ppermute | solution.py:610
  200.6 27.9 %collective-permute-start.28 = (bf16[2,256,2816]{2,1,0:T(8,128)(2,1)}, bf16[2,256,2816]{2,1,0:T(8,128)(2,1)}, u32[]{:S(2)}, u32[]{:S(2)}) collective-permute-start(bf16[2,256,2816]{2,1,0:T(8,128)(2,1)} %get-tuple-element.213), channel_id=1, source_target_pairs={{0,1},{1,0},{2,3},{3,2},{4,5},{5,4},{6,7},{7,6},{8,9},{9,8},{10,11... | collective-permute-start | bytes 8650760 | tf_op jit(solution)/shard_map/ppermute | solution.py:610
  201.1 35.7 %all-to-all-start.2 = ((bf16[8,320,128]{2,1,0:T(8,128)(2,1)}), bf16[8,320,128]{2,1,0:T(8,128)(2,1)S(1)}, u32[]{:S(2)}, u32[]{:S(2)}) async-start(bf16[8,320,128]{2,1,0:T(8,128)(2,1)} %get-tuple-element.209), calls=%async_computation.2 | async-start | bytes 1310720 | tf_op jit(solution)/shard_map/all_to_all | solution.py:709
  204.9 75.3 %collective-permute-start.33 = (bf16[256,3072]{1,0:T(8,128)(2,1)}, bf16[256,3072]{1,0:T(8,128)(2,1)}, u32[]{:S(2)}, u32[]{:S(2)}) collective-permute-start(bf16[256,3072]{1,0:T(8,128)(2,1)} %constant_dynamic-update-slice_fusion.refs_7_), channel_id=1, source_target_pairs={{0,1},{1,0},{2,3},{3,2},{4,5},{5,4},{6,7},{7,6},{8,9},{9,8},{10,11... | collective-permute-start | bytes 4718600 | tf_op jit(solution)/shard_map/ppermute | solution.py:610
  232.7 44.3 %collective-permute-start.32 = (bf16[256,2816]{1,0:T(8,128)(2,1)}, bf16[256,2816]{1,0:T(8,128)(2,1)}, u32[]{:S(2)}, u32[]{:S(2)}) collective-permute-start(bf16[256,2816]{1,0:T(8,128)(2,1)} %get-tuple-element.308), channel_id=1, source_target_pairs={{0,2},{1,3},{2,0},{3,1},{4,6},{5,7},{6,4},{7,5},{8,10},{9,11},{10,... | collective-permute-start | bytes 4325384 | tf_op jit(solution)/shard_map/ppermute | solution.py:610
  233.7 64.6 %collective-permute-start.34 = (bf16[256,2816]{1,0:T(8,128)(2,1)}, bf16[256,2816]{1,0:T(8,128)(2,1)}, u32[]{:S(2)}, u32[]{:S(2)}) collective-permute-start(bf16[256,2816]{1,0:T(8,128)(2,1)} %get-tuple-element.217), channel_id=1, source_target_pairs={{0,2},{1,3},{2,0},{3,1},{4,6},{5,7},{6,4},{7,5},{8,10},{9,11},{10,... | collective-permute-start | bytes 4325384 | tf_op jit(solution)/shard_map/ppermute | solution.py:610
  234.7 105.2 %collective-permute-start.40 = (bf16[704,1024]{1,0:T(8,128)(2,1)}, bf16[704,1024]{1,0:T(8,128)(2,1)}, u32[]{:S(2)}, u32[]{:S(2)}) collective-permute-start(bf16[704,1024]{1,0:T(8,128)(2,1)} %get-tuple-element.221), channel_id=1, source_target_pairs={{0,2},{1,3},{2,0},{3,1},{4,6},{5,7},{6,4},{7,5},{8,10},{9,11},{10,... | collective-permute-start | bytes 4325384 | tf_op jit(solution)/shard_map/ppermute | solution.py:610
  235.7 104.1 %collective-permute-start.43 = (bf16[256,1024]{1,0:T(8,128)(2,1)}, bf16[256,1024]{1,0:T(8,128)(2,1)}, u32[]{:S(2)}, u32[]{:S(2)}) collective-permute-start(bf16[256,1024]{1,0:T(8,128)(2,1)} %get-tuple-element.225), channel_id=1, source_target_pairs={{0,2},{1,3},{2,0},{3,1},{4,6},{5,7},{6,4},{7,5},{8,10},{9,11},{10,... | collective-permute-start | bytes 1572872 | tf_op jit(solution)/shard_map/ppermute | solution.py:610
  273.1 49.6 %all-to-all-start.4 = ((bf16[8,2,160,128]{3,2,1,0:T(8,128)(2,1)}), bf16[8,2,160,128]{3,2,1,0:T(8,128)(2,1)S(1)}, u32[]{:S(2)}, u32[]{:S(2)}) async-start(bf16[8,2,160,128]{3,2,1,0:T(8,128)(2,1)} %pad_maximum_fusion.8), calls=%async_computation.4 | async-start | bytes 1310720 | tf_op jit(solution)/shard_map/all_to_all | solution.py:709
  298.3 22.2 %collective-permute-start.36 = (bf16[128,2816]{1,0:T(8,128)(2,1)}, bf16[128,2816]{1,0:T(8,128)(2,1)}, u32[]{:S(2)}, u32[]{:S(2)}) collective-permute-start(bf16[128,2816]{1,0:T(8,128)(2,1)} %get-tuple-element.320), channel_id=1, source_target_pairs={{0,4},{4,0},{8,12},{12,8},{16,20},{20,16},{24,28},{28,24},{1,5},{5... | collective-permute-start | bytes 2162696 | tf_op jit(solution)/shard_map/ppermute | solution.py:610
  302.5 32.4 %collective-permute-start.41 = (bf16[128,2816]{1,0:T(8,128)(2,1)}, bf16[128,2816]{1,0:T(8,128)(2,1)}, u32[]{:S(2)}, u32[]{:S(2)}) collective-permute-start(bf16[128,2816]{1,0:T(8,128)(2,1)} %get-tuple-element.248), channel_id=1, source_target_pairs={{0,8},{4,12},{8,0},{12,4},{16,24},{20,28},{24,16},{28,20},{1,9},{5... | collective-permute-start | bytes 2162696 | tf_op jit(solution)/shard_map/ppermute | solution.py:610
  322.7 80.5 %all-to-all-start.3 = ((bf16[8,640,128]{2,1,0:T(8,128)(2,1)}), bf16[8,640,128]{2,1,0:T(8,128)(2,1)S(1)}, u32[]{:S(2)}, u32[]{:S(2)}) async-start(bf16[8,640,128]{2,1,0:T(8,128)(2,1)} %pad_maximum_fusion.1), calls=%async_computation.3 | async-start | bytes 2621440 | tf_op jit(solution)/shard_map/all_to_all | solution.py:709
  334.9 18.9 %collective-permute-start.39 = (bf16[64,2816]{1,0:T(8,128)(2,1)S(1)}, bf16[64,2816]{1,0:T(8,128)(2,1)S(1)}, u32[]{:S(2)}, u32[]{:S(2)}) collective-permute-start(bf16[64,2816]{1,0:T(8,128)(2,1)S(1)} %copy-done.29), channel_id=1, source_target_pairs={{0,8},{4,12},{8,0},{12,4},{16,24},{20,28},{24,16},{28,20},{1,9},{5... | collective-permute-start | bytes 1081352 | tf_op jit(solution)/shard_map/ppermute | solution.py:610
  338.3 21.5 %collective-permute-start.44 = (bf16[64,2816]{1,0:T(8,128)(2,1)S(1)}, bf16[64,2816]{1,0:T(8,128)(2,1)S(1)}, u32[]{:S(2)}, u32[]{:S(2)}) collective-permute-start(bf16[64,2816]{1,0:T(8,128)(2,1)S(1)} %get-tuple-element.252), channel_id=1, source_target_pairs={{0,4},{4,0},{8,12},{12,8},{16,20},{20,16},{24,28},{28,24},{1,5},{5... | collective-permute-start | bytes 1081352 | tf_op jit(solution)/shard_map/ppermute | solution.py:610
  344.1 34.0 %collective-permute-start.47 = (bf16[352,1024]{1,0:T(8,128)(2,1)}, bf16[352,1024]{1,0:T(8,128)(2,1)S(1)}, u32[]{:S(2)}, u32[]{:S(2)}) collective-permute-start(bf16[352,1024]{1,0:T(8,128)(2,1)} %get-tuple-element.253), channel_id=1, source_target_pairs={{0,4},{4,0},{8,12},{12,8},{16,20},{20,16},{24,28},{28,24},{1,5},{5... | collective-permute-start | bytes 2162696 | tf_op jit(solution)/shard_map/ppermute | solution.py:610
  353.9 18.6 %collective-permute-start.42 = (bf16[32,2816]{1,0:T(8,128)(2,1)S(1)}, bf16[32,2816]{1,0:T(8,128)(2,1)S(1)}, u32[]{:S(2)}, u32[]{:S(2)}) collective-permute-start(bf16[32,2816]{1,0:T(8,128)(2,1)S(1)} %add_convert_fusion.29), channel_id=1, source_target_pairs={{0,16},{4,20},{8,24},{12,28},{16,0},{20,4},{24,8},{28,12},{1,17},{... | collective-permute-start | bytes 540680 | tf_op jit(solution)/shard_map/ppermute | solution.py:610
  375.1 34.0 %collective-permute-start.35 = (bf16[256,3072]{1,0:T(8,128)(2,1)}, bf16[256,3072]{1,0:T(8,128)(2,1)}, u32[]{:S(2)}, u32[]{:S(2)}) collective-permute-start(bf16[256,3072]{1,0:T(8,128)(2,1)} %collective-permute-done.27.refs_9_), channel_id=1, source_target_pairs={{0,1},{1,0},{2,3},{3,2},{4,5},{5,4},{6,7},{7,6},{8,9},{9,8},{10,11... | collective-permute-start | bytes 4718600 | tf_op jit(solution)/shard_map/ppermute | solution.py:610
  375.1 28.1 %collective-permute-start.46 = (bf16[32,2816]{1,0:T(8,128)(2,1)}, bf16[32,2816]{1,0:T(8,128)(2,1)}, u32[]{:S(2)}, u32[]{:S(2)}) collective-permute-start(bf16[32,2816]{1,0:T(8,128)(2,1)} %add_convert_fusion.28), channel_id=1, source_target_pairs={{0,16},{4,20},{8,24},{12,28},{16,0},{20,4},{24,8},{28,12},{1,17},{... | collective-permute-start | bytes 540680 | tf_op jit(solution)/shard_map/ppermute | solution.py:610
  375.1 23.0 %collective-permute-start.54 = (bf16[32,2816]{1,0:T(8,128)(2,1)S(1)}, bf16[32,2816]{1,0:T(8,128)(2,1)S(1)}, u32[]{:S(2)}, u32[]{:S(2)}) collective-permute-start(bf16[32,2816]{1,0:T(8,128)(2,1)S(1)} %add_convert_fusion.25), channel_id=1, source_target_pairs={{0,16},{4,20},{8,24},{12,28},{16,0},{20,4},{24,8},{28,12},{1,17},{... | collective-permute-start | bytes 540680 | tf_op jit(solution)/shard_map/ppermute | solution.py:610
  378.1 24.2 %collective-permute-start.45 = (bf16[1,256,384]{2,1,0:T(8,128)(2,1)S(1)}, bf16[1,256,384]{2,1,0:T(8,128)(2,1)S(1)}, u32[]{:S(2)}, u32[]{:S(2)}) collective-permute-start(bf16[1,256,384]{2,1,0:T(8,128)(2,1)S(1)} %fusion.12), channel_id=1, source_target_pairs={{0,16},{4,20},{8,24},{12,28},{16,0},{20,4},{24,8},{28,12},{1,17},{... | collective-permute-start | bytes 589832 | tf_op jit(solution)/shard_map/ppermute | solution.py:610
  380.3 22.2 %collective-permute-start.52 = (bf16[176,1024]{1,0:T(8,128)(2,1)S(1)}, bf16[176,1024]{1,0:T(8,128)(2,1)S(1)}, u32[]{:S(2)}, u32[]{:S(2)}) collective-permute-start(bf16[176,1024]{1,0:T(8,128)(2,1)S(1)} %get-tuple-element.263), channel_id=1, source_target_pairs={{0,8},{4,12},{8,0},{12,4},{16,24},{20,28},{24,16},{28,20},{1,9},{5... | collective-permute-start | bytes 1081352 | tf_op jit(solution)/shard_map/ppermute | solution.py:610
  404.3 20.7 %collective-permute-start.51 = (bf16[64,2816]{1,0:T(8,128)(2,1)S(1)}, bf16[64,2816]{1,0:T(8,128)(2,1)}, u32[]{:S(2)}, u32[]{:S(2)}) collective-permute-start(bf16[64,2816]{1,0:T(8,128)(2,1)S(1)} %pad_maximum_fusion.11), channel_id=1, source_target_pairs={{0,8},{4,12},{8,0},{12,4},{16,24},{20,28},{24,16},{28,20},{1,9},{5... | collective-permute-start | bytes 1081352 | tf_op jit(solution)/shard_map/ppermute | solution.py:610
  404.3 24.0 %collective-permute-start.50 = (bf16[2,256,384]{2,1,0:T(8,128)(2,1)S(1)}, bf16[2,256,384]{2,1,0:T(8,128)(2,1)S(1)}, u32[]{:S(2)}, u32[]{:S(2)}) collective-permute-start(bf16[2,256,384]{2,1,0:T(8,128)(2,1)S(1)} %pad_maximum_fusion.10), channel_id=1, source_target_pairs={{0,8},{4,12},{8,0},{12,4},{16,24},{20,28},{24,16},{28,20},{1,9},{5... | collective-permute-start | bytes 1179656 | tf_op jit(solution)/shard_map/ppermute | solution.py:610
  409.1 20.7 %collective-permute-start.59 = (bf16[88,1024]{1,0:T(8,128)(2,1)S(1)}, bf16[88,1024]{1,0:T(8,128)(2,1)S(1)}, u32[]{:S(2)}, u32[]{:S(2)}) collective-permute-start(bf16[88,1024]{1,0:T(8,128)(2,1)S(1)} %copy-done.34), channel_id=1, source_target_pairs={{0,16},{4,20},{8,24},{12,28},{16,0},{20,4},{24,8},{28,12},{1,17},{... | collective-permute-start | bytes 540680 | tf_op jit(solution)/shard_map/ppermute | solution.py:610
  445.0 28.8 %collective-permute-start.63 = (bf16[128,2816]{1,0:T(8,128)(2,1)S(1)}, bf16[128,2816]{1,0:T(8,128)(2,1)S(1)}, u32[]{:S(2)}, u32[]{:S(2)}) collective-permute-start(bf16[128,2816]{1,0:T(8,128)(2,1)S(1)} %pad_maximum_fusion.4), channel_id=1, source_target_pairs={{0,4},{4,0},{8,12},{12,8},{16,20},{20,16},{24,28},{28,24},{1,5},{5... | collective-permute-start | bytes 2162696 | tf_op jit(solution)/shard_map/ppermute | solution.py:610
  446.1 30.4 %collective-permute-start.64 = (bf16[128,2816]{1,0:T(8,128)(2,1)S(1)}, bf16[128,2816]{1,0:T(8,128)(2,1)S(1)}, u32[]{:S(2)}, u32[]{:S(2)}) collective-permute-start(bf16[128,2816]{1,0:T(8,128)(2,1)S(1)} %pad_maximum_fusion.5), channel_id=1, source_target_pairs={{0,8},{4,12},{8,0},{12,4},{16,24},{20,28},{24,16},{28,20},{1,9},{5... | collective-permute-start | bytes 2162696 | tf_op jit(solution)/shard_map/ppermute | solution.py:610
  448.1 32.9 %collective-permute-start.55 = (bf16[4,256,384]{2,1,0:T(8,128)(2,1)S(1)}, bf16[4,256,384]{2,1,0:T(8,128)(2,1)S(1)}, u32[]{:S(2)}, u32[]{:S(2)}) collective-permute-start(bf16[4,256,384]{2,1,0:T(8,128)(2,1)S(1)} %pad_maximum_fusion.3), channel_id=1, source_target_pairs={{0,4},{4,0},{8,12},{12,8},{16,20},{20,16},{24,28},{28,24},{1,5},{5... | collective-permute-start | bytes 2359304 | tf_op jit(solution)/shard_map/ppermute | solution.py:610
  449.0 23.2 %collective-permute-start.65 = (bf16[176,1024]{1,0:T(8,128)(2,1)S(1)}, bf16[176,1024]{1,0:T(8,128)(2,1)S(1)}, u32[]{:S(2)}, u32[]{:S(2)}) collective-permute-start(bf16[176,1024]{1,0:T(8,128)(2,1)S(1)} %pad_maximum_fusion.13), channel_id=1, source_target_pairs={{0,8},{4,12},{8,0},{12,4},{16,24},{20,28},{24,16},{28,20},{1,9},{5... | collective-permute-start | bytes 1081352 | tf_op jit(solution)/shard_map/ppermute | solution.py:610
  473.2 19.6 %collective-permute-start.66 = (bf16[352,1024]{1,0:T(8,128)(2,1)}, bf16[352,1024]{1,0:T(8,128)(2,1)}, u32[]{:S(2)}, u32[]{:S(2)}) collective-permute-start(bf16[352,1024]{1,0:T(8,128)(2,1)} %pad_maximum_fusion.6), channel_id=1, source_target_pairs={{0,4},{4,0},{8,12},{12,8},{16,20},{20,16},{24,28},{28,24},{1,5},{5... | collective-permute-start | bytes 2162696 | tf_op jit(solution)/shard_map/ppermute | solution.py:610
  (68 other events, 630.5 us)

commit v3 on v2

--- a/solution.py
+++ b/solution.py
@@ -65,58 +65,76 @@
     return (high.astype(f32), middle.astype(f32), low.astype(f32))
 
 
-def project_kernel(heads, fresh, *refs):
-    x_ref, gain_ref, w_ref, qt_ref, kt_ref = refs[1:6]
-    qa_ref, ka_ref, va_ref, h1_ref = refs[6:] if fresh else refs[10:]
+def project_kernel(heads, segments, layout, aliased, *refs):
+    w_rows, x_ref = refs[1:3]
+    arrays = 1 + max(array for array, _ in layout)
+    w_refs = refs[3 : 3 + arrays]
+    code_ref = refs[3 + arrays]
+    qa_ref, ka_ref, va_ref, h1_ref, gain_row = refs[4 + arrays + aliased :]
+    piece_rows = w_refs[0].shape[1]
+    spans = []
+    for piece, (array, index) in enumerate(layout):
+        at = pl.ds(pl.multiple_of(w_rows[piece] * piece_rows, piece_rows), piece_rows)
+        spans.append(at)
+        columns = w_refs[array][index, :, 3 * LANES :].astype(f32)
+        gain_row[:, at] = columns.T[0:8, :]
     x = x_ref[...].astype(f32)
     scaling = lax.rsqrt(jnp.mean(x * x, axis=-1, keepdims=True) + EPSILON)
-    h1 = (x * scaling * gain_ref[...].astype(f32)).astype(bf16)
-    h1_ref[...] = h1
-    qkv = mm(h1, w_ref[...])
+    h1_ref[...] = (x * scaling * gain_row[0:1, :]).astype(bf16)
+    qkv = None
+    for at, (array, index) in zip(spans, layout):
+        part = mm(h1_ref[:, at], w_refs[array][index, :, : 3 * LANES])
+        qkv = part if qkv is None else qkv + part
     rows = x.shape[0]
     lane = lane_ids(rows)
     q = qkv[:, :LANES].astype(bf16) * jnp.asarray(HD**-0.5, bf16)
     k = qkv[:, LANES : 2 * LANES].astype(bf16)
     v = qkv[:, 2 * LANES :].astype(bf16)
-    ones = jnp.where(lane % HD < 3, 1.0, 0.0).astype(bf16)
+    place = lane % HD
+    code = code_ref[...]
+    same = place == code // 2
+    padded = code % 2 == 0
+    q_table = jnp.where(same | ((place == HD - 1) & padded), 1.0, 0.0).astype(bf16)
+    k_table = jnp.where(
+        place < segments,
+        jnp.where(same & ~padded, 0.0, BLOCKED),
+        jnp.where((place >= HD - 4) & (place < HD - 1), 1.0, 0.0),
+    ).astype(bf16)
+    ones = jnp.where(place < 3, 1.0, 0.0).astype(bf16)
     for head in range(heads):
         own = lane // HD == head
-        qa_ref[head] = jnp.where(own, q, qt_ref[...])
-        ka_ref[head] = jnp.where(own, k, kt_ref[...])
+        qa_ref[head] = jnp.where(own, q, q_table)
+        ka_ref[head] = jnp.where(own, k, k_table)
         va_ref[head] = jnp.where(own, v, ones)
 
 
-def project(slot, slots, heads, x, gain, w, q_table, k_table, previous):
+def project(slot, w_rows, slots, heads, segments, x, layout, arrays, codes, previous):
     rows, width = x.shape
     total = rows * slots
-    row_spec = pl.BlockSpec((rows, LANES), lambda i, s: (s[0], 0))
-    head_spec = pl.BlockSpec((heads, rows, LANES), lambda i, s: (0, s[0], 0))
+    head_spec = pl.BlockSpec((heads, rows, LANES), lambda i, s, w: (0, s[0], 0))
     shapes = [jax.ShapeDtypeStruct((heads, total, LANES), bf16)] * 3 + [
         jax.ShapeDtypeStruct((total, width), bf16)
     ]
-    fresh = previous is None
-    extra = () if fresh else tuple(previous)
+    extra = () if previous is None else tuple(previous)
+    first = 4 + len(arrays)
     return pl.pallas_call(
-        functools.partial(project_kernel, heads, fresh),
+        functools.partial(project_kernel, heads, segments, layout, len(extra)),
         grid_spec=pltpu.PrefetchScalarGridSpec(
-            num_scalar_prefetch=1,
+            num_scalar_prefetch=2,
             grid=(1,),
-            in_specs=[
-                pl.BlockSpec((rows, width), lambda i, s: (0, 0)),
-                pl.BlockSpec((1, width), lambda i, s: (0, 0)),
-                pl.BlockSpec(w.shape, lambda i, s: (0, 0)),
-                row_spec,
-                row_spec,
-            ]
+            in_specs=[pl.BlockSpec((rows, width), lambda i, s, w: (0, 0))]
+            + [pl.BlockSpec(a.shape, lambda i, s, w: (0, 0, 0)) for a in arrays]
+            + [pl.BlockSpec((rows, 1), lambda i, s, w: (s[0], 0))]
             + [anywhere()] * len(extra),
-            out_specs=[head_spec] * 3 + [pl.BlockSpec((rows, width), lambda i, s: (s[0], 0))],
+            out_specs=[head_spec] * 3 + [pl.BlockSpec((rows, width), lambda i, s, w: (s[0], 0))],
+            scratch_shapes=[pltpu.VMEM((8, width), f32)],
         ),
         out_shape=shapes,
-        input_output_aliases={} if fresh else {6 + i: i for i in range(4)},
+        input_output_aliases={first + i: i for i in range(len(extra))},
         compiler_params=params(),
-        cost_estimate=cost(2 * rows * width * 3 * LANES, 4 * rows * width + 2 * w.size),
+        cost_estimate=cost(2 * rows * width * 3 * LANES, 4 * rows * width + 8 * LANES * width),
         name="project",
-    )(slot, x, gain, w, q_table, k_table, *extra)
+    )(slot, w_rows, x, *arrays, codes, *extra)
 
 
 def forward_kernel(heads, q_ref, k_near, v_near, k_ref, v_ref, att_ref, sum_ref, qb_ref):
@@ -384,69 +402,107 @@
     )(w_rows, h1.reshape(slots, len(kvs), rows, width), dq, *kvs)
 
 
-def middle_kernel(parts, pieces, halves, step_width, layout, *refs):
+def load_rows(entries, sources, targets, sems, rows_of):
+    started = [[] for _ in targets]
+    for number, (target, source, index, place, step_rows, offset, column) in enumerate(entries):
+        begin = pl.multiple_of(rows_of[index][place] * step_rows + offset, 16)
+        at = pl.ds(begin, sources[source].shape[0])
+        width = targets[target].shape[1]
+        copy = pltpu.make_async_copy(
+            sources[source].at[:, column : column + width],
+            targets[target].at[at, :],
+            sems.at[number],
+        )
+        copy.start()
+        started[target].append(copy)
+    return started
+
+
+def store_rows(source, targets, sems, index, columns, shift=0):
+    moved = columns if shift == 0 else pl.ds(shift + columns.start, columns.size)
+    copies = []
+    halves = len(targets)
+    for piece in range(halves * targets[0].shape[0]):
+        step_rows = targets[0].shape[1]
+        at = pl.ds(pl.multiple_of(index[piece] * step_rows, step_rows), step_rows)
+        target = targets[piece % halves].at[piece // halves, :, moved]
+        copies.append(pltpu.make_async_copy(source.at[at, columns], target, sems.at[piece]))
+    return copies
+
+
+def pre_kernel(parts, entries, *refs):
     w_rows = refs[0]
     att_refs = refs[1 : 1 + parts]
-    x_ref, c_ref, gain_ref = refs[1 + parts : 4 + parts]
-    refs = refs[4 + parts :]
-    sources, refs = refs[: len(layout)], refs[len(layout) :]
-    out_ref, dmid_ref, da_ref = refs[:3]
-    refs = refs[3:]
-    og_refs, gg_refs, ug_refs, dg_refs = [refs[i * halves : (i + 1) * halves] for i in range(4)]
-    refs = refs[4 * halves :]
-    wo, wg, wu, wd, og, gg, ug, dg, att, h2_ref, h2t_ref, mid_ref, acc_out, acc_back = refs[:14]
-    in_sems, out_sems = refs[14:]
-
-    loads = [[], [], [], []]
-    targets = (wo, wg, wu, wd)
-    for place, (number, piece, offset) in enumerate(layout):
-        target = targets[number]
-        step_rows = target.shape[0] // pieces
-        begin = pl.multiple_of(w_rows[piece] * step_rows + offset, 16)
-        at = pl.ds(begin, sources[place].shape[0])
-        copy = pltpu.make_async_copy(sources[place], target.at[at, :], in_sems.at[place])
-        copy.start()
-        loads[number].append(copy)
-
+    x_ref, gain_ref = refs[1 + parts : 3 + parts]
+    sources = refs[3 + parts : -5]
+    mid_ref, h2_ref, att_ref, wo, sems = refs[-5:]
+    loads = load_rows(entries, sources, (wo,), sems, (w_rows,))
     rows, width = x_ref.shape
-    blocks = da_ref.shape[0]
+    blocks = att_refs[0].shape[0]
     block_width = width // blocks
     part_rows = rows // parts
     for part in range(parts):
         for block in range(blocks):
-            att[
+            att_ref[
                 part * part_rows : (part + 1) * part_rows,
                 block * block_width : (block + 1) * block_width,
             ] = att_refs[part][block][:, :block_width]
     for copy in loads[0]:
         copy.wait()
-    gain = gain_ref[...].astype(f32)
-    middle = x_ref[...].astype(f32) + mm(att[...], wo[...])
+    middle = x_ref[...].astype(f32) + mm(att_ref[...], wo[...])
     scaling = lax.rsqrt(jnp.mean(middle * middle, axis=-1, keepdims=True) + EPSILON)
-    h2 = (middle * scaling * gain).astype(bf16)
-    h2_ref[...] = h2
-    h2t_ref[...] = h2.T
+    h2_ref[...] = (middle * scaling * gain_ref[...].astype(f32)).astype(bf16)
     mid_ref[...] = middle
+
+
+def pre_stage(w_rows, att_parts, x, gain, entries, sources):
+    rows, width = x.shape
+    hbm = pl.BlockSpec(memory_space=pltpu.HBM)
+    return pl.pallas_call(
+        functools.partial(pre_kernel, len(att_parts), entries),
+        in_specs=[smem()] + [vmem()] * (len(att_parts) + 2) + [hbm] * len(sources),
+        out_specs=[vmem()] * 3,
+        out_shape=[
+            jax.ShapeDtypeStruct((rows, width), f32),
+            jax.ShapeDtypeStruct((rows, width), bf16),
+            jax.ShapeDtypeStruct((rows, width), bf16),
+        ],
+        scratch_shapes=[
+            pltpu.VMEM((width, width), bf16),
+            pltpu.SemaphoreType.DMA((len(entries),)),
+        ],
+        compiler_params=params(),
+        cost_estimate=cost(2 * rows * width * width, 2 * width * width),
+        name="pre_stage",
+    )(w_rows, *att_parts, x, gain, *sources)
+
+
+def main_kernel(groups, halves, entries, count, *refs):
+    w_rows, d_rows = refs[:2]
+    h2_refs, c_refs = refs[2 : 2 + groups], refs[2 + groups : 2 + 2 * groups]
+    refs = refs[2 + 2 * groups :]
+    sources, refs = refs[:count], refs[count:]
+    out_refs, back_refs = refs[:groups], refs[groups : 2 * groups]
+    refs = refs[2 * groups :]
+    gu_refs, dg_refs = refs[:halves], refs[halves : 2 * halves]
+    refs = refs[2 * halves :]
+    wg, wu, wd, gg, ug, dg, h2_all, h2t, c_all, acc_out, acc_back, in_sems, out_sems = refs
+    loads = load_rows(entries, sources, (wg, wu, wd), in_sems, (w_rows, d_rows))
+    rows = h2_refs[0].shape[0]
+    for group in range(groups):
+        span = slice(group * rows, (group + 1) * rows)
+        h2_all[span, :] = h2_refs[group][...]
+        c_all[span, :] = c_refs[group][...]
+    h2t[...] = h2_all[...].T
     acc_out[...] = jnp.zeros_like(acc_out)
     acc_back[...] = jnp.zeros_like(acc_back)
-    for copy in loads[1] + loads[2] + loads[3]:
-        copy.wait()
-
-    def row_copies(number, source, targets, columns):
-        step_rows = source.shape[0] // pieces
-        copies = []
-        for piece in range(pieces):
-            at = pl.ds(pl.multiple_of(w_rows[piece] * step_rows, step_rows), step_rows)
-            target = targets[piece % halves].at[piece // halves, :, columns]
-            copies.append(
-                pltpu.make_async_copy(source.at[at, columns], target, out_sems.at[number, piece])
-            )
-        return copies
-
-    def column_step(number, carry):
-        at = pl.ds(pl.multiple_of(number * step_width, step_width), step_width)
-        h2 = h2_ref[...]
-        c = c_ref[...]
+    for started in loads:
+        for copy in started:
+            copy.wait()
+
+    def columns_at(at):
+        h2 = h2_all[...]
+        c = c_all[...]
         gate = mm(h2, wg[:, at])
         up = mm(h2, wu[:, at])
         act_grad = mm_nt(c, wd[at, :])
@@ -460,26 +516,89 @@
         act = (curve * up).astype(bf16)
         d_up = (act_grad * curve).astype(bf16)
         d_gate = (act_grad * up * slope).astype(bf16)
+        acc_back[...] += mm_nt(d_gate, wg[:, at]) + mm_nt(d_up, wu[:, at])
+        gg[:, at] = mm(h2t[...], d_gate).astype(bf16)
+        ug[:, at] = mm(h2t[...], d_up).astype(bf16)
+        dg[at, :] = mm_tn(act, c).astype(bf16)
         acc_out[...] += mm(act, wd[at, :])
-        dg[at, :] = mm_tn(act, c).astype(bf16)
-        gg[:, at] = mm(h2t_ref[...], d_gate).astype(bf16)
-        ug[:, at] = mm(h2t_ref[...], d_up).astype(bf16)
-        acc_back[...] += mm_nt(d_gate, wg[:, at]) + mm_nt(d_up, wu[:, at])
-        for kind, source, targets in ((1, gg, gg_refs), (2, ug, ug_refs)):
-            for copy in row_copies(kind, source, targets, at):
+        for kind, source in ((0, gg), (1, ug)):
+            for copy in store_rows(source, gu_refs, out_sems.at[kind], w_rows, at, kind * width):
                 copy.start()
+
+    width = wg.shape[1]
+    step_width = 256
+    whole = width // step_width
+
+    def column_step(number, carry):
+        columns_at(pl.ds(pl.multiple_of(number * step_width, step_width), step_width))
         return carry
 
-    lax.fori_loop(0, wg.shape[1] // step_width, column_step, 0)
-
+    lax.fori_loop(0, whole, column_step, 0)
+    if width % step_width:
+        columns_at(pl.ds(whole * step_width, width % step_width))
     everything = slice(None)
-    stores = row_copies(3, dg, dg_refs, everything)
+    stores = store_rows(dg, dg_refs, out_sems.at[2], d_rows, everything)
     for copy in stores:
         copy.start()
+    for group in range(groups):
+        span = slice(group * rows, (group + 1) * rows)
+        kind = out_refs[group].dtype
+        out_refs[group][...] = acc_out[span, :].astype(kind)
+        back_refs[group][...] = acc_back[span, :].astype(kind)
+    whole = pl.ds(0, width)
+    stores += store_rows(gg, gu_refs, out_sems.at[0], w_rows, whole)
+    stores += store_rows(ug, gu_refs, out_sems.at[1], w_rows, whole, width)
+    for copy in stores:
+        copy.wait()
+
+
+def main_stage(w_rows, d_rows, h2s, cs, hidden, entries, sources, halves):
+    groups = len(h2s)
+    rows, width = h2s[0].shape
+    pieces, d_pieces = w_rows.shape[0], d_rows.shape[0]
+    hbm = pl.BlockSpec(memory_space=pltpu.HBM)
+    partial = [jax.ShapeDtypeStruct((rows, width), f32 if g == 0 else bf16) for g in range(groups)]
+    up_shape = jax.ShapeDtypeStruct((pieces // halves, width // pieces, 2 * hidden), bf16)
+    down_shape = jax.ShapeDtypeStruct((d_pieces // halves, hidden // d_pieces, width), bf16)
+    total = groups * rows
+    out = pl.pallas_call(
+        functools.partial(main_kernel, groups, halves, entries, len(sources)),
+        in_specs=[smem(), smem()] + [vmem()] * (2 * groups) + [hbm] * len(sources),
+        out_specs=[vmem()] * (2 * groups) + [hbm] * (2 * halves),
+        out_shape=partial * 2 + [up_shape] * halves + [down_shape] * halves,
+        scratch_shapes=[
+            pltpu.VMEM((width, hidden), bf16),
+            pltpu.VMEM((width, hidden), bf16),
+            pltpu.VMEM((hidden, width), bf16),
+            pltpu.VMEM((width, hidden), bf16),
+            pltpu.VMEM((width, hidden), bf16),
+            pltpu.VMEM((hidden, width), bf16),
+            pltpu.VMEM((total, width), bf16),
+            pltpu.VMEM((width, total), bf16),
+            pltpu.VMEM((total, width), bf16),
+            pltpu.VMEM((total, width), f32),
+            pltpu.VMEM((total, width), f32),
+            pltpu.SemaphoreType.DMA((len(entries),)),
+            pltpu.SemaphoreType.DMA((3, max(pieces, d_pieces))),
+        ],
+        compiler_params=params(),
+        cost_estimate=cost(18 * total * width * hidden, 12 * width * hidden),
+        name="main_stage",
+    )(w_rows, d_rows, *h2s, *cs, *sources)
+    outs, backs, grads = list(out[:groups]), list(out[groups : 2 * groups]), out[2 * groups :]
+    return (outs, backs, grads[:halves], grads[halves:])
+
+
+def post_kernel(groups, entries, count, *refs):
+    w_rows, mid_ref = refs[:2]
+    backs, refs = refs[2 : 2 + groups], refs[2 + groups :]
+    c_ref, gain_ref = refs[:2]
+    sources, refs = refs[2 : 2 + count], refs[2 + count :]
+    dmid_ref, branch_ref, da_ref, wo, in_sems = refs
+    loads = load_rows(entries, sources, (wo,), in_sems, (w_rows,))
     middle = mid_ref[...]
     scaling = lax.rsqrt(jnp.mean(middle * middle, axis=-1, keepdims=True) + EPSILON)
-    out_ref[...] = (middle + acc_out[...]).astype(bf16)
-    incoming = acc_back[...] * gain
+    incoming = sum(ref[...].astype(f32) for ref in backs) * gain_ref[...].astype(f32)
     centre = jnp.mean(incoming * middle, axis=-1, keepdims=True)
     d_middle = (
         c_ref[...].astype(f32)
@@ -488,69 +607,67 @@
     )
     dmid_ref[...] = d_middle
     branch = d_middle.astype(bf16)
-    og[...] = mm_tn(att[...], branch).astype(bf16)
-    last_stores = row_copies(0, og, og_refs, everything)
-    for copy in last_stores:
-        copy.start()
+    branch_ref[...] = branch
+    for copy in loads[0]:
+        copy.wait()
     d_att = mm_nt(branch, wo[...]).astype(bf16)
+    blocks = da_ref.shape[0]
+    block_width = d_att.shape[1] // blocks
     for block in range(blocks):
         piece = d_att[:, block * block_width : (block + 1) * block_width]
         if block_width < LANES:
             piece = jnp.concatenate([piece] * (LANES // block_width), axis=1)
         da_ref[block] = piece
-    stores += row_copies(1, gg, gg_refs, everything) + row_copies(2, ug, ug_refs, everything)
-    for copy in stores + last_stores:
-        copy.wait()
-
-
-def middle_stage(w_rows, att_parts, x, c, gain, wo, wg, wu, wd, pieces, halves):
-    parts = len(att_parts)
-    rows, width = x.shape
-    hidden = wg[0][2].shape[1]
-    layout = [
-        (number, piece, offset)
-        for number, entries in enumerate((wo, wg, wu, wd))
-        for piece, offset, _ in entries
-    ]
-    weights = [w for entries in (wo, wg, wu, wd) for _, _, w in entries]
-    slots = att_parts[0].shape[0]
-    step_width = 256
-    full = [(width, width), (width, hidden), (width, hidden), (hidden, width)]
-    piece_shapes = [(a // pieces, b) for a, b in full]
-    out_shape = [
-        jax.ShapeDtypeStruct((rows, width), bf16),
-        jax.ShapeDtypeStruct((rows, width), f32),
-        jax.ShapeDtypeStruct((slots, rows, LANES), bf16),
-    ] + [
-        jax.ShapeDtypeStruct((pieces // halves,) + s, bf16)
-        for s in piece_shapes
-        for _ in range(halves)
-    ]
+
+
+def post_stage(w_rows, middle, backs, c, gain, slots, entries, sources):
+    groups = len(backs)
+    rows, width = middle.shape
     hbm = pl.BlockSpec(memory_space=pltpu.HBM)
-    out = pl.pallas_call(
-        functools.partial(middle_kernel, parts, pieces, halves, step_width, layout),
-        in_specs=[smem()] + [vmem()] * (parts + 3) + [hbm] * len(weights),
-        out_specs=[vmem()] * 3 + [hbm] * (4 * halves),
-        out_shape=out_shape,
-        scratch_shapes=[pltpu.VMEM(s, bf16) for s in full]
-        + [pltpu.VMEM(s, bf16) for s in full]
-        + [
-            pltpu.VMEM((rows, width), bf16),
-            pltpu.VMEM((rows, width), bf16),
-            pltpu.VMEM((width, rows), bf16),
-            pltpu.VMEM((rows, width), f32),
-            pltpu.VMEM((rows, width), f32),
-            pltpu.VMEM((rows, width), f32),
-            pltpu.SemaphoreType.DMA((len(layout),)),
-            pltpu.SemaphoreType.DMA((4, pieces)),
+    return pl.pallas_call(
+        functools.partial(post_kernel, groups, entries, len(sources)),
+        in_specs=[smem()] + [vmem()] * (3 + groups) + [hbm] * len(sources),
+        out_specs=[vmem()] * 3,
+        out_shape=[
+            jax.ShapeDtypeStruct((rows, width), f32),
+            jax.ShapeDtypeStruct((rows, width), bf16),
+            jax.ShapeDtypeStruct((slots, rows, LANES), bf16),
+        ],
+        scratch_shapes=[
+            pltpu.VMEM((width, width), bf16),
+            pltpu.SemaphoreType.DMA((len(entries),)),
         ],
         compiler_params=params(),
-        cost_estimate=cost(
-            2 * rows * width * (9 * hidden + 3 * width), 4 * (width * width + 3 * width * hidden)
-        ),
-        name="middle_stage",
-    )(w_rows, *att_parts, x, c, gain, *weights)
-    return (out[:3], [out[3 + i * halves : 3 + (i + 1) * halves] for i in range(4)])
+        cost_estimate=cost(2 * rows * width * width, 4 * width * width),
+        name="post_stage",
+    )(w_rows, middle, *backs, c, gain, *sources)
+
+
+def out_kernel(halves, w_rows, att_ref, branch_ref, *refs):
+    og, sems = refs[halves:]
+    og[...] = mm_tn(att_ref[...], branch_ref[...]).astype(bf16)
+    stores = store_rows(og, refs[:halves], sems, w_rows, slice(None))
+    for copy in stores:
+        copy.start()
+    for copy in stores:
+        copy.wait()
+
+
+def out_terms(w_rows, att, branch, halves):
+    rows, width = att.shape
+    pieces = w_rows.shape[0]
+    hbm = pl.BlockSpec(memory_space=pltpu.HBM)
+    shape = jax.ShapeDtypeStruct((pieces // halves, width // pieces, width), bf16)
+    return pl.pallas_call(
+        functools.partial(out_kernel, halves),
+        in_specs=[smem(), vmem(), vmem()],
+        out_specs=[hbm] * halves,
+        out_shape=[shape] * halves,
+        scratch_shapes=[pltpu.VMEM((width, width), bf16), pltpu.SemaphoreType.DMA((pieces,))],
+        compiler_params=params(),
+        cost_estimate=cost(2 * rows * width * width, 4 * width * width),
+        name="out_terms",
+    )(w_rows, att, branch)
 
 
 def last_kernel(parts, pieces, *refs):
@@ -605,6 +722,37 @@
     )(w_rows, dq, *kvs, x, d_middle, gain, *weights)
 
 
+def finish_kernel(mine_ref, own_ref, other_ref, w_ref, gain_ref, *outs):
+    width = outs[0].shape[1]
+    mine = mine_ref[0]
+    for source, bit in ((own_ref, mine), (other_ref, 1 - mine)):
+        for index in range(4):
+            slot = (index % 2) * 4 + bit * 2 + index // 2
+            at = pl.ds(pl.multiple_of(slot * LANES, LANES), LANES)
+            for kind in range(3):
+                outs[kind][:, at] = source[index, :, kind * LANES : (kind + 1) * LANES].astype(f32)
+    total = None
+    for kind in range(3):
+        weight = w_ref[:, kind * width : (kind + 1) * width].astype(f32)
+        part = jnp.sum(outs[kind][...] * weight, axis=-1, keepdims=True)
+        total = part if total is None else total + part
+    outs[3][...] = total / gain_ref[...].astype(f32)
+
+
+def finish_own(mine, own, other, weights, gain):
+    rows, width = own.shape[1], weights.shape[1] // 3
+    return pl.pallas_call(
+        finish_kernel,
+        in_specs=[smem()] + [vmem()] * 4,
+        out_specs=[vmem()] * 4,
+        out_shape=[jax.ShapeDtypeStruct((rows, width), f32)] * 3
+        + [jax.ShapeDtypeStruct((rows, 1), f32)],
+        compiler_params=params(),
+        cost_estimate=cost(6 * rows * width, 20 * rows * width),
+        name="finish_own",
+    )(mine, own, other, weights, gain)
+
+
 def flip(values, axis, delta):
     count = lax.axis_size(axis)
     return lax.ppermute(values, axis, [(i, i ^ delta) for i in range(count)])
@@ -623,7 +771,7 @@
 
 
 def cut(values, start, size):
-    return lax.dynamic_slice_in_dim(values, start, size, axis=0)
+    return lax.dynamic_slice_in_dim(values, start, size, axis=-2)
 
 
 class Line:
@@ -639,19 +787,22 @@
 
 class Reduction:
     def __init__(self, kept, given, line):
-        self.kept, self.given, self.line = kept, given, line
+        self.own, self.given, self.line, self.joined = kept, given, line, None
 
     def core(self):
-        arrived = flip(self.given, "fsdp", 1)
-        self.own = add_low(self.kept[0], arrived[0])
-        self.send = add_low(self.kept[1], arrived[1])
+        self.arrived = flip(self.line.hold(self.given), "fsdp", 1)
+
+    def hold(self, *others):
+        self.arrived = lax.optimization_barrier((self.arrived, *others))[0]
 
     def across(self):
-        self.arrived = flip(self.send, "fsdp", 2)
+        given = self.line.hold(add_low(self.own[1], self.arrived[1]))
+        self.own = add_low(self.own[0], self.arrived[0])
+        self.arrived = flip(given, "fsdp", 2)
 
     def halve(self, bit):
         place = lax.axis_index("seq")
-        half = self.own.shape[0] // 2
+        half = self.own.shape[-2] // 2
         mine = (place // bit) % 2
         keep, give = mine * half, (1 - mine) * half
         given = add_low(cut(self.own, give, half), cut(self.arrived, give, half))
@@ -660,7 +811,20 @@
 
     def settle(self):
         self.own = add_low(self.own, self.arrived)
-        self.joined = None
+
+    def swap_columns(self):
+        self.settle()
+        self.arrived = flip(self.line.hold(self.own[1]), "fsdp", 2)
+
+    def join_columns(self):
+        upper = (lax.axis_index("fsdp") // 2) == 1
+        width = self.arrived.shape[-1] // 2
+        parts = []
+        for kind in range(2):
+            here = self.own[0, :, kind * width : (kind + 1) * width]
+            there = self.arrived[:, kind * width : (kind + 1) * width]
+            parts += [jnp.where(upper, there, here), jnp.where(upper, here, there)]
+        self.own = jnp.concatenate(parts, axis=-1)
 
     def widen(self, bit):
         self.join()
@@ -676,27 +840,15 @@
         self.own, self.joined = jnp.concatenate([first, second], axis=0), None
 
 
-def mask_tables(lengths_row, order_row, real_row):
+def token_codes(lengths_row, order_row, real_row):
     total = order_row.shape[0]
-    segments = lengths_row.shape[0]
     ends_at = jnp.cumsum(lengths_row)
     positions = jnp.arange(total, dtype=jnp.int32)
     packed_segment = jnp.sum((positions[:, None] >= ends_at[None, :]).astype(jnp.int32), axis=1)
     packed_code = packed_segment * 2 + (real_row > 0).astype(jnp.int32)
-    code = jnp.sum(
+    return jnp.sum(
         jnp.where(positions[:, None] == order_row[None, :], packed_code[None, :], 0), axis=1
     ).reshape(total, 1)
-    segment, real = code // 2, code % 2
-    lane = jnp.arange(LANES, dtype=jnp.int32)[None, :] % HD
-    same = lane == segment
-    q_table = jnp.where(same | ((lane == HD - 1) & (real == 0)), 1.0, 0.0).astype(bf16)
-    open_to = same & (real == 1)
-    k_table = jnp.where(
-        lane < segments,
-        jnp.where(open_to, 0.0, BLOCKED),
-        jnp.where((lane >= HD - 4) & (lane < HD - 1), 1.0, 0.0),
-    ).astype(bf16)
-    return (q_table, k_table)
 
 
 def move_chain(array, pairs):
@@ -747,73 +899,97 @@
         axis=1,
     )
     qkv_weight = jnp.concatenate([query_weight, key_weight, value_weight], axis=1)
-    q_table, k_table = mask_tables(lengths[0], token_order[0], real_token[0])
 
     if direct:
         w_rows = shard ^ jnp.arange(shards, dtype=jnp.int32)
         place = seq // 2
         half = shard_rows // 2
+        hidden = gate_weight.shape[1] // 2
         columns_x = flip(own_columns, "fsdp", 2)
         beside = flip(x, "seq", 1)
-        right_1 = move_chain(x, [(1, 0), (2, 1), (3, 2)])
-        left_1 = move_chain(x, [(0, 1), (1, 2), (2, 3)])
+        near = move_chain(x, [(0, 1), (1, 0), (2, 3), (3, 2)])
+        inner = move_chain(x, [(1, 2), (2, 1)])
         output_x = flip(output_weight, "fsdp", 2)
         both = jnp.stack([own_columns, columns_x])
         both_c = flip(both, "fsdp", 1)
-        column_pieces = jnp.stack([both[0], both_c[0], both[1], both_c[1]])
-        columns_full = jnp.take(column_pieces, w_rows, axis=0).reshape(width, 4 * LANES)
-        near = jnp.where(place % 2 == 0, right_1, left_1)
-        right_1, left_1, near, _, _ = lax.optimization_barrier(
-            (right_1, left_1, near, beside, output_x)
-        )
-        right_2 = move_chain(right_1, [(1, 0), (2, 1)])
-        left_2 = move_chain(left_1, [(1, 2), (2, 3)])
+        column_arrays = [both, both_c]
+        column_layout = ((0, 0), (1, 0), (0, 1), (1, 1))
+        near, inner, _ = lax.optimization_barrier((near, inner, beside))
+        far_inner = move_chain(near, [(1, 2), (2, 1)])
+        far_outer = move_chain(inner, [(1, 0), (2, 3)])
         near_beside = flip(near, "seq", 1)
-        gate_x1 = flip(after(gate_weight[:half], near), "fsdp", 2)
-        far = jnp.where(place < 2, right_2, left_2)
+        far_half = (1 - shard // 2) * hidden
+        near_half = (shard // 2) * hidden
+        up_own, up_sent = [
+            jnp.concatenate(
+                [
+                    lax.dynamic_slice_in_dim(after(w, own_columns), start, hidden, axis=1)
+                    for w in (gate_weight, up_weight)
+                ],
+                axis=1,
+            )
+            for start in (near_half, far_half)
+        ]
+        up_x1 = flip(after(up_sent[:half], near), "fsdp", 2)
+        token_order = after(token_order, near)
+        is_inner = (place == 1) | (place == 2)
         block_slots = [seq ^ d for d in range(slots)]
     else:
         w_rows = jnp.zeros((1,), jnp.int32)
-        columns_full = lax.all_gather(own_columns, "fsdp", axis=0, tiled=True)
+        column_arrays = [lax.all_gather(own_columns, "fsdp", axis=0, tiled=True)[None]]
+        column_layout = ((0, 0),)
         gathered = lax.all_gather(x, "seq", axis=0)
         x_blocks = [gathered[i] for i in range(slots)]
         block_slots = [jnp.asarray(i, jnp.int32) for i in range(slots)]
 
-    own_columns_full = columns_full[:, : 3 * LANES]
-    gain_1 = columns_full[:, 3 * LANES].reshape(1, width)
-    gain_2 = columns_full[:, 3 * LANES + 1].reshape(1, width)
+    codes = token_codes(lengths[0], token_order[0], real_token[0])
+    gain_pieces = jnp.stack(
+        [column_arrays[a][i, :, 3 * LANES : 3 * LANES + 2] for a, i in column_layout]
+    )
+    gain_rows = jnp.take(gain_pieces, w_rows, axis=0).reshape(width, 2)
+    gain_1, gain_2 = gain_rows[:, 0].reshape(1, width), gain_rows[:, 1].reshape(1, width)
     state = None
 
     def project_block(number, block, state):
         slot = block_slots[number].reshape(1).astype(jnp.int32)
         return project(
-            slot, slots, heads, block, gain_1, own_columns_full, q_table, k_table, state
+            slot,
+            w_rows,
+            slots,
+            heads,
+            lengths.shape[1],
+            block,
+            column_layout,
+            column_arrays,
+            codes,
+            state,
         )
 
     if direct:
         state = project_block(0, x, state)
         state = project_block(1, beside, state)
-        far, _, _, _ = lax.optimization_barrier((far, near_beside, gate_x1, state[0]))
-        third = move_chain(far, [(1, 0), (2, 3)])
+        far_inner, far_outer, _, _, _, _ = lax.optimization_barrier(
+            (far_inner, far_outer, near_beside, up_x1, output_x, state[0])
+        )
+        third = move_chain(far_inner, [(1, 0), (2, 3)])
+        far = jnp.where(is_inner, far_inner, far_outer)
         far_beside = flip(far, "seq", 1)
-        gate_x2 = flip(after(gate_weight[half:], far), "fsdp", 2)
-        gate_c = flip(after(gate_weight, far), "fsdp", 1)
+        up_x2 = flip(after(up_sent[half:], far_inner), "fsdp", 2)
+        up_c = flip(after(up_own, far_inner), "fsdp", 1)
         state = project_block(2, near, state)
         state = project_block(3, near_beside, state)
         state = project_block(4, far, state)
-        cross = jnp.where(
-            (place == 0) | (place == 3), third, jnp.where(place == 1, right_1, left_1)
+        third, _, _, _, _ = lax.optimization_barrier(
+            (third, far_beside, up_x2, up_c, state[0])
         )
-        cross, _, _, _, _ = lax.optimization_barrier(
-            (cross, far_beside, gate_x2, gate_c, state[0])
-        )
+        cross = jnp.where(is_inner, inner, third)
         cross_beside = flip(cross, "seq", 1)
-        up_x1 = flip(after(up_weight[:half], cross), "fsdp", 2)
-        gate_xc1 = flip(after(gate_x1, cross), "fsdp", 1)
-        up_c = flip(after(up_weight, cross), "fsdp", 1)
+        c_x = flip(after(c, cross), "fsdp", 2)
+        up_xc1 = flip(after(up_x1, cross), "fsdp", 1)
+        down_c = flip(after(down_weight, cross), "fsdp", 1)
         state = project_block(5, far_beside, state)
         state = project_block(6, cross, state)
-        cross_beside, _, _, _ = lax.optimization_barrier((cross_beside, up_x1, gate_xc1, up_c))
+        cross_beside, _, _, _ = lax.optimization_barrier((cross_beside, c_x, up_xc1, down_c))
         state = project_block(7, cross_beside, state)
     else:
         for number, block in enumerate(x_blocks):
@@ -823,172 +999,187 @@
     att_first, sums, qb = attend(qa, ka, va, 0, 2, slots, (0, slots), ())
     middle_slot = slots // 2
     if direct:
-        up_x2 = flip(after(up_weight[half:], qa), "fsdp", 2)
-        down_x = flip(after(down_weight, qa), "fsdp", 2)
-        gate_xc2 = flip(after(gate_x2, qa), "fsdp", 1)
+        qkv_x = flip(after(qkv_weight, qa), "fsdp", 2)
+        up_xc2 = flip(after(up_x2, qa), "fsdp", 1)
         output_c = flip(after(output_weight, qa), "fsdp", 1)
-        qb, _, _, _ = lax.optimization_barrier((qb, up_x2, gate_xc2, output_c))
+        output_xc = flip(after(output_x, qa), "fsdp", 1)
+        qb, _, _, _ = lax.optimization_barrier((qb, up_xc2, output_c, output_xc))
     att_turned = turn(att_first)
     att_second, sums, qb = attend(
         qa, ka, va, 1, 2, slots, (0, middle_slot), (sums, qb)
     )
     if direct:
-        output_xc = flip(after(output_x, att_first), "fsdp", 1)
-        up_xc1 = flip(after(up_x1, att_first), "fsdp", 1)
-        up_xc2 = flip(after(up_x2, att_first), "fsdp", 1)
-        qb, _, _, _, _ = lax.optimization_barrier((qb, output_xc, up_xc1, up_xc2, att_turned))
+        qb, _, _ = lax.optimization_barrier((qb, att_turned, qkv_x))
     att_second, sums, qb = attend(
         qa, ka, va, 1, 2, slots, (middle_slot, slots), (att_second, sums, qb)
     )
     if direct:
-        down_c = flip(after(down_weight, att_second), "fsdp", 1)
-        down_xc = flip(after(down_x, att_second), "fsdp", 1)
-        qkv_x = flip(after(qkv_weight, att_second), "fsdp", 2)
-        wg = [
-            (0, 0, gate_weight), (1, 0, gate_c), (2, 0, gate_x1), (2, half, gate_x2),
-            (3, 0, gate_xc1), (3, half, gate_xc2),
+        output_pieces = [output_weight, output_c, output_x, output_xc]
+        output_entries = [(0, p, 0, p, shard_rows, 0, 0) for p in range(4)]
+        d_rows = (shard % 2) ^ jnp.arange(2, dtype=jnp.int32)
+        ff_sources = [up_own, up_c, up_x1, up_x2, up_xc1, up_xc2, down_weight, down_c]
+        ff_entries = [
+            (kind, source, 0, place, shard_rows, offset, kind * hidden)
+            for kind in range(2)
+            for source, place, offset in (
+                (0, 0, 0), (1, 1, 0), (2, 2, 0), (3, 2, half), (4, 3, 0), (5, 3, half),
+            )
+        ] + [(2, 6, 1, 0, down_weight.shape[0], 0, 0), (2, 7, 1, 1, down_weight.shape[0], 0, 0)]
+    else:
+        output_pieces = [lax.all_gather(output_weight, "fsdp", axis=0, tiled=True)]
+        output_entries = [(0, 0, 0, 0, width, 0, 0)]
+        d_rows = w_rows
+        ff_sources = [
+            lax.all_gather(w, "fsdp", axis=0, tiled=True)
+            for w in (gate_weight, up_weight, down_weight)
         ]
-        wu = [
-            (0, 0, up_weight), (1, 0, up_c), (2, 0, up_x1), (2, half, up_x2),
-            (3, 0, up_xc1), (3, half, up_xc2),
-        ]
-        wd = [(0, 0, down_weight), (1, 0, down_c), (2, 0, down_x), (3, 0, down_xc)]
-        wo = [(0, 0, output_weight), (1, 0, output_c), (2, 0, output_x), (3, 0, output_xc)]
-        pieces = shards
-    else:
-        wo, wg, wu, wd = [
-            [(0, 0, lax.all_gather(w, "fsdp", axis=0, tiled=True))]
-            for w in (output_weight, gate_weight, up_weight, down_weight)
-        ]
-        pieces = 1
+        hidden = gate_weight.shape[1]
+        ff_entries = [(i, i, 0, 0, width, 0, 0) for i in range(3)]
     att_parts = [att_turned, turn(att_second)]
     total = rows * slots
     sums = sums.reshape(total, LANES)
     qb = qb.reshape(heads, total, LANES)
 
-    (layer_out, d_middle, d_att), (og, gg, ug, dg) = middle_stage(
-        w_rows, att_parts, x, c, gain_2, wo, wg, wu, wd, pieces, halves
-    )
+    middle, h2, att = pre_stage(w_rows, att_parts, x, gain_2, output_entries, output_pieces)
+    if direct:
+        h2s, cs = [h2, flip(h2, "fsdp", 2)], [c, c_x]
+    else:
+        h2s, cs = [h2], [c]
+    outs, backs, gu, dg = main_stage(
+        w_rows, d_rows, h2s, cs, hidden, ff_entries, ff_sources, halves
+    )
+    if direct:
+        line = Line()
+        backs[1] = flip(backs[1], "fsdp", 2)
+        up_r = Reduction(*gu, line)
+        down_r = Reduction(dg[0][0], dg[1][0], line)
+        up_r.core()
+        down_r.core()
+        up_r.halve(1)
+        down_r.halve(2)
+        backs[1] = lax.optimization_barrier((backs[1], up_r.own, down_r.own))[0]
+    d_middle, branch, d_att = post_stage(
+        w_rows, middle, backs, c, gain_2, slots, output_entries, output_pieces
+    )
+    og = out_terms(w_rows, att, branch, halves)
     grad_blocks = turn(d_att)
     parts = 4
     back = functools.partial(attend_back, qb, ka, va)
     if direct:
-        line = Line()
-        gate_r, up_r, down_r, output_r = [
-            Reduction(kept, given, line) for kept, given in (gg, ug, dg, og)
-        ]
-        gate_r.given = after(gate_r.given, qkv_x)
-        core_line = Line()
-        for r in (gate_r, up_r, down_r, output_r):
-            r.core()
-            r.own, r.send = core_line.hold(r.own), core_line.hold(r.send)
-            r.across()
         qkv_c = flip(after(qkv_weight, d_att), "fsdp", 1)
+        output_r = Reduction(*og, line)
+        down_r.hold(d_att)
+        down_r.halve(1)
+        output_r.core()
+        up_r.hold(d_att)
+        up_r.halve(2)
         grad_blocks = lax.optimization_barrier(
-            (grad_blocks, gate_r.send, up_r.send, down_r.send, output_r.send)
+            (grad_blocks, down_r.own, up_r.own, qkv_c)
         )[0]
     else:
         qkv_pieces = [lax.all_gather(qkv_weight, "fsdp", axis=0, tiled=True)]
     kv_0, dq, gb = back(0, parts, slots, sums, grad_blocks, None)
+    if direct:
+        for r in (down_r, up_r, output_r):
+            r.hold(kv_0)
+        down_r.halve(4)
+        up_r.halve(4)
+        output_r.across()
+        outs[1] = flip(after(outs[1], kv_0), "fsdp", 2)
+        qkv_xc = flip(after(qkv_x, kv_0), "fsdp", 1)
+        qkv_pieces = [qkv_weight, qkv_c, qkv_x, qkv_xc]
+        gb = lax.optimization_barrier((gb, down_r.own, up_r.own, output_r.own))[0]
     kv_1, dq = back(1, parts, slots, None, None, (gb, dq))
+    kv_early = turn(jnp.concatenate([kv_0, kv_1], axis=2))
     if direct:
-        gate_r.arrived = after(gate_r.arrived, kv_1)
-        gate_r.halve(1)
-        gb = lax.optimization_barrier((gb, gate_r.own, qkv_c))[0]
-    kv_early = turn(jnp.concatenate([kv_0, kv_1], axis=2))
+        for r in (down_r, up_r, output_r):
+            r.hold(kv_1)
+        up_r.swap_columns()
+        down_r.settle()
+        down_r.widen(4)
+        output_r.halve(2)
+        gb = lax.optimization_barrier((gb, down_r.own, up_r.own, output_r.own, qkv_xc, outs[1]))[0]
     kv_2, dq = back(2, parts, slots, None, None, (gb, dq))
     if direct:
-        up_r.arrived = after(up_r.arrived, kv_2)
-        up_r.halve(2)
-        gb = after(gb, up_r.own)
+        for r in (down_r, up_r, output_r):
+            r.hold(kv_2)
+        up_r.join_columns()
+        up_r.widen(4)
+        down_r.widen(1)
+        output_r.halve(1)
+        gb = lax.optimization_barrier((gb, down_r.own, up_r.own, output_r.own))[0]
     kv_3, dq = back(3, parts, slots, None, None, (gb, dq))
     kv_late = jnp.concatenate([kv_2, kv_3], axis=2)
     late = turn(jnp.concatenate([kv_late.reshape(slots, rows, LANES), dq], axis=1))
     kv_late = late[:, :rows].reshape(kv_late.shape)
     dq_turned = late[:, rows:]
     if direct:
-        gate_r.arrived = after(gate_r.arrived, kv_3)
-        gate_r.halve(2)
-        qkv_xc = flip(after(qkv_x, kv_2), "fsdp", 1)
-        qkv_pieces = [qkv_weight, qkv_c, qkv_x, qkv_xc]
-        dq = lax.optimization_barrier((dq, gate_r.own, kv_early))[0]
+        for r in (down_r, up_r, output_r):
+            r.hold(kv_3)
+        up_r.widen(2)
+        down_r.widen(2)
+        output_r.halve(4)
+        dq = lax.optimization_barrier((dq, down_r.own, up_r.own, output_r.own, kv_early))[0]
+    layer_out = (middle + sum(part.astype(f32) for part in outs)).astype(bf16)
     own = own_terms(w_rows, h1, dq, [kv_0, kv_1, kv_2, kv_3], shards, halves)
     if direct:
         own_r = Reduction(*own, line)
-        up_r.arrived = after(up_r.arrived, own[0])
-        down_r.arrived = after(down_r.arrived, own[0])
-        output_r.arrived = after(output_r.arrived, own[0])
         own_r.core()
-        up_r.halve(1)
-        down_r.halve(1)
+        for r in (up_r, output_r):
+            r.hold(own[0])
+        up_r.widen(1)
+        output_r.settle()
+        output_r.widen(4)
         own_r.across()
-        gate_r.halve(4)
-        up_r.halve(4)
-        output_r.halve(2)
-        gate_r.settle()
-        gate_r.widen(4)
+        output_r.widen(1)
         own_r.settle()
-        own_r.own = own_r.own[None]
+        own_r.own = after(own_r.own[None], down_r.arrived)
         own_r.widen(4)
-        up_r.settle()
-        up_r.widen(4)
-        output_r.halve(1)
-        down_r.halve(2)
-        gate_r.own = after(gate_r.own, late)
-        gate_r.widen(2)
+        output_r.widen(2)
+        own_r.widen(1)
+        own_r.arrived = after(own_r.arrived, late)
         own_r.widen(2)
-        up_r.widen(1)
-        output_r.halve(4)
-        down_r.halve(4)
-        gate_r.widen(1)
-        own_r.widen(1)
         input_grad = last_stage(
             w_rows, dq_turned, [kv_early, kv_late], x, d_middle, gain_1, qkv_pieces
         )
-        up_r.widen(2)
-        output_r.settle()
-        output_r.widen(4)
-        down_r.settle()
-        down_r.own = after(down_r.own, input_grad)
-        down_r.widen(4)
-        output_r.widen(1)
-        down_r.widen(2)
-        output_r.widen(2)
-        down_r.widen(1)
-        for r in (gate_r, up_r, down_r, output_r, own_r):
+        for r in (up_r, down_r, output_r):
             r.join()
-        gate_grad, up_grad, down_grad, output_grad = [
-            r.own for r in (gate_r, up_r, down_r, output_r)
-        ]
-        all_shares = own_r.own.reshape(2, 2, 2, shard_rows, 3 * LANES)
-        all_shares = all_shares.transpose(2, 1, 0, 3, 4)
+        gate_grad, up_grad = up_r.own[:, : 2 * hidden], up_r.own[:, 2 * hidden :]
+        down_grad, output_grad = down_r.own, output_r.own
+        query_grad, key_grad, value_grad, attention_gain_grad = finish_own(
+            ((seq // 2) % 2).reshape(1).astype(jnp.int32),
+            own_r.own,
+            own_r.arrived,
+            qkv_weight,
+            attention_gain.reshape(shard_rows, 1),
+        )
+        attention_gain_grad = attention_gain_grad.reshape(shard_rows)
     else:
         own_share = lax.psum_scatter(own[0][0], "fsdp", scatter_dimension=0, tiled=True)
         all_shares = lax.all_gather(own_share, "seq", axis=0)
         gate_grad, up_grad, down_grad, output_grad = [
-            lax.psum(lax.psum_scatter(g[0][0], "fsdp", scatter_dimension=0, tiled=True), "seq")
-            for g in (gg, ug, dg, og)
+            lax.psum(lax.psum_scatter(g, "fsdp", scatter_dimension=0, tiled=True), "seq")
+            for g in (gu[0][0, :, :hidden], gu[0][0, :, hidden:], dg[0][0], og[0][0])
         ]
-    all_shares = all_shares.reshape(slots, shard_rows, 3, LANES)[..., :own_width].astype(f32)
-    query_grad, key_grad, value_grad = [
-        all_shares[:, :, i, :].transpose(1, 0, 2).reshape(shard_rows, width) for i in range(3)
-    ]
+    def gain_grad(terms, gain):
+        summed = sum(jnp.sum(g * w.astype(f32), axis=1) for g, w in terms)
+        return summed / gain.astype(f32)
+
     if not direct:
+        all_shares = all_shares.reshape(slots, shard_rows, 3, LANES)[..., :own_width].astype(f32)
+        query_grad, key_grad, value_grad = [
+            all_shares[:, :, i, :].transpose(1, 0, 2).reshape(shard_rows, width) for i in range(3)
+        ]
         input_grad = last_stage(
             w_rows, dq_turned, [kv_early, kv_late], x, d_middle, gain_1, qkv_pieces
         )
-
-    def gain_grad(terms, gain):
-        summed = sum(jnp.sum(g * w.astype(f32), axis=1) for g, w in terms)
-        return summed / gain.astype(f32)
-
+        attention_gain_grad = gain_grad(
+            ((query_grad, query_weight), (key_grad, key_weight), (value_grad, value_weight)),
+            attention_gain,
+        )
     output_grad, gate_grad, up_grad, down_grad = [
         g.astype(f32) for g in (output_grad, gate_grad, up_grad, down_grad)
     ]
-    attention_gain_grad = gain_grad(
-        ((query_grad, query_weight), (key_grad, key_weight), (value_grad, value_weight)),
-        attention_gain,
-    )
     feedforward_gain_grad = gain_grad(
         ((gate_grad, gate_weight), (up_grad, up_weight)), feedforward_gain
     )

time: 505 us -> 472 us (0.935)
  Pallas kernels: 177 us -> 200 us
  other arithmetic: 73.4 us -> 51.9 us
  waiting for transfers between devices: 126 us -> 109 us
  local copies, waits for them, and re-layouts: 26.8 us -> 16.8 us
  starting transfers between devices: 91.9 us -> 84.3 us
    pallas_call x9 -> x13, Pallas kernels: 61 us -> 83.7 us  [the longest x1 32.8 us: main_stage(): pl.pallas_call(functools.partial(main_kernel, groups, halves, entries, le...]
    ppermute x62 -> x50, waiting for transfers between devices: 107 us -> 90.8 us  [flip(): return lax.ppermute(values, axis, [(i, i ^ delta) for i in range(count)])]
    convert_element_type x21 -> x14, other arithmetic: 35.3 us -> 21.9 us  [add_low(): return (a.astype(f32) + b.astype(f32)).astype(bf16)]
    unnamed x96 -> x70, local copies, waits for them, and re-layouts: 13.2 us -> 5.25 us
    convert_element_type x2 -> x0, other arithmetic: 5.32 us -> none  [the longest x1 2.69 us: mask_tables(): k_table = jnp.where(lane < segments, jnp.where(open_to, 0.0, BLOCKED), jn...]
    ppermute x62 -> x50, starting transfers between devices: 55.1 us -> 54.7 us  [flip(): return lax.ppermute(values, axis, [(i, i ^ delta) for i in range(count)])]
  transfers between devices with their start and end apart: 72 -> 60, of which waited for: 24 -> 20; matrix products, arithmetic and copies ran while one was open for 18% -> 13% of each run, Pallas kernels for 35% -> 31%
where the time goes in v3:
time: 472 us; the launch traced here: 465 us
  Pallas kernels  200 us (42%)
  waiting for transfers between devices  109 us (23%)
  starting transfers between devices  84.3 us (18%)
  other arithmetic  51.9 us (11%)
  local copies, waits for them, and re-layouts  16.8 us (4%)
    ppermute x50, waiting for transfers between devices, flip(): return lax.ppermute(values, axis, [(i, i ^ delta) for i in range(count)])  90.8 us
    pallas_call x4, Pallas kernels, attend_back(): pl.pallas_call(functools.partial(backward_kernel, heads, part, parts, 512...  65.6 us
    ppermute x50, starting transfers between devices, flip(): return lax.ppermute(values, axis, [(i, i ^ delta) for i in range(count)])  54.7 us
    pallas_call x3, Pallas kernels, attend(): pl.pallas_call(functools.partial(forward_body, heads, len(extra)), grid=(...  34.6 us
    pallas_call x1, Pallas kernels, main_stage(): pl.pallas_call(functools.partial(main_kernel, groups, halves, entries, le...  32.8 us
    pallas_call x8, Pallas kernels, project(): pl.pallas_call(functools.partial(project_kernel, heads, segments, layout,...  32.6 us
    all_to_all x5, starting transfers between devices, turn(): lax.all_to_all(blocks, 'seq', split_axis=0, concat_axis=0, tiled=True)  22.2 us
    convert_element_type x14, other arithmetic, add_low(): return (a.astype(f32) + b.astype(f32)).astype(bf16)  21.9 us
  transfers between devices with their start and end apart: 60, of which 20 were waited for; matrix products, arithmetic and copies ran while one was open for 13% of the time, Pallas kernels for 31%

profile of v3, /device:TPU:0, one launch (start us, length us, event | category | flops | bytes accessed | tf_op | source)
XLA Modules:
  0.0 464.5 jit_solution(4699405989964710305)
XLA Ops:
  0.7 3.0 collective-permute-start.2
  15.2 4.2 collective-permute-done.8
  28.0 2.9 select_reduce_fusion
  32.9 4.1 project.8
  37.0 4.2 project.9
  41.2 5.8 %collective-permute-done.4 = bf16[320,1024]{1,0:T(8,128)(2,1)} collective-permute-done((bf16[320,1024]{1,0:T(8,128)(2,1)}, bf16[320,1024]{1,0:T(8,128)(2,1)}, u32[]{:S(2)}, u32[]{:S(2)}) %collective-permute-start.4) | collective-permute-done | bytes 655392 | tf_op jit(solution)/shard_map/ppermute | solution.py:855
  51.9 4.1 project.10
  56.0 4.0 project.11
  60.0 4.0 project.12
  65.8 3.3 collective-permute-done.10
  75.1 4.1 project.13
  79.2 4.0 project.14
  83.2 4.7 %collective-permute-done.15.refs_5_ = bf16[320,1024]{1,0:T(8,128)(2,1)} collective-permute-done((bf16[320,1024]{1,0:T(8,128)(2,1)}, bf16[320,1024]{1,0:T(8,128)(2,1)}, u32[]{:S(2)}, u32[]{:S(2)}) %collective-permute-start.15) | collective-permute-done | bytes 655392 | tf_op jit(solution)/shard_map/ppermute | solution.py:758
  88.9 4.2 project.15
  95.3 15.9 %attend.3 = (bf16[8,160,128]{2,1,0:T(8,128)(2,1)}, f32[8,2,160,128]{3,2,1,0:T(8,128)}, bf16[2,8,2,160,128]{4,3,2,1,0:T(8,128)(2,1)}) custom-call(bf16[2,8,2,160,128]{4,3,2,1,0:T(8,128)(2,1)} %bitcast.77, bf16[2,8,2,160,128]{4,3,2,1,0:T(8,128)(2,1)} %bitcast.80, bf16[2,8,2,160,128]{4,3,2,1,0:T(8,128)(2,1)} %bitcast.87, ...), custom_call_target="tpu_custom_call" | custom-call | flops 6710886400 | bytes 2621440 | tf_op jit(solution)/shard_map/attend/pallas_call | solution.py:187
  111.2 4.3 all-to-all-start
  115.6 9.4 %attend.4 = (bf16[8,160,128]{2,1,0:T(8,128)(2,1)}, f32[8,2,160,128]{3,2,1,0:T(8,128)}, bf16[2,8,2,160,128]{4,3,2,1,0:T(8,128)(2,1)}) custom-call(bf16[2,8,2,160,128]{4,3,2,1,0:T(8,128)(2,1)} %bitcast.78, bf16[2,8,2,160,128]{4,3,2,1,0:T(8,128)(2,1)} %bitcast.81, bf16[2,8,2,160,128]{4,3,2,1,0:T(8,128)(2,1)} %bitcast.88, ...), custom_call_target="tpu_custom_call", output_to_operand_aliasing={{1}: (5, {}), {2}: (6, {})} | custom-call | flops 6710886400 | bytes 2621440 | tf_op jit(solution)/shard_map/attend/pallas_call | solution.py:187
  128.5 9.3 %attend.5 = (bf16[8,160,128]{2,1,0:T(8,128)(2,1)}, f32[8,2,160,128]{3,2,1,0:T(8,128)}, bf16[2,8,2,160,128]{4,3,2,1,0:T(8,128)(2,1)}) custom-call(bf16[2,8,2,160,128]{4,3,2,1,0:T(8,128)(2,1)} %bitcast.79, bf16[2,8,2,160,128]{4,3,2,1,0:T(8,128)(2,1)} %bitcast.82, ...), custom_call_target="tpu_custom_call", output_to_operand_aliasing={{0}: (5, {}), {1}: (6, {}), {2}: (7, {})} | custom-call | flops 6710886400 | bytes 2621440 | tf_op jit(solution)/shard_map/attend/pallas_call | solution.py:187
  137.8 3.9 all-to-all-start.1
  144.0 6.7 %all-to-all-done.1.refs_2_ = bf16[8,160,128]{2,1,0:T(8,128)(2,1)S(1)} async-done(((bf16[8,160,128]{2,1,0:T(8,128)(2,1)}), bf16[8,160,128]{2,1,0:T(8,128)(2,1)S(1)}, u32[]{:S(2)}, u32[]{:S(2)}) %all-to-all-start.1) | async-done | bytes 327712 | tf_op jit(solution)/shard_map/all_to_all | solution.py:861
  151.4 5.2 %pre_stage.1 = (f32[320,1024]{1,0:T(8,128)}, bf16[320,1024]{1,0:T(8,128)(2,1)}, bf16[320,1024]{1,0:T(8,128)(2,1)}) custom-call(s32[4]{0:T(128)} %iota_xor_fusion.1.refs_1_.refs_0_.w_rows, bf16[8,160,128]{2,1,0:T(8,128)(2,1)} %copy-done.19, bf16[8,160,128]{2,1,0:T(8,128)(2,1)} %copy-done.20, bf16[320,1024]{1,0:T(8,128)(2,1)} %bitcast.99, ...), custom_call_target="tpu_custom_call" | custom-call | flops 671088640 | bytes 2097152 | tf_op jit(solution)/shard_map/pre_stage/pallas_call | solution.py:461
  158.7 11.7 %collective-permute-done.22.refs_3_ = bf16[320,1024]{1,0:T(8,128)(2,1)S(1)} collective-permute-done((bf16[320,1024]{1,0:T(8,128)(2,1)}, bf16[320,1024]{1,0:T(8,128)(2,1)S(1)}, u32[]{:S(2)}, u32[]{:S(2)}) %collective-permute-start.22) | collective-permute-done | bytes 655392 | tf_op jit(solution)/shard_map/ppermute | solution.py:758
  171.2 32.8 %main_stage.1 = (f32[320,1024]{1,0:T(8,128)}, bf16[320,1024]{1,0:T(8,128)(2,1)}, f32[320,1024]{1,0:T(8,128)}, bf16[320,1024]{1,0:T(8,128)(2,1)}, bf16[2,256,2816...) custom-call(s32[4]{0:T(128)} %iota_xor_fusion.1.refs_1_.refs_0_.w_ro, ...), custom_call_target="tpu_custom_call" | custom-call | flops 16609443840 | bytes 17301504 | tf_op jit(solution)/shard_map/main_stage/pallas_call | solution.py:564
  206.3 3.5 collective-permute-done.24
  209.8 4.4 add_convert_fusion
  216.0 3.5 fusion.3
  221.7 5.4 %post_stage.1 = (f32[320,1024]{1,0:T(8,128)}, bf16[320,1024]{1,0:T(8,128)(2,1)}, bf16[8,320,128]{2,1,0:T(8,128)(2,1)}) custom-call(s32[4]{0:T(128)} %iota_xor_fusion.1.refs_1_.refs_0_.w_rows, f32[320,1024]{1,0:T(8,128)} %get-tuple-element.217.refs_1_, f32[320,1024]{1,0:T(8,128)} %get-tuple-element.223.refs_2_, ...), custom_call_target="tpu_custom_call" | custom-call | flops 671088640 | bytes 4194304 | tf_op jit(solution)/shard_map/post_stage/pallas_call | solution.py:627
  228.0 6.0 %all-to-all-start.2 = ((bf16[8,320,128]{2,1,0:T(8,128)(2,1)}), bf16[8,320,128]{2,1,0:T(8,128)(2,1)}, u32[]{:S(2)}, u32[]{:S(2)}) async-start(bf16[8,320,128]{2,1,0:T(8,128)(2,1)} %get-tuple-element.231), calls=%async_computation.2 | async-start | bytes 1310720 | tf_op jit(solution)/shard_map/all_to_all | solution.py:861
  234.8 3.9 out_terms.1
  238.7 11.7 %collective-permute-done.26 = bf16[352,1024]{1,0:T(8,128)(2,1)} collective-permute-done((bf16[352,1024]{1,0:T(8,128)(2,1)}, bf16[352,1024]{1,0:T(8,128)(2,1)}, u32[]{:S(2)}, u32[]{:S(2)}) %collective-permute-start.26) | collective-permute-done | bytes 720928 | tf_op jit(solution)/shard_map/ppermute | solution.py:758
  254.1 2.8 add_convert_fusion.2
  258.0 17.4 %attend_back.4 = (bf16[8,2,80,128]{3,2,1,0:T(8,128)(2,1)}, f32[2,2560,128]{2,1,0:T(8,128)}, bf16[2,2560,128]{2,1,0:T(8,128)(2,1)}) custom-call(bf16[2,2560,128]{2,1,0:T(8,128)(2,1)} %bitcast.110, bf16[2,8,4,80,128]{4,3,2,1,0:T(8,128)(2,1)} %bitcast.83, bf16[2,8,4,80,128]{4,3,2,1,0:T(8,128)(2,1)} %bitcast.90, f32[2560,128]{1,0:T(8,128)} %bitcast.109, ...), custom_call_target="tpu_custom_call" | custom-call | flops 8388608000 | bytes 7864320 | tf_op jit(solution)/shard_map/attend_back/pallas_call | solution.py:341
  276.6 6.4 %collective-permute-start.32 = (bf16[88,1024]{1,0:T(8,128)(2,1)S(1)}, bf16[88,1024]{1,0:T(8,128)(2,1)S(1)}, u32[]{:S(2)}, u32[]{:S(2)}) collective-permute-start(bf16[88,1024]{1,0:T(8,128)(2,1)S(1)} %get-tuple-element.250), channel_id=1, source_target_pairs={{0,16},{4,20},{8,24},{12,28},{16,0},{20,4},{24,8},{28,12},{1,17},{... | collective-permute-start | bytes 540680 | tf_op jit(solution)/shard_map/ppermute | solution.py:758
  289.1 16.2 %attend_back.5 = (bf16[8,2,80,128]{3,2,1,0:T(8,128)(2,1)}, f32[2,2560,128]{2,1,0:T(8,128)}) custom-call(bf16[2,2560,128]{2,1,0:T(8,128)(2,1)} %bitcast.111, bf16[2,8,4,80,128]{4,3,2,1,0:T(8,128)(2,1)} %bitcast.84, bf16[2,8,4,80,128]{4,3,2,1,0:T(8,128)(2,1)} %bitcast.91, bf16[2,2560,128]{2,1,0:T(8,128)(2,1)} %get-tuple-element.272.refs_3_, ...), custom_call_target="tpu_custom_call" | custom-call | flops 8388608000 | bytes 7864320 | tf_op jit(solution)/shard_map/attend_back/pallas_call | solution.py:341
  307.3 4.2 all-to-all-start.4
  317.1 2.9 collective-permute-start.37
  322.8 16.2 %attend_back.6 = (bf16[8,2,80,128]{3,2,1,0:T(8,128)(2,1)}, f32[2,2560,128]{2,1,0:T(8,128)}) custom-call(bf16[2,2560,128]{2,1,0:T(8,128)(2,1)} %bitcast.112, bf16[2,8,4,80,128]{4,3,2,1,0:T(8,128)(2,1)} %bitcast.85, bf16[2,8,4,80,128]{4,3,2,1,0:T(8,128)(2,1)} %bitcast.92, bf16[2,2560,128]{2,1,0:T(8,128)(2,1)} %get-tuple-element.272.refs_3_, ...), custom_call_target="tpu_custom_call" | custom-call | flops 8388608000 | bytes 7864320 | tf_op jit(solution)/shard_map/attend_back/pallas_call | solution.py:341
  341.9 15.8 %attend_back.7 = (bf16[8,2,80,128]{3,2,1,0:T(8,128)(2,1)}, bf16[8,320,128]{2,1,0:T(8,128)(2,1)}) custom-call(bf16[2,2560,128]{2,1,0:T(8,128)(2,1)} %bitcast.113, bf16[2,8,4,80,128]{4,3,2,1,0:T(8,128)(2,1)} %bitcast.86, bf16[2,8,4,80,128]{4,3,2,1,0:T(8,128)(2,1)} %bitcast.93, bf16[2,2560,128]{2,1,0:T(8,128)(2,1)} %get-tuple-element.272.refs_3_, ...), custom_call_target="tpu_custom_call" | custom-call | flops 8388608000 | bytes 7864320 | tf_op jit(solution)/shard_map/attend_back/pallas_call | solution.py:341
  358.8 8.5 %own_terms.1 = (bf16[2,256,384]{2,1,0:T(8,128)(2,1)}, bf16[2,256,384]{2,1,0:T(8,128)(2,1)}) custom-call(s32[4]{0:T(128)} %iota_xor_fusion.1.refs_1_.refs_0_.w_rows, bf16[8,4,80,1024]{3,2,1,0:T(8,128)(2,1)} %bitcast.76, bf16[8,320,128]{2,1,0:T(8,128)(2,1)} %get-tuple-element.284.refs_2_, bf16[8,2,80,128]{3,2,1,0:T(8,128)(2,1)} %get-tuple-element.238.refs_3_, ...), custom_call_target="tpu_custom_call" | custom-call | flops 2013265920 | bytes 5242880 | tf_op jit(solution)/shard_map/own_terms/pallas_call | solution.py:393
  368.5 3.0 collective-permute-start.44
  372.6 3.8 all-to-all-start.3
  385.0 32.2 %collective-permute-done.47 = bf16[352,1024]{1,0:T(8,128)(2,1)S(1)} collective-permute-done((bf16[352,1024]{1,0:T(8,128)(2,1)S(1)}, bf16[352,1024]{1,0:T(8,128)(2,1)S(1)}, u32[]{:S(2)}, u32[]{:S(2)}) %collective-permute-start.47) | collective-permute-done | bytes 720928 | tf_op jit(solution)/shard_map/ppermute | solution.py:758
  421.8 5.2 %collective-permute-done.50 = bf16[64,1024]{1,0:T(8,128)(2,1)S(1)} collective-permute-done((bf16[64,1024]{1,0:T(8,128)(2,1)S(1)}, bf16[64,1024]{1,0:T(8,128)(2,1)S(1)}, u32[]{:S(2)}, u32[]{:S(2)}) %collective-permute-start.50) | collective-permute-done | bytes 131104 | tf_op jit(solution)/shard_map/ppermute | solution.py:758
  433.6 2.8 collective-permute-done.53
  437.6 2.9 collective-permute-done.51
  442.9 7.7 %last_stage.1 = f32[320,1024]{1,0:T(8,128)} custom-call(s32[4]{0:T(128)} %iota_xor_fusion.1.refs_1_.refs_0_.w_rows, bf16[8,320,128]{2,1,0:T(8,128)(2,1)} %get-tuple-element.336.refs_1_, bf16[8,2,160,128]{3,2,1,0:T(8,128)(2,1)} %copy-done.12, bf16[8,2,160,128]{3,2,1,0:T(8,128)(2,1)} %bitcast.102, bf16[320,1024]{1,0:T(8,128)(2,1)} %bitcast.100, ...), custom_call_target="tpu_custom_call" | custom-call | flops 2013265920 | bytes 6291456 | tf_op jit(solution)/shard_map/last_stage/pallas_call | solution.py:713
  452.8 2.9 multiply_reduce_fusion
  458.7 3.7 finish_own.1
  (251 shorter events, 113.6 us)
Async XLA Ops:
  0.7 22.4 %collective-permute-start.2 = (bf16[320,1024]{1,0:T(8,128)(2,1)}, bf16[320,1024]{1,0:T(8,128)(2,1)}, u32[]{:S(2)}, u32[]{:S(2)}) collective-permute-start(bf16[320,1024]{1,0:T(8,128)(2,1)} %bitcast.95), channel_id=1, source_target_pairs={{0,4},{4,0},{8,12},{12,8},{16,20},{20,16},{24,28},{28,24},{1,5},{5... | collective-permute-start | bytes 1966088 | tf_op jit(solution)/shard_map/ppermute | solution.py:758
  3.7 19.4 %collective-permute-start = (bf16[320,1024]{1,0:T(8,128)(2,1)}, bf16[320,1024]{1,0:T(8,128)(2,1)}, u32[]{:S(2)}, u32[]{:S(2)}) collective-permute-start(bf16[320,1024]{1,0:T(8,128)(2,1)} %bitcast.96), channel_id=1, source_target_pairs={{0,8},{4,12},{8,0},{12,4},{16,24},{20,28},{24,16},{28,20},{1,9},{5... | collective-permute-start | bytes 1966088 | tf_op jit(solution)/shard_map/ppermute | solution.py:855
  5.3 17.8 %collective-permute-start.1 = (bf16[320,1024]{1,0:T(8,128)(2,1)}, bf16[320,1024]{1,0:T(8,128)(2,1)}, u32[]{:S(2)}, u32[]{:S(2)}) collective-permute-start(bf16[320,1024]{1,0:T(8,128)(2,1)} %bitcast.97), channel_id=1, source_target_pairs={{8,16},{12,20},{16,8},{20,12},{9,17},{13,21},{17,9},{21,13},{10,18... | collective-permute-start | bytes 1966088 | tf_op jit(solution)/shard_map/ppermute | solution.py:855
  11.7 29.5 %collective-permute-start.7 = (bf16[256,1024]{1,0:T(8,128)(2,1)}, bf16[256,1024]{1,0:T(8,128)(2,1)S(1)}, u32[]{:S(2)}, u32[]{:S(2)}) collective-permute-start(bf16[256,1024]{1,0:T(8,128)(2,1)} %refs_6_.1), channel_id=1, source_target_pairs={{0,2},{1,3},{2,0},{3,1},{4,6},{5,7},{6,4},{7,5},{8,10},{9,11},{10,... | collective-permute-start | bytes 1572872 | tf_op jit(solution)/shard_map/ppermute | solution.py:758
  23.1 18.1 %collective-permute-start.5 = (bf16[320,1024]{1,0:T(8,128)(2,1)}, bf16[320,1024]{1,0:T(8,128)(2,1)}, u32[]{:S(2)}, u32[]{:S(2)}) collective-permute-start(bf16[320,1024]{1,0:T(8,128)(2,1)} %collective-permute-done.refs_2_), channel_id=1, source_target_pairs={{0,4},{4,0},{8,12},{12,8},{16,20},{20,16},{24,28},{28,24},{1,5},{5... | collective-permute-start | bytes 1966088 | tf_op jit(solution)/shard_map/ppermute | solution.py:758
  23.7 17.5 %collective-permute-start.3 = (bf16[320,1024]{1,0:T(8,128)(2,1)}, bf16[320,1024]{1,0:T(8,128)(2,1)}, u32[]{:S(2)}, u32[]{:S(2)}) collective-permute-start(bf16[320,1024]{1,0:T(8,128)(2,1)} %collective-permute-done.refs_2_), channel_id=1, source_target_pairs={{8,16},{12,20},{16,8},{20,12},{9,17},{13,21},{17,9},{21,13},{10,18... | collective-permute-start | bytes 1966088 | tf_op jit(solution)/shard_map/ppermute | solution.py:855
  25.2 21.8 %collective-permute-start.6 = (bf16[128,2816]{1,0:T(8,128)(2,1)}, bf16[128,2816]{1,0:T(8,128)(2,1)}, u32[]{:S(2)}, u32[]{:S(2)}) collective-permute-start(bf16[128,2816]{1,0:T(8,128)(2,1)} %get-tuple-element.162), channel_id=1, source_target_pairs={{0,2},{1,3},{2,0},{3,1},{4,6},{5,7},{6,4},{7,5},{8,10},{9,11},{10,... | collective-permute-start | bytes 2162696 | tf_op jit(solution)/shard_map/ppermute | solution.py:758
  26.8 20.3 %collective-permute-start.4 = (bf16[320,1024]{1,0:T(8,128)(2,1)}, bf16[320,1024]{1,0:T(8,128)(2,1)}, u32[]{:S(2)}, u32[]{:S(2)}) collective-permute-start(bf16[320,1024]{1,0:T(8,128)(2,1)} %collective-permute-done.1), channel_id=1, source_target_pairs={{8,0},{12,4},{16,24},{20,28},{9,1},{13,5},{17,25},{21,29},{10,2},{... | collective-permute-start | bytes 1966088 | tf_op jit(solution)/shard_map/ppermute | solution.py:855
  47.0 22.1 %collective-permute-start.13 = (bf16[256,2816]{1,0:T(8,128)(2,1)S(1)}, bf16[256,2816]{1,0:T(8,128)(2,1)}, u32[]{:S(2)}, u32[]{:S(2)}) collective-permute-start(bf16[256,2816]{1,0:T(8,128)(2,1)S(1)} %copy-done.17), channel_id=1, source_target_pairs={{0,1},{1,0},{2,3},{3,2},{4,5},{5,4},{6,7},{7,6},{8,9},{9,8},{10,11... | collective-permute-start | bytes 4325384 | tf_op jit(solution)/shard_map/ppermute | solution.py:758
  47.1 22.1 %collective-permute-start.12 = (bf16[128,2816]{1,0:T(8,128)(2,1)}, bf16[128,2816]{1,0:T(8,128)(2,1)}, u32[]{:S(2)}, u32[]{:S(2)}) collective-permute-start(bf16[128,2816]{1,0:T(8,128)(2,1)} %get-tuple-element.171), channel_id=1, source_target_pairs={{0,2},{1,3},{2,0},{3,1},{4,6},{5,7},{6,4},{7,5},{8,10},{9,11},{10,... | collective-permute-start | bytes 2162696 | tf_op jit(solution)/shard_map/ppermute | solution.py:758
  48.8 17.0 %collective-permute-start.11 = (bf16[320,1024]{1,0:T(8,128)(2,1)S(1)}, bf16[320,1024]{1,0:T(8,128)(2,1)}, u32[]{:S(2)}, u32[]{:S(2)}) collective-permute-start(bf16[320,1024]{1,0:T(8,128)(2,1)S(1)} %broadcast_select_fusion.7.refs_2_), channel_id=1, source_target_pairs={{0,4},{4,0},{8,12},{12,8},{16,20},{20,16},{24,28},{28,24},{1,5},{5... | collective-permute-start | bytes 1966088 | tf_op jit(solution)/shard_map/ppermute | solution.py:758
  50.4 18.7 %collective-permute-start.10 = (bf16[320,1024]{1,0:T(8,128)(2,1)}, bf16[320,1024]{1,0:T(8,128)(2,1)}, u32[]{:S(2)}, u32[]{:S(2)}) collective-permute-start(bf16[320,1024]{1,0:T(8,128)(2,1)} %collective-permute-done.3), channel_id=1, source_target_pairs={{8,0},{12,4},{16,24},{20,28},{9,1},{13,5},{17,25},{21,29},{10,2},{... | collective-permute-start | bytes 1966088 | tf_op jit(solution)/shard_map/ppermute | solution.py:855
  70.3 18.6 %collective-permute-start.17 = (bf16[704,1024]{1,0:T(8,128)(2,1)}, bf16[704,1024]{1,0:T(8,128)(2,1)}, u32[]{:S(2)}, u32[]{:S(2)}) collective-permute-start(bf16[704,1024]{1,0:T(8,128)(2,1)} %refs_12_.1), channel_id=1, source_target_pairs={{0,1},{1,0},{2,3},{3,2},{4,5},{5,4},{6,7},{7,6},{8,9},{9,8},{10,11... | collective-permute-start | bytes 4325384 | tf_op jit(solution)/shard_map/ppermute | solution.py:758
  70.4 18.5 %collective-permute-start.16 = (bf16[128,2816]{1,0:T(8,128)(2,1)}, bf16[128,2816]{1,0:T(8,128)(2,1)}, u32[]{:S(2)}, u32[]{:S(2)}) collective-permute-start(bf16[128,2816]{1,0:T(8,128)(2,1)} %collective-permute-done.6.refs_8_), channel_id=1, source_target_pairs={{0,1},{1,0},{2,3},{3,2},{4,5},{5,4},{6,7},{7,6},{8,9},{9,8},{10,11... | collective-permute-start | bytes 2162696 | tf_op jit(solution)/shard_map/ppermute | solution.py:758
  70.9 17.0 %collective-permute-start.15 = (bf16[320,1024]{1,0:T(8,128)(2,1)}, bf16[320,1024]{1,0:T(8,128)(2,1)}, u32[]{:S(2)}, u32[]{:S(2)}) collective-permute-start(bf16[320,1024]{1,0:T(8,128)(2,1)} %bitcast.11.refs_4_), channel_id=1, source_target_pairs={{0,2},{1,3},{2,0},{3,1},{4,6},{5,7},{6,4},{7,5},{8,10},{9,11},{10,... | collective-permute-start | bytes 1966088 | tf_op jit(solution)/shard_map/ppermute | solution.py:758
  72.4 16.5 %collective-permute-start.14 = (bf16[320,1024]{1,0:T(8,128)(2,1)S(1)}, bf16[320,1024]{1,0:T(8,128)(2,1)}, u32[]{:S(2)}, u32[]{:S(2)}) collective-permute-start(bf16[320,1024]{1,0:T(8,128)(2,1)S(1)} %broadcast_select_fusion.6.refs_2_), channel_id=1, source_target_pairs={{0,4},{4,0},{8,12},{12,8},{16,20},{20,16},{24,28},{28,24},{1,5},{5... | collective-permute-start | bytes 1966088 | tf_op jit(solution)/shard_map/ppermute | solution.py:758
  93.1 35.3 %collective-permute-start.21 = (bf16[256,3072]{1,0:T(8,128)(2,1)S(1)}, bf16[256,3072]{1,0:T(8,128)(2,1)}, u32[]{:S(2)}, u32[]{:S(2)}) collective-permute-start(bf16[256,3072]{1,0:T(8,128)(2,1)S(1)} %constant_dynamic-update-slice_fusion.refs_7_.w_ref), channel_id=1, source_target_pairs={{0,2},{1,3},{2,0},{3,1},{4,6},{5,7},{6,4},{7,5},{8,10},{9,11},{10,... | collective-permute-start | bytes 4718600 | tf_op jit(solution)/shard_map/ppermute | solution.py:758
  93.8 21.8 %collective-permute-start.18 = (bf16[128,2816]{1,0:T(8,128)(2,1)}, bf16[128,2816]{1,0:T(8,128)(2,1)}, u32[]{:S(2)}, u32[]{:S(2)}) collective-permute-start(bf16[128,2816]{1,0:T(8,128)(2,1)} %collective-permute-done.12.refs_9_), channel_id=1, source_target_pairs={{0,1},{1,0},{2,3},{3,2},{4,5},{5,4},{6,7},{7,6},{8,9},{9,8},{10,11... | collective-permute-start | bytes 2162696 | tf_op jit(solution)/shard_map/ppermute | solution.py:758
  94.7 20.8 %collective-permute-start.20 = (bf16[256,1024]{1,0:T(8,128)(2,1)S(1)}, bf16[256,1024]{1,0:T(8,128)(2,1)S(1)}, u32[]{:S(2)}, u32[]{:S(2)}) collective-permute-start(bf16[256,1024]{1,0:T(8,128)(2,1)S(1)} %copy-done.15), channel_id=1, source_target_pairs={{0,1},{1,0},{2,3},{3,2},{4,5},{5,4},{6,7},{7,6},{8,9},{9,8},{10,11... | collective-permute-start | bytes 1572872 | tf_op jit(solution)/shard_map/ppermute | solution.py:758
  95.2 20.3 %collective-permute-start.19 = (bf16[256,1024]{1,0:T(8,128)(2,1)S(1)}, bf16[256,1024]{1,0:T(8,128)(2,1)}, u32[]{:S(2)}, u32[]{:S(2)}) collective-permute-start(bf16[256,1024]{1,0:T(8,128)(2,1)S(1)} %copy-done.13), channel_id=1, source_target_pairs={{0,1},{1,0},{2,3},{3,2},{4,5},{5,4},{6,7},{7,6},{8,9},{9,8},{10,11... | collective-permute-start | bytes 1572872 | tf_op jit(solution)/shard_map/ppermute | solution.py:758
  111.2 15.2 %all-to-all-start = ((bf16[8,160,128]{2,1,0:T(8,128)(2,1)}), bf16[8,160,128]{2,1,0:T(8,128)(2,1)S(1)}, u32[]{:S(2)}, u32[]{:S(2)}) async-start(bf16[8,160,128]{2,1,0:T(8,128)(2,1)} %get-tuple-element.204), calls=%async_computation | async-start | bytes 655360 | tf_op jit(solution)/shard_map/all_to_all | solution.py:861
  204.7 17.0 %collective-permute-start.23 = (bf16[320,1024]{1,0:T(8,128)(2,1)}, bf16[320,1024]{1,0:T(8,128)(2,1)}, u32[]{:S(2)}, u32[]{:S(2)}) collective-permute-start(bf16[320,1024]{1,0:T(8,128)(2,1)} %get-tuple-element.224), channel_id=1, source_target_pairs={{0,2},{1,3},{2,0},{3,1},{4,6},{5,7},{6,4},{7,5},{8,10},{9,11},{10,... | collective-permute-start | bytes 1966088 | tf_op jit(solution)/shard_map/ppermute | solution.py:758
  214.2 39.9 %collective-permute-start.27 = (bf16[2,128,2816]{2,1,0:T(8,128)(2,1)}, bf16[2,128,2816]{2,1,0:T(8,128)(2,1)}, u32[]{:S(2)}, u32[]{:S(2)}) collective-permute-start(bf16[2,128,2816]{2,1,0:T(8,128)(2,1)} %get-tuple-element.232), channel_id=1, source_target_pairs={{0,4},{4,0},{8,12},{12,8},{16,20},{20,16},{24,28},{28,24},{1,5},{5... | collective-permute-start | bytes 4325384 | tf_op jit(solution)/shard_map/ppermute | solution.py:758
  227.1 30.9 %collective-permute-start.28 = (bf16[256,3072]{1,0:T(8,128)(2,1)S(1)}, bf16[256,3072]{1,0:T(8,128)(2,1)}, u32[]{:S(2)}, u32[]{:S(2)}) collective-permute-start(bf16[256,3072]{1,0:T(8,128)(2,1)S(1)} %constant_dynamic-update-slice_fusion.refs_7_.w_ref), channel_id=1, source_target_pairs={{0,1},{1,0},{2,3},{3,2},{4,5},{5,4},{6,7},{7,6},{8,9},{9,8},{10,11... | collective-permute-start | bytes 4718600 | tf_op jit(solution)/shard_map/ppermute | solution.py:758
  227.1 23.3 %collective-permute-start.26 = (bf16[352,1024]{1,0:T(8,128)(2,1)}, bf16[352,1024]{1,0:T(8,128)(2,1)}, u32[]{:S(2)}, u32[]{:S(2)}) collective-permute-start(bf16[352,1024]{1,0:T(8,128)(2,1)} %get-tuple-element.233), channel_id=1, source_target_pairs={{0,8},{4,12},{8,0},{12,4},{16,24},{20,28},{24,16},{28,20},{1,9},{5... | collective-permute-start | bytes 2162696 | tf_op jit(solution)/shard_map/ppermute | solution.py:758
  228.0 30.0 %all-to-all-start.2 = ((bf16[8,320,128]{2,1,0:T(8,128)(2,1)}), bf16[8,320,128]{2,1,0:T(8,128)(2,1)}, u32[]{:S(2)}, u32[]{:S(2)}) async-start(bf16[8,320,128]{2,1,0:T(8,128)(2,1)} %get-tuple-element.231), calls=%async_computation.2 | async-start | bytes 1310720 | tf_op jit(solution)/shard_map/all_to_all | solution.py:861
  252.8 22.7 %collective-permute-start.30 = (bf16[176,1024]{1,0:T(8,128)(2,1)}, bf16[176,1024]{1,0:T(8,128)(2,1)}, u32[]{:S(2)}, u32[]{:S(2)}) collective-permute-start(bf16[176,1024]{1,0:T(8,128)(2,1)} %get-tuple-element.241), channel_id=1, source_target_pairs={{0,4},{4,0},{8,12},{12,8},{16,20},{20,16},{24,28},{28,24},{1,5},{5... | collective-permute-start | bytes 1081352 | tf_op jit(solution)/shard_map/ppermute | solution.py:758
  254.1 30.7 %collective-permute-start.34 = (bf16[2,256,1024]{2,1,0:T(8,128)(2,1)}, bf16[2,256,1024]{2,1,0:T(8,128)(2,1)}, u32[]{:S(2)}, u32[]{:S(2)}) collective-permute-start(bf16[2,256,1024]{2,1,0:T(8,128)(2,1)} %get-tuple-element.246), channel_id=1, source_target_pairs={{0,1},{1,0},{2,3},{3,2},{4,5},{5,4},{6,7},{7,6},{8,9},{9,8},{10,11... | collective-permute-start | bytes 3145736 | tf_op jit(solution)/shard_map/ppermute | solution.py:758
  256.8 29.6 %collective-permute-start.31 = (bf16[2,64,2816]{2,1,0:T(8,128)(2,1)}, bf16[2,64,2816]{2,1,0:T(8,128)(2,1)}, u32[]{:S(2)}, u32[]{:S(2)}) collective-permute-start(bf16[2,64,2816]{2,1,0:T(8,128)(2,1)} %get-tuple-element.247), channel_id=1, source_target_pairs={{0,8},{4,12},{8,0},{12,4},{16,24},{20,28},{24,16},{28,20},{1,9},{5... | collective-permute-start | bytes 2162696 | tf_op jit(solution)/shard_map/ppermute | solution.py:758
  276.6 28.6 %collective-permute-start.32 = (bf16[88,1024]{1,0:T(8,128)(2,1)S(1)}, bf16[88,1024]{1,0:T(8,128)(2,1)S(1)}, u32[]{:S(2)}, u32[]{:S(2)}) collective-permute-start(bf16[88,1024]{1,0:T(8,128)(2,1)S(1)} %get-tuple-element.250), channel_id=1, source_target_pairs={{0,16},{4,20},{8,24},{12,28},{16,0},{20,4},{24,8},{28,12},{1,17},{... | collective-permute-start | bytes 540680 | tf_op jit(solution)/shard_map/ppermute | solution.py:758
  283.1 39.7 %collective-permute-start.36 = (bf16[256,3072]{1,0:T(8,128)(2,1)}, bf16[256,3072]{1,0:T(8,128)(2,1)}, u32[]{:S(2)}, u32[]{:S(2)}) collective-permute-start(bf16[256,3072]{1,0:T(8,128)(2,1)} %collective-permute-done.21.refs_9_), channel_id=1, source_target_pairs={{0,1},{1,0},{2,3},{3,2},{4,5},{5,4},{6,7},{7,6},{8,9},{9,8},{10,11... | collective-permute-start | bytes 4718600 | tf_op jit(solution)/shard_map/ppermute | solution.py:758
  283.1 28.5 %collective-permute-start.29 = (bf16[320,1024]{1,0:T(8,128)(2,1)}, bf16[320,1024]{1,0:T(8,128)(2,1)}, u32[]{:S(2)}, u32[]{:S(2)}) collective-permute-start(bf16[320,1024]{1,0:T(8,128)(2,1)} %get-tuple-element.239), channel_id=1, source_target_pairs={{0,2},{1,3},{2,0},{3,1},{4,6},{5,7},{6,4},{7,5},{8,10},{9,11},{10,... | collective-permute-start | bytes 1966088 | tf_op jit(solution)/shard_map/ppermute | solution.py:758
  288.5 25.7 %collective-permute-start.33 = (bf16[2,32,2816]{2,1,0:T(8,128)(2,1)}, bf16[2,32,2816]{2,1,0:T(8,128)(2,1)}, u32[]{:S(2)}, u32[]{:S(2)}) collective-permute-start(bf16[2,32,2816]{2,1,0:T(8,128)(2,1)} %get-tuple-element.254), channel_id=1, source_target_pairs={{0,16},{4,20},{8,24},{12,28},{16,0},{20,4},{24,8},{28,12},{1,17},{... | collective-permute-start | bytes 1081352 | tf_op jit(solution)/shard_map/ppermute | solution.py:758
  288.8 31.2 %collective-permute-start.35 = (bf16[256,1024]{1,0:T(8,128)(2,1)S(1)}, bf16[256,1024]{1,0:T(8,128)(2,1)}, u32[]{:S(2)}, u32[]{:S(2)}) collective-permute-start(bf16[256,1024]{1,0:T(8,128)(2,1)S(1)} %get-tuple-element.258), channel_id=1, source_target_pairs={{0,2},{1,3},{2,0},{3,1},{4,6},{5,7},{6,4},{7,5},{8,10},{9,11},{10,... | collective-permute-start | bytes 1572872 | tf_op jit(solution)/shard_map/ppermute | solution.py:758
  307.3 51.5 %all-to-all-start.4 = ((bf16[8,2,160,128]{3,2,1,0:T(8,128)(2,1)}), bf16[8,2,160,128]{3,2,1,0:T(8,128)(2,1)S(1)}, u32[]{:S(2)}, u32[]{:S(2)}) async-start(bf16[8,2,160,128]{3,2,1,0:T(8,128)(2,1)} %pad_maximum_fusion.9), calls=%async_computation.4 | async-start | bytes 1310720 | tf_op jit(solution)/shard_map/all_to_all | solution.py:861
  315.3 23.6 %collective-permute-start.38 = (bf16[32,2816]{1,0:T(8,128)(2,1)S(1)}, bf16[32,2816]{1,0:T(8,128)(2,1)S(1)}, u32[]{:S(2)}, u32[]{:S(2)}) collective-permute-start(bf16[32,2816]{1,0:T(8,128)(2,1)S(1)} %slice_bitcast_fusion), channel_id=1, source_target_pairs={{0,2},{1,3},{2,0},{3,1},{4,6},{5,7},{6,4},{7,5},{8,10},{9,11},{10,... | collective-permute-start | bytes 540680 | tf_op jit(solution)/shard_map/ppermute | solution.py:758
  317.1 21.9 %collective-permute-start.37 = (bf16[88,1024]{1,0:T(8,128)(2,1)S(1)}, bf16[88,1024]{1,0:T(8,128)(2,1)S(1)}, u32[]{:S(2)}, u32[]{:S(2)}) collective-permute-start(bf16[88,1024]{1,0:T(8,128)(2,1)S(1)} %add_convert_fusion.14), channel_id=1, source_target_pairs={{0,16},{4,20},{8,24},{12,28},{16,0},{20,4},{24,8},{28,12},{1,17},{... | collective-permute-start | bytes 540680 | tf_op jit(solution)/shard_map/ppermute | solution.py:758
  321.2 17.8 %collective-permute-start.39 = (bf16[128,1024]{1,0:T(8,128)(2,1)S(1)}, bf16[128,1024]{1,0:T(8,128)(2,1)S(1)}, u32[]{:S(2)}, u32[]{:S(2)}) collective-permute-start(bf16[128,1024]{1,0:T(8,128)(2,1)S(1)} %get-tuple-element.268), channel_id=1, source_target_pairs={{0,8},{4,12},{8,0},{12,4},{16,24},{20,28},{24,16},{28,20},{1,9},{5... | collective-permute-start | bytes 786440 | tf_op jit(solution)/shard_map/ppermute | solution.py:758
  339.0 19.4 %collective-permute-start.41 = (bf16[32,5632]{1,0:T(8,128)(2,1)S(1)}, bf16[32,5632]{1,0:T(8,128)(2,1)S(1)}, u32[]{:S(2)}, u32[]{:S(2)}) collective-permute-start(bf16[32,5632]{1,0:T(8,128)(2,1)S(1)} %pad_maximum_fusion.13), channel_id=1, source_target_pairs={{0,16},{4,20},{8,24},{12,28},{16,0},{20,4},{24,8},{28,12},{1,17},{... | collective-permute-start | bytes 1081352 | tf_op jit(solution)/shard_map/ppermute | solution.py:758
  339.7 18.9 %collective-permute-start.40 = (bf16[176,1024]{1,0:T(8,128)(2,1)S(1)}, bf16[176,1024]{1,0:T(8,128)(2,1)S(1)}, u32[]{:S(2)}, u32[]{:S(2)}) collective-permute-start(bf16[176,1024]{1,0:T(8,128)(2,1)S(1)} %pad_maximum_fusion.12), channel_id=1, source_target_pairs={{0,4},{4,0},{8,12},{12,8},{16,20},{20,16},{24,28},{28,24},{1,5},{5... | collective-permute-start | bytes 1081352 | tf_op jit(solution)/shard_map/ppermute | solution.py:758
  341.3 16.5 %collective-permute-start.42 = (bf16[64,1024]{1,0:T(8,128)(2,1)S(1)}, bf16[64,1024]{1,0:T(8,128)(2,1)S(1)}, u32[]{:S(2)}, u32[]{:S(2)}) collective-permute-start(bf16[64,1024]{1,0:T(8,128)(2,1)S(1)} %get-tuple-element.280), channel_id=1, source_target_pairs={{0,4},{4,0},{8,12},{12,8},{16,20},{20,16},{24,28},{28,24},{1,5},{5... | collective-permute-start | bytes 393224 | tf_op jit(solution)/shard_map/ppermute | solution.py:758
  358.6 20.9 %collective-permute-start.45 = (bf16[64,5632]{1,0:T(8,128)(2,1)S(1)}, bf16[64,5632]{1,0:T(8,128)(2,1)}, u32[]{:S(2)}, u32[]{:S(2)}) collective-permute-start(bf16[64,5632]{1,0:T(8,128)(2,1)S(1)} %pad_maximum_fusion.7), channel_id=1, source_target_pairs={{0,8},{4,12},{8,0},{12,4},{16,24},{20,28},{24,16},{28,20},{1,9},{5... | collective-permute-start | bytes 2162696 | tf_op jit(solution)/shard_map/ppermute | solution.py:758
  372.6 67.8 %all-to-all-start.3 = ((bf16[8,640,128]{2,1,0:T(8,128)(2,1)}), bf16[8,640,128]{2,1,0:T(8,128)(2,1)S(1)}, u32[]{:S(2)}, u32[]{:S(2)}) async-start(bf16[8,640,128]{2,1,0:T(8,128)(2,1)} %pad_maximum_fusion.3), calls=%async_computation.3 | async-start | bytes 2621440 | tf_op jit(solution)/shard_map/all_to_all | solution.py:861
  376.4 40.8 %collective-permute-start.47 = (bf16[352,1024]{1,0:T(8,128)(2,1)S(1)}, bf16[352,1024]{1,0:T(8,128)(2,1)S(1)}, u32[]{:S(2)}, u32[]{:S(2)}) collective-permute-start(bf16[352,1024]{1,0:T(8,128)(2,1)S(1)} %pad_maximum_fusion.6), channel_id=1, source_target_pairs={{0,8},{4,12},{8,0},{12,4},{16,24},{20,28},{24,16},{28,20},{1,9},{5... | collective-permute-start | bytes 2162696 | tf_op jit(solution)/shard_map/ppermute | solution.py:758
  380.8 69.8 %collective-permute-start.54 = (bf16[128,5632]{1,0:T(8,128)(2,1)S(1)}, bf16[128,5632]{1,0:T(8,128)(2,1)}, u32[]{:S(2)}, u32[]{:S(2)}) collective-permute-start(bf16[128,5632]{1,0:T(8,128)(2,1)S(1)} %pad_maximum_fusion.2), channel_id=1, source_target_pairs={{0,4},{4,0},{8,12},{12,8},{16,20},{20,16},{24,28},{28,24},{1,5},{5... | collective-permute-start | bytes 4325384 | tf_op jit(solution)/shard_map/ppermute | solution.py:758
  382.3 35.0 %collective-permute-start.48 = (bf16[32,1024]{1,0:T(8,128)(2,1)S(1)}, bf16[32,1024]{1,0:T(8,128)(2,1)S(1)}, u32[]{:S(2)}, u32[]{:S(2)}) collective-permute-start(bf16[32,1024]{1,0:T(8,128)(2,1)S(1)} %add_convert_fusion.19), channel_id=1, source_target_pairs={{0,16},{4,20},{8,24},{12,28},{16,0},{20,4},{24,8},{28,12},{1,17},{... | collective-permute-start | bytes 196616 | tf_op jit(solution)/shard_map/ppermute | solution.py:758
  384.7 34.1 %collective-permute-start.46 = (bf16[256,384]{1,0:T(8,128)(2,1)S(1)}, bf16[256,384]{1,0:T(8,128)(2,1)S(1)}, u32[]{:S(2)}, u32[]{:S(2)}) collective-permute-start(bf16[256,384]{1,0:T(8,128)(2,1)S(1)} %fusion.14), channel_id=1, source_target_pairs={{0,2},{1,3},{2,0},{3,1},{4,6},{5,7},{6,4},{7,5},{8,10},{9,11},{10,... | collective-permute-start | bytes 589832 | tf_op jit(solution)/shard_map/ppermute | solution.py:758
  440.6 18.1 %collective-permute-start.52 = (bf16[4,256,384]{2,1,0:T(8,128)(2,1)S(1)}, bf16[4,256,384]{2,1,0:T(8,128)(2,1)}, u32[]{:S(2)}, u32[]{:S(2)}) collective-permute-start(bf16[4,256,384]{2,1,0:T(8,128)(2,1)S(1)} %pad_maximum_fusion.4.own_ref), channel_id=1, source_target_pairs={{0,8},{4,12},{8,0},{12,4},{16,24},{20,28},{24,16},{28,20},{1,9},{5... | collective-permute-start | bytes 2359304 | tf_op jit(solution)/shard_map/ppermute | solution.py:758
  (47 other events, 586.9 us)

commit v4 on v3

--- a/solution.py
+++ b/solution.py
@@ -70,7 +70,7 @@
     arrays = 1 + max(array for array, _ in layout)
     w_refs = refs[3 : 3 + arrays]
     code_ref = refs[3 + arrays]
-    qa_ref, ka_ref, va_ref, h1_ref, gain_row = refs[4 + arrays + aliased :]
+    qa_ref, ka_ref, va_ref, h1_ref, own_ref, gain_row = refs[4 + arrays + aliased :]
     piece_rows = w_refs[0].shape[1]
     spans = []
     for piece, (array, index) in enumerate(layout):
@@ -100,12 +100,16 @@
         jnp.where(same & ~padded, 0.0, BLOCKED),
         jnp.where((place >= HD - 4) & (place < HD - 1), 1.0, 0.0),
     ).astype(bf16)
-    ones = jnp.where(place < 3, 1.0, 0.0).astype(bf16)
+    ones = jnp.ones((rows, LANES), bf16)
+    product = q.astype(f32) * k.astype(f32)
     for head in range(heads):
         own = lane // HD == head
         qa_ref[head] = jnp.where(own, q, q_table)
         ka_ref[head] = jnp.where(own, k, k_table)
         va_ref[head] = jnp.where(own, v, ones)
+        score = jnp.sum(jnp.where(own, product, 0.0), axis=-1, keepdims=True)
+        score = jnp.where(padded, score, 4.0 * BLOCKED)
+        own_ref[head] = jnp.broadcast_to(score, (rows, LANES))
 
 
 def project(slot, w_rows, slots, heads, segments, x, layout, arrays, codes, previous):
@@ -113,7 +117,8 @@
     total = rows * slots
     head_spec = pl.BlockSpec((heads, rows, LANES), lambda i, s, w: (0, s[0], 0))
     shapes = [jax.ShapeDtypeStruct((heads, total, LANES), bf16)] * 3 + [
-        jax.ShapeDtypeStruct((total, width), bf16)
+        jax.ShapeDtypeStruct((total, width), bf16),
+        jax.ShapeDtypeStruct((heads, total, LANES), f32),
     ]
     extra = () if previous is None else tuple(previous)
     first = 4 + len(arrays)
@@ -126,7 +131,8 @@
             + [pl.BlockSpec(a.shape, lambda i, s, w: (0, 0, 0)) for a in arrays]
             + [pl.BlockSpec((rows, 1), lambda i, s, w: (s[0], 0))]
             + [anywhere()] * len(extra),
-            out_specs=[head_spec] * 3 + [pl.BlockSpec((rows, width), lambda i, s, w: (s[0], 0))],
+            out_specs=[head_spec] * 3
+            + [pl.BlockSpec((rows, width), lambda i, s, w: (s[0], 0)), head_spec],
             scratch_shapes=[pltpu.VMEM((8, width), f32)],
         ),
         out_shape=shapes,
@@ -137,93 +143,126 @@
     )(slot, w_rows, x, *arrays, codes, *extra)
 
 
-def forward_kernel(heads, q_ref, k_near, v_near, k_ref, v_ref, att_ref, sum_ref, qb_ref):
+def forward_kernel(
+    heads, step, q_ref, own_ref, v_near, k_ref, v_ref,
+    att_ref, sum_ref, qb_ref, weight_ref, scores, tops, acc,
+):
     pack, rows = q_ref.shape[1], q_ref.shape[3]
     span = pack * rows
+    total = k_ref.shape[1]
     lane = lane_ids(span)
+    folds = step // LANES
+
+    def queries(head):
+        return q_ref[head].reshape(span, LANES)
+
+    def find(head, at):
+        found = mm_nt(queries(head), k_ref[head, at, :])
+        scores[head, :, at] = found
+        top = tops[head]
+        for fold in range(folds):
+            top = jnp.maximum(top, found[:, fold * LANES : (fold + 1) * LANES])
+        tops[head] = top
+
+    def mix(head, at):
+        top = tops[head]
+        shifted = scores[head, :, at] - jnp.concatenate([top] * folds, axis=1)
+        acc[head] += mm(jnp.exp(shifted).astype(bf16), v_ref[head, at, :])
+
+    def settle(head):
+        top = jnp.max(tops[head], axis=-1, keepdims=True)
+        tops[head] = jnp.maximum(
+            jnp.broadcast_to(top, (span, LANES)), own_ref[head].reshape(span, LANES)
+        )
+
+    def sweep(first, second):
+        def run(number, carry):
+            at = pl.ds(pl.multiple_of(number * step, step), step)
+            if second is not None:
+                mix(second, at)
+            if first is not None:
+                find(first, at)
+            return carry
+
+        lax.fori_loop(0, total // step, run, 0)
+        if first is not None:
+            settle(first)
+
+    tops[...] = jnp.full_like(tops, 4.0 * BLOCKED)
+    acc[...] = jnp.zeros_like(acc)
+    for head in range(heads + 1):
+        sweep(head if head < heads else None, head - 1 if head > 0 else None)
     merged = None
     for head in range(heads):
-        q = q_ref[head].reshape(span, LANES)
-        key = k_near[head].reshape(span, LANES)
-        value = v_near[head].reshape(span, LANES)
         own = lane // HD == head
         other = HD if head == 0 else 0
-        scores = mm_nt(q, k_ref[head])
-        q_wide = q.astype(f32)
-        padded = q_wide[:, other + HD - 1 : other + HD] > 0.5
-        own_score = jnp.sum(jnp.where(own, q_wide * key.astype(f32), 0.0), axis=-1, keepdims=True)
-        top = jnp.max(scores, axis=-1, keepdims=True)
-        top = jnp.where(padded, jnp.maximum(top, own_score), top)
-        weights = jnp.exp(scores - top).astype(bf16)
-        mixed = mm(weights, v_ref[head])
-        own_weight = jnp.where(padded, jnp.exp(own_score - top), 0.0).astype(bf16).astype(f32)
-        mixed = mixed + own_weight * value.astype(f32)
-        total = mixed[:, other : other + 1]
-        log_total = top + jnp.log(total)
-        mixed = mixed * (1.0 / total)
+        top = tops[head]
+        value = v_near[head].reshape(span, LANES).astype(f32)
+        own_weight = jnp.exp(own_ref[head].reshape(span, LANES) - top).astype(bf16).astype(f32)
+        mixed = acc[head] + own_weight * value
+        swapped = pltpu.roll(mixed, HD, axis=1)
+        weight_sum = jnp.where(own, swapped, mixed)
+        inverse = 1.0 / weight_sum
+        weight_ref[head] = (own_weight * inverse).astype(bf16).reshape(pack, 1, rows, LANES)
+        log_total = top + jnp.log(weight_sum)
+        mixed = mixed * inverse
         merged = mixed if merged is None else jnp.where(own, mixed, merged)
-        filled = q_wide
+        filled = queries(head).astype(f32)
         for place, part in enumerate(split3(-log_total)):
             filled = jnp.where(lane == other + HD - 4 + place, part, filled)
         qb_ref[head] = filled.astype(bf16).reshape(pack, 1, rows, LANES)
-    att_ref[...] = merged.astype(bf16).reshape(pack, rows, LANES)
+    att_ref[...] = merged.astype(bf16).reshape(pack, 1, rows, LANES)
     sum_ref[...] = merged.reshape(pack, 1, rows, LANES)
 
 
-def forward_body(heads, aliased, *refs):
-    forward_kernel(heads, *(refs[:5] + refs[5 + aliased :]))
-
-
-def attend(qa, ka, va, part, parts, slots, span, previous):
+def attend(qa, ka, va, own, parts, slots):
     heads, total, _ = qa.shape
     rows = total // slots // parts
-    pack = max(1, min(slots, 320 // rows))
     shape = (heads, slots, parts, rows, LANES)
-    view = [a.reshape(shape) for a in (qa, ka, va)]
-    begin = span[0] // pack
-    block = pl.BlockSpec((heads, pack, 1, rows, LANES), lambda i: (0, begin + i, part, 0, 0))
+    view = [a.reshape(shape) for a in (qa, own, va)]
+    block = pl.BlockSpec((heads, slots, 1, rows, LANES), lambda i: (0, 0, i, 0, 0))
     whole = pl.BlockSpec(ka.shape, lambda i: (0, 0, 0))
-    extra = tuple(previous)
+    flat = pl.BlockSpec((slots, 1, rows, LANES), lambda i: (0, i, 0, 0))
+    span = slots * rows
     return pl.pallas_call(
-        functools.partial(forward_body, heads, len(extra)),
-        grid=((span[1] - span[0]) // pack,),
-        in_specs=[block, block, block, whole, whole] + [anywhere()] * len(extra),
-        out_specs=[
-            pl.BlockSpec((pack, rows, LANES), lambda i: (begin + i, 0, 0)),
-            pl.BlockSpec((pack, 1, rows, LANES), lambda i: (begin + i, part, 0, 0)),
-            block,
-        ],
+        functools.partial(forward_kernel, heads, 512),
+        grid=(parts,),
+        in_specs=[block, block, block, whole, whole],
+        out_specs=[flat, flat, block, block],
         out_shape=[
-            jax.ShapeDtypeStruct((slots, rows, LANES), bf16),
+            jax.ShapeDtypeStruct(shape[1:], bf16),
             jax.ShapeDtypeStruct(shape[1:], f32),
             jax.ShapeDtypeStruct(shape, bf16),
+            jax.ShapeDtypeStruct(shape, bf16),
         ],
-        input_output_aliases={5 + i: 3 - len(extra) + i for i in range(len(extra))},
+        scratch_shapes=[
+            pltpu.VMEM((heads, span, total), f32),
+            pltpu.VMEM((heads, span, LANES), f32),
+            pltpu.VMEM((heads, span, LANES), f32),
+        ],
         compiler_params=params(),
         cost_estimate=cost(
-            8 * heads * total * total * LANES // parts,
-            4 * heads * total * LANES,
-            heads * total * total // parts,
+            8 * heads * total * total * LANES, 4 * heads * total * LANES, heads * total * total
         ),
         name="attend",
-    )(*view, ka, va, *extra)
+    )(*view, ka, va)
 
 
 def backward_kernel(heads, part, parts, tile, *refs):
     first, last = part == 0, part == parts - 1
-    qb_ref, k_ref, v_ref = refs[:3]
+    qb_ref, k_ref, v_ref, weight_ref = refs[:4]
     if first:
-        sum_ref, grad_ref, kv_ref, dq_ref, gb_ref, dk_acc, dv_acc = refs[3:]
+        sum_ref, grad_ref, kv_ref, dq_ref, gb_ref, dk_acc, dv_acc = refs[4:]
         dq_acc = dq_ref
     elif last:
-        gb_ref, dq_in, kv_ref, dq_ref, dq_acc, dk_acc, dv_acc = refs[3:]
+        gb_ref, dq_in, kv_ref, dq_ref, dq_acc, dk_acc, dv_acc = refs[4:]
     else:
-        gb_ref, dq_in, kv_ref, dq_ref, dk_acc, dv_acc = refs[3:]
+        gb_ref, dq_in, kv_ref, dq_ref, dk_acc, dv_acc = refs[4:]
         dq_acc = dq_ref
     slots, rows = k_ref.shape[1], k_ref.shape[3]
     total = qb_ref.shape[1]
     span = slots * rows
-    pack = max(1, min(slots, 320 // rows))
+    pack = slots
     if first:
         block_rows = grad_ref.shape[1]
         lane = lane_ids(block_rows)
@@ -271,9 +310,7 @@
         lax.fori_loop(0, total // tile, step, 0)
         dk_all, dv_all = None, None
         for head in range(heads):
-            other = HD if head == 0 else 0
             own = lane // HD == head
-            counted = own | ((lane >= other + HD - 4) & (lane < other + HD - 1))
             starts = [
                 slot * (total // slots) + part * rows
                 for slot in range(index * pack, (index + 1) * pack)
@@ -282,12 +319,9 @@
             g = jnp.concatenate([gb_ref[head, b : b + rows, :] for b in starts], axis=0).astype(f32)
             k = k_ref[head, keys].reshape(width, LANES).astype(f32)
             v = v_ref[head, keys].reshape(width, LANES).astype(f32)
-            padded = q[:, other + HD - 1 : other + HD] > 0.5
-            score = jnp.sum(jnp.where(counted, q * k, 0.0), axis=-1, keepdims=True)
-            weight = jnp.where(padded, jnp.exp(score), 0.0)
+            weight = weight_ref[head, keys].reshape(width, LANES).astype(f32)
             inner = jnp.sum(v * g, axis=-1, keepdims=True)
             score_grad = (weight * inner).astype(bf16).astype(f32)
-            weight = weight.astype(bf16).astype(f32)
             dk = dk_acc[head] + score_grad * q
             dv = dv_acc[head] + weight * g
             dq = score_grad * k
@@ -308,14 +342,14 @@
             dq_ref[slot] = (dq * HD**-0.5).astype(bf16)
 
 
-def attend_back(qb, ka, va, part, parts, slots, sums, grads, state):
+def attend_back(qb, ka, va, weights, part, parts, slots, sums, grads, state):
     heads, total, _ = ka.shape
     rows = total // slots // parts
     first, last = part == 0, part == parts - 1
     shape = (heads, slots, parts, rows, LANES)
     near = pl.BlockSpec((heads, slots, 1, rows, LANES), lambda i: (0, 0, part, 0, 0))
     wide = pl.BlockSpec((heads, total, LANES), lambda i: (0, 0, 0))
-    pack = max(1, min(slots, 320 // rows))
+    pack = slots
     accumulator = pltpu.VMEM((heads, pack * rows, LANES), f32)
     if first:
         inputs = [sums, grads]
@@ -341,7 +375,7 @@
     return pl.pallas_call(
         functools.partial(backward_kernel, heads, part, parts, 512),
         grid=(1,),
-        in_specs=[wide, near, near] + in_specs,
+        in_specs=[wide, near, near, near] + in_specs,
         out_specs=out_specs,
         out_shape=out_shape,
         scratch_shapes=scratch,
@@ -352,7 +386,7 @@
             heads * total * total // parts,
         ),
         name="attend_back",
-    )(qb, ka.reshape(shape), va.reshape(shape), *inputs)
+    )(qb, ka.reshape(shape), va.reshape(shape), weights.reshape(shape), *inputs)
 
 
 def own_kernel(halves, *refs):
@@ -849,6 +883,10 @@
     return jnp.sum(
         jnp.where(positions[:, None] == order_row[None, :], packed_code[None, :], 0), axis=1
     ).reshape(total, 1)
+
+
+def parts_of(total):
+    return max(2, total // 1280)
 
 
 def move_chain(array, pairs):
@@ -994,25 +1032,15 @@
     else:
         for number, block in enumerate(x_blocks):
             state = project_block(number, block, state)
-    qa, ka, va, h1 = state
-
-    att_first, sums, qb = attend(qa, ka, va, 0, 2, slots, (0, slots), ())
-    middle_slot = slots // 2
+    qa, ka, va, h1, own_scores = state
+
+    att, sums, qb, own_weights = attend(qa, ka, va, own_scores, parts_of(slots * rows), slots)
     if direct:
         qkv_x = flip(after(qkv_weight, qa), "fsdp", 2)
         up_xc2 = flip(after(up_x2, qa), "fsdp", 1)
         output_c = flip(after(output_weight, qa), "fsdp", 1)
         output_xc = flip(after(output_x, qa), "fsdp", 1)
-        qb, _, _, _ = lax.optimization_barrier((qb, up_xc2, output_c, output_xc))
-    att_turned = turn(att_first)
-    att_second, sums, qb = attend(
-        qa, ka, va, 1, 2, slots, (0, middle_slot), (sums, qb)
-    )
-    if direct:
-        qb, _, _ = lax.optimization_barrier((qb, att_turned, qkv_x))
-    att_second, sums, qb = attend(
-        qa, ka, va, 1, 2, slots, (middle_slot, slots), (att_second, sums, qb)
-    )
+        att = lax.optimization_barrier((att, up_xc2, output_c, output_xc))[0]
     if direct:
         output_pieces = [output_weight, output_c, output_x, output_xc]
         output_entries = [(0, p, 0, p, shard_rows, 0, 0) for p in range(4)]
@@ -1035,7 +1063,9 @@
         ]
         hidden = gate_weight.shape[1]
         ff_entries = [(i, i, 0, 0, width, 0, 0) for i in range(3)]
-    att_parts = [att_turned, turn(att_second)]
+    att_parts = [turn(att.reshape(slots, rows, LANES))]
+    if direct:
+        x, _ = lax.optimization_barrier((x, qkv_x))
     total = rows * slots
     sums = sums.reshape(total, LANES)
     qb = qb.reshape(heads, total, LANES)
@@ -1064,7 +1094,7 @@
     og = out_terms(w_rows, att, branch, halves)
     grad_blocks = turn(d_att)
     parts = 4
-    back = functools.partial(attend_back, qb, ka, va)
+    back = functools.partial(attend_back, qb, ka, va, own_weights)
     if direct:
         qkv_c = flip(after(qkv_weight, d_att), "fsdp", 1)
         output_r = Reduction(*og, line)

time: 472 us -> 459 us (0.972)
  Pallas kernels: 200 us -> 187 us
  starting transfers between devices: 84.3 us -> 77.8 us
  waiting for transfers between devices: 109 us -> 114 us
    pallas_call x3 -> x1, Pallas kernels: 34.6 us -> 26.4 us  [attend(): pl.pallas_call(functools.partial(forward_kernel, heads, 512), grid=(parts...]
    pallas_call x4, Pallas kernels: 65.6 us -> 58.5 us  [attend_back(): pl.pallas_call(functools.partial(backward_kernel, heads, part, parts, 512...]
    all_to_all x5 -> x4, waiting for transfers between devices: 9.26 us -> 14.3 us  [turn(): lax.all_to_all(blocks, 'seq', split_axis=0, concat_axis=0, tiled=True)]
    all_to_all x5 -> x4, starting transfers between devices: 22.2 us -> 18.2 us  [turn(): lax.all_to_all(blocks, 'seq', split_axis=0, concat_axis=0, tiled=True)]
  transfers between devices with their start and end apart: 60 -> 59, of which waited for: 20 -> 19; matrix products, arithmetic and copies ran while one was open for 13% -> 14% of each run, Pallas kernels for 31% -> 31%
where the time goes in v4:
time: 459 us; the launch traced here: 451 us
  Pallas kernels  187 us (41%)
  waiting for transfers between devices  114 us (25%)
  starting transfers between devices  77.8 us (17%)
  other arithmetic  51.9 us (11%)
  local copies, waits for them, and re-layouts  18.5 us (4%)
    ppermute x50, waiting for transfers between devices, flip(): return lax.ppermute(values, axis, [(i, i ^ delta) for i in range(count)])  91.3 us
    pallas_call x4, Pallas kernels, attend_back(): pl.pallas_call(functools.partial(backward_kernel, heads, part, parts, 512...  58.5 us
    ppermute x50, starting transfers between devices, flip(): return lax.ppermute(values, axis, [(i, i ^ delta) for i in range(count)])  52.2 us
    pallas_call x8, Pallas kernels, project(): pl.pallas_call(functools.partial(project_kernel, heads, segments, layout,...  35.1 us
    pallas_call x1, Pallas kernels, main_stage(): pl.pallas_call(functools.partial(main_kernel, groups, halves, entries, le...  32.6 us
    pallas_call x1, Pallas kernels, attend(): pl.pallas_call(functools.partial(forward_kernel, heads, 512), grid=(parts...  26.4 us
    convert_element_type x14, other arithmetic, add_low(): return (a.astype(f32) + b.astype(f32)).astype(bf16)  21.9 us
    all_to_all x4, starting transfers between devices, turn(): lax.all_to_all(blocks, 'seq', split_axis=0, concat_axis=0, tiled=True)  18.2 us
  transfers between devices with their start and end apart: 59, of which 19 were waited for; matrix products, arithmetic and copies ran while one was open for 14% of the time, Pallas kernels for 31%

profile of v4, /device:TPU:0, one launch (start us, length us, event | category | flops | bytes accessed | tf_op | source)
XLA Modules:
  0.0 451.3 jit_solution(4590405758649950163)
XLA Ops:
  0.7 3.0 collective-permute-start.2
  15.2 4.2 collective-permute-done.8
  28.0 2.9 select_reduce_fusion
  32.9 4.4 project.8
  37.3 4.5 project.9
  41.8 5.2 %collective-permute-done.4 = bf16[320,1024]{1,0:T(8,128)(2,1)} collective-permute-done((bf16[320,1024]{1,0:T(8,128)(2,1)}, bf16[320,1024]{1,0:T(8,128)(2,1)}, u32[]{:S(2)}, u32[]{:S(2)}) %collective-permute-start.4) | collective-permute-done | bytes 655392 | tf_op jit(solution)/shard_map/ppermute | solution.py:893
  51.9 4.4 project.10
  56.2 4.4 project.11
  60.6 4.4 project.12
  65.8 3.3 collective-permute-done.10
  75.1 4.4 project.13
  79.5 4.4 project.14
  83.8 4.1 collective-permute-done.15.refs_5_
  88.9 4.5 project.15
  94.5 26.4 %attend.1 = (bf16[8,2,160,128]{3,2,1,0:T(8,128)(2,1)}, f32[8,2,160,128]{3,2,1,0:T(8,128)}, bf16[2,8,2,160,128]{4,3,2,1,0:T(8,128)(2,1)}, bf16[2,8,2,160,128]{4,3,2,1,0:T(8,128)(2,1)}) custom-call(bf16[2,8,2,160,128]{4,3,2,1,0:T(8,128)(2,1)} %bitcast.80, f32[2,8,2,160,128]{4,3,2,1,0:T(8,128)} %bitcast.79, bf16[2,8,2,160,128]{4,3,2,1,0:T(8,128)(2,1)} %bitcast.85, ...), custom_call_target="tpu_custom_call" | custom-call | flops 13421772800 | bytes 2621440 | tf_op jit(solution)/shard_map/attend/pallas_call | solution.py:227
  122.5 4.1 all-to-all-start
  130.9 13.4 %all-to-all-done.refs_1_ = bf16[8,320,128]{2,1,0:T(8,128)(2,1)S(1)} async-done(((bf16[8,320,128]{2,1,0:T(8,128)(2,1)}), bf16[8,320,128]{2,1,0:T(8,128)(2,1)S(1)}, u32[]{:S(2)}, u32[]{:S(2)}) %all-to-all-start) | async-done | bytes 655392 | tf_op jit(solution)/shard_map/all_to_all | solution.py:899
  145.1 5.2 %pre_stage.1 = (f32[320,1024]{1,0:T(8,128)}, bf16[320,1024]{1,0:T(8,128)(2,1)}, bf16[320,1024]{1,0:T(8,128)(2,1)}) custom-call(s32[4]{0:T(128)} %iota_xor_fusion.1.refs_1_.refs_0_.w_rows, bf16[8,320,128]{2,1,0:T(8,128)(2,1)} %copy-done.10, bf16[320,1024]{1,0:T(8,128)(2,1)} %bitcast.95, bf16[1,1024]{1,0:T(2,128)(2,1)} %get-tuple-element.374.refs_3_.refs_5_, ...), custom_call_target="tpu_custom_call" | custom-call | flops 671088640 | bytes 2097152 | tf_op jit(solution)/shard_map/pre_stage/pallas_call | solution.py:495
  152.4 13.5 %collective-permute-done.22.refs_3_ = bf16[320,1024]{1,0:T(8,128)(2,1)S(1)} collective-permute-done((bf16[320,1024]{1,0:T(8,128)(2,1)}, bf16[320,1024]{1,0:T(8,128)(2,1)S(1)}, u32[]{:S(2)}, u32[]{:S(2)}) %collective-permute-start.22) | collective-permute-done | bytes 655392 | tf_op jit(solution)/shard_map/ppermute | solution.py:792
  166.8 32.6 %main_stage.1 = (f32[320,1024]{1,0:T(8,128)}, bf16[320,1024]{1,0:T(8,128)(2,1)}, f32[320,1024]{1,0:T(8,128)}, bf16[320,1024]{1,0:T(8,128)(2,1)}, bf16[2,256,2816...) custom-call(s32[4]{0:T(128)} %iota_xor_fusion.1.refs_1_.refs_0_.w_ro, ...), custom_call_target="tpu_custom_call" | custom-call | flops 16609443840 | bytes 17301504 | tf_op jit(solution)/shard_map/main_stage/pallas_call | solution.py:598
  201.5 3.6 collective-permute-done.24
  205.1 4.4 add_convert_fusion
  211.4 3.5 fusion.3
  217.0 5.4 %post_stage.1 = (f32[320,1024]{1,0:T(8,128)}, bf16[320,1024]{1,0:T(8,128)(2,1)}, bf16[8,320,128]{2,1,0:T(8,128)(2,1)}) custom-call(s32[4]{0:T(128)} %iota_xor_fusion.1.refs_1_.refs_0_.w_rows, f32[320,1024]{1,0:T(8,128)} %get-tuple-element.222.refs_1_, f32[320,1024]{1,0:T(8,128)} %get-tuple-element.229.refs_2_, ...), custom_call_target="tpu_custom_call" | custom-call | flops 671088640 | bytes 4194304 | tf_op jit(solution)/shard_map/post_stage/pallas_call | solution.py:661
  222.6 6.0 %all-to-all-start.1 = ((bf16[8,320,128]{2,1,0:T(8,128)(2,1)}), bf16[8,320,128]{2,1,0:T(8,128)(2,1)}, u32[]{:S(2)}, u32[]{:S(2)}) async-start(bf16[8,320,128]{2,1,0:T(8,128)(2,1)} %get-tuple-element.237), calls=%async_computation.1 | async-start | bytes 1310720 | tf_op jit(solution)/shard_map/all_to_all | solution.py:899
  229.4 3.9 out_terms.1
  233.3 13.8 %collective-permute-done.26 = bf16[352,1024]{1,0:T(8,128)(2,1)} collective-permute-done((bf16[352,1024]{1,0:T(8,128)(2,1)}, bf16[352,1024]{1,0:T(8,128)(2,1)}, u32[]{:S(2)}, u32[]{:S(2)}) %collective-permute-start.26) | collective-permute-done | bytes 720928 | tf_op jit(solution)/shard_map/ppermute | solution.py:792
  249.6 2.8 add_convert_fusion.2
  253.3 15.7 %attend_back.4 = (bf16[8,2,80,128]{3,2,1,0:T(8,128)(2,1)}, f32[2,2560,128]{2,1,0:T(8,128)}, bf16[2,2560,128]{2,1,0:T(8,128)(2,1)}) custom-call(bf16[2,2560,128]{2,1,0:T(8,128)(2,1)} %bitcast.106, bf16[2,8,4,80,128]{4,3,2,1,0:T(8,128)(2,1)} %bitcast.81, bf16[2,8,4,80,128]{4,3,2,1,0:T(8,128)(2,1)} %bitcast.86, bf16[2,8,4,80,128]{4,3,2,1,0:T(8,128)(2,1)} %bitcast.110, ...), custom_call_target="tpu_custom_call" | custom-call | flops 8388608000 | bytes 7864320 | tf_op jit(solution)/shard_map/attend_back/pallas_call | solution.py:375
  270.2 5.5 %collective-permute-start.32 = (bf16[88,1024]{1,0:T(8,128)(2,1)S(1)}, bf16[88,1024]{1,0:T(8,128)(2,1)S(1)}, u32[]{:S(2)}, u32[]{:S(2)}) collective-permute-start(bf16[88,1024]{1,0:T(8,128)(2,1)S(1)} %get-tuple-element.256), channel_id=1, source_target_pairs={{0,16},{4,20},{8,24},{12,28},{16,0},{20,4},{24,8},{28,12},{1,17},{... | collective-permute-start | bytes 540680 | tf_op jit(solution)/shard_map/ppermute | solution.py:792
  281.8 14.5 %attend_back.5 = (bf16[8,2,80,128]{3,2,1,0:T(8,128)(2,1)}, f32[2,2560,128]{2,1,0:T(8,128)}) custom-call(bf16[2,2560,128]{2,1,0:T(8,128)(2,1)} %bitcast.107, bf16[2,8,4,80,128]{4,3,2,1,0:T(8,128)(2,1)} %bitcast.82, bf16[2,8,4,80,128]{4,3,2,1,0:T(8,128)(2,1)} %bitcast.87, bf16[2,8,4,80,128]{4,3,2,1,0:T(8,128)(2,1)} %bitcast.111, ...), custom_call_target="tpu_custom_call" | custom-call | flops 8388608000 | bytes 7864320 | tf_op jit(solution)/shard_map/attend_back/pallas_call | solution.py:375
  298.3 4.1 all-to-all-start.3
  302.4 2.7 fusion.6
  307.7 2.9 collective-permute-start.37
  313.4 14.5 %attend_back.6 = (bf16[8,2,80,128]{3,2,1,0:T(8,128)(2,1)}, f32[2,2560,128]{2,1,0:T(8,128)}) custom-call(bf16[2,2560,128]{2,1,0:T(8,128)(2,1)} %bitcast.108, bf16[2,8,4,80,128]{4,3,2,1,0:T(8,128)(2,1)} %bitcast.83, bf16[2,8,4,80,128]{4,3,2,1,0:T(8,128)(2,1)} %bitcast.88, bf16[2,8,4,80,128]{4,3,2,1,0:T(8,128)(2,1)} %bitcast.112, ...), custom_call_target="tpu_custom_call" | custom-call | flops 8388608000 | bytes 7864320 | tf_op jit(solution)/shard_map/attend_back/pallas_call | solution.py:375
  330.9 13.8 %attend_back.7 = (bf16[8,2,80,128]{3,2,1,0:T(8,128)(2,1)}, bf16[8,320,128]{2,1,0:T(8,128)(2,1)}) custom-call(bf16[2,2560,128]{2,1,0:T(8,128)(2,1)} %bitcast.109, bf16[2,8,4,80,128]{4,3,2,1,0:T(8,128)(2,1)} %bitcast.84, bf16[2,8,4,80,128]{4,3,2,1,0:T(8,128)(2,1)} %bitcast.89, bf16[2,8,4,80,128]{4,3,2,1,0:T(8,128)(2,1)} %bitcast.113, ...), custom_call_target="tpu_custom_call" | custom-call | flops 8388608000 | bytes 7864320 | tf_op jit(solution)/shard_map/attend_back/pallas_call | solution.py:375
  346.1 8.5 %own_terms.1 = (bf16[2,256,384]{2,1,0:T(8,128)(2,1)}, bf16[2,256,384]{2,1,0:T(8,128)(2,1)}) custom-call(s32[4]{0:T(128)} %iota_xor_fusion.1.refs_1_.refs_0_.w_rows, bf16[8,4,80,1024]{3,2,1,0:T(8,128)(2,1)} %bitcast.78, bf16[8,320,128]{2,1,0:T(8,128)(2,1)} %get-tuple-element.290.refs_2_, bf16[8,2,80,128]{3,2,1,0:T(8,128)(2,1)} %get-tuple-element.244.refs_3_, ...), custom_call_target="tpu_custom_call" | custom-call | flops 2013265920 | bytes 5242880 | tf_op jit(solution)/shard_map/own_terms/pallas_call | solution.py:427
  355.8 2.7 collective-permute-start.44
  359.6 4.0 all-to-all-start.2
  372.7 31.4 %collective-permute-done.47 = bf16[352,1024]{1,0:T(8,128)(2,1)S(1)} collective-permute-done((bf16[352,1024]{1,0:T(8,128)(2,1)S(1)}, bf16[352,1024]{1,0:T(8,128)(2,1)S(1)}, u32[]{:S(2)}, u32[]{:S(2)}) %collective-permute-start.47) | collective-permute-done | bytes 720928 | tf_op jit(solution)/shard_map/ppermute | solution.py:792
  408.7 5.2 %collective-permute-done.50 = bf16[64,1024]{1,0:T(8,128)(2,1)S(1)} collective-permute-done((bf16[64,1024]{1,0:T(8,128)(2,1)S(1)}, bf16[64,1024]{1,0:T(8,128)(2,1)S(1)}, u32[]{:S(2)}, u32[]{:S(2)}) %collective-permute-start.50) | collective-permute-done | bytes 131104 | tf_op jit(solution)/shard_map/ppermute | solution.py:792
  415.5 2.4 collective-permute-done.49
  420.6 2.8 collective-permute-done.53
  424.5 2.9 collective-permute-done.51
  429.9 7.7 %last_stage.1 = f32[320,1024]{1,0:T(8,128)} custom-call(s32[4]{0:T(128)} %iota_xor_fusion.1.refs_1_.refs_0_.w_rows, bf16[8,320,128]{2,1,0:T(8,128)(2,1)} %get-tuple-element.342.refs_1_, bf16[8,2,160,128]{3,2,1,0:T(8,128)(2,1)} %copy-done.11, bf16[8,2,160,128]{3,2,1,0:T(8,128)(2,1)} %bitcast.98, bf16[320,1024]{1,0:T(8,128)(2,1)} %bitcast.96, ...), custom_call_target="tpu_custom_call" | custom-call | flops 2013265920 | bytes 6291456 | tf_op jit(solution)/shard_map/last_stage/pallas_call | solution.py:747
  439.9 2.9 multiply_reduce_fusion
  443.3 2.4 collective-permute-done.52.other_ref
  445.7 3.7 finish_own.1
  (244 shorter events, 102.6 us)
Async XLA Ops:
  0.7 22.4 %collective-permute-start.2 = (bf16[320,1024]{1,0:T(8,128)(2,1)}, bf16[320,1024]{1,0:T(8,128)(2,1)}, u32[]{:S(2)}, u32[]{:S(2)}) collective-permute-start(bf16[320,1024]{1,0:T(8,128)(2,1)} %bitcast.91), channel_id=1, source_target_pairs={{0,4},{4,0},{8,12},{12,8},{16,20},{20,16},{24,28},{28,24},{1,5},{5... | collective-permute-start | bytes 1966088 | tf_op jit(solution)/shard_map/ppermute | solution.py:792
  3.7 19.3 %collective-permute-start = (bf16[320,1024]{1,0:T(8,128)(2,1)}, bf16[320,1024]{1,0:T(8,128)(2,1)}, u32[]{:S(2)}, u32[]{:S(2)}) collective-permute-start(bf16[320,1024]{1,0:T(8,128)(2,1)} %bitcast.92), channel_id=1, source_target_pairs={{0,8},{4,12},{8,0},{12,4},{16,24},{20,28},{24,16},{28,20},{1,9},{5... | collective-permute-start | bytes 1966088 | tf_op jit(solution)/shard_map/ppermute | solution.py:893
  5.3 17.8 %collective-permute-start.1 = (bf16[320,1024]{1,0:T(8,128)(2,1)}, bf16[320,1024]{1,0:T(8,128)(2,1)}, u32[]{:S(2)}, u32[]{:S(2)}) collective-permute-start(bf16[320,1024]{1,0:T(8,128)(2,1)} %bitcast.93), channel_id=1, source_target_pairs={{8,16},{12,20},{16,8},{20,12},{9,17},{13,21},{17,9},{21,13},{10,18... | collective-permute-start | bytes 1966088 | tf_op jit(solution)/shard_map/ppermute | solution.py:893
  11.6 30.1 %collective-permute-start.7 = (bf16[256,1024]{1,0:T(8,128)(2,1)}, bf16[256,1024]{1,0:T(8,128)(2,1)S(1)}, u32[]{:S(2)}, u32[]{:S(2)}) collective-permute-start(bf16[256,1024]{1,0:T(8,128)(2,1)} %refs_6_.1), channel_id=1, source_target_pairs={{0,2},{1,3},{2,0},{3,1},{4,6},{5,7},{6,4},{7,5},{8,10},{9,11},{10,... | collective-permute-start | bytes 1572872 | tf_op jit(solution)/shard_map/ppermute | solution.py:792
  23.1 18.7 %collective-permute-start.5 = (bf16[320,1024]{1,0:T(8,128)(2,1)}, bf16[320,1024]{1,0:T(8,128)(2,1)}, u32[]{:S(2)}, u32[]{:S(2)}) collective-permute-start(bf16[320,1024]{1,0:T(8,128)(2,1)} %collective-permute-done.refs_2_), channel_id=1, source_target_pairs={{0,4},{4,0},{8,12},{12,8},{16,20},{20,16},{24,28},{28,24},{1,5},{5... | collective-permute-start | bytes 1966088 | tf_op jit(solution)/shard_map/ppermute | solution.py:792
  23.6 18.1 %collective-permute-start.3 = (bf16[320,1024]{1,0:T(8,128)(2,1)}, bf16[320,1024]{1,0:T(8,128)(2,1)}, u32[]{:S(2)}, u32[]{:S(2)}) collective-permute-start(bf16[320,1024]{1,0:T(8,128)(2,1)} %collective-permute-done.refs_2_), channel_id=1, source_target_pairs={{8,16},{12,20},{16,8},{20,12},{9,17},{13,21},{17,9},{21,13},{10,18... | collective-permute-start | bytes 1966088 | tf_op jit(solution)/shard_map/ppermute | solution.py:893
  25.2 21.8 %collective-permute-start.6 = (bf16[128,2816]{1,0:T(8,128)(2,1)}, bf16[128,2816]{1,0:T(8,128)(2,1)}, u32[]{:S(2)}, u32[]{:S(2)}) collective-permute-start(bf16[128,2816]{1,0:T(8,128)(2,1)} %get-tuple-element.165), channel_id=1, source_target_pairs={{0,2},{1,3},{2,0},{3,1},{4,6},{5,7},{6,4},{7,5},{8,10},{9,11},{10,... | collective-permute-start | bytes 2162696 | tf_op jit(solution)/shard_map/ppermute | solution.py:792
  26.7 20.3 %collective-permute-start.4 = (bf16[320,1024]{1,0:T(8,128)(2,1)}, bf16[320,1024]{1,0:T(8,128)(2,1)}, u32[]{:S(2)}, u32[]{:S(2)}) collective-permute-start(bf16[320,1024]{1,0:T(8,128)(2,1)} %collective-permute-done.1), channel_id=1, source_target_pairs={{8,0},{12,4},{16,24},{20,28},{9,1},{13,5},{17,25},{21,29},{10,2},{... | collective-permute-start | bytes 1966088 | tf_op jit(solution)/shard_map/ppermute | solution.py:893
  47.0 22.1 %collective-permute-start.13 = (bf16[256,2816]{1,0:T(8,128)(2,1)S(1)}, bf16[256,2816]{1,0:T(8,128)(2,1)}, u32[]{:S(2)}, u32[]{:S(2)}) collective-permute-start(bf16[256,2816]{1,0:T(8,128)(2,1)S(1)} %copy-done.19), channel_id=1, source_target_pairs={{0,1},{1,0},{2,3},{3,2},{4,5},{5,4},{6,7},{7,6},{8,9},{9,8},{10,11... | collective-permute-start | bytes 4325384 | tf_op jit(solution)/shard_map/ppermute | solution.py:792
  47.0 22.1 %collective-permute-start.12 = (bf16[128,2816]{1,0:T(8,128)(2,1)}, bf16[128,2816]{1,0:T(8,128)(2,1)}, u32[]{:S(2)}, u32[]{:S(2)}) collective-permute-start(bf16[128,2816]{1,0:T(8,128)(2,1)} %get-tuple-element.175), channel_id=1, source_target_pairs={{0,2},{1,3},{2,0},{3,1},{4,6},{5,7},{6,4},{7,5},{8,10},{9,11},{10,... | collective-permute-start | bytes 2162696 | tf_op jit(solution)/shard_map/ppermute | solution.py:792
  48.8 17.0 %collective-permute-start.11 = (bf16[320,1024]{1,0:T(8,128)(2,1)S(1)}, bf16[320,1024]{1,0:T(8,128)(2,1)}, u32[]{:S(2)}, u32[]{:S(2)}) collective-permute-start(bf16[320,1024]{1,0:T(8,128)(2,1)S(1)} %broadcast_select_fusion.7.refs_2_), channel_id=1, source_target_pairs={{0,4},{4,0},{8,12},{12,8},{16,20},{20,16},{24,28},{28,24},{1,5},{5... | collective-permute-start | bytes 1966088 | tf_op jit(solution)/shard_map/ppermute | solution.py:792
  50.4 18.7 %collective-permute-start.10 = (bf16[320,1024]{1,0:T(8,128)(2,1)}, bf16[320,1024]{1,0:T(8,128)(2,1)}, u32[]{:S(2)}, u32[]{:S(2)}) collective-permute-start(bf16[320,1024]{1,0:T(8,128)(2,1)} %collective-permute-done.3), channel_id=1, source_target_pairs={{8,0},{12,4},{16,24},{20,28},{9,1},{13,5},{17,25},{21,29},{10,2},{... | collective-permute-start | bytes 1966088 | tf_op jit(solution)/shard_map/ppermute | solution.py:893
  70.3 18.6 %collective-permute-start.17 = (bf16[704,1024]{1,0:T(8,128)(2,1)}, bf16[704,1024]{1,0:T(8,128)(2,1)}, u32[]{:S(2)}, u32[]{:S(2)}) collective-permute-start(bf16[704,1024]{1,0:T(8,128)(2,1)} %refs_12_.1), channel_id=1, source_target_pairs={{0,1},{1,0},{2,3},{3,2},{4,5},{5,4},{6,7},{7,6},{8,9},{9,8},{10,11... | collective-permute-start | bytes 4325384 | tf_op jit(solution)/shard_map/ppermute | solution.py:792
  70.4 18.5 %collective-permute-start.16 = (bf16[128,2816]{1,0:T(8,128)(2,1)}, bf16[128,2816]{1,0:T(8,128)(2,1)}, u32[]{:S(2)}, u32[]{:S(2)}) collective-permute-start(bf16[128,2816]{1,0:T(8,128)(2,1)} %collective-permute-done.6.refs_8_), channel_id=1, source_target_pairs={{0,1},{1,0},{2,3},{3,2},{4,5},{5,4},{6,7},{7,6},{8,9},{9,8},{10,11... | collective-permute-start | bytes 2162696 | tf_op jit(solution)/shard_map/ppermute | solution.py:792
  70.9 17.0 %collective-permute-start.15 = (bf16[320,1024]{1,0:T(8,128)(2,1)}, bf16[320,1024]{1,0:T(8,128)(2,1)}, u32[]{:S(2)}, u32[]{:S(2)}) collective-permute-start(bf16[320,1024]{1,0:T(8,128)(2,1)} %bitcast.11.refs_4_), channel_id=1, source_target_pairs={{0,2},{1,3},{2,0},{3,1},{4,6},{5,7},{6,4},{7,5},{8,10},{9,11},{10,... | collective-permute-start | bytes 1966088 | tf_op jit(solution)/shard_map/ppermute | solution.py:792
  72.4 16.5 %collective-permute-start.14 = (bf16[320,1024]{1,0:T(8,128)(2,1)S(1)}, bf16[320,1024]{1,0:T(8,128)(2,1)}, u32[]{:S(2)}, u32[]{:S(2)}) collective-permute-start(bf16[320,1024]{1,0:T(8,128)(2,1)S(1)} %broadcast_select_fusion.6.refs_2_), channel_id=1, source_target_pairs={{0,4},{4,0},{8,12},{12,8},{16,20},{20,16},{24,28},{28,24},{1,5},{5... | collective-permute-start | bytes 1966088 | tf_op jit(solution)/shard_map/ppermute | solution.py:792
  93.4 28.3 %collective-permute-start.18 = (bf16[128,2816]{1,0:T(8,128)(2,1)}, bf16[128,2816]{1,0:T(8,128)(2,1)}, u32[]{:S(2)}, u32[]{:S(2)}) collective-permute-start(bf16[128,2816]{1,0:T(8,128)(2,1)} %collective-permute-done.12.refs_9_), channel_id=1, source_target_pairs={{0,1},{1,0},{2,3},{3,2},{4,5},{5,4},{6,7},{7,6},{8,9},{9,8},{10,11... | collective-permute-start | bytes 2162696 | tf_op jit(solution)/shard_map/ppermute | solution.py:792
  93.4 27.5 %collective-permute-start.20 = (bf16[256,1024]{1,0:T(8,128)(2,1)S(1)}, bf16[256,1024]{1,0:T(8,128)(2,1)S(1)}, u32[]{:S(2)}, u32[]{:S(2)}) collective-permute-start(bf16[256,1024]{1,0:T(8,128)(2,1)S(1)} %copy-done.16), channel_id=1, source_target_pairs={{0,1},{1,0},{2,3},{3,2},{4,5},{5,4},{6,7},{7,6},{8,9},{9,8},{10,11... | collective-permute-start | bytes 1572872 | tf_op jit(solution)/shard_map/ppermute | solution.py:792
  93.9 27.0 %collective-permute-start.19 = (bf16[256,1024]{1,0:T(8,128)(2,1)S(1)}, bf16[256,1024]{1,0:T(8,128)(2,1)S(1)}, u32[]{:S(2)}, u32[]{:S(2)}) collective-permute-start(bf16[256,1024]{1,0:T(8,128)(2,1)S(1)} %copy-done.14), channel_id=1, source_target_pairs={{0,1},{1,0},{2,3},{3,2},{4,5},{5,4},{6,7},{7,6},{8,9},{9,8},{10,11... | collective-permute-start | bytes 1572872 | tf_op jit(solution)/shard_map/ppermute | solution.py:792
  94.0 36.8 %collective-permute-start.21 = (bf16[256,3072]{1,0:T(8,128)(2,1)S(1)}, bf16[256,3072]{1,0:T(8,128)(2,1)}, u32[]{:S(2)}, u32[]{:S(2)}) collective-permute-start(bf16[256,3072]{1,0:T(8,128)(2,1)S(1)} %constant_dynamic-update-slice_fusion.refs_7_.w_ref), channel_id=1, source_target_pairs={{0,2},{1,3},{2,0},{3,1},{4,6},{5,7},{6,4},{7,5},{8,10},{9,11},{10,... | collective-permute-start | bytes 4718600 | tf_op jit(solution)/shard_map/ppermute | solution.py:792
  122.5 21.7 %all-to-all-start = ((bf16[8,320,128]{2,1,0:T(8,128)(2,1)}), bf16[8,320,128]{2,1,0:T(8,128)(2,1)S(1)}, u32[]{:S(2)}, u32[]{:S(2)}) async-start(bf16[8,320,128]{2,1,0:T(8,128)(2,1)} %bitcast.100), calls=%async_computation | async-start | bytes 1310720 | tf_op jit(solution)/shard_map/all_to_all | solution.py:899
  150.3 15.6 %collective-permute-start.22 = (bf16[320,1024]{1,0:T(8,128)(2,1)}, bf16[320,1024]{1,0:T(8,128)(2,1)S(1)}, u32[]{:S(2)}, u32[]{:S(2)}) collective-permute-start(bf16[320,1024]{1,0:T(8,128)(2,1)} %get-tuple-element.223.refs_2_), channel_id=1, source_target_pairs={{0,2},{1,3},{2,0},{3,1},{4,6},{5,7},{6,4},{7,5},{8,10},{9,11},{10,... | collective-permute-start | bytes 1966088 | tf_op jit(solution)/shard_map/ppermute | solution.py:792
  200.0 17.0 %collective-permute-start.23 = (bf16[320,1024]{1,0:T(8,128)(2,1)}, bf16[320,1024]{1,0:T(8,128)(2,1)}, u32[]{:S(2)}, u32[]{:S(2)}) collective-permute-start(bf16[320,1024]{1,0:T(8,128)(2,1)} %get-tuple-element.230), channel_id=1, source_target_pairs={{0,2},{1,3},{2,0},{3,1},{4,6},{5,7},{6,4},{7,5},{8,10},{9,11},{10,... | collective-permute-start | bytes 1966088 | tf_op jit(solution)/shard_map/ppermute | solution.py:792
  209.5 40.0 %collective-permute-start.27 = (bf16[2,128,2816]{2,1,0:T(8,128)(2,1)}, bf16[2,128,2816]{2,1,0:T(8,128)(2,1)}, u32[]{:S(2)}, u32[]{:S(2)}) collective-permute-start(bf16[2,128,2816]{2,1,0:T(8,128)(2,1)} %get-tuple-element.238), channel_id=1, source_target_pairs={{0,4},{4,0},{8,12},{12,8},{16,20},{20,16},{24,28},{28,24},{1,5},{5... | collective-permute-start | bytes 4325384 | tf_op jit(solution)/shard_map/ppermute | solution.py:792
  222.4 30.9 %collective-permute-start.28 = (bf16[256,3072]{1,0:T(8,128)(2,1)S(1)}, bf16[256,3072]{1,0:T(8,128)(2,1)}, u32[]{:S(2)}, u32[]{:S(2)}) collective-permute-start(bf16[256,3072]{1,0:T(8,128)(2,1)S(1)} %constant_dynamic-update-slice_fusion.refs_7_.w_ref), channel_id=1, source_target_pairs={{0,1},{1,0},{2,3},{3,2},{4,5},{5,4},{6,7},{7,6},{8,9},{9,8},{10,11... | collective-permute-start | bytes 4718600 | tf_op jit(solution)/shard_map/ppermute | solution.py:792
  222.5 24.6 %collective-permute-start.26 = (bf16[352,1024]{1,0:T(8,128)(2,1)}, bf16[352,1024]{1,0:T(8,128)(2,1)}, u32[]{:S(2)}, u32[]{:S(2)}) collective-permute-start(bf16[352,1024]{1,0:T(8,128)(2,1)} %get-tuple-element.239), channel_id=1, source_target_pairs={{0,8},{4,12},{8,0},{12,4},{16,24},{20,28},{24,16},{28,20},{1,9},{5... | collective-permute-start | bytes 2162696 | tf_op jit(solution)/shard_map/ppermute | solution.py:792
  222.6 30.7 %all-to-all-start.1 = ((bf16[8,320,128]{2,1,0:T(8,128)(2,1)}), bf16[8,320,128]{2,1,0:T(8,128)(2,1)}, u32[]{:S(2)}, u32[]{:S(2)}) async-start(bf16[8,320,128]{2,1,0:T(8,128)(2,1)} %get-tuple-element.237), calls=%async_computation.1 | async-start | bytes 1310720 | tf_op jit(solution)/shard_map/all_to_all | solution.py:899
  249.4 19.6 %collective-permute-start.30 = (bf16[176,1024]{1,0:T(8,128)(2,1)}, bf16[176,1024]{1,0:T(8,128)(2,1)}, u32[]{:S(2)}, u32[]{:S(2)}) collective-permute-start(bf16[176,1024]{1,0:T(8,128)(2,1)} %get-tuple-element.247), channel_id=1, source_target_pairs={{0,4},{4,0},{8,12},{12,8},{16,20},{20,16},{24,28},{28,24},{1,5},{5... | collective-permute-start | bytes 1081352 | tf_op jit(solution)/shard_map/ppermute | solution.py:792
  249.6 27.6 %collective-permute-start.34 = (bf16[2,256,1024]{2,1,0:T(8,128)(2,1)}, bf16[2,256,1024]{2,1,0:T(8,128)(2,1)}, u32[]{:S(2)}, u32[]{:S(2)}) collective-permute-start(bf16[2,256,1024]{2,1,0:T(8,128)(2,1)} %get-tuple-element.252), channel_id=1, source_target_pairs={{0,1},{1,0},{2,3},{3,2},{4,5},{5,4},{6,7},{7,6},{8,9},{9,8},{10,11... | collective-permute-start | bytes 3145736 | tf_op jit(solution)/shard_map/ppermute | solution.py:792
  252.3 26.6 %collective-permute-start.31 = (bf16[2,64,2816]{2,1,0:T(8,128)(2,1)}, bf16[2,64,2816]{2,1,0:T(8,128)(2,1)}, u32[]{:S(2)}, u32[]{:S(2)}) collective-permute-start(bf16[2,64,2816]{2,1,0:T(8,128)(2,1)} %get-tuple-element.253), channel_id=1, source_target_pairs={{0,8},{4,12},{8,0},{12,4},{16,24},{20,28},{24,16},{28,20},{1,9},{5... | collective-permute-start | bytes 2162696 | tf_op jit(solution)/shard_map/ppermute | solution.py:792
  270.2 26.0 %collective-permute-start.32 = (bf16[88,1024]{1,0:T(8,128)(2,1)S(1)}, bf16[88,1024]{1,0:T(8,128)(2,1)S(1)}, u32[]{:S(2)}, u32[]{:S(2)}) collective-permute-start(bf16[88,1024]{1,0:T(8,128)(2,1)S(1)} %get-tuple-element.256), channel_id=1, source_target_pairs={{0,16},{4,20},{8,24},{12,28},{16,0},{20,4},{24,8},{28,12},{1,17},{... | collective-permute-start | bytes 540680 | tf_op jit(solution)/shard_map/ppermute | solution.py:792
  275.7 37.7 %collective-permute-start.36 = (bf16[256,3072]{1,0:T(8,128)(2,1)}, bf16[256,3072]{1,0:T(8,128)(2,1)}, u32[]{:S(2)}, u32[]{:S(2)}) collective-permute-start(bf16[256,3072]{1,0:T(8,128)(2,1)} %collective-permute-done.21.refs_9_), channel_id=1, source_target_pairs={{0,1},{1,0},{2,3},{3,2},{4,5},{5,4},{6,7},{7,6},{8,9},{9,8},{10,11... | collective-permute-start | bytes 4718600 | tf_op jit(solution)/shard_map/ppermute | solution.py:792
  275.7 26.7 %collective-permute-start.29 = (bf16[320,1024]{1,0:T(8,128)(2,1)}, bf16[320,1024]{1,0:T(8,128)(2,1)}, u32[]{:S(2)}, u32[]{:S(2)}) collective-permute-start(bf16[320,1024]{1,0:T(8,128)(2,1)} %get-tuple-element.245), channel_id=1, source_target_pairs={{0,2},{1,3},{2,0},{3,1},{4,6},{5,7},{6,4},{7,5},{8,10},{9,11},{10,... | collective-permute-start | bytes 1966088 | tf_op jit(solution)/shard_map/ppermute | solution.py:792
  280.9 24.1 %collective-permute-start.33 = (bf16[2,32,2816]{2,1,0:T(8,128)(2,1)}, bf16[2,32,2816]{2,1,0:T(8,128)(2,1)}, u32[]{:S(2)}, u32[]{:S(2)}) collective-permute-start(bf16[2,32,2816]{2,1,0:T(8,128)(2,1)} %get-tuple-element.260), channel_id=1, source_target_pairs={{0,16},{4,20},{8,24},{12,28},{16,0},{20,4},{24,8},{28,12},{1,17},{... | collective-permute-start | bytes 1081352 | tf_op jit(solution)/shard_map/ppermute | solution.py:792
  281.2 29.4 %collective-permute-start.35 = (bf16[256,1024]{1,0:T(8,128)(2,1)S(1)}, bf16[256,1024]{1,0:T(8,128)(2,1)}, u32[]{:S(2)}, u32[]{:S(2)}) collective-permute-start(bf16[256,1024]{1,0:T(8,128)(2,1)S(1)} %get-tuple-element.264), channel_id=1, source_target_pairs={{0,2},{1,3},{2,0},{3,1},{4,6},{5,7},{6,4},{7,5},{8,10},{9,11},{10,... | collective-permute-start | bytes 1572872 | tf_op jit(solution)/shard_map/ppermute | solution.py:792
  298.3 47.8 %all-to-all-start.3 = ((bf16[8,2,160,128]{3,2,1,0:T(8,128)(2,1)}), bf16[8,2,160,128]{3,2,1,0:T(8,128)(2,1)S(1)}, u32[]{:S(2)}, u32[]{:S(2)}) async-start(bf16[8,2,160,128]{3,2,1,0:T(8,128)(2,1)} %pad_maximum_fusion.9), calls=%async_computation.3 | async-start | bytes 1310720 | tf_op jit(solution)/shard_map/all_to_all | solution.py:899
  306.2 21.7 %collective-permute-start.38 = (bf16[32,2816]{1,0:T(8,128)(2,1)S(1)}, bf16[32,2816]{1,0:T(8,128)(2,1)S(1)}, u32[]{:S(2)}, u32[]{:S(2)}) collective-permute-start(bf16[32,2816]{1,0:T(8,128)(2,1)S(1)} %slice_bitcast_fusion), channel_id=1, source_target_pairs={{0,2},{1,3},{2,0},{3,1},{4,6},{5,7},{6,4},{7,5},{8,10},{9,11},{10,... | collective-permute-start | bytes 540680 | tf_op jit(solution)/shard_map/ppermute | solution.py:792
  307.7 20.2 %collective-permute-start.37 = (bf16[88,1024]{1,0:T(8,128)(2,1)S(1)}, bf16[88,1024]{1,0:T(8,128)(2,1)S(1)}, u32[]{:S(2)}, u32[]{:S(2)}) collective-permute-start(bf16[88,1024]{1,0:T(8,128)(2,1)S(1)} %add_convert_fusion.14), channel_id=1, source_target_pairs={{0,16},{4,20},{8,24},{12,28},{16,0},{20,4},{24,8},{28,12},{1,17},{... | collective-permute-start | bytes 540680 | tf_op jit(solution)/shard_map/ppermute | solution.py:792
  311.9 16.1 %collective-permute-start.39 = (bf16[128,1024]{1,0:T(8,128)(2,1)S(1)}, bf16[128,1024]{1,0:T(8,128)(2,1)S(1)}, u32[]{:S(2)}, u32[]{:S(2)}) collective-permute-start(bf16[128,1024]{1,0:T(8,128)(2,1)S(1)} %get-tuple-element.274), channel_id=1, source_target_pairs={{0,8},{4,12},{8,0},{12,4},{16,24},{20,28},{24,16},{28,20},{1,9},{5... | collective-permute-start | bytes 786440 | tf_op jit(solution)/shard_map/ppermute | solution.py:792
  328.0 17.4 %collective-permute-start.41 = (bf16[32,5632]{1,0:T(8,128)(2,1)S(1)}, bf16[32,5632]{1,0:T(8,128)(2,1)S(1)}, u32[]{:S(2)}, u32[]{:S(2)}) collective-permute-start(bf16[32,5632]{1,0:T(8,128)(2,1)S(1)} %pad_maximum_fusion.13), channel_id=1, source_target_pairs={{0,16},{4,20},{8,24},{12,28},{16,0},{20,4},{24,8},{28,12},{1,17},{... | collective-permute-start | bytes 1081352 | tf_op jit(solution)/shard_map/ppermute | solution.py:792
  328.7 16.9 %collective-permute-start.40 = (bf16[176,1024]{1,0:T(8,128)(2,1)S(1)}, bf16[176,1024]{1,0:T(8,128)(2,1)S(1)}, u32[]{:S(2)}, u32[]{:S(2)}) collective-permute-start(bf16[176,1024]{1,0:T(8,128)(2,1)S(1)} %pad_maximum_fusion.12), channel_id=1, source_target_pairs={{0,4},{4,0},{8,12},{12,8},{16,20},{20,16},{24,28},{28,24},{1,5},{5... | collective-permute-start | bytes 1081352 | tf_op jit(solution)/shard_map/ppermute | solution.py:792
  345.5 20.9 %collective-permute-start.45 = (bf16[64,5632]{1,0:T(8,128)(2,1)S(1)}, bf16[64,5632]{1,0:T(8,128)(2,1)}, u32[]{:S(2)}, u32[]{:S(2)}) collective-permute-start(bf16[64,5632]{1,0:T(8,128)(2,1)S(1)} %pad_maximum_fusion.7), channel_id=1, source_target_pairs={{0,8},{4,12},{8,0},{12,4},{16,24},{20,28},{24,16},{28,20},{1,9},{5... | collective-permute-start | bytes 2162696 | tf_op jit(solution)/shard_map/ppermute | solution.py:792
  359.6 67.8 %all-to-all-start.2 = ((bf16[8,640,128]{2,1,0:T(8,128)(2,1)}), bf16[8,640,128]{2,1,0:T(8,128)(2,1)S(1)}, u32[]{:S(2)}, u32[]{:S(2)}) async-start(bf16[8,640,128]{2,1,0:T(8,128)(2,1)} %pad_maximum_fusion.3), calls=%async_computation.2 | async-start | bytes 2621440 | tf_op jit(solution)/shard_map/all_to_all | solution.py:899
  363.6 40.5 %collective-permute-start.47 = (bf16[352,1024]{1,0:T(8,128)(2,1)S(1)}, bf16[352,1024]{1,0:T(8,128)(2,1)S(1)}, u32[]{:S(2)}, u32[]{:S(2)}) collective-permute-start(bf16[352,1024]{1,0:T(8,128)(2,1)S(1)} %pad_maximum_fusion.6), channel_id=1, source_target_pairs={{0,8},{4,12},{8,0},{12,4},{16,24},{20,28},{24,16},{28,20},{1,9},{5... | collective-permute-start | bytes 2162696 | tf_op jit(solution)/shard_map/ppermute | solution.py:792
  367.8 69.8 %collective-permute-start.54 = (bf16[128,5632]{1,0:T(8,128)(2,1)S(1)}, bf16[128,5632]{1,0:T(8,128)(2,1)}, u32[]{:S(2)}, u32[]{:S(2)}) collective-permute-start(bf16[128,5632]{1,0:T(8,128)(2,1)S(1)} %pad_maximum_fusion.2), channel_id=1, source_target_pairs={{0,4},{4,0},{8,12},{12,8},{16,20},{20,16},{24,28},{28,24},{1,5},{5... | collective-permute-start | bytes 4325384 | tf_op jit(solution)/shard_map/ppermute | solution.py:792
  369.3 35.0 %collective-permute-start.48 = (bf16[32,1024]{1,0:T(8,128)(2,1)S(1)}, bf16[32,1024]{1,0:T(8,128)(2,1)S(1)}, u32[]{:S(2)}, u32[]{:S(2)}) collective-permute-start(bf16[32,1024]{1,0:T(8,128)(2,1)S(1)} %add_convert_fusion.19), channel_id=1, source_target_pairs={{0,16},{4,20},{8,24},{12,28},{16,0},{20,4},{24,8},{28,12},{1,17},{... | collective-permute-start | bytes 196616 | tf_op jit(solution)/shard_map/ppermute | solution.py:792
  371.6 34.1 %collective-permute-start.46 = (bf16[256,384]{1,0:T(8,128)(2,1)S(1)}, bf16[256,384]{1,0:T(8,128)(2,1)S(1)}, u32[]{:S(2)}, u32[]{:S(2)}) collective-permute-start(bf16[256,384]{1,0:T(8,128)(2,1)S(1)} %fusion.14), channel_id=1, source_target_pairs={{0,2},{1,3},{2,0},{3,1},{4,6},{5,7},{6,4},{7,5},{8,10},{9,11},{10,... | collective-permute-start | bytes 589832 | tf_op jit(solution)/shard_map/ppermute | solution.py:792
  427.6 18.1 %collective-permute-start.52 = (bf16[4,256,384]{2,1,0:T(8,128)(2,1)S(1)}, bf16[4,256,384]{2,1,0:T(8,128)(2,1)}, u32[]{:S(2)}, u32[]{:S(2)}) collective-permute-start(bf16[4,256,384]{2,1,0:T(8,128)(2,1)S(1)} %pad_maximum_fusion.4.own_ref), channel_id=1, source_target_pairs={{0,8},{4,12},{8,0},{12,4},{16,24},{20,28},{24,16},{28,20},{1,9},{5... | collective-permute-start | bytes 2359304 | tf_op jit(solution)/shard_map/ppermute | solution.py:792
  (44 other events, 468.6 us)

commit v5 on v4

--- a/solution.py
+++ b/solution.py
@@ -143,6 +143,10 @@
     )(slot, w_rows, x, *arrays, codes, *extra)
 
 
+def tile_of(total):
+    return total if total <= 2560 else 512
+
+
 def forward_kernel(
     heads, step, q_ref, own_ref, v_near, k_ref, v_ref,
     att_ref, sum_ref, qb_ref, weight_ref, scores, tops, acc,
@@ -225,7 +229,7 @@
     flat = pl.BlockSpec((slots, 1, rows, LANES), lambda i: (0, i, 0, 0))
     span = slots * rows
     return pl.pallas_call(
-        functools.partial(forward_kernel, heads, 512),
+        functools.partial(forward_kernel, heads, tile_of(total)),
         grid=(parts,),
         in_specs=[block, block, block, whole, whole],
         out_specs=[flat, flat, block, block],
@@ -373,7 +377,7 @@
         out_shape.append(jax.ShapeDtypeStruct((heads, total, LANES), bf16))
         out_specs.append(wide)
     return pl.pallas_call(
-        functools.partial(backward_kernel, heads, part, parts, 512),
+        functools.partial(backward_kernel, heads, part, parts, tile_of(total)),
         grid=(1,),
         in_specs=[wide, near, near, near] + in_specs,
         out_specs=out_specs,
@@ -394,19 +398,16 @@
     parts = len(refs) - 4 - halves
     kv_refs, outs, term = refs[3 : 3 + parts], refs[3 + parts : -1], refs[-1]
     slots, _, rows, width = h_ref.shape
-    total = slots * parts * rows
-    term[:, :LANES] = mm_tn(
-        h_ref[...].reshape(total, width), dq_ref[...].reshape(total, LANES)
-    ).astype(bf16)
-    for kind in range(2):
-        summed = None
-        for part in range(parts):
-            piece = mm_tn(
-                h_ref[:, part].reshape(slots * rows, width),
-                kv_refs[part][:, kind].reshape(slots * rows, LANES),
-            )
-            summed = piece if summed is None else summed + piece
-        term[:, (kind + 1) * LANES : (kind + 2) * LANES] = summed.astype(bf16)
+    summed = None
+    for part in range(parts):
+        span = slots * rows
+        grads = [dq_ref[:, part * rows : (part + 1) * rows]] + [
+            kv_refs[part][:, kind] for kind in range(2)
+        ]
+        grads = jnp.concatenate([g.reshape(span, LANES) for g in grads], axis=1)
+        piece = mm_tn(h_ref[:, part].reshape(span, width), grads)
+        summed = piece if summed is None else summed + piece
+    term[...] = summed.astype(bf16)
     place_rows(halves, w_rows, term, outs)
 
 
@@ -1148,8 +1149,7 @@
             r.hold(kv_3)
         up_r.widen(2)
         down_r.widen(2)
-        output_r.halve(4)
-        dq = lax.optimization_barrier((dq, down_r.own, up_r.own, output_r.own, kv_early))[0]
+        dq = lax.optimization_barrier((dq, down_r.own, up_r.own, kv_early))[0]
     layer_out = (middle + sum(part.astype(f32) for part in outs)).astype(bf16)
     own = own_terms(w_rows, h1, dq, [kv_0, kv_1, kv_2, kv_3], shards, halves)
     if direct:
@@ -1158,9 +1158,10 @@
         for r in (up_r, output_r):
             r.hold(own[0])
         up_r.widen(1)
+        output_r.halve(4)
+        own_r.across()
         output_r.settle()
         output_r.widen(4)
-        own_r.across()
         output_r.widen(1)
         own_r.settle()
         own_r.own = after(own_r.own[None], down_r.arrived)

time: 459 us -> 446 us (0.972)
  Pallas kernels: 187 us -> 176 us
    pallas_call x5, Pallas kernels: 84.8 us -> 75 us  [the longest x4 54.4 us: attend_back(): pl.pallas_call(functools.partial(backward_kernel, heads, part, parts, til...]
    all_to_all x4, waiting for transfers between devices: 14.3 us -> 8.83 us  [turn(): lax.all_to_all(blocks, 'seq', split_axis=0, concat_axis=0, tiled=True)]
  transfers between devices with their start and end apart: 59 -> 59, of which waited for: 19 -> 22; matrix products, arithmetic and copies ran while one was open for 14% -> 14% of each run, Pallas kernels for 31% -> 30%
where the time goes in v5:
time: 446 us; the launch traced here: 439 us
  Pallas kernels  176 us (39%)
  waiting for transfers between devices  111 us (25%)
  starting transfers between devices  79.2 us (18%)
  other arithmetic  52.4 us (12%)
  local copies, waits for them, and re-layouts  17.8 us (4%)
    ppermute x50, waiting for transfers between devices, flip(): return lax.ppermute(values, axis, [(i, i ^ delta) for i in range(count)])  93.8 us
    pallas_call x4, Pallas kernels, attend_back(): pl.pallas_call(functools.partial(backward_kernel, heads, part, parts, til...  54.4 us
    ppermute x50, starting transfers between devices, flip(): return lax.ppermute(values, axis, [(i, i ^ delta) for i in range(count)])  52.8 us
    pallas_call x8, Pallas kernels, project(): pl.pallas_call(functools.partial(project_kernel, heads, segments, layout,...  35.1 us
    pallas_call x1, Pallas kernels, main_stage(): pl.pallas_call(functools.partial(main_kernel, groups, halves, entries, le...  32.8 us
    convert_element_type x14, other arithmetic, add_low(): return (a.astype(f32) + b.astype(f32)).astype(bf16)  20.8 us
    pallas_call x1, Pallas kernels, attend(): pl.pallas_call(functools.partial(forward_kernel, heads, tile_of(total)),...  20.6 us
    all_to_all x4, starting transfers between devices, turn(): lax.all_to_all(blocks, 'seq', split_axis=0, concat_axis=0, tiled=True)  19 us
  transfers between devices with their start and end apart: 59, of which 22 were waited for; matrix products, arithmetic and copies ran while one was open for 14% of the time, Pallas kernels for 30%

profile of v5, /device:TPU:0, one launch (start us, length us, event | category | flops | bytes accessed | tf_op | source)
XLA Modules:
  0.0 438.6 jit_solution(6624556204247612078)
XLA Ops:
  0.7 3.0 collective-permute-start.2
  16.5 3.8 collective-permute-done.8
  28.3 2.9 select_reduce_fusion
  33.2 4.4 project.8
  37.5 4.5 %project.9 = (bf16[2,2560,128]{2,1,0:T(8,128)(2,1)}, bf16[2,2560,128]{2,1,0:T(8,128)(2,1)}, bf16[2,2560,128]{2,1,0:T(8,128)(2,1)}, bf16[2560,1024]{1,0:T(8,128)(2,1)}, f32[2,2560,128]{2,1,0:T(8,128)}) custom-call(s32[1]{0:T(128)} %bitcast.2.refs_0_, ...), custom_call_target="tpu_custom_call", output_to_operand_aliasing={{0}: (6, {}), {1}: (7, {}), {2}: (8, {}), {3}: (9, {}), {4}... | custom-call | flops 251658240 | bytes 2359296 | tf_op jit(solution)/shard_map/project/pallas_call | solution.py:125
  42.0 5.2 %collective-permute-done.4 = bf16[320,1024]{1,0:T(8,128)(2,1)} collective-permute-done((bf16[320,1024]{1,0:T(8,128)(2,1)}, bf16[320,1024]{1,0:T(8,128)(2,1)}, u32[]{:S(2)}, u32[]{:S(2)}) %collective-permute-start.4) | collective-permute-done | bytes 655392 | tf_op jit(solution)/shard_map/ppermute | solution.py:894
  52.2 4.4 project.10
  56.5 4.4 project.11
  60.9 4.4 project.12
  66.0 3.3 collective-permute-done.10
  74.4 4.4 project.13
  78.8 4.4 project.14
  83.1 5.1 %collective-permute-done.15.refs_5_ = bf16[320,1024]{1,0:T(8,128)(2,1)} collective-permute-done((bf16[320,1024]{1,0:T(8,128)(2,1)}, bf16[320,1024]{1,0:T(8,128)(2,1)}, u32[]{:S(2)}, u32[]{:S(2)}) %collective-permute-start.15) | collective-permute-done | bytes 655392 | tf_op jit(solution)/shard_map/ppermute | solution.py:793
  89.3 4.5 %project.15 = (bf16[2,2560,128]{2,1,0:T(8,128)(2,1)}, bf16[2,2560,128]{2,1,0:T(8,128)(2,1)}, bf16[2,2560,128]{2,1,0:T(8,128)(2,1)}, bf16[2560,1024]{1,0:T(8,128)(2,1)}, f32[2,2560,128]{2,1,0:T(8,128)}) custom-call(s32[1]{0:T(128)} %bitcast.refs_0_, ...), custom_call_target="tpu_custom_call", output_to_operand_aliasing={{0}: (6, {}), {1}: (7, {}), {2}: (8, {}), {3}: (9, {}), {4}... | custom-call | flops 251658240 | bytes 2359296 | tf_op jit(solution)/shard_map/project/pallas_call | solution.py:125
  94.9 20.6 %attend.1 = (bf16[8,2,160,128]{3,2,1,0:T(8,128)(2,1)}, f32[8,2,160,128]{3,2,1,0:T(8,128)}, bf16[2,8,2,160,128]{4,3,2,1,0:T(8,128)(2,1)}, bf16[2,8,2,160,128]{4,3,2,1,0:T(8,128)(2,1)}) custom-call(bf16[2,8,2,160,128]{4,3,2,1,0:T(8,128)(2,1)} %bitcast.80, f32[2,8,2,160,128]{4,3,2,1,0:T(8,128)} %bitcast.79, bf16[2,8,2,160,128]{4,3,2,1,0:T(8,128)(2,1)} %bitcast.85, ...), custom_call_target="tpu_custom_call" | custom-call | flops 13421772800 | bytes 2621440 | tf_op jit(solution)/shard_map/attend/pallas_call | solution.py:231
  117.1 4.4 %all-to-all-start = ((bf16[8,320,128]{2,1,0:T(8,128)(2,1)}), bf16[8,320,128]{2,1,0:T(8,128)(2,1)S(1)}, u32[]{:S(2)}, u32[]{:S(2)}) async-start(bf16[8,320,128]{2,1,0:T(8,128)(2,1)} %bitcast.100), calls=%async_computation | async-start | bytes 1310720 | tf_op jit(solution)/shard_map/all_to_all | solution.py:900
  124.8 6.4 %collective-permute-done.21.refs_9_ = bf16[256,3072]{1,0:T(8,128)(2,1)} collective-permute-done((bf16[256,3072]{1,0:T(8,128)(2,1)S(1)}, bf16[256,3072]{1,0:T(8,128)(2,1)}, u32[]{:S(2)}, u32[]{:S(2)}) %collective-permute-start.21) | collective-permute-done | bytes 1572896 | tf_op jit(solution)/shard_map/ppermute | solution.py:793
  131.2 7.9 %all-to-all-done.refs_1_ = bf16[8,320,128]{2,1,0:T(8,128)(2,1)S(1)} async-done(((bf16[8,320,128]{2,1,0:T(8,128)(2,1)}), bf16[8,320,128]{2,1,0:T(8,128)(2,1)S(1)}, u32[]{:S(2)}, u32[]{:S(2)}) %all-to-all-start) | async-done | bytes 655392 | tf_op jit(solution)/shard_map/all_to_all | solution.py:900
  139.9 5.3 %pre_stage.1 = (f32[320,1024]{1,0:T(8,128)}, bf16[320,1024]{1,0:T(8,128)(2,1)}, bf16[320,1024]{1,0:T(8,128)(2,1)}) custom-call(s32[4]{0:T(128)} %iota_xor_fusion.1.refs_1_.refs_0_.w_rows, bf16[8,320,128]{2,1,0:T(8,128)(2,1)} %copy-done.10, bf16[320,1024]{1,0:T(8,128)(2,1)} %bitcast.95, bf16[1,1024]{1,0:T(2,128)(2,1)} %get-tuple-element.372.refs_3_.refs_5_, ...), custom_call_target="tpu_custom_call" | custom-call | flops 671088640 | bytes 2097152 | tf_op jit(solution)/shard_map/pre_stage/pallas_call | solution.py:496
  147.2 13.6 %collective-permute-done.22.refs_3_ = bf16[320,1024]{1,0:T(8,128)(2,1)S(1)} collective-permute-done((bf16[320,1024]{1,0:T(8,128)(2,1)}, bf16[320,1024]{1,0:T(8,128)(2,1)S(1)}, u32[]{:S(2)}, u32[]{:S(2)}) %collective-permute-start.22) | collective-permute-done | bytes 655392 | tf_op jit(solution)/shard_map/ppermute | solution.py:793
  161.6 32.8 %main_stage.1 = (f32[320,1024]{1,0:T(8,128)}, bf16[320,1024]{1,0:T(8,128)(2,1)}, f32[320,1024]{1,0:T(8,128)}, bf16[320,1024]{1,0:T(8,128)(2,1)}, bf16[2,256,2816...) custom-call(s32[4]{0:T(128)} %iota_xor_fusion.1.refs_1_.refs_0_.w_ro, ...), custom_call_target="tpu_custom_call" | custom-call | flops 16609443840 | bytes 17301504 | tf_op jit(solution)/shard_map/main_stage/pallas_call | solution.py:599
  196.6 3.6 collective-permute-done.24
  200.2 4.4 %add_convert_fusion = (bf16[2,128,2816]{2,1,0:T(8,128)(2,1)}, bf16[2,128,2816]{2,1,0:T(8,128)(2,1)S(1)}) fusion(bf16[2,256,2816]{2,1,0:T(8,128)(2,1)} %collective-permute-done.24, s32[]{:T(128)S(6)} %select_n.376, bf16[2,256,2816]{2,1,0:T(8,128)(2,1)} %get-tuple-element.231, s32[]{:T(128)S(6)} %select_n.371), kind=kLoop, calls=%fused_computation.7 | loop fusion | flops 5767168 | bytes 8650760 | tf_op jit(solution)/shard_map/convert_element_type | solution.py:805
  206.5 3.5 fusion.3
  212.1 5.4 %post_stage.1 = (f32[320,1024]{1,0:T(8,128)}, bf16[320,1024]{1,0:T(8,128)(2,1)}, bf16[8,320,128]{2,1,0:T(8,128)(2,1)}) custom-call(s32[4]{0:T(128)} %iota_xor_fusion.1.refs_1_.refs_0_.w_rows, f32[320,1024]{1,0:T(8,128)} %get-tuple-element.222.refs_1_, f32[320,1024]{1,0:T(8,128)} %get-tuple-element.229.refs_2_, ...), custom_call_target="tpu_custom_call" | custom-call | flops 671088640 | bytes 4194304 | tf_op jit(solution)/shard_map/post_stage/pallas_call | solution.py:662
  217.6 5.5 %all-to-all-start.1 = ((bf16[8,320,128]{2,1,0:T(8,128)(2,1)}), bf16[8,320,128]{2,1,0:T(8,128)(2,1)}, u32[]{:S(2)}, u32[]{:S(2)}) async-start(bf16[8,320,128]{2,1,0:T(8,128)(2,1)} %get-tuple-element.237), calls=%async_computation.1 | async-start | bytes 1310720 | tf_op jit(solution)/shard_map/all_to_all | solution.py:900
  223.9 3.9 out_terms.1
  227.8 14.4 %collective-permute-done.26 = bf16[352,1024]{1,0:T(8,128)(2,1)} collective-permute-done((bf16[352,1024]{1,0:T(8,128)(2,1)}, bf16[352,1024]{1,0:T(8,128)(2,1)}, u32[]{:S(2)}, u32[]{:S(2)}) %collective-permute-start.26) | collective-permute-done | bytes 720928 | tf_op jit(solution)/shard_map/ppermute | solution.py:793
  244.6 2.8 add_convert_fusion.2
  248.3 14.8 %attend_back.4 = (bf16[8,2,80,128]{3,2,1,0:T(8,128)(2,1)}, f32[2,2560,128]{2,1,0:T(8,128)}, bf16[2,2560,128]{2,1,0:T(8,128)(2,1)}) custom-call(bf16[2,2560,128]{2,1,0:T(8,128)(2,1)} %bitcast.104, bf16[2,8,4,80,128]{4,3,2,1,0:T(8,128)(2,1)} %bitcast.81, bf16[2,8,4,80,128]{4,3,2,1,0:T(8,128)(2,1)} %bitcast.86, bf16[2,8,4,80,128]{4,3,2,1,0:T(8,128)(2,1)} %bitcast.108, ...), custom_call_target="tpu_custom_call" | custom-call | flops 8388608000 | bytes 7864320 | tf_op jit(solution)/shard_map/attend_back/pallas_call | solution.py:379
  264.4 5.5 %collective-permute-start.32 = (bf16[88,1024]{1,0:T(8,128)(2,1)S(1)}, bf16[88,1024]{1,0:T(8,128)(2,1)S(1)}, u32[]{:S(2)}, u32[]{:S(2)}) collective-permute-start(bf16[88,1024]{1,0:T(8,128)(2,1)S(1)} %get-tuple-element.256), channel_id=1, source_target_pairs={{0,16},{4,20},{8,24},{12,28},{16,0},{20,4},{24,8},{28,12},{1,17},{... | collective-permute-start | bytes 540680 | tf_op jit(solution)/shard_map/ppermute | solution.py:793
  276.7 13.7 %attend_back.5 = (bf16[8,2,80,128]{3,2,1,0:T(8,128)(2,1)}, f32[2,2560,128]{2,1,0:T(8,128)}) custom-call(bf16[2,2560,128]{2,1,0:T(8,128)(2,1)} %bitcast.105, bf16[2,8,4,80,128]{4,3,2,1,0:T(8,128)(2,1)} %bitcast.82, bf16[2,8,4,80,128]{4,3,2,1,0:T(8,128)(2,1)} %bitcast.87, bf16[2,8,4,80,128]{4,3,2,1,0:T(8,128)(2,1)} %bitcast.109, ...), custom_call_target="tpu_custom_call" | custom-call | flops 8388608000 | bytes 7864320 | tf_op jit(solution)/shard_map/attend_back/pallas_call | solution.py:379
  292.4 4.0 all-to-all-start.3
  296.5 2.7 fusion.6
  300.8 2.9 collective-permute-start.37
  306.5 13.2 %attend_back.6 = (bf16[8,2,80,128]{3,2,1,0:T(8,128)(2,1)}, f32[2,2560,128]{2,1,0:T(8,128)}) custom-call(bf16[2,2560,128]{2,1,0:T(8,128)(2,1)} %bitcast.106, bf16[2,8,4,80,128]{4,3,2,1,0:T(8,128)(2,1)} %bitcast.83, bf16[2,8,4,80,128]{4,3,2,1,0:T(8,128)(2,1)} %bitcast.88, bf16[2,8,4,80,128]{4,3,2,1,0:T(8,128)(2,1)} %bitcast.110, ...), custom_call_target="tpu_custom_call" | custom-call | flops 8388608000 | bytes 7864320 | tf_op jit(solution)/shard_map/attend_back/pallas_call | solution.py:379
  324.0 12.8 %attend_back.7 = (bf16[8,2,80,128]{3,2,1,0:T(8,128)(2,1)}, bf16[8,320,128]{2,1,0:T(8,128)(2,1)}) custom-call(bf16[2,2560,128]{2,1,0:T(8,128)(2,1)} %bitcast.107, bf16[2,8,4,80,128]{4,3,2,1,0:T(8,128)(2,1)} %bitcast.84, bf16[2,8,4,80,128]{4,3,2,1,0:T(8,128)(2,1)} %bitcast.89, bf16[2,8,4,80,128]{4,3,2,1,0:T(8,128)(2,1)} %bitcast.111, ...), custom_call_target="tpu_custom_call" | custom-call | flops 8388608000 | bytes 7864320 | tf_op jit(solution)/shard_map/attend_back/pallas_call | solution.py:379
  342.6 5.1 %all-to-all-start.2 = ((bf16[8,640,128]{2,1,0:T(8,128)(2,1)}), bf16[8,640,128]{2,1,0:T(8,128)(2,1)S(1)}, u32[]{:S(2)}, u32[]{:S(2)}) async-start(bf16[8,640,128]{2,1,0:T(8,128)(2,1)} %pad_maximum_fusion.3), calls=%async_computation.2 | async-start | bytes 2621440 | tf_op jit(solution)/shard_map/all_to_all | solution.py:900
  347.7 7.1 %own_terms.1 = (bf16[2,256,384]{2,1,0:T(8,128)(2,1)}, bf16[2,256,384]{2,1,0:T(8,128)(2,1)}) custom-call(s32[4]{0:T(128)} %iota_xor_fusion.1.refs_1_.refs_0_.w_rows, bf16[8,4,80,1024]{3,2,1,0:T(8,128)(2,1)} %bitcast.78, bf16[8,320,128]{2,1,0:T(8,128)(2,1)} %get-tuple-element.289.refs_2_, bf16[8,2,80,128]{3,2,1,0:T(8,128)(2,1)} %get-tuple-element.244.refs_3_, ...), custom_call_target="tpu_custom_call" | custom-call | flops 2013265920 | bytes 5242880 | tf_op jit(solution)/shard_map/own_terms/pallas_call | solution.py:428
  355.0 10.0 %collective-permute-done.44 = bf16[64,5632]{1,0:T(8,128)(2,1)} collective-permute-done((bf16[64,5632]{1,0:T(8,128)(2,1)S(1)}, bf16[64,5632]{1,0:T(8,128)(2,1)}, u32[]{:S(2)}, u32[]{:S(2)}) %collective-permute-start.44) | collective-permute-done | bytes 720928 | tf_op jit(solution)/shard_map/ppermute | solution.py:793
  370.5 22.0 %collective-permute-done.47 = bf16[32,1024]{1,0:T(8,128)(2,1)S(1)} collective-permute-done((bf16[32,1024]{1,0:T(8,128)(2,1)S(1)}, bf16[32,1024]{1,0:T(8,128)(2,1)S(1)}, u32[]{:S(2)}, u32[]{:S(2)}) %collective-permute-start.47) | collective-permute-done | bytes 65568 | tf_op jit(solution)/shard_map/ppermute | solution.py:793
  392.5 3.4 collective-permute-start.48
  400.4 3.1 collective-permute-start.49
  403.5 3.6 collective-permute-done.50
  414.7 2.8 collective-permute-done.51
  419.5 7.7 %last_stage.1 = f32[320,1024]{1,0:T(8,128)} custom-call(s32[4]{0:T(128)} %iota_xor_fusion.1.refs_1_.refs_0_.w_rows, bf16[8,320,128]{2,1,0:T(8,128)(2,1)} %get-tuple-element.342.refs_1_, bf16[8,2,160,128]{3,2,1,0:T(8,128)(2,1)} %copy-done.11, bf16[8,2,160,128]{3,2,1,0:T(8,128)(2,1)} %bitcast.98, bf16[320,1024]{1,0:T(8,128)(2,1)} %bitcast.96, ...), custom_call_target="tpu_custom_call" | custom-call | flops 2013265920 | bytes 6291456 | tf_op jit(solution)/shard_map/last_stage/pallas_call | solution.py:748
  429.4 2.9 multiply_reduce_fusion
  432.9 3.7 finish_own.1
  (255 shorter events, 102.8 us)
Async XLA Ops:
  0.7 22.6 %collective-permute-start.2 = (bf16[320,1024]{1,0:T(8,128)(2,1)}, bf16[320,1024]{1,0:T(8,128)(2,1)}, u32[]{:S(2)}, u32[]{:S(2)}) collective-permute-start(bf16[320,1024]{1,0:T(8,128)(2,1)} %bitcast.91), channel_id=1, source_target_pairs={{0,4},{4,0},{8,12},{12,8},{16,20},{20,16},{24,28},{28,24},{1,5},{5... | collective-permute-start | bytes 1966088 | tf_op jit(solution)/shard_map/ppermute | solution.py:793
  3.7 19.6 %collective-permute-start = (bf16[320,1024]{1,0:T(8,128)(2,1)}, bf16[320,1024]{1,0:T(8,128)(2,1)}, u32[]{:S(2)}, u32[]{:S(2)}) collective-permute-start(bf16[320,1024]{1,0:T(8,128)(2,1)} %bitcast.92), channel_id=1, source_target_pairs={{0,8},{4,12},{8,0},{12,4},{16,24},{20,28},{24,16},{28,20},{1,9},{5... | collective-permute-start | bytes 1966088 | tf_op jit(solution)/shard_map/ppermute | solution.py:894
  5.3 18.0 %collective-permute-start.1 = (bf16[320,1024]{1,0:T(8,128)(2,1)}, bf16[320,1024]{1,0:T(8,128)(2,1)}, u32[]{:S(2)}, u32[]{:S(2)}) collective-permute-start(bf16[320,1024]{1,0:T(8,128)(2,1)} %bitcast.93), channel_id=1, source_target_pairs={{8,16},{12,20},{16,8},{20,12},{9,17},{13,21},{17,9},{21,13},{10,18... | collective-permute-start | bytes 1966088 | tf_op jit(solution)/shard_map/ppermute | solution.py:894
  12.3 29.7 %collective-permute-start.7 = (bf16[256,1024]{1,0:T(8,128)(2,1)}, bf16[256,1024]{1,0:T(8,128)(2,1)S(1)}, u32[]{:S(2)}, u32[]{:S(2)}) collective-permute-start(bf16[256,1024]{1,0:T(8,128)(2,1)} %refs_6_.1), channel_id=1, source_target_pairs={{0,2},{1,3},{2,0},{3,1},{4,6},{5,7},{6,4},{7,5},{8,10},{9,11},{10,... | collective-permute-start | bytes 1572872 | tf_op jit(solution)/shard_map/ppermute | solution.py:793
  23.3 18.7 %collective-permute-start.5 = (bf16[320,1024]{1,0:T(8,128)(2,1)}, bf16[320,1024]{1,0:T(8,128)(2,1)}, u32[]{:S(2)}, u32[]{:S(2)}) collective-permute-start(bf16[320,1024]{1,0:T(8,128)(2,1)} %collective-permute-done.refs_2_), channel_id=1, source_target_pairs={{0,4},{4,0},{8,12},{12,8},{16,20},{20,16},{24,28},{28,24},{1,5},{5... | collective-permute-start | bytes 1966088 | tf_op jit(solution)/shard_map/ppermute | solution.py:793
  23.9 18.1 %collective-permute-start.3 = (bf16[320,1024]{1,0:T(8,128)(2,1)}, bf16[320,1024]{1,0:T(8,128)(2,1)}, u32[]{:S(2)}, u32[]{:S(2)}) collective-permute-start(bf16[320,1024]{1,0:T(8,128)(2,1)} %collective-permute-done.refs_2_), channel_id=1, source_target_pairs={{8,16},{12,20},{16,8},{20,12},{9,17},{13,21},{17,9},{21,13},{10,18... | collective-permute-start | bytes 1966088 | tf_op jit(solution)/shard_map/ppermute | solution.py:894
  25.4 21.8 %collective-permute-start.6 = (bf16[128,2816]{1,0:T(8,128)(2,1)}, bf16[128,2816]{1,0:T(8,128)(2,1)}, u32[]{:S(2)}, u32[]{:S(2)}) collective-permute-start(bf16[128,2816]{1,0:T(8,128)(2,1)} %get-tuple-element.165), channel_id=1, source_target_pairs={{0,2},{1,3},{2,0},{3,1},{4,6},{5,7},{6,4},{7,5},{8,10},{9,11},{10,... | collective-permute-start | bytes 2162696 | tf_op jit(solution)/shard_map/ppermute | solution.py:793
  27.0 20.3 %collective-permute-start.4 = (bf16[320,1024]{1,0:T(8,128)(2,1)}, bf16[320,1024]{1,0:T(8,128)(2,1)}, u32[]{:S(2)}, u32[]{:S(2)}) collective-permute-start(bf16[320,1024]{1,0:T(8,128)(2,1)} %collective-permute-done.1), channel_id=1, source_target_pairs={{8,0},{12,4},{16,24},{20,28},{9,1},{13,5},{17,25},{21,29},{10,2},{... | collective-permute-start | bytes 1966088 | tf_op jit(solution)/shard_map/ppermute | solution.py:894
  47.3 22.1 %collective-permute-start.13 = (bf16[256,2816]{1,0:T(8,128)(2,1)S(1)}, bf16[256,2816]{1,0:T(8,128)(2,1)}, u32[]{:S(2)}, u32[]{:S(2)}) collective-permute-start(bf16[256,2816]{1,0:T(8,128)(2,1)S(1)} %copy-done.19), channel_id=1, source_target_pairs={{0,1},{1,0},{2,3},{3,2},{4,5},{5,4},{6,7},{7,6},{8,9},{9,8},{10,11... | collective-permute-start | bytes 4325384 | tf_op jit(solution)/shard_map/ppermute | solution.py:793
  47.3 22.1 %collective-permute-start.12 = (bf16[128,2816]{1,0:T(8,128)(2,1)S(1)}, bf16[128,2816]{1,0:T(8,128)(2,1)}, u32[]{:S(2)}, u32[]{:S(2)}) collective-permute-start(bf16[128,2816]{1,0:T(8,128)(2,1)S(1)} %copy-done.22), channel_id=1, source_target_pairs={{0,2},{1,3},{2,0},{3,1},{4,6},{5,7},{6,4},{7,5},{8,10},{9,11},{10,... | collective-permute-start | bytes 2162696 | tf_op jit(solution)/shard_map/ppermute | solution.py:793
  49.1 17.0 %collective-permute-start.11 = (bf16[320,1024]{1,0:T(8,128)(2,1)S(1)}, bf16[320,1024]{1,0:T(8,128)(2,1)}, u32[]{:S(2)}, u32[]{:S(2)}) collective-permute-start(bf16[320,1024]{1,0:T(8,128)(2,1)S(1)} %broadcast_select_fusion.7.refs_2_), channel_id=1, source_target_pairs={{0,4},{4,0},{8,12},{12,8},{16,20},{20,16},{24,28},{28,24},{1,5},{5... | collective-permute-start | bytes 1966088 | tf_op jit(solution)/shard_map/ppermute | solution.py:793
  50.7 18.7 %collective-permute-start.10 = (bf16[320,1024]{1,0:T(8,128)(2,1)}, bf16[320,1024]{1,0:T(8,128)(2,1)}, u32[]{:S(2)}, u32[]{:S(2)}) collective-permute-start(bf16[320,1024]{1,0:T(8,128)(2,1)} %collective-permute-done.3), channel_id=1, source_target_pairs={{8,0},{12,4},{16,24},{20,28},{9,1},{13,5},{17,25},{21,29},{10,2},{... | collective-permute-start | bytes 1966088 | tf_op jit(solution)/shard_map/ppermute | solution.py:894
  70.6 18.6 %collective-permute-start.17 = (bf16[704,1024]{1,0:T(8,128)(2,1)}, bf16[704,1024]{1,0:T(8,128)(2,1)}, u32[]{:S(2)}, u32[]{:S(2)}) collective-permute-start(bf16[704,1024]{1,0:T(8,128)(2,1)} %refs_12_.1), channel_id=1, source_target_pairs={{0,1},{1,0},{2,3},{3,2},{4,5},{5,4},{6,7},{7,6},{8,9},{9,8},{10,11... | collective-permute-start | bytes 4325384 | tf_op jit(solution)/shard_map/ppermute | solution.py:793
  70.7 18.5 %collective-permute-start.16 = (bf16[128,2816]{1,0:T(8,128)(2,1)}, bf16[128,2816]{1,0:T(8,128)(2,1)}, u32[]{:S(2)}, u32[]{:S(2)}) collective-permute-start(bf16[128,2816]{1,0:T(8,128)(2,1)} %collective-permute-done.6.refs_8_), channel_id=1, source_target_pairs={{0,1},{1,0},{2,3},{3,2},{4,5},{5,4},{6,7},{7,6},{8,9},{9,8},{10,11... | collective-permute-start | bytes 2162696 | tf_op jit(solution)/shard_map/ppermute | solution.py:793
  71.2 17.0 %collective-permute-start.15 = (bf16[320,1024]{1,0:T(8,128)(2,1)}, bf16[320,1024]{1,0:T(8,128)(2,1)}, u32[]{:S(2)}, u32[]{:S(2)}) collective-permute-start(bf16[320,1024]{1,0:T(8,128)(2,1)} %bitcast.11.refs_4_), channel_id=1, source_target_pairs={{0,2},{1,3},{2,0},{3,1},{4,6},{5,7},{6,4},{7,5},{8,10},{9,11},{10,... | collective-permute-start | bytes 1966088 | tf_op jit(solution)/shard_map/ppermute | solution.py:793
  72.7 16.5 %collective-permute-start.14 = (bf16[320,1024]{1,0:T(8,128)(2,1)S(1)}, bf16[320,1024]{1,0:T(8,128)(2,1)}, u32[]{:S(2)}, u32[]{:S(2)}) collective-permute-start(bf16[320,1024]{1,0:T(8,128)(2,1)S(1)} %broadcast_select_fusion.6.refs_2_), channel_id=1, source_target_pairs={{0,4},{4,0},{8,12},{12,8},{16,20},{20,16},{24,28},{28,24},{1,5},{5... | collective-permute-start | bytes 1966088 | tf_op jit(solution)/shard_map/ppermute | solution.py:793
  93.8 22.5 %collective-permute-start.18 = (bf16[128,2816]{1,0:T(8,128)(2,1)}, bf16[128,2816]{1,0:T(8,128)(2,1)}, u32[]{:S(2)}, u32[]{:S(2)}) collective-permute-start(bf16[128,2816]{1,0:T(8,128)(2,1)} %collective-permute-done.12.refs_9_), channel_id=1, source_target_pairs={{0,1},{1,0},{2,3},{3,2},{4,5},{5,4},{6,7},{7,6},{8,9},{9,8},{10,11... | collective-permute-start | bytes 2162696 | tf_op jit(solution)/shard_map/ppermute | solution.py:793
  93.8 21.7 %collective-permute-start.20 = (bf16[256,1024]{1,0:T(8,128)(2,1)S(1)}, bf16[256,1024]{1,0:T(8,128)(2,1)S(1)}, u32[]{:S(2)}, u32[]{:S(2)}) collective-permute-start(bf16[256,1024]{1,0:T(8,128)(2,1)S(1)} %copy-done.16), channel_id=1, source_target_pairs={{0,1},{1,0},{2,3},{3,2},{4,5},{5,4},{6,7},{7,6},{8,9},{9,8},{10,11... | collective-permute-start | bytes 1572872 | tf_op jit(solution)/shard_map/ppermute | solution.py:793
  94.3 21.2 %collective-permute-start.19 = (bf16[256,1024]{1,0:T(8,128)(2,1)S(1)}, bf16[256,1024]{1,0:T(8,128)(2,1)S(1)}, u32[]{:S(2)}, u32[]{:S(2)}) collective-permute-start(bf16[256,1024]{1,0:T(8,128)(2,1)S(1)} %copy-done.14), channel_id=1, source_target_pairs={{0,1},{1,0},{2,3},{3,2},{4,5},{5,4},{6,7},{7,6},{8,9},{9,8},{10,11... | collective-permute-start | bytes 1572872 | tf_op jit(solution)/shard_map/ppermute | solution.py:793
  94.3 36.8 %collective-permute-start.21 = (bf16[256,3072]{1,0:T(8,128)(2,1)S(1)}, bf16[256,3072]{1,0:T(8,128)(2,1)}, u32[]{:S(2)}, u32[]{:S(2)}) collective-permute-start(bf16[256,3072]{1,0:T(8,128)(2,1)S(1)} %constant_dynamic-update-slice_fusion.refs_7_.w_ref), channel_id=1, source_target_pairs={{0,2},{1,3},{2,0},{3,1},{4,6},{5,7},{6,4},{7,5},{8,10},{9,11},{10,... | collective-permute-start | bytes 4718600 | tf_op jit(solution)/shard_map/ppermute | solution.py:793
  117.1 22.0 %all-to-all-start = ((bf16[8,320,128]{2,1,0:T(8,128)(2,1)}), bf16[8,320,128]{2,1,0:T(8,128)(2,1)S(1)}, u32[]{:S(2)}, u32[]{:S(2)}) async-start(bf16[8,320,128]{2,1,0:T(8,128)(2,1)} %bitcast.100), calls=%async_computation | async-start | bytes 1310720 | tf_op jit(solution)/shard_map/all_to_all | solution.py:900
  145.2 15.6 %collective-permute-start.22 = (bf16[320,1024]{1,0:T(8,128)(2,1)}, bf16[320,1024]{1,0:T(8,128)(2,1)S(1)}, u32[]{:S(2)}, u32[]{:S(2)}) collective-permute-start(bf16[320,1024]{1,0:T(8,128)(2,1)} %get-tuple-element.223.refs_2_), channel_id=1, source_target_pairs={{0,2},{1,3},{2,0},{3,1},{4,6},{5,7},{6,4},{7,5},{8,10},{9,11},{10,... | collective-permute-start | bytes 1966088 | tf_op jit(solution)/shard_map/ppermute | solution.py:793
  195.1 17.0 %collective-permute-start.23 = (bf16[320,1024]{1,0:T(8,128)(2,1)}, bf16[320,1024]{1,0:T(8,128)(2,1)}, u32[]{:S(2)}, u32[]{:S(2)}) collective-permute-start(bf16[320,1024]{1,0:T(8,128)(2,1)} %get-tuple-element.230), channel_id=1, source_target_pairs={{0,2},{1,3},{2,0},{3,1},{4,6},{5,7},{6,4},{7,5},{8,10},{9,11},{10,... | collective-permute-start | bytes 1966088 | tf_op jit(solution)/shard_map/ppermute | solution.py:793
  204.6 40.0 %collective-permute-start.27 = (bf16[2,128,2816]{2,1,0:T(8,128)(2,1)}, bf16[2,128,2816]{2,1,0:T(8,128)(2,1)}, u32[]{:S(2)}, u32[]{:S(2)}) collective-permute-start(bf16[2,128,2816]{2,1,0:T(8,128)(2,1)} %get-tuple-element.238), channel_id=1, source_target_pairs={{0,4},{4,0},{8,12},{12,8},{16,20},{20,16},{24,28},{28,24},{1,5},{5... | collective-permute-start | bytes 4325384 | tf_op jit(solution)/shard_map/ppermute | solution.py:793
  217.5 30.9 %collective-permute-start.28 = (bf16[256,3072]{1,0:T(8,128)(2,1)S(1)}, bf16[256,3072]{1,0:T(8,128)(2,1)}, u32[]{:S(2)}, u32[]{:S(2)}) collective-permute-start(bf16[256,3072]{1,0:T(8,128)(2,1)S(1)} %constant_dynamic-update-slice_fusion.refs_7_.w_ref), channel_id=1, source_target_pairs={{0,1},{1,0},{2,3},{3,2},{4,5},{5,4},{6,7},{7,6},{8,9},{9,8},{10,11... | collective-permute-start | bytes 4718600 | tf_op jit(solution)/shard_map/ppermute | solution.py:793
  217.5 24.6 %collective-permute-start.26 = (bf16[352,1024]{1,0:T(8,128)(2,1)}, bf16[352,1024]{1,0:T(8,128)(2,1)}, u32[]{:S(2)}, u32[]{:S(2)}) collective-permute-start(bf16[352,1024]{1,0:T(8,128)(2,1)} %get-tuple-element.239), channel_id=1, source_target_pairs={{0,8},{4,12},{8,0},{12,4},{16,24},{20,28},{24,16},{28,20},{1,9},{5... | collective-permute-start | bytes 2162696 | tf_op jit(solution)/shard_map/ppermute | solution.py:793
  217.6 30.7 %all-to-all-start.1 = ((bf16[8,320,128]{2,1,0:T(8,128)(2,1)}), bf16[8,320,128]{2,1,0:T(8,128)(2,1)}, u32[]{:S(2)}, u32[]{:S(2)}) async-start(bf16[8,320,128]{2,1,0:T(8,128)(2,1)} %get-tuple-element.237), calls=%async_computation.1 | async-start | bytes 1310720 | tf_op jit(solution)/shard_map/all_to_all | solution.py:900
  244.5 18.7 %collective-permute-start.30 = (bf16[176,1024]{1,0:T(8,128)(2,1)}, bf16[176,1024]{1,0:T(8,128)(2,1)}, u32[]{:S(2)}, u32[]{:S(2)}) collective-permute-start(bf16[176,1024]{1,0:T(8,128)(2,1)} %get-tuple-element.247), channel_id=1, source_target_pairs={{0,4},{4,0},{8,12},{12,8},{16,20},{20,16},{24,28},{28,24},{1,5},{5... | collective-permute-start | bytes 1081352 | tf_op jit(solution)/shard_map/ppermute | solution.py:793
  244.6 26.8 %collective-permute-start.34 = (bf16[2,256,1024]{2,1,0:T(8,128)(2,1)}, bf16[2,256,1024]{2,1,0:T(8,128)(2,1)}, u32[]{:S(2)}, u32[]{:S(2)}) collective-permute-start(bf16[2,256,1024]{2,1,0:T(8,128)(2,1)} %get-tuple-element.252), channel_id=1, source_target_pairs={{0,1},{1,0},{2,3},{3,2},{4,5},{5,4},{6,7},{7,6},{8,9},{9,8},{10,11... | collective-permute-start | bytes 3145736 | tf_op jit(solution)/shard_map/ppermute | solution.py:793
  247.4 26.5 %collective-permute-start.31 = (bf16[2,64,2816]{2,1,0:T(8,128)(2,1)}, bf16[2,64,2816]{2,1,0:T(8,128)(2,1)}, u32[]{:S(2)}, u32[]{:S(2)}) collective-permute-start(bf16[2,64,2816]{2,1,0:T(8,128)(2,1)} %get-tuple-element.253), channel_id=1, source_target_pairs={{0,8},{4,12},{8,0},{12,4},{16,24},{20,28},{24,16},{28,20},{1,9},{5... | collective-permute-start | bytes 2162696 | tf_op jit(solution)/shard_map/ppermute | solution.py:793
  264.4 26.0 %collective-permute-start.32 = (bf16[88,1024]{1,0:T(8,128)(2,1)S(1)}, bf16[88,1024]{1,0:T(8,128)(2,1)S(1)}, u32[]{:S(2)}, u32[]{:S(2)}) collective-permute-start(bf16[88,1024]{1,0:T(8,128)(2,1)S(1)} %get-tuple-element.256), channel_id=1, source_target_pairs={{0,16},{4,20},{8,24},{12,28},{16,0},{20,4},{24,8},{28,12},{1,17},{... | collective-permute-start | bytes 540680 | tf_op jit(solution)/shard_map/ppermute | solution.py:793
  269.9 36.6 %collective-permute-start.36 = (bf16[256,3072]{1,0:T(8,128)(2,1)}, bf16[256,3072]{1,0:T(8,128)(2,1)}, u32[]{:S(2)}, u32[]{:S(2)}) collective-permute-start(bf16[256,3072]{1,0:T(8,128)(2,1)} %collective-permute-done.21.refs_9_), channel_id=1, source_target_pairs={{0,1},{1,0},{2,3},{3,2},{4,5},{5,4},{6,7},{7,6},{8,9},{9,8},{10,11... | collective-permute-start | bytes 4718600 | tf_op jit(solution)/shard_map/ppermute | solution.py:793
  269.9 26.6 %collective-permute-start.29 = (bf16[320,1024]{1,0:T(8,128)(2,1)}, bf16[320,1024]{1,0:T(8,128)(2,1)}, u32[]{:S(2)}, u32[]{:S(2)}) collective-permute-start(bf16[320,1024]{1,0:T(8,128)(2,1)} %get-tuple-element.245), channel_id=1, source_target_pairs={{0,2},{1,3},{2,0},{3,1},{4,6},{5,7},{6,4},{7,5},{8,10},{9,11},{10,... | collective-permute-start | bytes 1966088 | tf_op jit(solution)/shard_map/ppermute | solution.py:793
  275.9 23.3 %collective-permute-start.33 = (bf16[2,32,2816]{2,1,0:T(8,128)(2,1)}, bf16[2,32,2816]{2,1,0:T(8,128)(2,1)S(1)}, u32[]{:S(2)}, u32[]{:S(2)}) collective-permute-start(bf16[2,32,2816]{2,1,0:T(8,128)(2,1)} %get-tuple-element.260), channel_id=1, source_target_pairs={{0,16},{4,20},{8,24},{12,28},{16,0},{20,4},{24,8},{28,12},{1,17},{... | collective-permute-start | bytes 1081352 | tf_op jit(solution)/shard_map/ppermute | solution.py:793
  276.2 27.6 %collective-permute-start.35 = (bf16[256,1024]{1,0:T(8,128)(2,1)}, bf16[256,1024]{1,0:T(8,128)(2,1)}, u32[]{:S(2)}, u32[]{:S(2)}) collective-permute-start(bf16[256,1024]{1,0:T(8,128)(2,1)} %get-tuple-element.264), channel_id=1, source_target_pairs={{0,2},{1,3},{2,0},{3,1},{4,6},{5,7},{6,4},{7,5},{8,10},{9,11},{10,... | collective-permute-start | bytes 1572872 | tf_op jit(solution)/shard_map/ppermute | solution.py:793
  292.4 50.2 %all-to-all-start.3 = ((bf16[8,2,160,128]{3,2,1,0:T(8,128)(2,1)}), bf16[8,2,160,128]{3,2,1,0:T(8,128)(2,1)S(1)}, u32[]{:S(2)}, u32[]{:S(2)}) async-start(bf16[8,2,160,128]{3,2,1,0:T(8,128)(2,1)} %pad_maximum_fusion.9), calls=%async_computation.3 | async-start | bytes 1310720 | tf_op jit(solution)/shard_map/all_to_all | solution.py:900
  299.2 20.4 %collective-permute-start.38 = (bf16[32,2816]{1,0:T(8,128)(2,1)S(1)}, bf16[32,2816]{1,0:T(8,128)(2,1)S(1)}, u32[]{:S(2)}, u32[]{:S(2)}) collective-permute-start(bf16[32,2816]{1,0:T(8,128)(2,1)S(1)} %slice_bitcast_fusion), channel_id=1, source_target_pairs={{0,2},{1,3},{2,0},{3,1},{4,6},{5,7},{6,4},{7,5},{8,10},{9,11},{10,... | collective-permute-start | bytes 540680 | tf_op jit(solution)/shard_map/ppermute | solution.py:793
  300.8 20.3 %collective-permute-start.37 = (bf16[88,1024]{1,0:T(8,128)(2,1)S(1)}, bf16[88,1024]{1,0:T(8,128)(2,1)S(1)}, u32[]{:S(2)}, u32[]{:S(2)}) collective-permute-start(bf16[88,1024]{1,0:T(8,128)(2,1)S(1)} %add_convert_fusion.14), channel_id=1, source_target_pairs={{0,16},{4,20},{8,24},{12,28},{16,0},{20,4},{24,8},{28,12},{1,17},{... | collective-permute-start | bytes 540680 | tf_op jit(solution)/shard_map/ppermute | solution.py:793
  321.1 16.8 %collective-permute-start.41 = (bf16[32,5632]{1,0:T(8,128)(2,1)S(1)}, bf16[32,5632]{1,0:T(8,128)(2,1)S(1)}, u32[]{:S(2)}, u32[]{:S(2)}) collective-permute-start(bf16[32,5632]{1,0:T(8,128)(2,1)S(1)} %pad_maximum_fusion.13), channel_id=1, source_target_pairs={{0,16},{4,20},{8,24},{12,28},{16,0},{20,4},{24,8},{28,12},{1,17},{... | collective-permute-start | bytes 1081352 | tf_op jit(solution)/shard_map/ppermute | solution.py:793
  321.2 19.7 %collective-permute-start.40 = (bf16[176,1024]{1,0:T(8,128)(2,1)S(1)}, bf16[176,1024]{1,0:T(8,128)(2,1)S(1)}, u32[]{:S(2)}, u32[]{:S(2)}) collective-permute-start(bf16[176,1024]{1,0:T(8,128)(2,1)S(1)} %pad_maximum_fusion.12), channel_id=1, source_target_pairs={{0,4},{4,0},{8,12},{12,8},{16,20},{20,16},{24,28},{28,24},{1,5},{5... | collective-permute-start | bytes 1081352 | tf_op jit(solution)/shard_map/ppermute | solution.py:793
  323.5 17.5 %collective-permute-start.43 = (bf16[64,1024]{1,0:T(8,128)(2,1)S(1)}, bf16[64,1024]{1,0:T(8,128)(2,1)S(1)}, u32[]{:S(2)}, u32[]{:S(2)}) collective-permute-start(bf16[64,1024]{1,0:T(8,128)(2,1)S(1)} %get-tuple-element.286), channel_id=1, source_target_pairs={{0,4},{4,0},{8,12},{12,8},{16,20},{20,16},{24,28},{28,24},{1,5},{5... | collective-permute-start | bytes 393224 | tf_op jit(solution)/shard_map/ppermute | solution.py:793
  338.1 26.9 %collective-permute-start.44 = (bf16[64,5632]{1,0:T(8,128)(2,1)S(1)}, bf16[64,5632]{1,0:T(8,128)(2,1)}, u32[]{:S(2)}, u32[]{:S(2)}) collective-permute-start(bf16[64,5632]{1,0:T(8,128)(2,1)S(1)} %pad_maximum_fusion.7), channel_id=1, source_target_pairs={{0,8},{4,12},{8,0},{12,4},{16,24},{20,28},{24,16},{28,20},{1,9},{5... | collective-permute-start | bytes 2162696 | tf_op jit(solution)/shard_map/ppermute | solution.py:793
  341.7 54.3 %collective-permute-start.46 = (bf16[352,1024]{1,0:T(8,128)(2,1)S(1)}, bf16[352,1024]{1,0:T(8,128)(2,1)}, u32[]{:S(2)}, u32[]{:S(2)}) collective-permute-start(bf16[352,1024]{1,0:T(8,128)(2,1)S(1)} %pad_maximum_fusion.6), channel_id=1, source_target_pairs={{0,8},{4,12},{8,0},{12,4},{16,24},{20,28},{24,16},{28,20},{1,9},{5... | collective-permute-start | bytes 2162696 | tf_op jit(solution)/shard_map/ppermute | solution.py:793
  342.6 74.9 %all-to-all-start.2 = ((bf16[8,640,128]{2,1,0:T(8,128)(2,1)}), bf16[8,640,128]{2,1,0:T(8,128)(2,1)S(1)}, u32[]{:S(2)}, u32[]{:S(2)}) async-start(bf16[8,640,128]{2,1,0:T(8,128)(2,1)} %pad_maximum_fusion.3), calls=%async_computation.2 | async-start | bytes 2621440 | tf_op jit(solution)/shard_map/all_to_all | solution.py:900
  366.3 26.2 %collective-permute-start.47 = (bf16[32,1024]{1,0:T(8,128)(2,1)S(1)}, bf16[32,1024]{1,0:T(8,128)(2,1)S(1)}, u32[]{:S(2)}, u32[]{:S(2)}) collective-permute-start(bf16[32,1024]{1,0:T(8,128)(2,1)S(1)} %add_convert_fusion.21), channel_id=1, source_target_pairs={{0,16},{4,20},{8,24},{12,28},{16,0},{20,4},{24,8},{28,12},{1,17},{... | collective-permute-start | bytes 196616 | tf_op jit(solution)/shard_map/ppermute | solution.py:793
  367.2 60.0 %collective-permute-start.54 = (bf16[128,5632]{1,0:T(8,128)(2,1)S(1)}, bf16[128,5632]{1,0:T(8,128)(2,1)}, u32[]{:S(2)}, u32[]{:S(2)}) collective-permute-start(bf16[128,5632]{1,0:T(8,128)(2,1)S(1)} %pad_maximum_fusion.2), channel_id=1, source_target_pairs={{0,4},{4,0},{8,12},{12,8},{16,20},{20,16},{24,28},{28,24},{1,5},{5... | collective-permute-start | bytes 4325384 | tf_op jit(solution)/shard_map/ppermute | solution.py:793
  369.0 31.3 %collective-permute-start.45 = (bf16[256,384]{1,0:T(8,128)(2,1)S(1)}, bf16[256,384]{1,0:T(8,128)(2,1)S(1)}, u32[]{:S(2)}, u32[]{:S(2)}) collective-permute-start(bf16[256,384]{1,0:T(8,128)(2,1)S(1)} %fusion.14), channel_id=1, source_target_pairs={{0,2},{1,3},{2,0},{3,1},{4,6},{5,7},{6,4},{7,5},{8,10},{9,11},{10,... | collective-permute-start | bytes 589832 | tf_op jit(solution)/shard_map/ppermute | solution.py:793
  417.7 15.2 %collective-permute-start.52 = (bf16[4,256,384]{2,1,0:T(8,128)(2,1)S(1)}, bf16[4,256,384]{2,1,0:T(8,128)(2,1)}, u32[]{:S(2)}, u32[]{:S(2)}) collective-permute-start(bf16[4,256,384]{2,1,0:T(8,128)(2,1)S(1)} %pad_maximum_fusion.4.own_ref), channel_id=1, source_target_pairs={{0,8},{4,12},{8,0},{12,4},{16,24},{20,28},{24,16},{28,20},{1,9},{5... | collective-permute-start | bytes 2359304 | tf_op jit(solution)/shard_map/ppermute | solution.py:793
  (50 other events, 485.3 us)

commit v6 on v5

--- a/solution.py
+++ b/solution.py
@@ -561,7 +561,7 @@
                 copy.start()
 
     width = wg.shape[1]
-    step_width = 256
+    step_width = 512
     whole = width // step_width
 
     def column_step(number, carry):

time: 446 us -> 442 us (level)
  no operation moved by 1% of the time
where the time goes in v6:
time: 442 us; the launch traced here: 435 us
  Pallas kernels  172 us (39%)
  waiting for transfers between devices  111 us (25%)
  starting transfers between devices  79.1 us (18%)
  other arithmetic  52.4 us (12%)
  local copies, waits for them, and re-layouts  17.8 us (4%)
    ppermute x50, waiting for transfers between devices, flip(): return lax.ppermute(values, axis, [(i, i ^ delta) for i in range(count)])  93.9 us
    pallas_call x4, Pallas kernels, attend_back(): pl.pallas_call(functools.partial(backward_kernel, heads, part, parts, til...  54.4 us
    ppermute x50, starting transfers between devices, flip(): return lax.ppermute(values, axis, [(i, i ^ delta) for i in range(count)])  52.7 us
    pallas_call x8, Pallas kernels, project(): pl.pallas_call(functools.partial(project_kernel, heads, segments, layout,...  35.1 us
    pallas_call x1, Pallas kernels, main_stage(): pl.pallas_call(functools.partial(main_kernel, groups, halves, entries, le...  28.8 us
    convert_element_type x14, other arithmetic, add_low(): return (a.astype(f32) + b.astype(f32)).astype(bf16)  20.8 us
    pallas_call x1, Pallas kernels, attend(): pl.pallas_call(functools.partial(forward_kernel, heads, tile_of(total)),...  20.6 us
    all_to_all x4, starting transfers between devices, turn(): lax.all_to_all(blocks, 'seq', split_axis=0, concat_axis=0, tiled=True)  19 us
  transfers between devices with their start and end apart: 59, of which 22 were waited for; matrix products, arithmetic and copies ran while one was open for 14% of the time, Pallas kernels for 30%

profile of v6, /device:TPU:0, one launch (start us, length us, event | category | flops | bytes accessed | tf_op | source)
XLA Modules:
  0.0 434.6 jit_solution(17655723130254478631)
XLA Ops:
  0.7 3.0 collective-permute-start.2
  16.5 3.8 collective-permute-done.8
  28.3 2.9 select_reduce_fusion
  33.2 4.4 %project.8 = (bf16[2,2560,128]{2,1,0:T(8,128)(2,1)}, bf16[2,2560,128]{2,1,0:T(8,128)(2,1)}, bf16[2,2560,128]{2,1,0:T(8,128)(2,1)}, bf16[2560,1024]{1,0:T(8,128)(2,1)}, f32[2,2560,128]{2,1,0:T(8,128)}) custom-call(s32[1]{0:T(128)} %bitcast.7.refs_0_, s32[4]{0:T(128)} %iota_xor_fusion.1.refs_1_.refs_0_.w_rows, bf16[320,1024]{1,0:T(8,128)(2,1)} %bitcast.94, ...), custom_call_target="tpu_custom_call" | custom-call | flops 251658240 | bytes 2359296 | tf_op jit(solution)/shard_map/project/pallas_call | solution.py:125
  37.5 4.5 %project.9 = (bf16[2,2560,128]{2,1,0:T(8,128)(2,1)}, bf16[2,2560,128]{2,1,0:T(8,128)(2,1)}, bf16[2,2560,128]{2,1,0:T(8,128)(2,1)}, bf16[2560,1024]{1,0:T(8,128)(2,1)}, f32[2,2560,128]{2,1,0:T(8,128)}) custom-call(s32[1]{0:T(128)} %bitcast.2.refs_0_, ...), custom_call_target="tpu_custom_call", output_to_operand_aliasing={{0}: (6, {}), {1}: (7, {}), {2}: (8, {}), {3}: (9, {}), {4}... | custom-call | flops 251658240 | bytes 2359296 | tf_op jit(solution)/shard_map/project/pallas_call | solution.py:125
  42.0 5.2 %collective-permute-done.4 = bf16[320,1024]{1,0:T(8,128)(2,1)} collective-permute-done((bf16[320,1024]{1,0:T(8,128)(2,1)}, bf16[320,1024]{1,0:T(8,128)(2,1)}, u32[]{:S(2)}, u32[]{:S(2)}) %collective-permute-start.4) | collective-permute-done | bytes 655392 | tf_op jit(solution)/shard_map/ppermute | solution.py:894
  52.2 4.4 %project.10 = (bf16[2,2560,128]{2,1,0:T(8,128)(2,1)}, bf16[2,2560,128]{2,1,0:T(8,128)(2,1)}, bf16[2,2560,128]{2,1,0:T(8,128)(2,1)}, bf16[2560,1024]{1,0:T(8,128)(2,1)}, f32[2,2560,128]{2,1,0:T(8,128)}) custom-call(s32[1]{0:T(128)} %bitcast.10.refs_0_, ...), custom_call_target="tpu_custom_call", output_to_operand_aliasing={{0}: (6, {}), {1}: (7, {}), {2}: (8, {}), {3}: (9, {}), {4}... | custom-call | flops 251658240 | bytes 2359296 | tf_op jit(solution)/shard_map/project/pallas_call | solution.py:125
  56.5 4.4 %project.11 = (bf16[2,2560,128]{2,1,0:T(8,128)(2,1)}, bf16[2,2560,128]{2,1,0:T(8,128)(2,1)}, bf16[2,2560,128]{2,1,0:T(8,128)(2,1)}, bf16[2560,1024]{1,0:T(8,128)(2,1)}, f32[2,2560,128]{2,1,0:T(8,128)}) custom-call(s32[1]{0:T(128)} %bitcast.9.refs_0_, ...), custom_call_target="tpu_custom_call", output_to_operand_aliasing={{0}: (6, {}), {1}: (7, {}), {2}: (8, {}), {3}: (9, {}), {4}... | custom-call | flops 251658240 | bytes 2359296 | tf_op jit(solution)/shard_map/project/pallas_call | solution.py:125
  60.9 4.4 %project.12 = (bf16[2,2560,128]{2,1,0:T(8,128)(2,1)}, bf16[2,2560,128]{2,1,0:T(8,128)(2,1)}, bf16[2,2560,128]{2,1,0:T(8,128)(2,1)}, bf16[2560,1024]{1,0:T(8,128)(2,1)}, f32[2,2560,128]{2,1,0:T(8,128)}) custom-call(s32[1]{0:T(128)} %bitcast.8.refs_0_, ...), custom_call_target="tpu_custom_call", output_to_operand_aliasing={{0}: (6, {}), {1}: (7, {}), {2}: (8, {}), {3}: (9, {}), {4}... | custom-call | flops 251658240 | bytes 2359296 | tf_op jit(solution)/shard_map/project/pallas_call | solution.py:125
  66.0 3.3 collective-permute-done.10
  74.4 4.4 %project.13 = (bf16[2,2560,128]{2,1,0:T(8,128)(2,1)}, bf16[2,2560,128]{2,1,0:T(8,128)(2,1)}, bf16[2,2560,128]{2,1,0:T(8,128)(2,1)}, bf16[2560,1024]{1,0:T(8,128)(2,1)}, f32[2,2560,128]{2,1,0:T(8,128)}) custom-call(s32[1]{0:T(128)} %bitcast.13.refs_0_, ...), custom_call_target="tpu_custom_call", output_to_operand_aliasing={{0}: (6, {}), {1}: (7, {}), {2}: (8, {}), {3}: (9, {}), {4}... | custom-call | flops 251658240 | bytes 2359296 | tf_op jit(solution)/shard_map/project/pallas_call | solution.py:125
  78.8 4.4 %project.14 = (bf16[2,2560,128]{2,1,0:T(8,128)(2,1)}, bf16[2,2560,128]{2,1,0:T(8,128)(2,1)}, bf16[2,2560,128]{2,1,0:T(8,128)(2,1)}, bf16[2560,1024]{1,0:T(8,128)(2,1)}, f32[2,2560,128]{2,1,0:T(8,128)}) custom-call(s32[1]{0:T(128)} %bitcast.12.refs_0_, ...), custom_call_target="tpu_custom_call", output_to_operand_aliasing={{0}: (6, {}), {1}: (7, {}), {2}: (8, {}), {3}: (9, {}), {4}... | custom-call | flops 251658240 | bytes 2359296 | tf_op jit(solution)/shard_map/project/pallas_call | solution.py:125
  83.1 5.1 %collective-permute-done.15.refs_5_ = bf16[320,1024]{1,0:T(8,128)(2,1)} collective-permute-done((bf16[320,1024]{1,0:T(8,128)(2,1)}, bf16[320,1024]{1,0:T(8,128)(2,1)}, u32[]{:S(2)}, u32[]{:S(2)}) %collective-permute-start.15) | collective-permute-done | bytes 655392 | tf_op jit(solution)/shard_map/ppermute | solution.py:793
  89.3 4.5 %project.15 = (bf16[2,2560,128]{2,1,0:T(8,128)(2,1)}, bf16[2,2560,128]{2,1,0:T(8,128)(2,1)}, bf16[2,2560,128]{2,1,0:T(8,128)(2,1)}, bf16[2560,1024]{1,0:T(8,128)(2,1)}, f32[2,2560,128]{2,1,0:T(8,128)}) custom-call(s32[1]{0:T(128)} %bitcast.refs_0_, ...), custom_call_target="tpu_custom_call", output_to_operand_aliasing={{0}: (6, {}), {1}: (7, {}), {2}: (8, {}), {3}: (9, {}), {4}... | custom-call | flops 251658240 | bytes 2359296 | tf_op jit(solution)/shard_map/project/pallas_call | solution.py:125
  94.9 20.6 %attend.1 = (bf16[8,2,160,128]{3,2,1,0:T(8,128)(2,1)}, f32[8,2,160,128]{3,2,1,0:T(8,128)}, bf16[2,8,2,160,128]{4,3,2,1,0:T(8,128)(2,1)}, bf16[2,8,2,160,128]{4,3,2,1,0:T(8,128)(2,1)}) custom-call(bf16[2,8,2,160,128]{4,3,2,1,0:T(8,128)(2,1)} %bitcast.80, f32[2,8,2,160,128]{4,3,2,1,0:T(8,128)} %bitcast.79, bf16[2,8,2,160,128]{4,3,2,1,0:T(8,128)(2,1)} %bitcast.85, ...), custom_call_target="tpu_custom_call" | custom-call | flops 13421772800 | bytes 2621440 | tf_op jit(solution)/shard_map/attend/pallas_call | solution.py:231
  117.1 4.4 %all-to-all-start = ((bf16[8,320,128]{2,1,0:T(8,128)(2,1)}), bf16[8,320,128]{2,1,0:T(8,128)(2,1)S(1)}, u32[]{:S(2)}, u32[]{:S(2)}) async-start(bf16[8,320,128]{2,1,0:T(8,128)(2,1)} %bitcast.100), calls=%async_computation | async-start | bytes 1310720 | tf_op jit(solution)/shard_map/all_to_all | solution.py:900
  124.8 6.4 %collective-permute-done.21.refs_9_ = bf16[256,3072]{1,0:T(8,128)(2,1)} collective-permute-done((bf16[256,3072]{1,0:T(8,128)(2,1)S(1)}, bf16[256,3072]{1,0:T(8,128)(2,1)}, u32[]{:S(2)}, u32[]{:S(2)}) %collective-permute-start.21) | collective-permute-done | bytes 1572896 | tf_op jit(solution)/shard_map/ppermute | solution.py:793
  131.2 7.9 %all-to-all-done.refs_1_ = bf16[8,320,128]{2,1,0:T(8,128)(2,1)S(1)} async-done(((bf16[8,320,128]{2,1,0:T(8,128)(2,1)}), bf16[8,320,128]{2,1,0:T(8,128)(2,1)S(1)}, u32[]{:S(2)}, u32[]{:S(2)}) %all-to-all-start) | async-done | bytes 655392 | tf_op jit(solution)/shard_map/all_to_all | solution.py:900
  139.9 5.3 %pre_stage.1 = (f32[320,1024]{1,0:T(8,128)}, bf16[320,1024]{1,0:T(8,128)(2,1)}, bf16[320,1024]{1,0:T(8,128)(2,1)}) custom-call(s32[4]{0:T(128)} %iota_xor_fusion.1.refs_1_.refs_0_.w_rows, bf16[8,320,128]{2,1,0:T(8,128)(2,1)} %copy-done.10, bf16[320,1024]{1,0:T(8,128)(2,1)} %bitcast.95, bf16[1,1024]{1,0:T(2,128)(2,1)} %get-tuple-element.372.refs_3_.refs_5_, ...), custom_call_target="tpu_custom_call" | custom-call | flops 671088640 | bytes 2097152 | tf_op jit(solution)/shard_map/pre_stage/pallas_call | solution.py:496
  147.2 13.6 %collective-permute-done.22.refs_3_ = bf16[320,1024]{1,0:T(8,128)(2,1)S(1)} collective-permute-done((bf16[320,1024]{1,0:T(8,128)(2,1)}, bf16[320,1024]{1,0:T(8,128)(2,1)S(1)}, u32[]{:S(2)}, u32[]{:S(2)}) %collective-permute-start.22) | collective-permute-done | bytes 655392 | tf_op jit(solution)/shard_map/ppermute | solution.py:793
  161.6 28.8 %main_stage.1 = (f32[320,1024]{1,0:T(8,128)}, bf16[320,1024]{1,0:T(8,128)(2,1)}, f32[320,1024]{1,0:T(8,128)}, bf16[320,1024]{1,0:T(8,128)(2,1)}, bf16[2,256,2816...) custom-call(s32[4]{0:T(128)} %iota_xor_fusion.1.refs_1_.refs_0_.w_ro, ...), custom_call_target="tpu_custom_call" | custom-call | flops 16609443840 | bytes 17301504 | tf_op jit(solution)/shard_map/main_stage/pallas_call | solution.py:599
  192.5 3.6 collective-permute-done.24
  196.1 4.4 %add_convert_fusion = (bf16[2,128,2816]{2,1,0:T(8,128)(2,1)}, bf16[2,128,2816]{2,1,0:T(8,128)(2,1)S(1)}) fusion(bf16[2,256,2816]{2,1,0:T(8,128)(2,1)} %collective-permute-done.24, s32[]{:T(128)S(6)} %select_n.376, bf16[2,256,2816]{2,1,0:T(8,128)(2,1)} %get-tuple-element.231, s32[]{:T(128)S(6)} %select_n.371), kind=kLoop, calls=%fused_computation.7 | loop fusion | flops 5767168 | bytes 8650760 | tf_op jit(solution)/shard_map/convert_element_type | solution.py:805
  202.4 3.5 fusion.3
  208.0 5.3 %post_stage.1 = (f32[320,1024]{1,0:T(8,128)}, bf16[320,1024]{1,0:T(8,128)(2,1)}, bf16[8,320,128]{2,1,0:T(8,128)(2,1)}) custom-call(s32[4]{0:T(128)} %iota_xor_fusion.1.refs_1_.refs_0_.w_rows, f32[320,1024]{1,0:T(8,128)} %get-tuple-element.222.refs_1_, f32[320,1024]{1,0:T(8,128)} %get-tuple-element.229.refs_2_, ...), custom_call_target="tpu_custom_call" | custom-call | flops 671088640 | bytes 4194304 | tf_op jit(solution)/shard_map/post_stage/pallas_call | solution.py:662
  213.6 5.5 %all-to-all-start.1 = ((bf16[8,320,128]{2,1,0:T(8,128)(2,1)}), bf16[8,320,128]{2,1,0:T(8,128)(2,1)}, u32[]{:S(2)}, u32[]{:S(2)}) async-start(bf16[8,320,128]{2,1,0:T(8,128)(2,1)} %get-tuple-element.237), calls=%async_computation.1 | async-start | bytes 1310720 | tf_op jit(solution)/shard_map/all_to_all | solution.py:900
  219.8 3.9 out_terms.1
  223.7 14.5 %collective-permute-done.26 = bf16[352,1024]{1,0:T(8,128)(2,1)} collective-permute-done((bf16[352,1024]{1,0:T(8,128)(2,1)}, bf16[352,1024]{1,0:T(8,128)(2,1)}, u32[]{:S(2)}, u32[]{:S(2)}) %collective-permute-start.26) | collective-permute-done | bytes 720928 | tf_op jit(solution)/shard_map/ppermute | solution.py:793
  240.6 2.8 add_convert_fusion.2
  244.3 14.8 %attend_back.4 = (bf16[8,2,80,128]{3,2,1,0:T(8,128)(2,1)}, f32[2,2560,128]{2,1,0:T(8,128)}, bf16[2,2560,128]{2,1,0:T(8,128)(2,1)}) custom-call(bf16[2,2560,128]{2,1,0:T(8,128)(2,1)} %bitcast.104, bf16[2,8,4,80,128]{4,3,2,1,0:T(8,128)(2,1)} %bitcast.81, bf16[2,8,4,80,128]{4,3,2,1,0:T(8,128)(2,1)} %bitcast.86, bf16[2,8,4,80,128]{4,3,2,1,0:T(8,128)(2,1)} %bitcast.108, ...), custom_call_target="tpu_custom_call" | custom-call | flops 8388608000 | bytes 7864320 | tf_op jit(solution)/shard_map/attend_back/pallas_call | solution.py:379
  260.3 5.5 %collective-permute-start.32 = (bf16[88,1024]{1,0:T(8,128)(2,1)S(1)}, bf16[88,1024]{1,0:T(8,128)(2,1)S(1)}, u32[]{:S(2)}, u32[]{:S(2)}) collective-permute-start(bf16[88,1024]{1,0:T(8,128)(2,1)S(1)} %get-tuple-element.256), channel_id=1, source_target_pairs={{0,16},{4,20},{8,24},{12,28},{16,0},{20,4},{24,8},{28,12},{1,17},{... | collective-permute-start | bytes 540680 | tf_op jit(solution)/shard_map/ppermute | solution.py:793
  272.6 13.7 %attend_back.5 = (bf16[8,2,80,128]{3,2,1,0:T(8,128)(2,1)}, f32[2,2560,128]{2,1,0:T(8,128)}) custom-call(bf16[2,2560,128]{2,1,0:T(8,128)(2,1)} %bitcast.105, bf16[2,8,4,80,128]{4,3,2,1,0:T(8,128)(2,1)} %bitcast.82, bf16[2,8,4,80,128]{4,3,2,1,0:T(8,128)(2,1)} %bitcast.87, bf16[2,8,4,80,128]{4,3,2,1,0:T(8,128)(2,1)} %bitcast.109, ...), custom_call_target="tpu_custom_call" | custom-call | flops 8388608000 | bytes 7864320 | tf_op jit(solution)/shard_map/attend_back/pallas_call | solution.py:379
  288.3 4.0 all-to-all-start.3
  292.4 2.7 fusion.6
  296.7 2.9 collective-permute-start.37
  302.4 13.2 %attend_back.6 = (bf16[8,2,80,128]{3,2,1,0:T(8,128)(2,1)}, f32[2,2560,128]{2,1,0:T(8,128)}) custom-call(bf16[2,2560,128]{2,1,0:T(8,128)(2,1)} %bitcast.106, bf16[2,8,4,80,128]{4,3,2,1,0:T(8,128)(2,1)} %bitcast.83, bf16[2,8,4,80,128]{4,3,2,1,0:T(8,128)(2,1)} %bitcast.88, bf16[2,8,4,80,128]{4,3,2,1,0:T(8,128)(2,1)} %bitcast.110, ...), custom_call_target="tpu_custom_call" | custom-call | flops 8388608000 | bytes 7864320 | tf_op jit(solution)/shard_map/attend_back/pallas_call | solution.py:379
  320.0 12.8 %attend_back.7 = (bf16[8,2,80,128]{3,2,1,0:T(8,128)(2,1)}, bf16[8,320,128]{2,1,0:T(8,128)(2,1)}) custom-call(bf16[2,2560,128]{2,1,0:T(8,128)(2,1)} %bitcast.107, bf16[2,8,4,80,128]{4,3,2,1,0:T(8,128)(2,1)} %bitcast.84, bf16[2,8,4,80,128]{4,3,2,1,0:T(8,128)(2,1)} %bitcast.89, bf16[2,8,4,80,128]{4,3,2,1,0:T(8,128)(2,1)} %bitcast.111, ...), custom_call_target="tpu_custom_call" | custom-call | flops 8388608000 | bytes 7864320 | tf_op jit(solution)/shard_map/attend_back/pallas_call | solution.py:379
  338.6 5.1 %all-to-all-start.2 = ((bf16[8,640,128]{2,1,0:T(8,128)(2,1)}), bf16[8,640,128]{2,1,0:T(8,128)(2,1)S(1)}, u32[]{:S(2)}, u32[]{:S(2)}) async-start(bf16[8,640,128]{2,1,0:T(8,128)(2,1)} %pad_maximum_fusion.3), calls=%async_computation.2 | async-start | bytes 2621440 | tf_op jit(solution)/shard_map/all_to_all | solution.py:900
  343.7 7.1 %own_terms.1 = (bf16[2,256,384]{2,1,0:T(8,128)(2,1)}, bf16[2,256,384]{2,1,0:T(8,128)(2,1)}) custom-call(s32[4]{0:T(128)} %iota_xor_fusion.1.refs_1_.refs_0_.w_rows, bf16[8,4,80,1024]{3,2,1,0:T(8,128)(2,1)} %bitcast.78, bf16[8,320,128]{2,1,0:T(8,128)(2,1)} %get-tuple-element.289.refs_2_, bf16[8,2,80,128]{3,2,1,0:T(8,128)(2,1)} %get-tuple-element.244.refs_3_, ...), custom_call_target="tpu_custom_call" | custom-call | flops 2013265920 | bytes 5242880 | tf_op jit(solution)/shard_map/own_terms/pallas_call | solution.py:428
  350.9 10.0 %collective-permute-done.44 = bf16[64,5632]{1,0:T(8,128)(2,1)} collective-permute-done((bf16[64,5632]{1,0:T(8,128)(2,1)S(1)}, bf16[64,5632]{1,0:T(8,128)(2,1)}, u32[]{:S(2)}, u32[]{:S(2)}) %collective-permute-start.44) | collective-permute-done | bytes 720928 | tf_op jit(solution)/shard_map/ppermute | solution.py:793
  366.5 22.0 %collective-permute-done.47 = bf16[32,1024]{1,0:T(8,128)(2,1)S(1)} collective-permute-done((bf16[32,1024]{1,0:T(8,128)(2,1)S(1)}, bf16[32,1024]{1,0:T(8,128)(2,1)S(1)}, u32[]{:S(2)}, u32[]{:S(2)}) %collective-permute-start.47) | collective-permute-done | bytes 65568 | tf_op jit(solution)/shard_map/ppermute | solution.py:793
  388.5 3.4 collective-permute-start.48
  396.3 3.1 collective-permute-start.49
  399.4 3.6 collective-permute-done.50
  410.6 2.8 collective-permute-done.51
  415.4 7.7 %last_stage.1 = f32[320,1024]{1,0:T(8,128)} custom-call(s32[4]{0:T(128)} %iota_xor_fusion.1.refs_1_.refs_0_.w_rows, bf16[8,320,128]{2,1,0:T(8,128)(2,1)} %get-tuple-element.342.refs_1_, bf16[8,2,160,128]{3,2,1,0:T(8,128)(2,1)} %copy-done.11, bf16[8,2,160,128]{3,2,1,0:T(8,128)(2,1)} %bitcast.98, bf16[320,1024]{1,0:T(8,128)(2,1)} %bitcast.96, ...), custom_call_target="tpu_custom_call" | custom-call | flops 2013265920 | bytes 6291456 | tf_op jit(solution)/shard_map/last_stage/pallas_call | solution.py:748
  425.4 2.9 multiply_reduce_fusion
  428.8 3.7 finish_own.1
  (255 shorter events, 102.7 us)
Async XLA Ops:
  0.7 22.6 %collective-permute-start.2 = (bf16[320,1024]{1,0:T(8,128)(2,1)}, bf16[320,1024]{1,0:T(8,128)(2,1)}, u32[]{:S(2)}, u32[]{:S(2)}) collective-permute-start(bf16[320,1024]{1,0:T(8,128)(2,1)} %bitcast.91), channel_id=1, source_target_pairs={{0,4},{4,0},{8,12},{12,8},{16,20},{20,16},{24,28},{28,24},{1,5},{5... | collective-permute-start | bytes 1966088 | tf_op jit(solution)/shard_map/ppermute | solution.py:793
  3.7 19.6 %collective-permute-start = (bf16[320,1024]{1,0:T(8,128)(2,1)}, bf16[320,1024]{1,0:T(8,128)(2,1)}, u32[]{:S(2)}, u32[]{:S(2)}) collective-permute-start(bf16[320,1024]{1,0:T(8,128)(2,1)} %bitcast.92), channel_id=1, source_target_pairs={{0,8},{4,12},{8,0},{12,4},{16,24},{20,28},{24,16},{28,20},{1,9},{5... | collective-permute-start | bytes 1966088 | tf_op jit(solution)/shard_map/ppermute | solution.py:894
  5.3 18.0 %collective-permute-start.1 = (bf16[320,1024]{1,0:T(8,128)(2,1)}, bf16[320,1024]{1,0:T(8,128)(2,1)}, u32[]{:S(2)}, u32[]{:S(2)}) collective-permute-start(bf16[320,1024]{1,0:T(8,128)(2,1)} %bitcast.93), channel_id=1, source_target_pairs={{8,16},{12,20},{16,8},{20,12},{9,17},{13,21},{17,9},{21,13},{10,18... | collective-permute-start | bytes 1966088 | tf_op jit(solution)/shard_map/ppermute | solution.py:894
  12.3 29.7 %collective-permute-start.7 = (bf16[256,1024]{1,0:T(8,128)(2,1)}, bf16[256,1024]{1,0:T(8,128)(2,1)S(1)}, u32[]{:S(2)}, u32[]{:S(2)}) collective-permute-start(bf16[256,1024]{1,0:T(8,128)(2,1)} %refs_6_.1), channel_id=1, source_target_pairs={{0,2},{1,3},{2,0},{3,1},{4,6},{5,7},{6,4},{7,5},{8,10},{9,11},{10,... | collective-permute-start | bytes 1572872 | tf_op jit(solution)/shard_map/ppermute | solution.py:793
  23.3 18.7 %collective-permute-start.5 = (bf16[320,1024]{1,0:T(8,128)(2,1)}, bf16[320,1024]{1,0:T(8,128)(2,1)}, u32[]{:S(2)}, u32[]{:S(2)}) collective-permute-start(bf16[320,1024]{1,0:T(8,128)(2,1)} %collective-permute-done.refs_2_), channel_id=1, source_target_pairs={{0,4},{4,0},{8,12},{12,8},{16,20},{20,16},{24,28},{28,24},{1,5},{5... | collective-permute-start | bytes 1966088 | tf_op jit(solution)/shard_map/ppermute | solution.py:793
  23.9 18.1 %collective-permute-start.3 = (bf16[320,1024]{1,0:T(8,128)(2,1)}, bf16[320,1024]{1,0:T(8,128)(2,1)}, u32[]{:S(2)}, u32[]{:S(2)}) collective-permute-start(bf16[320,1024]{1,0:T(8,128)(2,1)} %collective-permute-done.refs_2_), channel_id=1, source_target_pairs={{8,16},{12,20},{16,8},{20,12},{9,17},{13,21},{17,9},{21,13},{10,18... | collective-permute-start | bytes 1966088 | tf_op jit(solution)/shard_map/ppermute | solution.py:894
  25.4 21.8 %collective-permute-start.6 = (bf16[128,2816]{1,0:T(8,128)(2,1)}, bf16[128,2816]{1,0:T(8,128)(2,1)}, u32[]{:S(2)}, u32[]{:S(2)}) collective-permute-start(bf16[128,2816]{1,0:T(8,128)(2,1)} %get-tuple-element.165), channel_id=1, source_target_pairs={{0,2},{1,3},{2,0},{3,1},{4,6},{5,7},{6,4},{7,5},{8,10},{9,11},{10,... | collective-permute-start | bytes 2162696 | tf_op jit(solution)/shard_map/ppermute | solution.py:793
  27.0 20.3 %collective-permute-start.4 = (bf16[320,1024]{1,0:T(8,128)(2,1)}, bf16[320,1024]{1,0:T(8,128)(2,1)}, u32[]{:S(2)}, u32[]{:S(2)}) collective-permute-start(bf16[320,1024]{1,0:T(8,128)(2,1)} %collective-permute-done.1), channel_id=1, source_target_pairs={{8,0},{12,4},{16,24},{20,28},{9,1},{13,5},{17,25},{21,29},{10,2},{... | collective-permute-start | bytes 1966088 | tf_op jit(solution)/shard_map/ppermute | solution.py:894
  47.3 22.1 %collective-permute-start.13 = (bf16[256,2816]{1,0:T(8,128)(2,1)S(1)}, bf16[256,2816]{1,0:T(8,128)(2,1)}, u32[]{:S(2)}, u32[]{:S(2)}) collective-permute-start(bf16[256,2816]{1,0:T(8,128)(2,1)S(1)} %copy-done.19), channel_id=1, source_target_pairs={{0,1},{1,0},{2,3},{3,2},{4,5},{5,4},{6,7},{7,6},{8,9},{9,8},{10,11... | collective-permute-start | bytes 4325384 | tf_op jit(solution)/shard_map/ppermute | solution.py:793
  47.3 22.1 %collective-permute-start.12 = (bf16[128,2816]{1,0:T(8,128)(2,1)S(1)}, bf16[128,2816]{1,0:T(8,128)(2,1)}, u32[]{:S(2)}, u32[]{:S(2)}) collective-permute-start(bf16[128,2816]{1,0:T(8,128)(2,1)S(1)} %copy-done.22), channel_id=1, source_target_pairs={{0,2},{1,3},{2,0},{3,1},{4,6},{5,7},{6,4},{7,5},{8,10},{9,11},{10,... | collective-permute-start | bytes 2162696 | tf_op jit(solution)/shard_map/ppermute | solution.py:793
  49.1 17.0 %collective-permute-start.11 = (bf16[320,1024]{1,0:T(8,128)(2,1)S(1)}, bf16[320,1024]{1,0:T(8,128)(2,1)}, u32[]{:S(2)}, u32[]{:S(2)}) collective-permute-start(bf16[320,1024]{1,0:T(8,128)(2,1)S(1)} %broadcast_select_fusion.7.refs_2_), channel_id=1, source_target_pairs={{0,4},{4,0},{8,12},{12,8},{16,20},{20,16},{24,28},{28,24},{1,5},{5... | collective-permute-start | bytes 1966088 | tf_op jit(solution)/shard_map/ppermute | solution.py:793
  50.7 18.7 %collective-permute-start.10 = (bf16[320,1024]{1,0:T(8,128)(2,1)}, bf16[320,1024]{1,0:T(8,128)(2,1)}, u32[]{:S(2)}, u32[]{:S(2)}) collective-permute-start(bf16[320,1024]{1,0:T(8,128)(2,1)} %collective-permute-done.3), channel_id=1, source_target_pairs={{8,0},{12,4},{16,24},{20,28},{9,1},{13,5},{17,25},{21,29},{10,2},{... | collective-permute-start | bytes 1966088 | tf_op jit(solution)/shard_map/ppermute | solution.py:894
  70.6 18.6 %collective-permute-start.17 = (bf16[704,1024]{1,0:T(8,128)(2,1)}, bf16[704,1024]{1,0:T(8,128)(2,1)}, u32[]{:S(2)}, u32[]{:S(2)}) collective-permute-start(bf16[704,1024]{1,0:T(8,128)(2,1)} %refs_12_.1), channel_id=1, source_target_pairs={{0,1},{1,0},{2,3},{3,2},{4,5},{5,4},{6,7},{7,6},{8,9},{9,8},{10,11... | collective-permute-start | bytes 4325384 | tf_op jit(solution)/shard_map/ppermute | solution.py:793
  70.7 18.5 %collective-permute-start.16 = (bf16[128,2816]{1,0:T(8,128)(2,1)}, bf16[128,2816]{1,0:T(8,128)(2,1)}, u32[]{:S(2)}, u32[]{:S(2)}) collective-permute-start(bf16[128,2816]{1,0:T(8,128)(2,1)} %collective-permute-done.6.refs_8_), channel_id=1, source_target_pairs={{0,1},{1,0},{2,3},{3,2},{4,5},{5,4},{6,7},{7,6},{8,9},{9,8},{10,11... | collective-permute-start | bytes 2162696 | tf_op jit(solution)/shard_map/ppermute | solution.py:793
  71.2 17.0 %collective-permute-start.15 = (bf16[320,1024]{1,0:T(8,128)(2,1)}, bf16[320,1024]{1,0:T(8,128)(2,1)}, u32[]{:S(2)}, u32[]{:S(2)}) collective-permute-start(bf16[320,1024]{1,0:T(8,128)(2,1)} %bitcast.11.refs_4_), channel_id=1, source_target_pairs={{0,2},{1,3},{2,0},{3,1},{4,6},{5,7},{6,4},{7,5},{8,10},{9,11},{10,... | collective-permute-start | bytes 1966088 | tf_op jit(solution)/shard_map/ppermute | solution.py:793
  72.7 16.5 %collective-permute-start.14 = (bf16[320,1024]{1,0:T(8,128)(2,1)S(1)}, bf16[320,1024]{1,0:T(8,128)(2,1)}, u32[]{:S(2)}, u32[]{:S(2)}) collective-permute-start(bf16[320,1024]{1,0:T(8,128)(2,1)S(1)} %broadcast_select_fusion.6.refs_2_), channel_id=1, source_target_pairs={{0,4},{4,0},{8,12},{12,8},{16,20},{20,16},{24,28},{28,24},{1,5},{5... | collective-permute-start | bytes 1966088 | tf_op jit(solution)/shard_map/ppermute | solution.py:793
  93.8 22.5 %collective-permute-start.18 = (bf16[128,2816]{1,0:T(8,128)(2,1)}, bf16[128,2816]{1,0:T(8,128)(2,1)}, u32[]{:S(2)}, u32[]{:S(2)}) collective-permute-start(bf16[128,2816]{1,0:T(8,128)(2,1)} %collective-permute-done.12.refs_9_), channel_id=1, source_target_pairs={{0,1},{1,0},{2,3},{3,2},{4,5},{5,4},{6,7},{7,6},{8,9},{9,8},{10,11... | collective-permute-start | bytes 2162696 | tf_op jit(solution)/shard_map/ppermute | solution.py:793
  93.8 21.7 %collective-permute-start.20 = (bf16[256,1024]{1,0:T(8,128)(2,1)S(1)}, bf16[256,1024]{1,0:T(8,128)(2,1)S(1)}, u32[]{:S(2)}, u32[]{:S(2)}) collective-permute-start(bf16[256,1024]{1,0:T(8,128)(2,1)S(1)} %copy-done.16), channel_id=1, source_target_pairs={{0,1},{1,0},{2,3},{3,2},{4,5},{5,4},{6,7},{7,6},{8,9},{9,8},{10,11... | collective-permute-start | bytes 1572872 | tf_op jit(solution)/shard_map/ppermute | solution.py:793
  94.3 21.2 %collective-permute-start.19 = (bf16[256,1024]{1,0:T(8,128)(2,1)S(1)}, bf16[256,1024]{1,0:T(8,128)(2,1)S(1)}, u32[]{:S(2)}, u32[]{:S(2)}) collective-permute-start(bf16[256,1024]{1,0:T(8,128)(2,1)S(1)} %copy-done.14), channel_id=1, source_target_pairs={{0,1},{1,0},{2,3},{3,2},{4,5},{5,4},{6,7},{7,6},{8,9},{9,8},{10,11... | collective-permute-start | bytes 1572872 | tf_op jit(solution)/shard_map/ppermute | solution.py:793
  94.3 36.8 %collective-permute-start.21 = (bf16[256,3072]{1,0:T(8,128)(2,1)S(1)}, bf16[256,3072]{1,0:T(8,128)(2,1)}, u32[]{:S(2)}, u32[]{:S(2)}) collective-permute-start(bf16[256,3072]{1,0:T(8,128)(2,1)S(1)} %constant_dynamic-update-slice_fusion.refs_7_.w_ref), channel_id=1, source_target_pairs={{0,2},{1,3},{2,0},{3,1},{4,6},{5,7},{6,4},{7,5},{8,10},{9,11},{10,... | collective-permute-start | bytes 4718600 | tf_op jit(solution)/shard_map/ppermute | solution.py:793
  117.1 22.0 %all-to-all-start = ((bf16[8,320,128]{2,1,0:T(8,128)(2,1)}), bf16[8,320,128]{2,1,0:T(8,128)(2,1)S(1)}, u32[]{:S(2)}, u32[]{:S(2)}) async-start(bf16[8,320,128]{2,1,0:T(8,128)(2,1)} %bitcast.100), calls=%async_computation | async-start | bytes 1310720 | tf_op jit(solution)/shard_map/all_to_all | solution.py:900
  145.2 15.6 %collective-permute-start.22 = (bf16[320,1024]{1,0:T(8,128)(2,1)}, bf16[320,1024]{1,0:T(8,128)(2,1)S(1)}, u32[]{:S(2)}, u32[]{:S(2)}) collective-permute-start(bf16[320,1024]{1,0:T(8,128)(2,1)} %get-tuple-element.223.refs_2_), channel_id=1, source_target_pairs={{0,2},{1,3},{2,0},{3,1},{4,6},{5,7},{6,4},{7,5},{8,10},{9,11},{10,... | collective-permute-start | bytes 1966088 | tf_op jit(solution)/shard_map/ppermute | solution.py:793
  191.0 17.0 %collective-permute-start.23 = (bf16[320,1024]{1,0:T(8,128)(2,1)}, bf16[320,1024]{1,0:T(8,128)(2,1)}, u32[]{:S(2)}, u32[]{:S(2)}) collective-permute-start(bf16[320,1024]{1,0:T(8,128)(2,1)} %get-tuple-element.230), channel_id=1, source_target_pairs={{0,2},{1,3},{2,0},{3,1},{4,6},{5,7},{6,4},{7,5},{8,10},{9,11},{10,... | collective-permute-start | bytes 1966088 | tf_op jit(solution)/shard_map/ppermute | solution.py:793
  200.6 40.0 %collective-permute-start.27 = (bf16[2,128,2816]{2,1,0:T(8,128)(2,1)}, bf16[2,128,2816]{2,1,0:T(8,128)(2,1)}, u32[]{:S(2)}, u32[]{:S(2)}) collective-permute-start(bf16[2,128,2816]{2,1,0:T(8,128)(2,1)} %get-tuple-element.238), channel_id=1, source_target_pairs={{0,4},{4,0},{8,12},{12,8},{16,20},{20,16},{24,28},{28,24},{1,5},{5... | collective-permute-start | bytes 4325384 | tf_op jit(solution)/shard_map/ppermute | solution.py:793
  213.4 30.9 %collective-permute-start.28 = (bf16[256,3072]{1,0:T(8,128)(2,1)S(1)}, bf16[256,3072]{1,0:T(8,128)(2,1)}, u32[]{:S(2)}, u32[]{:S(2)}) collective-permute-start(bf16[256,3072]{1,0:T(8,128)(2,1)S(1)} %constant_dynamic-update-slice_fusion.refs_7_.w_ref), channel_id=1, source_target_pairs={{0,1},{1,0},{2,3},{3,2},{4,5},{5,4},{6,7},{7,6},{8,9},{9,8},{10,11... | collective-permute-start | bytes 4718600 | tf_op jit(solution)/shard_map/ppermute | solution.py:793
  213.5 24.7 %collective-permute-start.26 = (bf16[352,1024]{1,0:T(8,128)(2,1)}, bf16[352,1024]{1,0:T(8,128)(2,1)}, u32[]{:S(2)}, u32[]{:S(2)}) collective-permute-start(bf16[352,1024]{1,0:T(8,128)(2,1)} %get-tuple-element.239), channel_id=1, source_target_pairs={{0,8},{4,12},{8,0},{12,4},{16,24},{20,28},{24,16},{28,20},{1,9},{5... | collective-permute-start | bytes 2162696 | tf_op jit(solution)/shard_map/ppermute | solution.py:793
  213.6 30.7 %all-to-all-start.1 = ((bf16[8,320,128]{2,1,0:T(8,128)(2,1)}), bf16[8,320,128]{2,1,0:T(8,128)(2,1)}, u32[]{:S(2)}, u32[]{:S(2)}) async-start(bf16[8,320,128]{2,1,0:T(8,128)(2,1)} %get-tuple-element.237), calls=%async_computation.1 | async-start | bytes 1310720 | tf_op jit(solution)/shard_map/all_to_all | solution.py:900
  240.5 18.6 %collective-permute-start.30 = (bf16[176,1024]{1,0:T(8,128)(2,1)}, bf16[176,1024]{1,0:T(8,128)(2,1)}, u32[]{:S(2)}, u32[]{:S(2)}) collective-permute-start(bf16[176,1024]{1,0:T(8,128)(2,1)} %get-tuple-element.247), channel_id=1, source_target_pairs={{0,4},{4,0},{8,12},{12,8},{16,20},{20,16},{24,28},{28,24},{1,5},{5... | collective-permute-start | bytes 1081352 | tf_op jit(solution)/shard_map/ppermute | solution.py:793
  240.6 26.8 %collective-permute-start.34 = (bf16[2,256,1024]{2,1,0:T(8,128)(2,1)}, bf16[2,256,1024]{2,1,0:T(8,128)(2,1)}, u32[]{:S(2)}, u32[]{:S(2)}) collective-permute-start(bf16[2,256,1024]{2,1,0:T(8,128)(2,1)} %get-tuple-element.252), channel_id=1, source_target_pairs={{0,1},{1,0},{2,3},{3,2},{4,5},{5,4},{6,7},{7,6},{8,9},{9,8},{10,11... | collective-permute-start | bytes 3145736 | tf_op jit(solution)/shard_map/ppermute | solution.py:793
  243.3 26.5 %collective-permute-start.31 = (bf16[2,64,2816]{2,1,0:T(8,128)(2,1)}, bf16[2,64,2816]{2,1,0:T(8,128)(2,1)}, u32[]{:S(2)}, u32[]{:S(2)}) collective-permute-start(bf16[2,64,2816]{2,1,0:T(8,128)(2,1)} %get-tuple-element.253), channel_id=1, source_target_pairs={{0,8},{4,12},{8,0},{12,4},{16,24},{20,28},{24,16},{28,20},{1,9},{5... | collective-permute-start | bytes 2162696 | tf_op jit(solution)/shard_map/ppermute | solution.py:793
  260.3 26.0 %collective-permute-start.32 = (bf16[88,1024]{1,0:T(8,128)(2,1)S(1)}, bf16[88,1024]{1,0:T(8,128)(2,1)S(1)}, u32[]{:S(2)}, u32[]{:S(2)}) collective-permute-start(bf16[88,1024]{1,0:T(8,128)(2,1)S(1)} %get-tuple-element.256), channel_id=1, source_target_pairs={{0,16},{4,20},{8,24},{12,28},{16,0},{20,4},{24,8},{28,12},{1,17},{... | collective-permute-start | bytes 540680 | tf_op jit(solution)/shard_map/ppermute | solution.py:793
  265.8 36.6 %collective-permute-start.36 = (bf16[256,3072]{1,0:T(8,128)(2,1)}, bf16[256,3072]{1,0:T(8,128)(2,1)}, u32[]{:S(2)}, u32[]{:S(2)}) collective-permute-start(bf16[256,3072]{1,0:T(8,128)(2,1)} %collective-permute-done.21.refs_9_), channel_id=1, source_target_pairs={{0,1},{1,0},{2,3},{3,2},{4,5},{5,4},{6,7},{7,6},{8,9},{9,8},{10,11... | collective-permute-start | bytes 4718600 | tf_op jit(solution)/shard_map/ppermute | solution.py:793
  265.8 26.6 %collective-permute-start.29 = (bf16[320,1024]{1,0:T(8,128)(2,1)}, bf16[320,1024]{1,0:T(8,128)(2,1)}, u32[]{:S(2)}, u32[]{:S(2)}) collective-permute-start(bf16[320,1024]{1,0:T(8,128)(2,1)} %get-tuple-element.245), channel_id=1, source_target_pairs={{0,2},{1,3},{2,0},{3,1},{4,6},{5,7},{6,4},{7,5},{8,10},{9,11},{10,... | collective-permute-start | bytes 1966088 | tf_op jit(solution)/shard_map/ppermute | solution.py:793
  271.8 23.3 %collective-permute-start.33 = (bf16[2,32,2816]{2,1,0:T(8,128)(2,1)}, bf16[2,32,2816]{2,1,0:T(8,128)(2,1)S(1)}, u32[]{:S(2)}, u32[]{:S(2)}) collective-permute-start(bf16[2,32,2816]{2,1,0:T(8,128)(2,1)} %get-tuple-element.260), channel_id=1, source_target_pairs={{0,16},{4,20},{8,24},{12,28},{16,0},{20,4},{24,8},{28,12},{1,17},{... | collective-permute-start | bytes 1081352 | tf_op jit(solution)/shard_map/ppermute | solution.py:793
  272.1 27.6 %collective-permute-start.35 = (bf16[256,1024]{1,0:T(8,128)(2,1)}, bf16[256,1024]{1,0:T(8,128)(2,1)}, u32[]{:S(2)}, u32[]{:S(2)}) collective-permute-start(bf16[256,1024]{1,0:T(8,128)(2,1)} %get-tuple-element.264), channel_id=1, source_target_pairs={{0,2},{1,3},{2,0},{3,1},{4,6},{5,7},{6,4},{7,5},{8,10},{9,11},{10,... | collective-permute-start | bytes 1572872 | tf_op jit(solution)/shard_map/ppermute | solution.py:793
  288.3 50.2 %all-to-all-start.3 = ((bf16[8,2,160,128]{3,2,1,0:T(8,128)(2,1)}), bf16[8,2,160,128]{3,2,1,0:T(8,128)(2,1)S(1)}, u32[]{:S(2)}, u32[]{:S(2)}) async-start(bf16[8,2,160,128]{3,2,1,0:T(8,128)(2,1)} %pad_maximum_fusion.9), calls=%async_computation.3 | async-start | bytes 1310720 | tf_op jit(solution)/shard_map/all_to_all | solution.py:900
  295.2 20.4 %collective-permute-start.38 = (bf16[32,2816]{1,0:T(8,128)(2,1)S(1)}, bf16[32,2816]{1,0:T(8,128)(2,1)S(1)}, u32[]{:S(2)}, u32[]{:S(2)}) collective-permute-start(bf16[32,2816]{1,0:T(8,128)(2,1)S(1)} %slice_bitcast_fusion), channel_id=1, source_target_pairs={{0,2},{1,3},{2,0},{3,1},{4,6},{5,7},{6,4},{7,5},{8,10},{9,11},{10,... | collective-permute-start | bytes 540680 | tf_op jit(solution)/shard_map/ppermute | solution.py:793
  296.7 20.3 %collective-permute-start.37 = (bf16[88,1024]{1,0:T(8,128)(2,1)S(1)}, bf16[88,1024]{1,0:T(8,128)(2,1)S(1)}, u32[]{:S(2)}, u32[]{:S(2)}) collective-permute-start(bf16[88,1024]{1,0:T(8,128)(2,1)S(1)} %add_convert_fusion.14), channel_id=1, source_target_pairs={{0,16},{4,20},{8,24},{12,28},{16,0},{20,4},{24,8},{28,12},{1,17},{... | collective-permute-start | bytes 540680 | tf_op jit(solution)/shard_map/ppermute | solution.py:793
  317.1 16.8 %collective-permute-start.41 = (bf16[32,5632]{1,0:T(8,128)(2,1)S(1)}, bf16[32,5632]{1,0:T(8,128)(2,1)S(1)}, u32[]{:S(2)}, u32[]{:S(2)}) collective-permute-start(bf16[32,5632]{1,0:T(8,128)(2,1)S(1)} %pad_maximum_fusion.13), channel_id=1, source_target_pairs={{0,16},{4,20},{8,24},{12,28},{16,0},{20,4},{24,8},{28,12},{1,17},{... | collective-permute-start | bytes 1081352 | tf_op jit(solution)/shard_map/ppermute | solution.py:793
  317.2 19.7 %collective-permute-start.40 = (bf16[176,1024]{1,0:T(8,128)(2,1)S(1)}, bf16[176,1024]{1,0:T(8,128)(2,1)S(1)}, u32[]{:S(2)}, u32[]{:S(2)}) collective-permute-start(bf16[176,1024]{1,0:T(8,128)(2,1)S(1)} %pad_maximum_fusion.12), channel_id=1, source_target_pairs={{0,4},{4,0},{8,12},{12,8},{16,20},{20,16},{24,28},{28,24},{1,5},{5... | collective-permute-start | bytes 1081352 | tf_op jit(solution)/shard_map/ppermute | solution.py:793
  319.4 17.5 %collective-permute-start.43 = (bf16[64,1024]{1,0:T(8,128)(2,1)S(1)}, bf16[64,1024]{1,0:T(8,128)(2,1)S(1)}, u32[]{:S(2)}, u32[]{:S(2)}) collective-permute-start(bf16[64,1024]{1,0:T(8,128)(2,1)S(1)} %get-tuple-element.286), channel_id=1, source_target_pairs={{0,4},{4,0},{8,12},{12,8},{16,20},{20,16},{24,28},{28,24},{1,5},{5... | collective-permute-start | bytes 393224 | tf_op jit(solution)/shard_map/ppermute | solution.py:793
  334.0 26.9 %collective-permute-start.44 = (bf16[64,5632]{1,0:T(8,128)(2,1)S(1)}, bf16[64,5632]{1,0:T(8,128)(2,1)}, u32[]{:S(2)}, u32[]{:S(2)}) collective-permute-start(bf16[64,5632]{1,0:T(8,128)(2,1)S(1)} %pad_maximum_fusion.7), channel_id=1, source_target_pairs={{0,8},{4,12},{8,0},{12,4},{16,24},{20,28},{24,16},{28,20},{1,9},{5... | collective-permute-start | bytes 2162696 | tf_op jit(solution)/shard_map/ppermute | solution.py:793
  337.6 54.3 %collective-permute-start.46 = (bf16[352,1024]{1,0:T(8,128)(2,1)S(1)}, bf16[352,1024]{1,0:T(8,128)(2,1)}, u32[]{:S(2)}, u32[]{:S(2)}) collective-permute-start(bf16[352,1024]{1,0:T(8,128)(2,1)S(1)} %pad_maximum_fusion.6), channel_id=1, source_target_pairs={{0,8},{4,12},{8,0},{12,4},{16,24},{20,28},{24,16},{28,20},{1,9},{5... | collective-permute-start | bytes 2162696 | tf_op jit(solution)/shard_map/ppermute | solution.py:793
  338.6 74.9 %all-to-all-start.2 = ((bf16[8,640,128]{2,1,0:T(8,128)(2,1)}), bf16[8,640,128]{2,1,0:T(8,128)(2,1)S(1)}, u32[]{:S(2)}, u32[]{:S(2)}) async-start(bf16[8,640,128]{2,1,0:T(8,128)(2,1)} %pad_maximum_fusion.3), calls=%async_computation.2 | async-start | bytes 2621440 | tf_op jit(solution)/shard_map/all_to_all | solution.py:900
  362.2 26.2 %collective-permute-start.47 = (bf16[32,1024]{1,0:T(8,128)(2,1)S(1)}, bf16[32,1024]{1,0:T(8,128)(2,1)S(1)}, u32[]{:S(2)}, u32[]{:S(2)}) collective-permute-start(bf16[32,1024]{1,0:T(8,128)(2,1)S(1)} %add_convert_fusion.21), channel_id=1, source_target_pairs={{0,16},{4,20},{8,24},{12,28},{16,0},{20,4},{24,8},{28,12},{1,17},{... | collective-permute-start | bytes 196616 | tf_op jit(solution)/shard_map/ppermute | solution.py:793
  363.2 60.0 %collective-permute-start.54 = (bf16[128,5632]{1,0:T(8,128)(2,1)S(1)}, bf16[128,5632]{1,0:T(8,128)(2,1)}, u32[]{:S(2)}, u32[]{:S(2)}) collective-permute-start(bf16[128,5632]{1,0:T(8,128)(2,1)S(1)} %pad_maximum_fusion.2), channel_id=1, source_target_pairs={{0,4},{4,0},{8,12},{12,8},{16,20},{20,16},{24,28},{28,24},{1,5},{5... | collective-permute-start | bytes 4325384 | tf_op jit(solution)/shard_map/ppermute | solution.py:793
  365.0 31.3 %collective-permute-start.45 = (bf16[256,384]{1,0:T(8,128)(2,1)S(1)}, bf16[256,384]{1,0:T(8,128)(2,1)S(1)}, u32[]{:S(2)}, u32[]{:S(2)}) collective-permute-start(bf16[256,384]{1,0:T(8,128)(2,1)S(1)} %fusion.14), channel_id=1, source_target_pairs={{0,2},{1,3},{2,0},{3,1},{4,6},{5,7},{6,4},{7,5},{8,10},{9,11},{10,... | collective-permute-start | bytes 589832 | tf_op jit(solution)/shard_map/ppermute | solution.py:793
  413.6 15.2 %collective-permute-start.52 = (bf16[4,256,384]{2,1,0:T(8,128)(2,1)S(1)}, bf16[4,256,384]{2,1,0:T(8,128)(2,1)}, u32[]{:S(2)}, u32[]{:S(2)}) collective-permute-start(bf16[4,256,384]{2,1,0:T(8,128)(2,1)S(1)} %pad_maximum_fusion.4.own_ref), channel_id=1, source_target_pairs={{0,8},{4,12},{8,0},{12,4},{16,24},{20,28},{24,16},{28,20},{1,9},{5... | collective-permute-start | bytes 2359304 | tf_op jit(solution)/shard_map/ppermute | solution.py:793
  (50 other events, 481.2 us)
